TPU v7x, 128 devices: a whole 4x4x4 slice. The times are simulated.
128 devices in a mesh: chan: 8 (over x, z_lo), facet: 16 (over y, z_hi, core).
Axes of the slice: x: 4, y: 4, z: 4 (z_hi: 2, z_lo: 2; z = z_hi * 2 + z_lo), core: 2. Of those that a mesh axis runs over, the one named last changes fastest.
Arguments:
- image_field: float32 [8, 2048, 2048], P('chan', 'facet'), may hold values from -6 to 6
- weights: bfloat16 [8, 2048, 2048], P('chan', None, 'facet'), may hold values from 0.049804688 to 1
- measured: bfloat16 [8, 2, 2048, 2048], P('chan', None, None, 'facet'), may hold values from -6 to 6
- dual_field: bfloat16 [8, 2, 2048, 2048], P(None, None, 'facet', 'chan'), may hold values from -3 to 3
Outputs:
- image_next: float32 [8, 2048, 2048], P(None, 'facet', 'chan')
- dual_next: bfloat16 [8, 2, 2048, 2048], P(None, None, 'facet', 'chan')
All inputs are finite; a program needn't handle non-finite values.
Results may differ from a plain program's by a relative error of at most 0.001.
Values sent between devices are 32-bit elements; how exact they have to be, the bound alone decides.
No kernel may reach another device: no remote copies, remote signals or barrier semaphores. Data moves between devices by JAX's collectives and lax.ppermute only.
A program may use at most 64 MiB of HBM per device.

v0:
```python
from functools import partial
import math

import jax
import jax.numpy as jnp
import ml_dtypes
import numpy as np
from jax import lax
from jax.experimental import pallas as pl
from jax.experimental.pallas import tpu as pltpu
from jax.sharding import PartitionSpec as P

GRID = 2048
RADIX = 16
LANES = 128
CHANNELS = 8

step_primal = 0.5
step_dual = 0.5
clip_radius = 4.0

PARAMS = pltpu.CompilerParams(vmem_limit_bytes=48 * 1024 * 1024)


def host_tables():
    index = np.arange(LANES)
    angle = 2.0 * np.pi * (index[:, None] * index[None, :] % LANES) / LANES
    cos, sin = np.cos(angle), np.sin(angle)
    forward = np.block([[cos, -sin], [sin, cos]])
    inverse = np.block([[cos, sin], [-sin, cos]])
    turn = 2.0 * np.pi * np.arange(RADIX)[:, None] * index[None, :] / GRID
    twiddle = np.stack([np.cos(turn), np.sin(turn)]).astype(np.float32)
    place = np.zeros((LANES, LANES))
    for at in range(LANES):
        place[at, 16 * (at % 8) + at // 8] = 1.0
    return forward, inverse, twiddle, place


def halves(table):
    high = table.astype(ml_dtypes.bfloat16)
    low = (table - high.astype(np.float64)).astype(ml_dtypes.bfloat16)
    return np.stack([high, low])


def c_add(a, b):
    return (a[0] + b[0], b[1] if a[1] is None else a[1] if b[1] is None else a[1] + b[1])


def c_sub(a, b):
    imag = None
    if a[1] is not None and b[1] is not None:
        imag = a[1] - b[1]
    elif a[1] is not None:
        imag = a[1]
    elif b[1] is not None:
        imag = -b[1]
    return (a[0] - b[0], imag)


def add_turned(a, b, sign):
    real = a[0] if b[1] is None else (a[0] - b[1] if sign > 0 else a[0] + b[1])
    if a[1] is None:
        imag = b[0] if sign > 0 else -b[0]
    else:
        imag = a[1] + b[0] if sign > 0 else a[1] - b[0]
    return (real, imag)


def four(a, b, c, d, sign):
    sum_even, diff_even = c_add(a, c), c_sub(a, c)
    sum_odd, diff_odd = c_add(b, d), c_sub(b, d)
    return (
        c_add(sum_even, sum_odd),
        add_turned(diff_even, diff_odd, sign),
        c_sub(sum_even, sum_odd),
        add_turned(diff_even, diff_odd, -sign),
    )


def turned(a, power, sign):
    power = power % 16
    if power == 0:
        return a
    cos, sin = math.cos(2 * math.pi * power / 16), sign * math.sin(2 * math.pi * power / 16)
    real, imag = a
    if imag is None:
        if power == 4:
            return (jnp.zeros_like(real), real if sign > 0 else -real)
        return (real * cos, real * sin)
    if power == 4:
        return (-imag, real) if sign > 0 else (imag, -real)
    if abs(abs(cos) - abs(sin)) < 1e-9:
        root = math.sqrt(0.5)
        cs, ss = (1 if cos > 0 else -1), (1 if sin > 0 else -1)
        new_real = (real if cs > 0 else -real) - (imag if ss > 0 else -imag)
        new_imag = (real if ss > 0 else -real) + (imag if cs > 0 else -imag)
        return (new_real * root, new_imag * root)
    return (real * cos - imag * sin, real * sin + imag * cos)


def sixteen(values, sign):
    inner = [four(*(values[n0 + 4 * n1] for n1 in range(4)), sign) for n0 in range(4)]
    out = [None] * 16
    for k1 in range(4):
        parts = [turned(inner[n0][k1], n0 * k1, sign) for n0 in range(4)]
        for k2, value in enumerate(four(*parts, sign)):
            out[k1 + 4 * k2] = value
    return out


def split(value):
    high = value.astype(jnp.bfloat16)
    low = (value - high.astype(jnp.float32)).astype(jnp.bfloat16)
    return high, low


def dot(a, b, dims):
    return lax.dot_general(a, b, (dims, ((), ())), preferred_element_type=jnp.float32)


def rows_forward(image, twiddle, table, out, held_high, held_low):
    chunk = 16

    def body(step, carry):
        at = pl.multiple_of(step * chunk, chunk)
        values = [
            (image[pl.ds(at, chunk), b * LANES : (b + 1) * LANES], None) for b in range(RADIX)
        ]
        mixed = sixteen(values, -1)
        for f in range(RADIX):
            real, imag = mixed[f]
            if imag is None:
                imag = jnp.zeros_like(real)
            cos, sin = twiddle[0, f : f + 1, :], twiddle[1, f : f + 1, :]
            high_r, low_r = split(real * cos + imag * sin)
            high_i, low_i = split(imag * cos - real * sin)
            rows = pl.ds(f * LANES + at, chunk)
            held_high[rows, :LANES] = high_r
            held_high[rows, LANES:] = high_i
            held_low[rows, :LANES] = low_r
            held_low[rows, LANES:] = low_i
        return carry

    lax.fori_loop(0, LANES // chunk, body, 0)
    high_t, low_t = table[0], table[1]
    dims = ((1,), (1,))
    for g in range(RADIX // 2):
        high, low = held_high[256 * g : 256 * g + 256, :], held_low[256 * g : 256 * g + 256, :]
        result = dot(high_t, high, dims) + dot(high_t, low, dims) + dot(low_t, high, dims)
        for h in range(2):
            for c in range(2):
                block = result[c * LANES : (c + 1) * LANES, h * LANES : (h + 1) * LANES]
                out[:, c, 2 * g + h] = block.reshape(RADIX, 8, LANES)


def data_prepared(weights, measured, place, out, held):
    for n in range(3):
        source = weights[...] if n == 0 else measured[n - 1]
        held[...] = source.astype(jnp.float32)
        for f in range(RADIX):
            rows = held[pl.ds(f, LANES, stride=RADIX), :].astype(jnp.bfloat16)
            out[n, f] = dot(place[...], rows, ((1,), (1,))).astype(jnp.bfloat16)


def columns(cols, data, twiddle, forward, inverse, out, held_high, held_low):
    chunk = 32
    rows_all = RADIX * chunk
    dims = ((1,), (0,))

    def store(f, real, imag):
        high_r, low_r = split(real)
        high_i, low_i = split(imag)
        rows = slice(f * chunk, (f + 1) * chunk)
        held_high[rows, :LANES] = high_r
        held_high[rows, LANES:] = high_i
        held_low[rows, :LANES] = low_r
        held_low[rows, LANES:] = low_i

    def product(table):
        high, low = held_high[...], held_low[...]
        return dot(high, table[0], dims) + dot(low, table[0], dims) + dot(high, table[1], dims)

    def body(step, carry):
        at = pl.multiple_of(step * chunk, chunk)
        here = pl.ds(at, chunk)
        mixed = sixteen([(cols[b, 0, here, :], cols[b, 1, here, :]) for b in range(RADIX)], -1)
        for f in range(RADIX):
            real, imag = mixed[f]
            cos, sin = twiddle[0, f : f + 1, :], twiddle[1, f : f + 1, :]
            store(f, real * cos + imag * sin, imag * cos - real * sin)
        spectrum = product(forward)
        for f in range(RADIX):
            piece = spectrum[f * chunk : (f + 1) * chunk]
            weight = data[0, f, here, :].astype(jnp.float32)
            real = weight * piece[:, :LANES] - data[1, f, here, :].astype(jnp.float32)
            imag = weight * piece[:, LANES:] - data[2, f, here, :].astype(jnp.float32)
            store(f, real, imag)
        back = product(inverse)
        values = []
        for f in range(RADIX):
            real = back[f * chunk : (f + 1) * chunk, :LANES]
            imag = back[f * chunk : (f + 1) * chunk, LANES:]
            cos, sin = twiddle[0, f : f + 1, :], twiddle[1, f : f + 1, :]
            values.append((real * cos - imag * sin, imag * cos + real * sin))
        mixed = sixteen(values, 1)
        for b in range(RADIX):
            out[b, 0, here, :] = mixed[b][0]
            out[b, 1, here, :] = mixed[b][1]
        return carry

    lax.fori_loop(0, LANES // chunk, body, 0)


def rows_back(lines, image, twiddle, table, out, held):
    dims = ((0,), (0,))
    high_t, low_t = table[0], table[1]
    for f in range(RADIX):
        real = lines[:, 0, f].reshape(LANES, LANES)
        imag = lines[:, 1, f].reshape(LANES, LANES)
        high, low = split(jnp.concatenate([real, imag], axis=0))
        held[f] = dot(high, high_t, dims) + dot(low, high_t, dims) + dot(high, low_t, dims)
    chunk = 16

    def body(step, carry):
        at = pl.multiple_of(step * chunk, chunk)
        here = pl.ds(at, chunk)
        values = []
        for f in range(RADIX):
            real, imag = held[f, here, :LANES], held[f, here, LANES:]
            cos, sin = twiddle[0, f : f + 1, :], twiddle[1, f : f + 1, :]
            values.append((real * cos - imag * sin, imag * cos + real * sin))
        mixed = sixteen(values, 1)
        for b in range(RADIX):
            low_lane = (b % 2) * LANES
            out[b // 2, 1, here, low_lane : low_lane + LANES] = mixed[b][0]
            out[b // 2, 0, here, low_lane : low_lane + LANES] = image[
                here, b * LANES : (b + 1) * LANES
            ]
        return carry

    lax.fori_loop(0, LANES // chunk, body, 0)


def dual_edges(dual, last_row, last_column):
    rows, cols = [], []
    for c in range(CHANNELS):
        rows.append(dual[c, 0, 112:128, :].astype(jnp.float32)[15:16, :])
        cols.append(dual[c, 1, :, LANES:].astype(jnp.float32)[:, LANES - 1 :])
    last_row[...] = jnp.concatenate(rows, axis=0)
    last_column[...] = jnp.concatenate(cols, axis=1).T


def primal(tile, dual, above, left, image_next, extrapolated, first_row, first_column):
    left_columns = left[...].T
    row_at = lax.broadcasted_iota(jnp.int32, (LANES, 2 * LANES), 0)
    lane_at = lax.broadcasted_iota(jnp.int32, (LANES, 2 * LANES), 1)
    rows, cols = [], []
    for c in range(CHANNELS):
        p = dual[c, 0].astype(jnp.float32)
        q = dual[c, 1].astype(jnp.float32)
        prev_p = jnp.where(row_at == 0, above[c : c + 1, :], pltpu.roll(p, 1, 0))
        prev_q = jnp.where(lane_at == 0, left_columns[:, c : c + 1], pltpu.roll(q, 1, 1))
        adjoint = prev_p - p + prev_q - q
        image = tile[c, 0]
        updated = image - step_primal * (tile[c, 1] + adjoint)
        ahead = 2.0 * updated - image
        image_next[c] = updated
        extrapolated[c] = ahead
        rows.append(ahead[0:1, :])
        cols.append(ahead[:, 0:1])
    first_row[...] = jnp.concatenate(rows, axis=0)
    first_column[...] = jnp.concatenate(cols, axis=1).T


def dual_step(extrapolated, dual, below, right, out):
    chunk = 16
    right_columns = right[...].T
    row_at = lax.broadcasted_iota(jnp.int32, (chunk, 2 * LANES), 0)
    lane_at = lax.broadcasted_iota(jnp.int32, (chunk, 2 * LANES), 1)
    for step in range(LANES // chunk):
        at = step * chunk
        here = slice(at, at + chunk)
        firsts, seconds, total = [], [], None
        for c in range(CHANNELS):
            ahead = extrapolated[c, here, :]
            if step + 1 < LANES // chunk:
                next_row = extrapolated[c, at + chunk : at + chunk + 1, :]
            else:
                next_row = below[c : c + 1, :]
            down = jnp.where(row_at == chunk - 1, next_row, pltpu.roll(ahead, chunk - 1, 0))
            beside = jnp.where(
                lane_at == 2 * LANES - 1,
                right_columns[here, c : c + 1],
                pltpu.roll(ahead, 2 * LANES - 1, 1),
            )
            first = dual[c, 0, here, :].astype(jnp.float32) + step_dual * (down - ahead)
            second = dual[c, 1, here, :].astype(jnp.float32) + step_dual * (beside - ahead)
            firsts.append(first)
            seconds.append(second)
            squares = first * first + second * second
            total = squares if total is None else total + squares
        factor = 1.0 / jnp.maximum(1.0, jnp.sqrt(total) / clip_radius)
        for c in range(CHANNELS):
            out[c, 0, here, :] = (firsts[c] * factor).astype(jnp.bfloat16)
            out[c, 1, here, :] = (seconds[c] * factor).astype(jnp.bfloat16)


def shape(dims, dtype=jnp.float32):
    return jax.ShapeDtypeStruct(dims, dtype)


def passed_along(x, axis, by):
    devices = lax.axis_size(axis)
    pairs = [(i, i + by) for i in range(devices) if 0 <= i + by < devices]
    return lax.ppermute(x, axis, pairs)


def shards(image_field, weights, measured, dual_field):
    forward, inverse, twiddle, place = host_tables()
    scale = 1.0 / GRID
    place = jnp.asarray(place, jnp.bfloat16)
    twiddle = jnp.asarray(twiddle)
    image = image_field[0]
    bf16 = jnp.bfloat16

    last_row, last_column = pl.pallas_call(
        dual_edges,
        out_shape=(shape((CHANNELS, 2 * LANES)), shape((CHANNELS, LANES))),
        name="dual_edges",
        compiler_params=PARAMS,
    )(dual_field)
    above = passed_along(last_row, "facet", 1)
    left = passed_along(last_column, "chan", 1)

    spread = pl.pallas_call(
        rows_forward,
        out_shape=shape((RADIX, 2, RADIX, 8, LANES)),
        scratch_shapes=[pltpu.VMEM((GRID, 256), bf16), pltpu.VMEM((GRID, 256), bf16)],
        name="rows_forward",
        compiler_params=PARAMS,
    )(image, twiddle, jnp.asarray(halves(forward.T * scale)))
    cols = lax.all_to_all(
        spread.reshape(RADIX, 2 * LANES, LANES), "facet", split_axis=0, concat_axis=0, tiled=True
    ).reshape(RADIX, 2, LANES, LANES)
    data = pl.pallas_call(
        data_prepared,
        out_shape=shape((3, RADIX, LANES, LANES), bf16),
        scratch_shapes=[pltpu.VMEM((GRID, LANES), jnp.float32)],
        name="data_prepared",
        compiler_params=PARAMS,
    )(weights[0], measured[0], place)
    back = pl.pallas_call(
        columns,
        out_shape=shape((RADIX, 2, LANES, LANES)),
        scratch_shapes=[pltpu.VMEM((RADIX * 32, 256), bf16), pltpu.VMEM((RADIX * 32, 256), bf16)],
        name="columns",
        compiler_params=PARAMS,
    )(cols, data, twiddle, jnp.asarray(halves(forward)), jnp.asarray(halves(inverse)))
    lines = lax.all_to_all(
        back.reshape(RADIX, 2 * LANES, LANES), "facet", split_axis=0, concat_axis=0, tiled=True
    ).reshape(RADIX, 2, RADIX, 8, LANES)
    tiles = pl.pallas_call(
        rows_back,
        out_shape=shape((CHANNELS, 2, LANES, 2 * LANES)),
        scratch_shapes=[pltpu.VMEM((RADIX, LANES, 256), jnp.float32)],
        name="rows_back",
        compiler_params=PARAMS,
    )(lines, image, twiddle, jnp.asarray(halves(inverse * scale)))
    tile = lax.all_to_all(
        tiles.reshape(CHANNELS, 2 * LANES, 2 * LANES),
        "chan",
        split_axis=0,
        concat_axis=0,
        tiled=True,
    ).reshape(CHANNELS, 2, LANES, 2 * LANES)
    image_next, extrapolated, first_row, first_column = pl.pallas_call(
        primal,
        out_shape=(
            shape((CHANNELS, LANES, 2 * LANES)),
            shape((CHANNELS, LANES, 2 * LANES)),
            shape((CHANNELS, 2 * LANES)),
            shape((CHANNELS, LANES)),
        ),
        name="primal",
        compiler_params=PARAMS,
    )(tile, dual_field, above, left)
    below = passed_along(first_row, "facet", -1)
    right = passed_along(first_column, "chan", -1)
    dual_next = pl.pallas_call(
        dual_step,
        out_shape=shape((CHANNELS, 2, LANES, 2 * LANES), bf16),
        name="dual_step",
        compiler_params=PARAMS,
    )(extrapolated, dual_field, below, right)
    return (image_next, dual_next)


def solution(mesh):
    placed = (
        P("chan", "facet", None),
        P("chan", None, "facet"),
        P("chan", None, None, "facet"),
        P(None, None, "facet", "chan"),
    )
    return jax.shard_map(
        shards,
        mesh=mesh,
        in_specs=placed,
        out_specs=(P(None, "facet", "chan"), P(None, None, "facet", "chan")),
        check_vma=False,
    )
```

profile of v0, /device:TPU:8, one launch (start us, length us, event | category | flops | bytes accessed | tf_op | source)
XLA Modules:
  0.0 136.0 jit_solution(1251887773178459251)
XLA Ops:
  0.6 0.0 copy-start.2
  0.6 1.2 copy-done.2
  1.9 0.0 copy-start.5
  1.9 0.9 copy-done.5
  2.8 0.0 copy-start.10
  2.8 0.7 copy-done.10
  3.5 3.1 %rows_forward.1 = f32[16,2,16,8,128]{4,3,2,1,0:T(8,128)} custom-call(f32[128,2048]{1,0:T(8,128)S(1)} %bitcast.13, f32[2,16,128]{2,1,0:T(8,128)S(1)} %copy-done.10, bf16[2,256,256]{2,1,0:T(8,128)(2,1)S(1)} %copy-done.5), custom_call_target="tpu_custom_call" | custom-call | tf_op jit(solution)/shard_map/rows_forward/pallas_call | solution.py:335
  6.7 0.0 copy-start.4
  6.7 0.0 copy-start.7
  6.7 0.0 copy-start.12
  6.7 8.4 %all-to-all-start = ((f32[16,256,128]{2,1,0:T(8,128)}), f32[16,256,128]{2,1,0:T(8,128)}, u32[]{:S(2)}, u32[]{:S(2)}) async-start(f32[16,256,128]{2,1,0:T(8,128)} %bitcast.1), calls=%async_computation | async-start | bytes 4194304 | tf_op jit(solution)/shard_map/all_to_all | solution.py:342
  15.1 0.0 copy-start.8
  15.1 0.0 copy-start.11
  15.1 0.0 copy-done.4
  15.1 0.0 copy-done.7
  15.1 0.0 copy-done.12
  15.1 1.5 %data_prepared.1.data = bf16[3,16,128,128]{3,2,1,0:T(8,128)(2,1)S(1)} custom-call(bf16[2048,128]{1,0:T(8,128)(2,1)S(1)} %bitcast.16, bf16[2,2048,128]{2,1,0:T(8,128)(2,1)S(1)} %bitcast.15, bf16[128,128]{1,0:T(8,128)(2,1)S(1)} %copy-done.12), custom_call_target="tpu_custom_call" | custom-call | tf_op jit(solution)/shard_map/data_prepared/pallas_call | solution.py:345
  16.6 26.2 %all-to-all-done = f32[16,256,128]{2,1,0:T(8,128)} async-done(((f32[16,256,128]{2,1,0:T(8,128)}), f32[16,256,128]{2,1,0:T(8,128)}, u32[]{:S(2)}, u32[]{:S(2)}) %all-to-all-start) | async-done | bytes 2097184 | tf_op jit(solution)/shard_map/all_to_all | solution.py:342
  42.8 0.0 copy-done.8
  42.8 0.0 copy-done.11
  42.8 0.0 copy-start.9
  42.8 0.9 copy-done.9
  43.8 6.6 %columns.1 = f32[16,2,128,128]{3,2,1,0:T(8,128)S(1)} custom-call(f32[16,2,128,128]{3,2,1,0:T(8,128)} %bitcast.2.cols, bf16[3,16,128,128]{3,2,1,0:T(8,128)(2,1)S(1)} %data_prepared.1.data, f32[2,16,128]{2,1,0:T(8,128)S(1)} %copy-done.11, bf16[2,256,256]{2,1,0:T(8,128)(2,1)S(1)} %copy-done.8, bf16[2,256,256]{2,1,0:T(8,128)(2,1)S(1)} %copy-done.9), custom_call_target="tpu_custom_call" | custom-call | tf_op jit(solution)/shard_map/columns/pallas_call | solution.py:352
  50.3 0.0 copy-start.3
  50.3 0.0 copy-start.6
  50.4 33.2 %all_to_all.15 = f32[16,256,128]{2,1,0:T(8,128)S(1)} all-to-all(f32[16,256,128]{2,1,0:T(8,128)S(1)} %bitcast.9), channel_id=1, replica_groups=mesh['chan'=8,'facet'=16] {'facet'}, dimensions={0} | all-to-all | bytes 4194304 | tf_op jit(solution)/shard_map/all_to_all | solution.py:359
  83.6 0.0 copy-done.3
  83.6 0.0 copy-done.6
  83.6 1.6 %rows_back.1 = f32[8,2,128,256]{3,2,1,0:T(8,128)S(1)} custom-call(f32[16,2,16,8,128]{4,3,2,1,0:T(8,128)S(1)} %bitcast.12, f32[128,2048]{1,0:T(8,128)S(1)} %bitcast.14, f32[2,16,128]{2,1,0:T(8,128)S(1)} %copy-done.11, bf16[2,256,256]{2,1,0:T(8,128)(2,1)S(1)} %copy-done.6), custom_call_target="tpu_custom_call" | custom-call | tf_op jit(solution)/shard_map/rows_back/pallas_call | solution.py:362
  85.2 0.0 copy-start.1
  85.2 1.3 copy-done.1
  86.5 0.0 copy-start
  86.5 4.9 %all-to-all-start.2 = ((f32[8,256,256]{2,1,0:T(8,128)}), f32[8,256,256]{2,1,0:T(8,128)S(1)}, u32[]{:S(2)}, u32[]{:S(2)}) async-start(f32[8,256,256]{2,1,0:T(8,128)} %bitcast.11), calls=%async_computation.2 | async-start | bytes 4194304 | tf_op jit(solution)/shard_map/all_to_all | solution.py:369
  91.4 0.0 copy-done
  91.4 0.2 dual_edges.1
  91.6 1.9 %collective-permute-start = (f32[8,256]{1,0:T(8,128)S(1)}, f32[8,256]{1,0:T(8,128)S(1)}, u32[]{:S(2)}, u32[]{:S(2)}) collective-permute-start(f32[8,256]{1,0:T(8,128)S(1)} %get-tuple-element.8), channel_id=1, source_target_pairs={{0,1},{1,2},{2,3},{3,4},{4,5},{5,6},{6,7},{7,8},{8,9},{9,10},{10,1... | collective-permute-start | bytes 24584 | tf_op jit(solution)/shard_map/ppermute | solution.py:315
  93.5 3.9 %collective-permute-start.1 = (f32[8,128]{1,0:T(8,128)S(1)}, f32[8,128]{1,0:T(8,128)S(1)}, u32[]{:S(2)}, u32[]{:S(2)}) collective-permute-start(f32[8,128]{1,0:T(8,128)S(1)} %get-tuple-element.9), channel_id=1, source_target_pairs={{0,16},{16,32},{32,48},{48,64},{64,80},{80,96},{96,112},{1,17},{17... | collective-permute-start | bytes 12296 | tf_op jit(solution)/shard_map/ppermute | solution.py:315
  97.5 11.5 %collective-permute-done.1.left = f32[8,128]{1,0:T(8,128)S(1)} collective-permute-done((f32[8,128]{1,0:T(8,128)S(1)}, f32[8,128]{1,0:T(8,128)S(1)}, u32[]{:S(2)}, u32[]{:S(2)}) %collective-permute-start.1) | collective-permute-done | bytes 4128 | tf_op jit(solution)/shard_map/ppermute | solution.py:315
  109.0 0.0 collective-permute-done.above
  109.0 14.2 %all-to-all-done.2 = f32[8,256,256]{2,1,0:T(8,128)S(1)} async-done(((f32[8,256,256]{2,1,0:T(8,128)}), f32[8,256,256]{2,1,0:T(8,128)S(1)}, u32[]{:S(2)}, u32[]{:S(2)}) %all-to-all-start.2) | async-done | bytes 2097184 | tf_op jit(solution)/shard_map/all_to_all | solution.py:369
  123.1 1.7 %primal.1 = (f32[8,128,256]{2,1,0:T(8,128)}, f32[8,128,256]{2,1,0:T(8,128)S(1)}, f32[8,256]{1,0:T(8,128)S(1)}, f32[8,128]{1,0:T(8,128)S(1)}) custom-call(f32[8,2,128,256]{3,2,1,0:T(8,128)S(1)} %bitcast.10, bf16[8,2,128,256]{3,2,1,0:T(8,128)(2,1)S(1)} %copy-done, f32[8,256]{1,0:T(8,128)S(1)} %collective-permute-done.above, ...), custom_call_target="tpu_custom_call" | custom-call | tf_op jit(solution)/shard_map/primal/pallas_call | solution.py:376
  124.9 3.7 %collective-permute-start.2 = (f32[8,256]{1,0:T(8,128)S(1)}, f32[8,256]{1,0:T(8,128)S(1)}, u32[]{:S(2)}, u32[]{:S(2)}) collective-permute-start(f32[8,256]{1,0:T(8,128)S(1)} %get-tuple-element.12), channel_id=1, source_target_pairs={{1,0},{2,1},{3,2},{4,3},{5,4},{6,5},{7,6},{8,7},{9,8},{10,9},{11,1... | collective-permute-start | bytes 24584 | tf_op jit(solution)/shard_map/ppermute | solution.py:315
  128.6 1.3 collective-permute-start.3
  129.9 4.2 %collective-permute-done.3.right = f32[8,128]{1,0:T(8,128)S(1)} collective-permute-done((f32[8,128]{1,0:T(8,128)S(1)}, f32[8,128]{1,0:T(8,128)S(1)}, u32[]{:S(2)}, u32[]{:S(2)}) %collective-permute-start.3) | collective-permute-done | bytes 4128 | tf_op jit(solution)/shard_map/ppermute | solution.py:315
  134.1 0.0 collective-permute-done.2.below
  134.1 1.9 %dual_step.1 = bf16[8,2,128,256]{3,2,1,0:T(8,128)(2,1)} custom-call(f32[8,128,256]{2,1,0:T(8,128)S(1)} %get-tuple-element.11.extrapolated, bf16[8,2,128,256]{3,2,1,0:T(8,128)(2,1)S(1)} %copy-done, f32[8,256]{1,0:T(8,128)S(1)} %collective-permute-done.2.below, f32[8,128]{1,0:T(8,128)S(1)} %collective-permute-done.3.right), custom_call_target="tpu_custom_call" | custom-call | tf_op jit(solution)/shard_map/dual_step/pallas_call | solution.py:389
Async XLA Ops:
  0.6 1.2 copy-start.2
  1.9 0.9 copy-start.5
  2.8 0.7 copy-start.10
  6.7 8.4 %copy-start.4 = (bf16[1,2,2048,128]{3,2,1,0:T(8,128)(2,1)S(1)}, bf16[1,2,2048,128]{3,2,1,0:T(8,128)(2,1)}, u32[]{:S(2)}) copy-start(bf16[1,2,2048,128]{3,2,1,0:T(8,128)(2,1)} %param.12) | copy-start | bytes 3145732
  6.7 8.4 %copy-start.7 = (bf16[1,2048,128]{2,1,0:T(8,128)(2,1)S(1)}, bf16[1,2048,128]{2,1,0:T(8,128)(2,1)}, u32[]{:S(2)}) copy-start(bf16[1,2048,128]{2,1,0:T(8,128)(2,1)} %param.11) | copy-start | bytes 1572868
  6.7 8.4 %copy-start.12 = (bf16[128,128]{1,0:T(8,128)(2,1)S(1)}, bf16[128,128]{1,0:T(8,128)(2,1)}, u32[]{:S(2)}) copy-start(bf16[128,128]{1,0:T(8,128)(2,1)} %constant.10.clone.place) | copy-start | bytes 98308
  6.7 36.1 %all-to-all-start = ((f32[16,256,128]{2,1,0:T(8,128)}), f32[16,256,128]{2,1,0:T(8,128)}, u32[]{:S(2)}, u32[]{:S(2)}) async-start(f32[16,256,128]{2,1,0:T(8,128)} %bitcast.1), calls=%async_computation | async-start | bytes 4194304 | tf_op jit(solution)/shard_map/all_to_all | solution.py:342
  15.1 27.7 %copy-start.8 = (bf16[2,256,256]{2,1,0:T(8,128)(2,1)S(1)}, bf16[2,256,256]{2,1,0:T(8,128)(2,1)}, u32[]{:S(2)}) copy-start(bf16[2,256,256]{2,1,0:T(8,128)(2,1)} %constant.13.clone.forward) | copy-start | bytes 786436
  15.1 27.7 %copy-start.11 = (f32[2,16,128]{2,1,0:T(8,128)S(1)}, f32[2,16,128]{2,1,0:T(8,128)}, u32[]{:S(2)}) copy-start(f32[2,16,128]{2,1,0:T(8,128)} %constant.11.clone.twiddle) | copy-start | bytes 49156
  42.8 1.0 copy-start.9
  50.3 33.3 %copy-start.3 = (f32[1,128,2048]{2,1,0:T(8,128)S(1)}, f32[1,128,2048]{2,1,0:T(8,128)}, u32[]{:S(2)}) copy-start(f32[1,128,2048]{2,1,0:T(8,128)} %param.10) | copy-start | bytes 3145732
  50.3 33.3 %copy-start.6 = (bf16[2,256,256]{2,1,0:T(8,128)(2,1)S(1)}, bf16[2,256,256]{2,1,0:T(8,128)(2,1)}, u32[]{:S(2)}) copy-start(bf16[2,256,256]{2,1,0:T(8,128)(2,1)} %constant.12.clone.table) | copy-start | bytes 786436
  85.2 1.3 copy-start.1
  86.5 4.9 %copy-start = (bf16[8,2,128,256]{3,2,1,0:T(8,128)(2,1)S(1)}, bf16[8,2,128,256]{3,2,1,0:T(8,128)(2,1)}, u32[]{:S(2)}) copy-start(bf16[8,2,128,256]{3,2,1,0:T(8,128)(2,1)} %dual.5) | copy-start | bytes 3145732
  86.5 36.6 %all-to-all-start.2 = ((f32[8,256,256]{2,1,0:T(8,128)}), f32[8,256,256]{2,1,0:T(8,128)S(1)}, u32[]{:S(2)}, u32[]{:S(2)}) async-start(f32[8,256,256]{2,1,0:T(8,128)} %bitcast.11), calls=%async_computation.2 | async-start | bytes 4194304 | tf_op jit(solution)/shard_map/all_to_all | solution.py:369
  91.6 17.4 %collective-permute-start = (f32[8,256]{1,0:T(8,128)S(1)}, f32[8,256]{1,0:T(8,128)S(1)}, u32[]{:S(2)}, u32[]{:S(2)}) collective-permute-start(f32[8,256]{1,0:T(8,128)S(1)} %get-tuple-element.8), channel_id=1, source_target_pairs={{0,1},{1,2},{2,3},{3,4},{4,5},{5,6},{6,7},{7,8},{8,9},{9,10},{10,1... | collective-permute-start | bytes 24584 | tf_op jit(solution)/shard_map/ppermute | solution.py:315
  93.5 15.4 %collective-permute-start.1 = (f32[8,128]{1,0:T(8,128)S(1)}, f32[8,128]{1,0:T(8,128)S(1)}, u32[]{:S(2)}, u32[]{:S(2)}) collective-permute-start(f32[8,128]{1,0:T(8,128)S(1)} %get-tuple-element.9), channel_id=1, source_target_pairs={{0,16},{16,32},{32,48},{48,64},{64,80},{80,96},{96,112},{1,17},{17... | collective-permute-start | bytes 12296 | tf_op jit(solution)/shard_map/ppermute | solution.py:315
  124.9 9.2 %collective-permute-start.2 = (f32[8,256]{1,0:T(8,128)S(1)}, f32[8,256]{1,0:T(8,128)S(1)}, u32[]{:S(2)}, u32[]{:S(2)}) collective-permute-start(f32[8,256]{1,0:T(8,128)S(1)} %get-tuple-element.12), channel_id=1, source_target_pairs={{1,0},{2,1},{3,2},{4,3},{5,4},{6,5},{7,6},{8,7},{9,8},{10,9},{11,1... | collective-permute-start | bytes 24584 | tf_op jit(solution)/shard_map/ppermute | solution.py:315
  128.6 5.5 %collective-permute-start.3 = (f32[8,128]{1,0:T(8,128)S(1)}, f32[8,128]{1,0:T(8,128)S(1)}, u32[]{:S(2)}, u32[]{:S(2)}) collective-permute-start(f32[8,128]{1,0:T(8,128)S(1)} %get-tuple-element.13), channel_id=1, source_target_pairs={{16,0},{32,16},{48,32},{64,48},{80,64},{96,80},{112,96},{17,1},{33... | collective-permute-start | bytes 12296 | tf_op jit(solution)/shard_map/ppermute | solution.py:315
where the time goes:
time: 137 us; the launch traced here: 136 us
  waiting for transfers between devices  56.1 us (41%)
  blocking collectives  33.2 us (24%)
  starting transfers between devices  24.1 us (18%)
  Pallas kernels  16.6 us (12%)
  local copies, waits for them, and re-layouts  5.2 us (4%)
    all_to_all x1, blocking collectives, shards(): lax.all_to_all(back.reshape(RADIX, 2 * LANES, LANES), 'facet', split_axis...  33.2 us
    all_to_all x1, waiting for transfers between devices, shards(): lax.all_to_all(spread.reshape(RADIX, 2 * LANES, LANES), 'facet', split_ax...  26.2 us
    ppermute x4, waiting for transfers between devices, passed_along(): return lax.ppermute(x, axis, pairs)  15.7 us
    all_to_all x1, waiting for transfers between devices, shards(): lax.all_to_all(tiles.reshape(CHANNELS, 2 * LANES, 2 * LANES), 'chan', spl...  14.2 us
    ppermute x4, starting transfers between devices, passed_along(): return lax.ppermute(x, axis, pairs)  10.9 us
    all_to_all x1, starting transfers between devices, shards(): lax.all_to_all(spread.reshape(RADIX, 2 * LANES, LANES), 'facet', split_ax...  8.38 us
    pallas_call x1, Pallas kernels, shards(): pl.pallas_call(columns, out_shape=shape((RADIX, 2, LANES, LANES)), scratc...  6.57 us
    unnamed x26, local copies, waits for them, and re-layouts  5.2 us
  transfers between devices with their start and end apart: 6, of which 4 were waited for; matrix products, arithmetic and copies ran while one was open for 0% of the time, Pallas kernels for 1%

commit v1 on v0

v1 whole, which is shorter than its diff:
```python
from functools import partial
import math

import jax
import jax.numpy as jnp
import ml_dtypes
import numpy as np
from jax import lax
from jax.experimental import pallas as pl
from jax.experimental.pallas import tpu as pltpu
from jax.sharding import PartitionSpec as P

GRID = 2048
RADIX = 16
LANES = 128
CHANNELS = 8

step_primal = 0.5
step_dual = 0.5
clip_radius = 4.0

PARAMS = pltpu.CompilerParams(vmem_limit_bytes=48 * 1024 * 1024)


def host_tables():
    index = np.arange(LANES)
    angle = 2.0 * np.pi * (index[:, None] * index[None, :] % LANES) / LANES
    cos, sin = np.cos(angle), np.sin(angle)
    forward = np.block([[cos, -sin], [sin, cos]])
    inverse = np.block([[cos, sin], [-sin, cos]])
    turn = 2.0 * np.pi * np.arange(RADIX)[:, None] * index[None, :] / GRID
    twiddle = np.stack([np.cos(turn), np.sin(turn)]).astype(np.float32)
    place = np.zeros((LANES, LANES))
    for at in range(LANES):
        place[at, 16 * (at % 8) + at // 8] = 1.0
    return forward, inverse, twiddle, place


def halves(table):
    high = table.astype(ml_dtypes.bfloat16)
    low = (table - high.astype(np.float64)).astype(ml_dtypes.bfloat16)
    return np.concatenate([high, high, low], axis=0)


def c_add(a, b):
    return (a[0] + b[0], b[1] if a[1] is None else a[1] if b[1] is None else a[1] + b[1])


def c_sub(a, b):
    imag = None
    if a[1] is not None and b[1] is not None:
        imag = a[1] - b[1]
    elif a[1] is not None:
        imag = a[1]
    elif b[1] is not None:
        imag = -b[1]
    return (a[0] - b[0], imag)


def add_turned(a, b, sign):
    real = a[0] if b[1] is None else (a[0] - b[1] if sign > 0 else a[0] + b[1])
    if a[1] is None:
        imag = b[0] if sign > 0 else -b[0]
    else:
        imag = a[1] + b[0] if sign > 0 else a[1] - b[0]
    return (real, imag)


def four(a, b, c, d, sign):
    sum_even, diff_even = c_add(a, c), c_sub(a, c)
    sum_odd, diff_odd = c_add(b, d), c_sub(b, d)
    return (
        c_add(sum_even, sum_odd),
        add_turned(diff_even, diff_odd, sign),
        c_sub(sum_even, sum_odd),
        add_turned(diff_even, diff_odd, -sign),
    )


def turned(a, power, sign):
    power = power % 16
    if power == 0:
        return a
    cos, sin = math.cos(2 * math.pi * power / 16), sign * math.sin(2 * math.pi * power / 16)
    real, imag = a
    if imag is None:
        if power == 4:
            return (jnp.zeros_like(real), real if sign > 0 else -real)
        return (real * cos, real * sin)
    if power == 4:
        return (-imag, real) if sign > 0 else (imag, -real)
    if abs(abs(cos) - abs(sin)) < 1e-9:
        root = math.sqrt(0.5)
        cs, ss = (1 if cos > 0 else -1), (1 if sin > 0 else -1)
        new_real = (real if cs > 0 else -real) - (imag if ss > 0 else -imag)
        new_imag = (real if ss > 0 else -real) + (imag if cs > 0 else -imag)
        return (new_real * root, new_imag * root)
    return (real * cos - imag * sin, real * sin + imag * cos)


def sixteen(values, sign):
    inner = [four(*(values[n0 + 4 * n1] for n1 in range(4)), sign) for n0 in range(4)]
    out = [None] * 16
    for k1 in range(4):
        parts = [turned(inner[n0][k1], n0 * k1, sign) for n0 in range(4)]
        for k2, value in enumerate(four(*parts, sign)):
            out[k1 + 4 * k2] = value
    return out


def split(value):
    high = value.astype(jnp.bfloat16)
    low = (value - high.astype(jnp.float32)).astype(jnp.bfloat16)
    return high, low


def dot(a, b, dims):
    return lax.dot_general(a, b, (dims, ((), ())), preferred_element_type=jnp.float32)


def fetched(source, target, semaphore):
    copy = pltpu.make_async_copy(source, target, semaphore)
    copy.start()
    return copy


def three_pass(pair, table, dims):
    high = pair[:, :256] if dims[0][0] == 1 else pair[:256, :]
    return dot(pair, table[:512, :], dims) + dot(high, table[512:, :], dims)


def store_pair(held, rows, real, imag):
    high_r, low_r = split(real)
    high_i, low_i = split(imag)
    held[rows, 0:LANES] = high_r
    held[rows, LANES : 2 * LANES] = high_i
    held[rows, 2 * LANES : 3 * LANES] = low_r
    held[rows, 3 * LANES : 4 * LANES] = low_i


def rows_forward(
    where, image, twiddle, table, out, *rest
):
    pieces, (image_v, twiddle_v, table_v, out_v, held, in_sems, out_sems) = rest[:4], rest[4:]
    chunk = 16
    steps = LANES // chunk

    def incoming(step):
        rows = pl.ds(pl.multiple_of(step * chunk, chunk), chunk)
        return pltpu.make_async_copy(image.at[rows, :], image_v.at[rows, :], in_sems.at[step])

    for step in range(steps):
        incoming(step).start()
    get_twiddle = fetched(twiddle, twiddle_v, in_sems.at[steps])
    get_table = fetched(table, table_v, in_sems.at[steps + 1])
    sent = []
    for k in range(4):
        lanes = pl.ds(pl.multiple_of((where[0] + k) % 4 * 512, 512), 512)
        sent.append(fetched(image.at[:, lanes], pieces[k], out_sems.at[8 + k]))
    get_twiddle.wait()

    def body(step, carry):
        incoming(step).wait()
        at = pl.multiple_of(step * chunk, chunk)
        values = [
            (image_v[pl.ds(at, chunk), b * LANES : (b + 1) * LANES], None) for b in range(RADIX)
        ]
        mixed = sixteen(values, -1)
        for f in range(RADIX):
            real, imag = mixed[f]
            if imag is None:
                imag = jnp.zeros_like(real)
            cos, sin = twiddle_v[0, f : f + 1, :], twiddle_v[1, f : f + 1, :]
            store_pair(
                held,
                pl.ds(f * LANES + at, chunk),
                real * cos + imag * sin,
                imag * cos - real * sin,
            )
        return carry

    lax.fori_loop(0, steps, body, 0)
    get_table.wait()
    dims = ((1,), (1,))
    for g in range(RADIX // 2):
        pair = held[256 * g : 256 * g + 256, :]
        result = dot(table_v[:, :512], pair, dims) + dot(table_v[:, 512:], pair[:, :256], dims)
        for h in range(2):
            for c in range(2):
                block = result[c * LANES : (c + 1) * LANES, h * LANES : (h + 1) * LANES]
                out_v[:, c, 2 * g + h] = block.reshape(RADIX, 8, LANES)
        both = pl.ds(2 * g, 2)
        sent.append(fetched(out_v.at[:, :, both], out.at[:, :, both], out_sems.at[g]))
    for copy in sent:
        copy.wait()


def data_prepared(weights, measured, place, out, held, out_v, sems):
    copies = []
    for n in range(3):
        source = weights[...] if n == 0 else measured[n - 1]
        held[...] = source.astype(jnp.float32)
        for f in range(RADIX):
            rows = held[pl.ds(f, LANES, stride=RADIX), :].astype(jnp.bfloat16)
            out_v[n, f] = dot(place[...], rows, ((1,), (1,))).astype(jnp.bfloat16)
        copies.append(fetched(out_v.at[n], out.at[n], sems.at[n]))
    for copy in copies:
        copy.wait()


def columns(
    cols, data, twiddle, forward, inverse, out,
    cols_v, data_v, forward_v, inverse_v, out_v, edge_v, held, in_sems, data_sems, out_sems,
):
    chunk = 32
    steps = LANES // chunk
    dims = ((1,), (0,))

    def incoming(step):
        rows = pl.ds(pl.multiple_of(step * chunk, chunk), chunk)
        return pltpu.make_async_copy(
            cols.at[:, :, rows, :], cols_v.at[:, :, rows, :], in_sems.at[step]
        )

    def incoming_data(step):
        rows = pl.ds(pl.multiple_of(step * chunk, chunk), chunk)
        return pltpu.make_async_copy(
            data.at[:, :, rows, :], data_v.at[:, :, rows, :], data_sems.at[step]
        )

    def outgoing(step, c):
        rows = pl.ds(pl.multiple_of(step * chunk, chunk), chunk)
        to_rows = pl.ds(pl.multiple_of(c * LANES + step * chunk, chunk), chunk)
        return pltpu.make_async_copy(
            out_v.at[:, c, rows, :], out.at[:, to_rows, :], out_sems.at[step, c]
        )

    for step in range(steps):
        incoming(step).start()
        incoming_data(step).start()
    get_forward = fetched(forward, forward_v, in_sems.at[steps])
    get_inverse = fetched(inverse, inverse_v, in_sems.at[steps + 1])
    edge_v[...] = jnp.zeros_like(edge_v)
    get_forward.wait()
    get_inverse.wait()
    lane_at = lax.broadcasted_iota(jnp.int32, (8, LANES), 1)

    def body(step, carry):
        incoming(step).wait()
        here = pl.ds(pl.multiple_of(step * chunk, chunk), chunk)
        mixed = sixteen([(cols_v[b, 0, here, :], cols_v[b, 1, here, :]) for b in range(RADIX)], -1)
        for f in range(RADIX):
            real, imag = mixed[f]
            cos, sin = twiddle[0, f : f + 1, :], twiddle[1, f : f + 1, :]
            rows = slice(f * chunk, (f + 1) * chunk)
            store_pair(held, rows, real * cos + imag * sin, imag * cos - real * sin)
        incoming_data(step).wait()
        spectrum = three_pass(held[...], forward_v, dims)
        for f in range(RADIX):
            rows = slice(f * chunk, (f + 1) * chunk)
            weight = data_v[0, f, here, :].astype(jnp.float32)
            real = weight * spectrum[rows, :LANES] - data_v[1, f, here, :].astype(jnp.float32)
            imag = weight * spectrum[rows, LANES:] - data_v[2, f, here, :].astype(jnp.float32)
            store_pair(held, rows, real, imag)
        back = three_pass(held[...], inverse_v, dims)
        values = []
        for f in range(RADIX):
            rows = slice(f * chunk, (f + 1) * chunk)
            real, imag = back[rows, :LANES], back[rows, LANES:]
            cos, sin = twiddle[0, f : f + 1, :], twiddle[1, f : f + 1, :]
            values.append((real * cos - imag * sin, imag * cos + real * sin))
        mixed = sixteen(values, 1)
        for b in range(RADIX):
            for c in range(2):
                out_v[b, c, here, :] = mixed[b][c]
                if b > 0:
                    edge = edge_v[b - 1]
                    for i in range(chunk // 8):
                        first = mixed[b][c][8 * i : 8 * i + 8, 0:1]
                        at_lane = lane_at == c * RADIX + step * (chunk // 8) + i
                        edge = jnp.where(at_lane, first, edge)
                    edge_v[b - 1] = edge
        outgoing(step, 0).start()
        outgoing(step, 1).start()
        return carry

    lax.fori_loop(0, steps, body, 0)
    send_edge = fetched(edge_v, out.at[:, 2 * LANES :, :], in_sems.at[0])
    for step in range(steps):
        outgoing(step, 0).wait()
        outgoing(step, 1).wait()
    send_edge.wait()


def rows_back(
    lines, twiddle, table, out, lines_v, edge_v, table_v, held, out_v, side_v, in_sems, out_sems
):
    dims = ((0,), (0,))
    get_table = fetched(table, table_v, in_sems.at[5])
    arriving = []
    for g in range(4):
        for c in range(2):
            rows = pl.ds(c * LANES + 32 * g, 32)
            arriving.append(
                fetched(
                    lines.at[:, rows, :], lines_v.at[:, pl.ds(c * LANES + 32 * g, 32), :],
                    out_sems.at[2 * g + c],
                )
            )
    get_edge = fetched(lines.at[:, 2 * LANES :, :], edge_v, in_sems.at[4])
    get_table.wait()
    for f in range(RADIX):
        if f % 4 == 0:
            arriving[f // 2].wait()
            arriving[f // 2 + 1].wait()
        real = lines_v[:, 8 * f : 8 * f + 8, :].reshape(LANES, LANES)
        imag = lines_v[:, LANES + 8 * f : LANES + 8 * f + 8, :].reshape(LANES, LANES)
        high_r, low_r = split(real)
        high_i, low_i = split(imag)
        pair = jnp.concatenate([high_r, high_i, low_r, low_i], axis=0)
        held[f] = three_pass(pair, table_v, dims)
    get_edge.wait()
    high, low = split(edge_v[...].reshape(LANES, LANES))
    edge = (
        dot(high, table_v[0:LANES, :], dims)
        + dot(low, table_v[0:LANES, :], dims)
        + dot(high, table_v[512 : 512 + LANES, :], dims)
    )
    edge_r = edge[:RADIX, :LANES] - edge[RADIX : 2 * RADIX, LANES:]
    edge_i = edge[:RADIX, LANES:] + edge[RADIX : 2 * RADIX, :LANES]
    cos, sin = twiddle[0], twiddle[1]
    edge_r, edge_i = edge_r * cos - edge_i * sin, edge_i * cos + edge_r * sin
    mixed = sixteen([(edge_r[f : f + 1], edge_i[f : f + 1]) for f in range(RADIX)], 1)
    for d in range(CHANNELS):
        out_v[d, LANES : LANES + 1, :] = jnp.concatenate(
            [mixed[2 * d][0], mixed[2 * d + 1][0]], axis=1
        )
    chunk = 16
    steps = LANES // chunk
    lane_at = lax.broadcasted_iota(jnp.int32, (chunk, LANES), 1)

    def outgoing(step):
        rows = pl.ds(pl.multiple_of(step * chunk, chunk), chunk)
        return pltpu.make_async_copy(out_v.at[:, rows, :], out.at[:, rows, :], out_sems.at[step])

    def body(step, carry):
        at = pl.multiple_of(step * chunk, chunk)
        here = pl.ds(at, chunk)
        values = []
        for f in range(RADIX):
            real, imag = held[f, here, :LANES], held[f, here, LANES:]
            cos, sin = twiddle[0, f : f + 1, :], twiddle[1, f : f + 1, :]
            values.append((real * cos - imag * sin, imag * cos + real * sin))
        mixed = sixteen(values, 1)
        side = jnp.zeros((chunk, LANES), jnp.float32)
        for b in range(RADIX):
            low_lane = (b % 2) * LANES
            out_v[b // 2, here, low_lane : low_lane + LANES] = mixed[b][0]
            if b > 0 and b % 2 == 0:
                side = jnp.where(lane_at == b // 2 - 1, mixed[b][0][:, 0:1], side)
        side_v[here, :] = side
        outgoing(step).start()
        return carry

    lax.fori_loop(0, steps, body, 0)
    beside = side_v[...].T
    for d in range(CHANNELS):
        out_v[d, LANES + 1 : LANES + 2, :LANES] = beside[d : d + 1, :]
    last = fetched(
        out_v.at[:, pl.ds(LANES, 8), :], out.at[:, pl.ds(LANES, 8), :], in_sems.at[4]
    )
    for step in range(steps):
        outgoing(step).wait()
    last.wait()


def dual_edges(dual, last_row, last_column):
    rows, cols = [], []
    for c in range(CHANNELS):
        rows.append(dual[c, 0, 112:128, :].astype(jnp.float32)[15:16, :])
        cols.append(dual[c, 1, :, LANES:].astype(jnp.float32)[:, LANES - 1 :])
    last_row[...] = jnp.concatenate(rows, axis=0)
    last_column[...] = jnp.concatenate(cols, axis=1).T


def swap_ready(where, *refs):
    pieces, out, sems = refs[:4], refs[4], refs[5]
    lanes = pl.ds(pl.multiple_of((1 - where[1]) * 256, 256), 256)
    copies = [fetched(pieces[k].at[:, lanes], out.at[k], sems.at[k]) for k in range(4)]
    for copy in copies:
        copy.wait()


def tile_ready(where, *refs):
    pieces, (swapped, dual, above, left) = refs[:4], refs[4:8]
    for_image, for_ahead, first_row, first_column = refs[8:]
    row_at = lax.broadcasted_iota(jnp.int32, (LANES, 2 * LANES), 0)
    lane_at = lax.broadcasted_iota(jnp.int32, (LANES, 2 * LANES), 1)
    for k in range(4):
        for other in range(2):
            lanes = where[1] * (1 - other) + (1 - where[1]) * other
            c = (where[0] + 4 - k) % 4 * 2 + lanes
            p = dual[c, 0].astype(jnp.float32)
            q = dual[c, 1].astype(jnp.float32)
            beside = jnp.broadcast_to(left[pl.ds(c, 1), :], (LANES, LANES)).T[:, 0:1]
            prev_p = jnp.where(row_at == 0, above[pl.ds(c, 1), :], pltpu.roll(p, 1, 0))
            prev_q = jnp.where(lane_at == 0, beside, pltpu.roll(q, 1, 1))
            adjoint = prev_p - p + prev_q - q
            if other:
                image = swapped[k]
            else:
                own = pl.ds(pl.multiple_of(where[1] * 256, 256), 256)
                image = pieces[k][:, own]
            ahead = image - adjoint
            for_image[c] = image - step_primal * adjoint
            for_ahead[c] = ahead
            first_row[pl.ds(c, 1), :] = ahead[0:1, :]
            first_column[pl.ds(c, 1), :] = ahead[:, :LANES].T[0:1, :]


def finish(
    gradient, for_image, for_ahead, dual, below, right, image_next, dual_next,
    ahead_v, side_v, image_v, dual_v, image_sems, dual_sems,
):
    sides = []
    for c in range(CHANNELS):
        sides.append(gradient[c, LANES + 1 : LANES + 2, :LANES])
    side_v[:, :CHANNELS] = (right[...] - jnp.concatenate(sides, axis=0)).T
    for c in range(CHANNELS):
        slope = gradient[c, :LANES, :]
        image_v[c] = for_image[c] - step_primal * slope
        ahead_v[c, :LANES, :] = for_ahead[c] - slope
        ahead_v[c, LANES : LANES + 1, :] = (
            below[c : c + 1, :] - gradient[c, LANES : LANES + 1, :]
        )
        pltpu.make_async_copy(image_v.at[c], image_next.at[c], image_sems.at[c]).start()
    chunk = 16
    steps = LANES // chunk
    row_at = lax.broadcasted_iota(jnp.int32, (chunk, 2 * LANES), 0)
    lane_at = lax.broadcasted_iota(jnp.int32, (chunk, 2 * LANES), 1)

    def outgoing(step):
        rows = pl.ds(pl.multiple_of(step * chunk, chunk), chunk)
        return pltpu.make_async_copy(
            dual_v.at[:, :, rows, :], dual_next.at[:, :, rows, :], dual_sems.at[step]
        )

    def body(step, carry):
        at = pl.multiple_of(step * chunk, chunk)
        here = pl.ds(at, chunk)
        after = pl.ds(pl.multiple_of(at + chunk, chunk), 8)
        firsts, seconds, total = [], [], None
        for c in range(CHANNELS):
            ahead = ahead_v[c, here, :]
            next_row = ahead_v[c, after, :][0:1, :]
            down = jnp.where(row_at == chunk - 1, next_row, pltpu.roll(ahead, chunk - 1, 0))
            beside = jnp.where(
                lane_at == 2 * LANES - 1,
                side_v[here, c : c + 1],
                pltpu.roll(ahead, 2 * LANES - 1, 1),
            )
            first = dual[c, 0, here, :].astype(jnp.float32) + step_dual * (down - ahead)
            second = dual[c, 1, here, :].astype(jnp.float32) + step_dual * (beside - ahead)
            firsts.append(first)
            seconds.append(second)
            squares = first * first + second * second
            total = squares if total is None else total + squares
        factor = 1.0 / jnp.maximum(1.0, jnp.sqrt(total) / clip_radius)
        for c in range(CHANNELS):
            dual_v[c, 0, here, :] = (firsts[c] * factor).astype(jnp.bfloat16)
            dual_v[c, 1, here, :] = (seconds[c] * factor).astype(jnp.bfloat16)
        outgoing(step).start()
        return carry

    lax.fori_loop(0, steps, body, 0)
    for c in range(CHANNELS):
        pltpu.make_async_copy(image_v.at[c], image_next.at[c], image_sems.at[c]).wait()
    for step in range(steps):
        outgoing(step).wait()


def shape(dims, dtype=jnp.float32):
    return jax.ShapeDtypeStruct(dims, dtype)


def passed_along(x, axis, by):
    devices = lax.axis_size(axis)
    pairs = [(i, i + by) for i in range(devices) if 0 <= i + by < devices]
    return lax.ppermute(x, axis, pairs)


ANY = pl.BlockSpec(memory_space=pl.ANY)
HBM = pl.BlockSpec(memory_space=pltpu.HBM)
VM = pl.BlockSpec(memory_space=pltpu.VMEM)
SM = pl.BlockSpec(memory_space=pltpu.SMEM)
DMA = pltpu.SemaphoreType.DMA


def call(kernel, out_shape, in_specs, out_specs, scratch):
    return pl.pallas_call(
        kernel,
        out_shape=out_shape,
        in_specs=in_specs,
        out_specs=out_specs,
        scratch_shapes=scratch,
        name=kernel.__name__,
        compiler_params=PARAMS,
    )


def shards(image_field, weights, measured, dual_field):
    forward, inverse, twiddle, place = host_tables()
    scale = 1.0 / GRID
    place = jnp.asarray(place, jnp.bfloat16)
    twiddle = jnp.asarray(twiddle)
    image = image_field[0]
    f32, bf16 = jnp.float32, jnp.bfloat16
    chan = lax.axis_index("chan")
    where = jnp.stack([chan // 2, chan % 2]).astype(jnp.int32)

    last_row, last_column = call(
        dual_edges,
        (shape((CHANNELS, 2 * LANES)), shape((CHANNELS, LANES))),
        [VM],
        (VM, VM),
        [],
    )(dual_field)
    above = passed_along(last_row, "facet", 1)
    left = passed_along(last_column, "chan", 1)

    spread, *pieces = call(
        rows_forward,
        (shape((RADIX, 2, RADIX, 8, LANES)),) + (shape((LANES, 512)),) * 4,
        [SM, HBM, HBM, HBM],
        (HBM,) * 5,
        [
            pltpu.VMEM((LANES, GRID), f32),
            pltpu.VMEM((2, RADIX, LANES), f32),
            pltpu.VMEM((256, 768), bf16),
            pltpu.VMEM((RADIX, 2, RADIX, 8, LANES), f32),
            pltpu.VMEM((GRID, 512), bf16),
            DMA((10,)),
            DMA((12,)),
        ],
    )(where, image, twiddle, jnp.asarray(halves(forward * scale).T))
    for k in range(1, 4):
        pairs = [(2 * x + z, (x + k) % 4 * 2 + z) for x in range(4) for z in range(2)]
        pieces[k] = lax.ppermute(pieces[k], "chan", pairs)
    cols = lax.all_to_all(
        spread.reshape(RADIX, 2 * LANES, LANES), "facet", split_axis=0, concat_axis=0, tiled=True
    )
    data = call(
        data_prepared,
        shape((3, RADIX, LANES, LANES), bf16),
        [VM] * 3,
        HBM,
        [pltpu.VMEM((GRID, LANES), f32), pltpu.VMEM((3, RADIX, LANES, LANES), bf16), DMA((3,))],
    )(weights[0], measured[0], place)
    to_swap = call(
        swap_ready, shape((4, LANES, 256)), [SM] + [HBM] * 4, HBM, [DMA((4,))]
    )(where, *pieces)
    cols, to_swap, above, left, data = lax.optimization_barrier(
        (cols, to_swap, above, left, data)
    )
    swapped = lax.ppermute(to_swap, "chan", [(i, i ^ 1) for i in range(8)])
    back = call(
        columns,
        shape((RADIX, 2 * LANES + 8, LANES)),
        [HBM, HBM, VM, HBM, HBM],
        HBM,
        [
            pltpu.VMEM((RADIX, 2, LANES, LANES), f32),
            pltpu.VMEM((3, RADIX, LANES, LANES), bf16),
            pltpu.VMEM((768, 256), bf16),
            pltpu.VMEM((768, 256), bf16),
            pltpu.VMEM((RADIX, 2, LANES, LANES), f32),
            pltpu.VMEM((RADIX, 8, LANES), f32),
            pltpu.VMEM((RADIX * 32, 512), bf16),
            DMA((6,)),
            DMA((4,)),
            DMA((4, 2)),
        ],
    )(
        cols.reshape(RADIX, 2, LANES, LANES),
        data,
        twiddle,
        jnp.asarray(halves(forward)),
        jnp.asarray(halves(inverse)),
    )
    lines = lax.all_to_all(back, "facet", split_axis=0, concat_axis=0, tiled=True)
    for_image, for_ahead, first_row, first_column = call(
        tile_ready,
        (
            shape((CHANNELS, LANES, 2 * LANES)),
            shape((CHANNELS, LANES, 2 * LANES)),
            shape((CHANNELS, 2 * LANES)),
            shape((CHANNELS, LANES)),
        ),
        [SM] + [VM] * 8,
        (VM,) * 4,
        [],
    )(where, *pieces, swapped, dual_field, above, left)
    below = passed_along(first_row, "facet", -1)
    right = passed_along(first_column, "chan", -1)
    lines, for_image, for_ahead, below, right = lax.optimization_barrier(
        (lines, for_image, for_ahead, below, right)
    )
    slopes = call(
        rows_back,
        shape((CHANNELS, LANES + 8, 2 * LANES)),
        [ANY, VM, HBM],
        ANY,
        [
            pltpu.VMEM((RADIX, 2 * LANES, LANES), f32),
            pltpu.VMEM((RADIX, 8, LANES), f32),
            pltpu.VMEM((768, 256), bf16),
            pltpu.VMEM((RADIX, LANES, 256), f32),
            pltpu.VMEM((CHANNELS, LANES + 8, 2 * LANES), f32),
            pltpu.VMEM((LANES, LANES), f32),
            DMA((6,)),
            DMA((8,)),
        ],
    )(lines, twiddle, jnp.asarray(halves(inverse * scale)))
    gradient = lax.all_to_all(slopes, "chan", split_axis=0, concat_axis=0, tiled=True)
    return call(
        finish,
        (shape((CHANNELS, LANES, 2 * LANES)), shape((CHANNELS, 2, LANES, 2 * LANES), bf16)),
        [VM] * 6,
        (ANY, ANY),
        [
            pltpu.VMEM((CHANNELS, LANES + 8, 2 * LANES), f32),
            pltpu.VMEM((LANES, LANES), f32),
            pltpu.VMEM((CHANNELS, LANES, 2 * LANES), f32),
            pltpu.VMEM((CHANNELS, 2, LANES, 2 * LANES), bf16),
            DMA((8,)),
            DMA((8,)),
        ],
    )(gradient, for_image, for_ahead, dual_field, below, right)


def solution(mesh):
    placed = (
        P("chan", "facet", None),
        P("chan", None, "facet"),
        P("chan", None, None, "facet"),
        P(None, None, "facet", "chan"),
    )
    return jax.shard_map(
        shards,
        mesh=mesh,
        in_specs=placed,
        out_specs=(P(None, "facet", "chan"), P(None, None, "facet", "chan")),
        check_vma=False,
    )
```

time: 137 us -> 146 us (1.066)
  local copies, waits for them, and re-layouts: 5.2 us -> 20.2 us
  blocking collectives: 33.2 us -> 18.6 us
  starting transfers between devices: 24.1 us -> 32.3 us
  Pallas kernels: 16.6 us -> 24.2 us
  waiting for transfers between devices: 56.1 us -> 49.1 us
    ppermute x0 -> x4, waiting for transfers between devices: none -> 37.2 us  [the longest x1 35.6 us: shards(): swapped = lax.ppermute(to_swap, 'chan', [(i, i ^ 1) for i in range(8)])]
    all_to_all x1, waiting for transfers between devices: 26.2 us -> 0.39 us  [shards(): lax.all_to_all(spread.reshape(RADIX, 2 * LANES, LANES), 'facet', split_ax...]
    unnamed x26 -> x56, local copies, waits for them, and re-layouts: 5.2 us -> 20.2 us
    all_to_all x1, blocking collectives: 33.2 us -> 18.6 us  [shards(): lax.all_to_all(slopes, 'chan', split_axis=0, concat_axis=0, tiled=True)]
    all_to_all x1, waiting for transfers between devices: 14.2 us -> 0.01 us  [shards(): lax.all_to_all(back, 'facet', split_axis=0, concat_axis=0, tiled=True)]
    pallas_call x7 -> x8, Pallas kernels: 16.6 us -> 24.2 us  [the longest x1 7.6 us: shards(): call(columns, shape((RADIX, 2 * LANES + 8, LANES)), [HBM, HBM, VM, HBM, H...]
    ppermute x0 -> x4, starting transfers between devices: none -> 6.64 us  [the longest x3 5.66 us: shards(): pieces[k] = lax.ppermute(pieces[k], 'chan', pairs)]
    ppermute x4, waiting for transfers between devices: 15.7 us -> 11.6 us  [passed_along(): return lax.ppermute(x, axis, pairs)]
  transfers between devices with their start and end apart: 6 -> 10, of which waited for: 4 -> 5; matrix products, arithmetic and copies ran while one was open for 0% -> 0% of each run, Pallas kernels for 1% -> 3%
where the time goes in v1:
time: 146 us; the launch traced here: 145 us
  waiting for transfers between devices  49.1 us (34%)
  starting transfers between devices  32.3 us (22%)
  Pallas kernels  24.2 us (17%)
  local copies, waits for them, and re-layouts  20.2 us (14%)
  blocking collectives  18.6 us (13%)
    ppermute x1, waiting for transfers between devices, shards(): swapped = lax.ppermute(to_swap, 'chan', [(i, i ^ 1) for i in range(8)])  35.6 us
    unnamed x56, local copies, waits for them, and re-layouts  20.2 us
    all_to_all x1, blocking collectives, shards(): lax.all_to_all(slopes, 'chan', split_axis=0, concat_axis=0, tiled=True)  18.6 us
    ppermute x4, waiting for transfers between devices, passed_along(): return lax.ppermute(x, axis, pairs)  11.6 us
    ppermute x4, starting transfers between devices, passed_along(): return lax.ppermute(x, axis, pairs)  10.8 us
    all_to_all x1, starting transfers between devices, shards(): lax.all_to_all(spread.reshape(RADIX, 2 * LANES, LANES), 'facet', split_ax...  8.38 us
    pallas_call x1, Pallas kernels, shards(): call(columns, shape((RADIX, 2 * LANES + 8, LANES)), [HBM, HBM, VM, HBM, H...  7.6 us
    pallas_call x1, Pallas kernels, shards(): call(rows_forward, (shape((RADIX, 2, RADIX, 8, LANES)),) + (shape((LANES,...  6.49 us
  transfers between devices with their start and end apart: 10, of which 5 were waited for; matrix products, arithmetic and copies ran while one was open for 0% of the time, Pallas kernels for 3%

profile of v1, /device:TPU:8, one launch (start us, length us, event | category | flops | bytes accessed | tf_op | source)
XLA Modules:
  0.0 145.3 jit_solution(10060909362705829663)
XLA Ops:
  0.6 0.1 pad_add_fusion.where
  0.7 1.2 copy-done.9
  2.0 1.0 copy-done.21
  2.9 0.7 copy-done.22
  3.7 6.5 %rows_forward.1 = (f32[16,2,16,8,128]{4,3,2,1,0:T(8,128)S(1)}, f32[128,512]{1,0:T(8,128)S(1)}, f32[128,512]{1,0:T(8,128)S(1)}, f32[128,512]{1,0:T(8,128)S(1)}, f32[128,512]{1,0:T(8,128)S(1)}) custom-call(s32[2]{0:T(128)S(1)} %pad_add_fusion.where, f32[128,2048]{1,0:T(8,128)S(1)} %bitcast.10, f32[2,16,128]{2,1,0:T(8,128)S(1)} %copy-done.22, ...), custom_call_target="tpu_custom_call" | custom-call | tf_op jit(solution)/shard_map/rows_forward/pallas_call | solution.py:531
  10.2 1.4 copy-done.3
  11.5 0.7 copy-done.27
  12.2 0.7 copy-done.25
  12.9 0.1 copy-done.26
  13.0 8.4 %all-to-all-start = ((f32[16,256,128]{2,1,0:T(8,128)}), f32[16,256,128]{2,1,0:T(8,128)S(1)}, u32[]{:S(2)}, u32[]{:S(2)}) async-start(f32[16,256,128]{2,1,0:T(8,128)} %bitcast.8), calls=%async_computation | async-start | bytes 4194304 | tf_op jit(solution)/shard_map/all_to_all | solution.py:549
  21.4 1.5 %collective-permute-start = (f32[128,512]{1,0:T(8,128)}, f32[128,512]{1,0:T(8,128)S(1)}, u32[]{:S(2)}, u32[]{:S(2)}) collective-permute-start(f32[128,512]{1,0:T(8,128)} %copy-done.27), channel_id=1, source_target_pairs={{0,32},{16,48},{32,64},{48,80},{64,96},{80,112},{96,0},{112,16},{1... | collective-permute-start | bytes 786440 | tf_op jit(solution)/shard_map/ppermute | solution.py:548
  22.9 2.7 %collective-permute-start.1 = (f32[128,512]{1,0:T(8,128)}, f32[128,512]{1,0:T(8,128)S(1)}, u32[]{:S(2)}, u32[]{:S(2)}) collective-permute-start(f32[128,512]{1,0:T(8,128)} %copy-done.26), channel_id=1, source_target_pairs={{0,64},{16,80},{32,96},{48,112},{64,0},{80,16},{96,32},{112,48},{1... | collective-permute-start | bytes 786440 | tf_op jit(solution)/shard_map/ppermute | solution.py:548
  25.6 1.4 collective-permute-start.2
  27.1 0.2 dual_edges.1
  27.2 1.9 %collective-permute-start.3 = (f32[8,256]{1,0:T(8,128)S(1)}, f32[8,256]{1,0:T(8,128)S(1)}, u32[]{:S(2)}, u32[]{:S(2)}) collective-permute-start(f32[8,256]{1,0:T(8,128)S(1)} %get-tuple-element.28), channel_id=1, source_target_pairs={{0,1},{1,2},{2,3},{3,4},{4,5},{5,6},{6,7},{7,8},{8,9},{9,10},{10,1... | collective-permute-start | bytes 24584 | tf_op jit(solution)/shard_map/ppermute | solution.py:489
  29.2 2.9 %collective-permute-start.4 = (f32[8,128]{1,0:T(8,128)S(1)}, f32[8,128]{1,0:T(8,128)S(1)}, u32[]{:S(2)}, u32[]{:S(2)}) collective-permute-start(f32[8,128]{1,0:T(8,128)S(1)} %get-tuple-element.29), channel_id=1, source_target_pairs={{0,16},{16,32},{32,48},{48,64},{64,80},{80,96},{96,112},{1,17},{17... | collective-permute-start | bytes 12296 | tf_op jit(solution)/shard_map/ppermute | solution.py:489
  32.1 0.0 copy-start.4
  32.1 1.2 copy-done.4
  33.3 1.0 copy-done.16
  34.4 1.8 %data_prepared.1.data = bf16[3,16,128,128]{3,2,1,0:T(8,128)(2,1)S(1)} custom-call(bf16[2048,128]{1,0:T(8,128)(2,1)S(1)} %bitcast.11, bf16[2,2048,128]{2,1,0:T(8,128)(2,1)S(1)} %bitcast.9, bf16[128,128]{1,0:T(8,128)(2,1)S(1)} %copy-done.24), custom_call_target="tpu_custom_call" | custom-call | tf_op jit(solution)/shard_map/data_prepared/pallas_call | solution.py:552
  36.2 1.6 %collective-permute-done.1.refs_2_ = f32[128,512]{1,0:T(8,128)S(1)} collective-permute-done((f32[128,512]{1,0:T(8,128)}, f32[128,512]{1,0:T(8,128)S(1)}, u32[]{:S(2)}, u32[]{:S(2)}) %collective-permute-start.1) | collective-permute-done | bytes 262176 | tf_op jit(solution)/shard_map/ppermute | solution.py:548
  37.8 0.7 swap_ready.1
  38.5 0.7 copy-done.10
  39.2 0.7 copy-done.12
  39.9 0.7 copy-done.14
  40.6 0.8 copy-done.17
  41.4 7.4 %collective-permute-done.3.refs_6_ = f32[8,256]{1,0:T(8,128)S(1)} collective-permute-done((f32[8,256]{1,0:T(8,128)S(1)}, f32[8,256]{1,0:T(8,128)S(1)}, u32[]{:S(2)}, u32[]{:S(2)}) %collective-permute-start.3) | collective-permute-done | bytes 8224 | tf_op jit(solution)/shard_map/ppermute | solution.py:489
  48.7 0.4 all-to-all-done
  49.1 1.4 copy-done.2
  50.5 1.0 copy-done.19
  51.5 1.0 copy-done.20
  52.5 7.6 %columns.1 = f32[16,264,128]{2,1,0:T(8,128)} custom-call(f32[16,2,128,128]{3,2,1,0:T(8,128)S(1)} %bitcast.7, bf16[3,16,128,128]{3,2,1,0:T(8,128)(2,1)S(1)} %copy-done.2, f32[2,16,128]{2,1,0:T(8,128)S(1)} %copy-done.23, bf16[768,256]{1,0:T(8,128)(2,1)S(1)} %copy-done.20, bf16[768,256]{1,0:T(8,128)(2,1)S(1)} %copy-done.19), custom_call_target="tpu_custom_call" | custom-call | tf_op jit(solution)/shard_map/columns/pallas_call | solution.py:566
  60.1 6.5 %all-to-all-start.1 = ((f32[16,264,128]{2,1,0:T(8,128)}), f32[16,264,128]{2,1,0:T(8,128)S(1)}, u32[]{:S(2)}, u32[]{:S(2)}) async-start(f32[16,264,128]{2,1,0:T(8,128)} %columns.1), calls=%async_computation.1 | async-start | bytes 4325376 | tf_op jit(solution)/shard_map/all_to_all | solution.py:590
  66.6 1.0 collective-permute-start.5
  67.6 35.6 %collective-permute-done.5.refs_4_ = f32[4,128,256]{2,1,0:T(8,128)S(1)} collective-permute-done((f32[4,128,256]{2,1,0:T(8,128)}, f32[4,128,256]{2,1,0:T(8,128)S(1)}, u32[]{:S(2)}, u32[]{:S(2)}) %collective-permute-start.5) | collective-permute-done | bytes 524320 | tf_op jit(solution)/shard_map/ppermute | solution.py:565
  103.2 0.9 copy-done.11
  104.2 0.9 copy-done.13
  105.1 0.9 copy-done.15
  106.1 1.3 tile_ready.1
  107.4 1.0 copy-done.5
  108.4 1.0 copy-done.7
  109.4 4.7 %collective-permute-start.6 = (f32[8,256]{1,0:T(8,128)S(1)}, f32[8,256]{1,0:T(8,128)S(1)}, u32[]{:S(2)}, u32[]{:S(2)}) collective-permute-start(f32[8,256]{1,0:T(8,128)S(1)} %get-tuple-element.37), channel_id=1, source_target_pairs={{1,0},{2,1},{3,2},{4,3},{5,4},{6,5},{7,6},{8,7},{9,8},{10,9},{11,1... | collective-permute-start | bytes 24584 | tf_op jit(solution)/shard_map/ppermute | solution.py:489
  114.1 1.3 collective-permute-start.7
  115.4 4.2 %collective-permute-done.7.right = f32[8,128]{1,0:T(8,128)S(1)} collective-permute-done((f32[8,128]{1,0:T(8,128)S(1)}, f32[8,128]{1,0:T(8,128)S(1)}, u32[]{:S(2)}, u32[]{:S(2)}) %collective-permute-start.7) | collective-permute-done | bytes 4128 | tf_op jit(solution)/shard_map/ppermute | solution.py:489
  119.6 1.0 copy-done.18
  120.6 3.7 %rows_back.1 = f32[8,136,256]{2,1,0:T(8,128)S(1)} custom-call(f32[16,264,128]{2,1,0:T(8,128)S(1)} %all-to-all-done.1.lines, f32[2,16,128]{2,1,0:T(8,128)S(1)} %copy-done.23, bf16[768,256]{1,0:T(8,128)(2,1)S(1)} %copy-done.18), custom_call_target="tpu_custom_call" | custom-call | tf_op jit(solution)/shard_map/rows_back/pallas_call | solution.py:608
  124.3 18.6 %all_to_all.15.gradient = f32[8,136,256]{2,1,0:T(8,128)S(1)} all-to-all(f32[8,136,256]{2,1,0:T(8,128)S(1)} %rows_back.1), channel_id=1, replica_groups=mesh['chan'=8,'facet'=16] {'chan'}, dimensions={0} | all-to-all | bytes 2228224 | tf_op jit(solution)/shard_map/all_to_all | solution.py:624
  142.9 2.4 %finish.1 = (f32[8,128,256]{2,1,0:T(8,128)}, bf16[8,2,128,256]{3,2,1,0:T(8,128)(2,1)}) custom-call(f32[8,136,256]{2,1,0:T(8,128)S(1)} %all_to_all.15.gradient, f32[8,128,256]{2,1,0:T(8,128)S(1)} %copy-done.6, f32[8,128,256]{2,1,0:T(8,128)S(1)} %copy-done.8, bf16[8,2,128,256]{3,2,1,0:T(8,128)(2,1)S(1)} %copy-done, f32[8,256]{1,0:T(8,128)S(1)} %collective-permute-done.6.below, ...), custom_call_target="tpu_custom_call" | custom-call | tf_op jit(solution)/shard_map/finish/pallas_call | solution.py:625
  (38 shorter events, 0.1 us)
Async XLA Ops:
  0.7 1.2 copy-start.9
  1.9 1.0 copy-start.21
  2.9 0.7 copy-start.22
  10.2 1.4 copy-start.3
  11.5 0.7 copy-start.27
  12.2 0.7 copy-start.25
  12.2 0.8 copy-start.26
  13.0 14.0 %copy-start = (bf16[8,2,128,256]{3,2,1,0:T(8,128)(2,1)S(1)}, bf16[8,2,128,256]{3,2,1,0:T(8,128)(2,1)}, u32[]{:S(2)}) copy-start(bf16[8,2,128,256]{3,2,1,0:T(8,128)(2,1)} %dual.3) | copy-start | bytes 3145732
  13.0 19.1 %copy-start.24 = (bf16[128,128]{1,0:T(8,128)(2,1)S(1)}, bf16[128,128]{1,0:T(8,128)(2,1)}, u32[]{:S(2)}) copy-start(bf16[128,128]{1,0:T(8,128)(2,1)} %constant.42.clone.place) | copy-start | bytes 98308
  13.0 36.1 %all-to-all-start = ((f32[16,256,128]{2,1,0:T(8,128)}), f32[16,256,128]{2,1,0:T(8,128)S(1)}, u32[]{:S(2)}, u32[]{:S(2)}) async-start(f32[16,256,128]{2,1,0:T(8,128)} %bitcast.8), calls=%async_computation | async-start | bytes 4194304 | tf_op jit(solution)/shard_map/all_to_all | solution.py:549
  21.4 14.8 %collective-permute-start = (f32[128,512]{1,0:T(8,128)}, f32[128,512]{1,0:T(8,128)S(1)}, u32[]{:S(2)}, u32[]{:S(2)}) collective-permute-start(f32[128,512]{1,0:T(8,128)} %copy-done.27), channel_id=1, source_target_pairs={{0,32},{16,48},{32,64},{48,80},{64,96},{80,112},{96,0},{112,16},{1... | collective-permute-start | bytes 786440 | tf_op jit(solution)/shard_map/ppermute | solution.py:548
  22.9 14.9 %collective-permute-start.1 = (f32[128,512]{1,0:T(8,128)}, f32[128,512]{1,0:T(8,128)S(1)}, u32[]{:S(2)}, u32[]{:S(2)}) collective-permute-start(f32[128,512]{1,0:T(8,128)} %copy-done.26), channel_id=1, source_target_pairs={{0,64},{16,80},{32,96},{48,112},{64,0},{80,16},{96,32},{112,48},{1... | collective-permute-start | bytes 786440 | tf_op jit(solution)/shard_map/ppermute | solution.py:548
  25.6 12.2 %collective-permute-start.2 = (f32[128,512]{1,0:T(8,128)}, f32[128,512]{1,0:T(8,128)S(1)}, u32[]{:S(2)}, u32[]{:S(2)}) collective-permute-start(f32[128,512]{1,0:T(8,128)} %copy-done.25), channel_id=1, source_target_pairs={{0,96},{16,112},{32,0},{48,16},{64,32},{80,48},{96,64},{112,80},{1... | collective-permute-start | bytes 786440 | tf_op jit(solution)/shard_map/ppermute | solution.py:548
  27.2 21.5 %collective-permute-start.3 = (f32[8,256]{1,0:T(8,128)S(1)}, f32[8,256]{1,0:T(8,128)S(1)}, u32[]{:S(2)}, u32[]{:S(2)}) collective-permute-start(f32[8,256]{1,0:T(8,128)S(1)} %get-tuple-element.28), channel_id=1, source_target_pairs={{0,1},{1,2},{2,3},{3,4},{4,5},{5,6},{6,7},{7,8},{8,9},{9,10},{10,1... | collective-permute-start | bytes 24584 | tf_op jit(solution)/shard_map/ppermute | solution.py:489
  29.2 12.2 %collective-permute-start.4 = (f32[8,128]{1,0:T(8,128)S(1)}, f32[8,128]{1,0:T(8,128)S(1)}, u32[]{:S(2)}, u32[]{:S(2)}) collective-permute-start(f32[8,128]{1,0:T(8,128)S(1)} %get-tuple-element.29), channel_id=1, source_target_pairs={{0,16},{16,32},{32,48},{48,64},{64,80},{80,96},{96,112},{1,17},{17... | collective-permute-start | bytes 12296 | tf_op jit(solution)/shard_map/ppermute | solution.py:489
  32.1 1.2 copy-start.4
  33.3 1.0 copy-start.16
  34.4 14.7 %copy-start.23 = (f32[2,16,128]{2,1,0:T(8,128)S(1)}, f32[2,16,128]{2,1,0:T(8,128)}, u32[]{:S(2)}) copy-start(f32[2,16,128]{2,1,0:T(8,128)} %constant.43.clone.twiddle) | copy-start | bytes 49156
  36.2 5.2 %copy-start.1 = (bf16[3,16,128,128]{3,2,1,0:T(8,128)(2,1)}, bf16[3,16,128,128]{3,2,1,0:T(8,128)(2,1)S(1)}, u32[]{:S(2)}) copy-start(bf16[3,16,128,128]{3,2,1,0:T(8,128)(2,1)S(1)} %data_prepared.1.data) | copy-start | bytes 4718596
  38.5 0.7 copy-start.10
  39.2 0.7 copy-start.12
  39.9 0.7 copy-start.14
  40.6 0.8 copy-start.17
  49.1 1.4 copy-start.2
  50.5 1.0 copy-start.19
  51.5 1.0 copy-start.20
  60.1 59.4 %all-to-all-start.1 = ((f32[16,264,128]{2,1,0:T(8,128)}), f32[16,264,128]{2,1,0:T(8,128)S(1)}, u32[]{:S(2)}, u32[]{:S(2)}) async-start(f32[16,264,128]{2,1,0:T(8,128)} %columns.1), calls=%async_computation.1 | async-start | bytes 4325376 | tf_op jit(solution)/shard_map/all_to_all | solution.py:590
  66.6 36.6 %collective-permute-start.5 = (f32[4,128,256]{2,1,0:T(8,128)}, f32[4,128,256]{2,1,0:T(8,128)S(1)}, u32[]{:S(2)}, u32[]{:S(2)}) collective-permute-start(f32[4,128,256]{2,1,0:T(8,128)} %copy-done.17), channel_id=1, source_target_pairs={{0,16},{16,0},{32,48},{48,32},{64,80},{80,64},{96,112},{112,96},{1... | collective-permute-start | bytes 1572872 | tf_op jit(solution)/shard_map/ppermute | solution.py:565
  103.2 1.0 copy-start.11
  104.2 0.9 copy-start.13
  105.1 0.9 copy-start.15
  107.4 1.0 copy-start.5
  108.4 1.0 copy-start.7
  109.4 10.2 %collective-permute-start.6 = (f32[8,256]{1,0:T(8,128)S(1)}, f32[8,256]{1,0:T(8,128)S(1)}, u32[]{:S(2)}, u32[]{:S(2)}) collective-permute-start(f32[8,256]{1,0:T(8,128)S(1)} %get-tuple-element.37), channel_id=1, source_target_pairs={{1,0},{2,1},{3,2},{4,3},{5,4},{6,5},{7,6},{8,7},{9,8},{10,9},{11,1... | collective-permute-start | bytes 24584 | tf_op jit(solution)/shard_map/ppermute | solution.py:489
  114.1 5.5 %collective-permute-start.7 = (f32[8,128]{1,0:T(8,128)S(1)}, f32[8,128]{1,0:T(8,128)S(1)}, u32[]{:S(2)}, u32[]{:S(2)}) collective-permute-start(f32[8,128]{1,0:T(8,128)S(1)} %get-tuple-element.38), channel_id=1, source_target_pairs={{16,0},{32,16},{48,32},{64,48},{80,64},{96,80},{112,96},{17,1},{33... | collective-permute-start | bytes 12296 | tf_op jit(solution)/shard_map/ppermute | solution.py:489
  119.6 1.0 copy-start.18
  120.6 22.4 %copy-start.6 = (f32[8,128,256]{2,1,0:T(8,128)S(1)}, f32[8,128,256]{2,1,0:T(8,128)}, u32[]{:S(2)}) copy-start(f32[8,128,256]{2,1,0:T(8,128)} %copy-done.5) | copy-start | bytes 3145732
  120.6 22.4 %copy-start.8 = (f32[8,128,256]{2,1,0:T(8,128)S(1)}, f32[8,128,256]{2,1,0:T(8,128)}, u32[]{:S(2)}) copy-start(f32[8,128,256]{2,1,0:T(8,128)} %copy-done.7) | copy-start | bytes 3145732

commit v2 on v1

--- a/solution.py
+++ b/solution.py
@@ -19,7 +19,7 @@
 step_dual = 0.5
 clip_radius = 4.0
 
-PARAMS = pltpu.CompilerParams(vmem_limit_bytes=48 * 1024 * 1024)
+PARAMS = pltpu.CompilerParams(vmem_limit_bytes=63 * 1024 * 1024)
 
 
 def host_tables():
@@ -420,20 +420,37 @@
 
 def finish(
     gradient, for_image, for_ahead, dual, below, right, image_next, dual_next,
-    ahead_v, side_v, image_v, dual_v, image_sems, dual_sems,
+    gradient_v, base_v, dual_in, ahead_v, side_v, image_v, dual_v,
+    in_sems, dual_in_sems, image_sems, dual_sems,
 ):
+    arriving = []
+    for c in range(CHANNELS):
+        arriving.append(
+            [
+                fetched(gradient.at[c], gradient_v.at[c], in_sems.at[c, 0]),
+                fetched(for_image.at[c], base_v.at[0, c], in_sems.at[c, 1]),
+                fetched(for_ahead.at[c], base_v.at[1, c], in_sems.at[c, 2]),
+            ]
+        )
+    arriving_dual = [
+        fetched(dual.at[c], dual_in.at[c], dual_in_sems.at[c]) for c in range(CHANNELS)
+    ]
     sides = []
+    leaving = []
     for c in range(CHANNELS):
-        sides.append(gradient[c, LANES + 1 : LANES + 2, :LANES])
+        for copy in arriving[c]:
+            copy.wait()
+        slope = gradient_v[c, :LANES, :]
+        image_v[c] = base_v[0, c] - step_primal * slope
+        leaving.append(fetched(image_v.at[c], image_next.at[c], image_sems.at[c]))
+        ahead_v[c, :LANES, :] = base_v[1, c] - slope
+        ahead_v[c, LANES : LANES + 1, :] = (
+            below[c : c + 1, :] - gradient_v[c, LANES : LANES + 1, :]
+        )
+        sides.append(gradient_v[c, LANES + 1 : LANES + 2, :LANES])
     side_v[:, :CHANNELS] = (right[...] - jnp.concatenate(sides, axis=0)).T
-    for c in range(CHANNELS):
-        slope = gradient[c, :LANES, :]
-        image_v[c] = for_image[c] - step_primal * slope
-        ahead_v[c, :LANES, :] = for_ahead[c] - slope
-        ahead_v[c, LANES : LANES + 1, :] = (
-            below[c : c + 1, :] - gradient[c, LANES : LANES + 1, :]
-        )
-        pltpu.make_async_copy(image_v.at[c], image_next.at[c], image_sems.at[c]).start()
+    for copy in arriving_dual:
+        copy.wait()
     chunk = 16
     steps = LANES // chunk
     row_at = lax.broadcasted_iota(jnp.int32, (chunk, 2 * LANES), 0)
@@ -459,8 +476,8 @@
                 side_v[here, c : c + 1],
                 pltpu.roll(ahead, 2 * LANES - 1, 1),
             )
-            first = dual[c, 0, here, :].astype(jnp.float32) + step_dual * (down - ahead)
-            second = dual[c, 1, here, :].astype(jnp.float32) + step_dual * (beside - ahead)
+            first = dual_in[c, 0, here, :].astype(jnp.float32) + step_dual * (down - ahead)
+            second = dual_in[c, 1, here, :].astype(jnp.float32) + step_dual * (beside - ahead)
             firsts.append(first)
             seconds.append(second)
             squares = first * first + second * second
@@ -473,8 +490,8 @@
         return carry
 
     lax.fori_loop(0, steps, body, 0)
-    for c in range(CHANNELS):
-        pltpu.make_async_copy(image_v.at[c], image_next.at[c], image_sems.at[c]).wait()
+    for copy in leaving:
+        copy.wait()
     for step in range(steps):
         outgoing(step).wait()
 
@@ -559,9 +576,7 @@
     to_swap = call(
         swap_ready, shape((4, LANES, 256)), [SM] + [HBM] * 4, HBM, [DMA((4,))]
     )(where, *pieces)
-    cols, to_swap, above, left, data = lax.optimization_barrier(
-        (cols, to_swap, above, left, data)
-    )
+    cols, above, left, data = lax.optimization_barrier((cols, above, left, data))
     swapped = lax.ppermute(to_swap, "chan", [(i, i ^ 1) for i in range(8)])
     back = call(
         columns,
@@ -587,6 +602,7 @@
         jnp.asarray(halves(forward)),
         jnp.asarray(halves(inverse)),
     )
+    back, swapped = lax.optimization_barrier((back, swapped))
     lines = lax.all_to_all(back, "facet", split_axis=0, concat_axis=0, tiled=True)
     for_image, for_ahead, first_row, first_column = call(
         tile_ready,
@@ -625,13 +641,18 @@
     return call(
         finish,
         (shape((CHANNELS, LANES, 2 * LANES)), shape((CHANNELS, 2, LANES, 2 * LANES), bf16)),
-        [VM] * 6,
-        (ANY, ANY),
+        [HBM] * 4 + [VM] * 2,
+        (HBM, HBM),
         [
+            pltpu.VMEM((CHANNELS, LANES + 8, 2 * LANES), f32),
+            pltpu.VMEM((2, CHANNELS, LANES, 2 * LANES), f32),
+            pltpu.VMEM((CHANNELS, 2, LANES, 2 * LANES), bf16),
             pltpu.VMEM((CHANNELS, LANES + 8, 2 * LANES), f32),
             pltpu.VMEM((LANES, LANES), f32),
             pltpu.VMEM((CHANNELS, LANES, 2 * LANES), f32),
             pltpu.VMEM((CHANNELS, 2, LANES, 2 * LANES), bf16),
+            DMA((8, 3)),
+            DMA((8,)),
             DMA((8,)),
             DMA((8,)),
         ],

time: 146 us -> 173 us (1.18)
  Pallas kernels: 24.2 us -> 82.4 us
  waiting for transfers between devices: 49.1 us -> 29.8 us
  local copies, waits for them, and re-layouts: 20.2 us -> 1.59 us
  blocking collectives: 18.6 us -> 21.8 us
    ppermute x1, waiting for transfers between devices: 35.6 us -> 0.01 us  [shards(): swapped = lax.ppermute(to_swap, 'chan', [(i, i ^ 1) for i in range(8)])]
    pallas_call x1, Pallas kernels: 6.49 us -> 33.8 us  [shards(): call(rows_forward, (shape((RADIX, 2, RADIX, 8, LANES)),) + (shape((LANES,...]
    unnamed x56 -> x22, local copies, waits for them, and re-layouts: 20.2 us -> 1.59 us
    pallas_call x1, Pallas kernels: 0.67 us -> 17.7 us  [shards(): call(swap_ready, shape((4, LANES, 256)), [SM] + [HBM] * 4, HBM, [DMA((4,))])]
    ppermute x3, waiting for transfers between devices: 1.56 us -> 10.5 us  [shards(): pieces[k] = lax.ppermute(pieces[k], 'chan', pairs)]
    all_to_all x1, waiting for transfers between devices: 0.01 us -> 4.32 us  [shards(): lax.all_to_all(back, 'facet', split_axis=0, concat_axis=0, tiled=True)]
    ppermute x4, waiting for transfers between devices: 11.6 us -> 15 us  [passed_along(): return lax.ppermute(x, axis, pairs)]
    pallas_call x1, Pallas kernels: 2.39 us -> 5.62 us  [shards(): call(finish, (shape((CHANNELS, LANES, 2 * LANES)), shape((CHANNELS, 2, LA...]
  transfers between devices with their start and end apart: 10 -> 10, of which waited for: 5 -> 6; matrix products, arithmetic and copies ran while one was open for 0% -> 0% of each run, Pallas kernels for 3% -> 22%
where the time goes in v2:
time: 173 us; the launch traced here: 171 us
  Pallas kernels  82.4 us (48%)
  starting transfers between devices  33.9 us (20%)
  waiting for transfers between devices  29.8 us (17%)
  blocking collectives  21.8 us (13%)
    pallas_call x1, Pallas kernels, shards(): call(rows_forward, (shape((RADIX, 2, RADIX, 8, LANES)),) + (shape((LANES,...  33.8 us
    all_to_all x1, blocking collectives, shards(): lax.all_to_all(slopes, 'chan', split_axis=0, concat_axis=0, tiled=True)  21.8 us
    pallas_call x1, Pallas kernels, shards(): call(swap_ready, shape((4, LANES, 256)), [SM] + [HBM] * 4, HBM, [DMA((4,))])  17.7 us
    ppermute x4, waiting for transfers between devices, passed_along(): return lax.ppermute(x, axis, pairs)  15 us
    ppermute x4, starting transfers between devices, passed_along(): return lax.ppermute(x, axis, pairs)  10.7 us
    ppermute x3, waiting for transfers between devices, shards(): pieces[k] = lax.ppermute(pieces[k], 'chan', pairs)  10.5 us
    pallas_call x1, Pallas kernels, shards(): call(columns, shape((RADIX, 2 * LANES + 8, LANES)), [HBM, HBM, VM, HBM, H...  9.84 us
    all_to_all x1, starting transfers between devices, shards(): lax.all_to_all(spread.reshape(RADIX, 2 * LANES, LANES), 'facet', split_ax...  8.39 us
  transfers between devices with their start and end apart: 10, of which 6 were waited for; matrix products, arithmetic and copies ran while one was open for 0% of the time, Pallas kernels for 22%

profile of v2, /device:TPU:8, one launch (start us, length us, event | category | flops | bytes accessed | tf_op | source)
XLA Modules:
  0.0 170.9 jit_solution(14476114687136797257)
XLA Ops:
  0.6 0.7 pad_add_fusion.where
  1.3 33.8 %rows_forward.1 = (f32[16,2,16,8,128]{4,3,2,1,0:T(8,128)}, f32[128,512]{1,0:T(8,128)}, f32[128,512]{1,0:T(8,128)}, f32[128,512]{1,0:T(8,128)}, f32[128,512]{1,0:T(8,128)}) custom-call(s32[2]{0:T(128)} %pad_add_fusion.where, f32[128,2048]{1,0:T(8,128)} %bitcast.9, f32[2,16,128]{2,1,0:T(8,128)} %constant.43.clone.twiddle, bf16[256,768]{1,0:T(8,128)(2,1)} %constant.44.clone.table), custom_call_target="tpu_custom_call" | custom-call | tf_op jit(solution)/shard_map/rows_forward/pallas_call | solution.py:548
  35.1 0.0 copy-start.10
  35.1 0.0 copy-start.9
  35.1 0.0 copy-start.8
  35.1 8.4 %all-to-all-start = ((f32[16,256,128]{2,1,0:T(8,128)}), f32[16,256,128]{2,1,0:T(8,128)}, u32[]{:S(2)}, u32[]{:S(2)}) async-start(f32[16,256,128]{2,1,0:T(8,128)} %bitcast.7), calls=%async_computation | async-start | bytes 4194304 | tf_op jit(solution)/shard_map/all_to_all | solution.py:566
  43.5 0.0 copy-done.10
  43.5 1.6 collective-permute-start.2
  45.1 0.0 copy-done.9
  45.1 2.7 %collective-permute-start.3 = (f32[128,512]{1,0:T(8,128)S(1)}, f32[128,512]{1,0:T(8,128)S(1)}, u32[]{:S(2)}, u32[]{:S(2)}) collective-permute-start(f32[128,512]{1,0:T(8,128)S(1)} %copy-done.9), channel_id=1, source_target_pairs={{0,64},{16,80},{32,96},{48,112},{64,0},{80,16},{96,32},{112,48},{1... | collective-permute-start | bytes 786440 | tf_op jit(solution)/shard_map/ppermute | solution.py:565
  47.8 0.0 copy-done.8
  47.8 1.4 collective-permute-start.4
  49.2 3.9 %collective-permute-done.2.refs_1_ = f32[128,512]{1,0:T(8,128)S(1)} collective-permute-done((f32[128,512]{1,0:T(8,128)S(1)}, f32[128,512]{1,0:T(8,128)S(1)}, u32[]{:S(2)}, u32[]{:S(2)}) %collective-permute-start.2) | collective-permute-done | bytes 262176 | tf_op jit(solution)/shard_map/ppermute | solution.py:565
  53.1 0.0 copy-start
  53.1 6.6 %collective-permute-done.3.refs_2_ = f32[128,512]{1,0:T(8,128)S(1)} collective-permute-done((f32[128,512]{1,0:T(8,128)S(1)}, f32[128,512]{1,0:T(8,128)S(1)}, u32[]{:S(2)}, u32[]{:S(2)}) %collective-permute-start.3) | collective-permute-done | bytes 262176 | tf_op jit(solution)/shard_map/ppermute | solution.py:565
  59.7 0.0 copy-start.1
  59.7 0.0 collective-permute-done.4.refs_3_
  59.8 0.0 copy-start.2
  59.8 0.0 copy-done
  59.8 0.7 copy-done.1
  60.4 0.1 copy-done.2
  60.5 17.7 %swap_ready.1 = f32[4,128,256]{2,1,0:T(8,128)} custom-call(s32[2]{0:T(128)} %pad_add_fusion.where, f32[128,512]{1,0:T(8,128)} %get-tuple-element.29.refs_0_, f32[128,512]{1,0:T(8,128)} %copy-done, f32[128,512]{1,0:T(8,128)} %copy-done.1, f32[128,512]{1,0:T(8,128)} %copy-done.2), custom_call_target="tpu_custom_call" | custom-call | tf_op jit(solution)/shard_map/swap_ready/pallas_call | solution.py:576
  78.2 1.1 collective-permute-start.5
  79.3 2.0 %dual_edges.1 = (f32[8,256]{1,0:T(8,128)}, f32[8,128]{1,0:T(8,128)}) custom-call(bf16[8,2,128,256]{3,2,1,0:T(8,128)(2,1)} %dual.3), custom_call_target="tpu_custom_call" | custom-call | tf_op jit(solution)/shard_map/dual_edges/pallas_call | solution.py:538
  81.3 1.9 %collective-permute-start = (f32[8,256]{1,0:T(8,128)}, f32[8,256]{1,0:T(8,128)S(1)}, u32[]{:S(2)}, u32[]{:S(2)}) collective-permute-start(f32[8,256]{1,0:T(8,128)} %get-tuple-element.25), channel_id=1, source_target_pairs={{0,1},{1,2},{2,3},{3,4},{4,5},{5,6},{6,7},{7,8},{8,9},{9,10},{10,1... | collective-permute-start | bytes 24584 | tf_op jit(solution)/shard_map/ppermute | solution.py:506
  83.2 2.9 %collective-permute-start.1 = (f32[8,128]{1,0:T(8,128)}, f32[8,128]{1,0:T(8,128)S(1)}, u32[]{:S(2)}, u32[]{:S(2)}) collective-permute-start(f32[8,128]{1,0:T(8,128)} %get-tuple-element.26), channel_id=1, source_target_pairs={{0,16},{16,32},{32,48},{48,64},{64,80},{80,96},{96,112},{1,17},{17... | collective-permute-start | bytes 12296 | tf_op jit(solution)/shard_map/ppermute | solution.py:506
  86.2 3.6 %data_prepared.1.data = bf16[3,16,128,128]{3,2,1,0:T(8,128)(2,1)} custom-call(bf16[2048,128]{1,0:T(8,128)(2,1)} %bitcast.10, bf16[2,2048,128]{2,1,0:T(8,128)(2,1)} %bitcast.8, bf16[128,128]{1,0:T(8,128)(2,1)} %constant.42.clone.place), custom_call_target="tpu_custom_call" | custom-call | tf_op jit(solution)/shard_map/data_prepared/pallas_call | solution.py:569
  89.8 0.6 collective-permute-done.1.refs_7_
  90.4 0.0 collective-permute-done.refs_6_
  90.4 0.0 all-to-all-done
  90.4 9.8 %columns.1 = f32[16,264,128]{2,1,0:T(8,128)} custom-call(f32[16,2,128,128]{3,2,1,0:T(8,128)} %bitcast.6.cols, bf16[3,16,128,128]{3,2,1,0:T(8,128)(2,1)} %data_prepared.1.data, f32[2,16,128]{2,1,0:T(8,128)} %constant.43.clone.twiddle, bf16[768,256]{1,0:T(8,128)(2,1)} %constant.45.clone.forward, bf16[768,256]{1,0:T(8,128)(2,1)} %constant.46.clone.inverse), custom_call_target="tpu_custom_call" | custom-call | tf_op jit(solution)/shard_map/columns/pallas_call | solution.py:581
  100.3 0.0 copy-done.6
  100.3 0.0 copy-done.4
  100.3 0.0 collective-permute-done.5.refs_4_
  100.3 0.0 copy-start.3
  100.3 0.8 copy-done.3
  101.1 7.9 %all-to-all-start.1 = ((f32[16,264,128]{2,1,0:T(8,128)}), f32[16,264,128]{2,1,0:T(8,128)}, u32[]{:S(2)}, u32[]{:S(2)}) async-start(f32[16,264,128]{2,1,0:T(8,128)} %columns.1), calls=%async_computation.1 | async-start | bytes 4325376 | tf_op jit(solution)/shard_map/all_to_all | solution.py:606
  109.1 3.8 %tile_ready.1 = (f32[8,128,256]{2,1,0:T(8,128)}, f32[8,128,256]{2,1,0:T(8,128)}, f32[8,256]{1,0:T(8,128)}, f32[8,128]{1,0:T(8,128)}) custom-call(s32[2]{0:T(128)} %pad_add_fusion.where, f32[128,512]{1,0:T(8,128)} %get-tuple-element.29.refs_0_, f32[128,512]{1,0:T(8,128)} %copy-done, f32[128,512]{1,0:T(8,128)} %copy-done.1, f32[128,512]{1,0:T(8,128)} %copy-done.2, ...), custom_call_target="tpu_custom_call" | custom-call | tf_op jit(solution)/shard_map/tile_ready/pallas_call | solution.py:607
  112.9 4.6 %collective-permute-start.6 = (f32[8,256]{1,0:T(8,128)}, f32[8,256]{1,0:T(8,128)S(1)}, u32[]{:S(2)}, u32[]{:S(2)}) collective-permute-start(f32[8,256]{1,0:T(8,128)} %get-tuple-element.39), channel_id=1, source_target_pairs={{1,0},{2,1},{3,2},{4,3},{5,4},{6,5},{7,6},{8,7},{9,8},{10,9},{11,1... | collective-permute-start | bytes 24584 | tf_op jit(solution)/shard_map/ppermute | solution.py:506
  117.5 1.3 collective-permute-start.7
  118.8 7.9 %collective-permute-done.7.right = f32[8,128]{1,0:T(8,128)S(1)} collective-permute-done((f32[8,128]{1,0:T(8,128)}, f32[8,128]{1,0:T(8,128)S(1)}, u32[]{:S(2)}, u32[]{:S(2)}) %collective-permute-start.7) | collective-permute-done | bytes 4128 | tf_op jit(solution)/shard_map/ppermute | solution.py:506
  126.7 6.5 %collective-permute-done.6.below = f32[8,256]{1,0:T(8,128)S(1)} collective-permute-done((f32[8,256]{1,0:T(8,128)}, f32[8,256]{1,0:T(8,128)S(1)}, u32[]{:S(2)}, u32[]{:S(2)}) %collective-permute-start.6) | collective-permute-done | bytes 8224 | tf_op jit(solution)/shard_map/ppermute | solution.py:506
  133.2 4.3 %all-to-all-done.1.lines = f32[16,264,128]{2,1,0:T(8,128)} async-done(((f32[16,264,128]{2,1,0:T(8,128)}), f32[16,264,128]{2,1,0:T(8,128)}, u32[]{:S(2)}, u32[]{:S(2)}) %all-to-all-start.1) | async-done | bytes 2162720 | tf_op jit(solution)/shard_map/all_to_all | solution.py:606
  137.5 6.1 %rows_back.1 = f32[8,136,256]{2,1,0:T(8,128)} custom-call(f32[16,264,128]{2,1,0:T(8,128)} %all-to-all-done.1.lines, f32[2,16,128]{2,1,0:T(8,128)} %constant.43.clone.twiddle, bf16[768,256]{1,0:T(8,128)(2,1)} %constant.47.clone.table), custom_call_target="tpu_custom_call" | custom-call | tf_op jit(solution)/shard_map/rows_back/pallas_call | solution.py:624
  143.6 21.8 %all_to_all.15.gradient = f32[8,136,256]{2,1,0:T(8,128)} all-to-all(f32[8,136,256]{2,1,0:T(8,128)} %rows_back.1), channel_id=1, replica_groups=mesh['chan'=8,'facet'=16] {'chan'}, dimensions={0} | all-to-all | bytes 2228224 | tf_op jit(solution)/shard_map/all_to_all | solution.py:640
  165.3 0.0 copy-done.7
  165.3 0.0 copy-done.5
  165.3 5.6 %finish.1 = (f32[8,128,256]{2,1,0:T(8,128)}, bf16[8,2,128,256]{3,2,1,0:T(8,128)(2,1)}) custom-call(f32[8,136,256]{2,1,0:T(8,128)} %all_to_all.15.gradient, f32[8,128,256]{2,1,0:T(8,128)} %get-tuple-element.42.for_image, f32[8,128,256]{2,1,0:T(8,128)} %get-tuple-element.43.for_ahead, bf16[8,2,128,256]{3,2,1,0:T(8,128)(2,1)} %dual.3, f32[8,256]{1,0:T(8,128)} %copy-done.5, ...), custom_call_target="tpu_custom_call" | custom-call | tf_op jit(solution)/shard_map/finish/pallas_call | solution.py:641
  (4 shorter events, 0.0 us)
Async XLA Ops:
  35.1 8.4 %copy-start.10 = (f32[128,512]{1,0:T(8,128)S(1)}, f32[128,512]{1,0:T(8,128)}, u32[]{:S(2)}) copy-start(f32[128,512]{1,0:T(8,128)} %get-tuple-element.30) | copy-start | bytes 786436
  35.1 10.0 %copy-start.9 = (f32[128,512]{1,0:T(8,128)S(1)}, f32[128,512]{1,0:T(8,128)}, u32[]{:S(2)}) copy-start(f32[128,512]{1,0:T(8,128)} %get-tuple-element.31) | copy-start | bytes 786436
  35.1 12.7 %copy-start.8 = (f32[128,512]{1,0:T(8,128)S(1)}, f32[128,512]{1,0:T(8,128)}, u32[]{:S(2)}) copy-start(f32[128,512]{1,0:T(8,128)} %get-tuple-element.32) | copy-start | bytes 786436
  35.1 55.3 %all-to-all-start = ((f32[16,256,128]{2,1,0:T(8,128)}), f32[16,256,128]{2,1,0:T(8,128)}, u32[]{:S(2)}, u32[]{:S(2)}) async-start(f32[16,256,128]{2,1,0:T(8,128)} %bitcast.7), calls=%async_computation | async-start | bytes 4194304 | tf_op jit(solution)/shard_map/all_to_all | solution.py:566
  43.5 9.6 %collective-permute-start.2 = (f32[128,512]{1,0:T(8,128)S(1)}, f32[128,512]{1,0:T(8,128)S(1)}, u32[]{:S(2)}, u32[]{:S(2)}) collective-permute-start(f32[128,512]{1,0:T(8,128)S(1)} %copy-done.10), channel_id=1, source_target_pairs={{0,32},{16,48},{32,64},{48,80},{64,96},{80,112},{96,0},{112,16},{1... | collective-permute-start | bytes 786440 | tf_op jit(solution)/shard_map/ppermute | solution.py:565
  45.1 14.7 %collective-permute-start.3 = (f32[128,512]{1,0:T(8,128)S(1)}, f32[128,512]{1,0:T(8,128)S(1)}, u32[]{:S(2)}, u32[]{:S(2)}) collective-permute-start(f32[128,512]{1,0:T(8,128)S(1)} %copy-done.9), channel_id=1, source_target_pairs={{0,64},{16,80},{32,96},{48,112},{64,0},{80,16},{96,32},{112,48},{1... | collective-permute-start | bytes 786440 | tf_op jit(solution)/shard_map/ppermute | solution.py:565
  47.8 12.0 %collective-permute-start.4 = (f32[128,512]{1,0:T(8,128)S(1)}, f32[128,512]{1,0:T(8,128)S(1)}, u32[]{:S(2)}, u32[]{:S(2)}) collective-permute-start(f32[128,512]{1,0:T(8,128)S(1)} %copy-done.8), channel_id=1, source_target_pairs={{0,96},{16,112},{32,0},{48,16},{64,32},{80,48},{96,64},{112,80},{1... | collective-permute-start | bytes 786440 | tf_op jit(solution)/shard_map/ppermute | solution.py:565
  53.1 6.6 %copy-start = (f32[128,512]{1,0:T(8,128)}, f32[128,512]{1,0:T(8,128)S(1)}, u32[]{:S(2)}) copy-start(f32[128,512]{1,0:T(8,128)S(1)} %collective-permute-done.2.refs_1_) | copy-start | bytes 786436
  59.7 0.7 copy-start.1
  59.8 0.8 copy-start.2
  78.2 22.1 %collective-permute-start.5 = (f32[4,128,256]{2,1,0:T(8,128)}, f32[4,128,256]{2,1,0:T(8,128)S(1)}, u32[]{:S(2)}, u32[]{:S(2)}) collective-permute-start(f32[4,128,256]{2,1,0:T(8,128)} %swap_ready.1), channel_id=1, source_target_pairs={{0,16},{16,0},{32,48},{48,32},{64,80},{80,64},{96,112},{112,96},{1... | collective-permute-start | bytes 1572872 | tf_op jit(solution)/shard_map/ppermute | solution.py:580
  81.3 9.1 %collective-permute-start = (f32[8,256]{1,0:T(8,128)}, f32[8,256]{1,0:T(8,128)S(1)}, u32[]{:S(2)}, u32[]{:S(2)}) collective-permute-start(f32[8,256]{1,0:T(8,128)} %get-tuple-element.25), channel_id=1, source_target_pairs={{0,1},{1,2},{2,3},{3,4},{4,5},{5,6},{6,7},{7,8},{8,9},{9,10},{10,1... | collective-permute-start | bytes 24584 | tf_op jit(solution)/shard_map/ppermute | solution.py:506
  83.2 7.2 %collective-permute-start.1 = (f32[8,128]{1,0:T(8,128)}, f32[8,128]{1,0:T(8,128)S(1)}, u32[]{:S(2)}, u32[]{:S(2)}) collective-permute-start(f32[8,128]{1,0:T(8,128)} %get-tuple-element.26), channel_id=1, source_target_pairs={{0,16},{16,32},{32,48},{48,64},{64,80},{80,96},{96,112},{1,17},{17... | collective-permute-start | bytes 12296 | tf_op jit(solution)/shard_map/ppermute | solution.py:506
  90.4 9.9 %copy-start.6 = (f32[8,128]{1,0:T(8,128)}, f32[8,128]{1,0:T(8,128)S(1)}, u32[]{:S(2)}) copy-start(f32[8,128]{1,0:T(8,128)S(1)} %collective-permute-done.1.refs_7_) | copy-start | bytes 12292
  90.4 9.9 %copy-start.4 = (f32[8,256]{1,0:T(8,128)}, f32[8,256]{1,0:T(8,128)S(1)}, u32[]{:S(2)}) copy-start(f32[8,256]{1,0:T(8,128)S(1)} %collective-permute-done.refs_6_) | copy-start | bytes 24580
  100.3 0.8 copy-start.3
  101.1 36.4 %all-to-all-start.1 = ((f32[16,264,128]{2,1,0:T(8,128)}), f32[16,264,128]{2,1,0:T(8,128)}, u32[]{:S(2)}, u32[]{:S(2)}) async-start(f32[16,264,128]{2,1,0:T(8,128)} %columns.1), calls=%async_computation.1 | async-start | bytes 4325376 | tf_op jit(solution)/shard_map/all_to_all | solution.py:606
  112.9 20.3 %collective-permute-start.6 = (f32[8,256]{1,0:T(8,128)}, f32[8,256]{1,0:T(8,128)S(1)}, u32[]{:S(2)}, u32[]{:S(2)}) collective-permute-start(f32[8,256]{1,0:T(8,128)} %get-tuple-element.39), channel_id=1, source_target_pairs={{1,0},{2,1},{3,2},{4,3},{5,4},{6,5},{7,6},{8,7},{9,8},{10,9},{11,1... | collective-permute-start | bytes 24584 | tf_op jit(solution)/shard_map/ppermute | solution.py:506
  117.5 9.2 %collective-permute-start.7 = (f32[8,128]{1,0:T(8,128)}, f32[8,128]{1,0:T(8,128)S(1)}, u32[]{:S(2)}, u32[]{:S(2)}) collective-permute-start(f32[8,128]{1,0:T(8,128)} %get-tuple-element.40), channel_id=1, source_target_pairs={{16,0},{32,16},{48,32},{64,48},{80,64},{96,80},{112,96},{17,1},{33... | collective-permute-start | bytes 12296 | tf_op jit(solution)/shard_map/ppermute | solution.py:506
  126.7 38.6 %copy-start.7 = (f32[8,128]{1,0:T(8,128)}, f32[8,128]{1,0:T(8,128)S(1)}, u32[]{:S(2)}) copy-start(f32[8,128]{1,0:T(8,128)S(1)} %collective-permute-done.7.right) | copy-start | bytes 12292
  133.2 32.2 %copy-start.5 = (f32[8,256]{1,0:T(8,128)}, f32[8,256]{1,0:T(8,128)S(1)}, u32[]{:S(2)}) copy-start(f32[8,256]{1,0:T(8,128)S(1)} %collective-permute-done.6.below) | copy-start | bytes 24580

commit v3 on v1

--- a/solution.py
+++ b/solution.py
@@ -19,7 +19,7 @@
 step_dual = 0.5
 clip_radius = 4.0
 
-PARAMS = pltpu.CompilerParams(vmem_limit_bytes=48 * 1024 * 1024)
+MIB = 1024 * 1024
 
 
 def host_tables():
@@ -154,9 +154,6 @@
     get_twiddle = fetched(twiddle, twiddle_v, in_sems.at[steps])
     get_table = fetched(table, table_v, in_sems.at[steps + 1])
     sent = []
-    for k in range(4):
-        lanes = pl.ds(pl.multiple_of((where[0] + k) % 4 * 512, 512), 512)
-        sent.append(fetched(image.at[:, lanes], pieces[k], out_sems.at[8 + k]))
     get_twiddle.wait()
 
     def body(step, carry):
@@ -180,6 +177,9 @@
         return carry
 
     lax.fori_loop(0, steps, body, 0)
+    for k in range(4):
+        lanes = pl.ds(pl.multiple_of((where[0] // 2 + k) % 4 * 512, 512), 512)
+        sent.append(fetched(image_v.at[:, lanes], pieces[k], out_sems.at[8 + k]))
     get_table.wait()
     dims = ((1,), (1,))
     for g in range(RADIX // 2):
@@ -195,74 +195,46 @@
         copy.wait()
 
 
-def data_prepared(weights, measured, place, out, held, out_v, sems):
-    copies = []
+def data_prepared(
+    weights, measured, place, forward, inverse, twiddle,
+    out, forward_kept, inverse_kept, twiddle_kept, held,
+):
+    forward_kept[...] = forward[...]
+    inverse_kept[...] = inverse[...]
+    twiddle_kept[...] = twiddle[...]
     for n in range(3):
         source = weights[...] if n == 0 else measured[n - 1]
         held[...] = source.astype(jnp.float32)
         for f in range(RADIX):
             rows = held[pl.ds(f, LANES, stride=RADIX), :].astype(jnp.bfloat16)
-            out_v[n, f] = dot(place[...], rows, ((1,), (1,))).astype(jnp.bfloat16)
-        copies.append(fetched(out_v.at[n], out.at[n], sems.at[n]))
-    for copy in copies:
-        copy.wait()
-
-
-def columns(
-    cols, data, twiddle, forward, inverse, out,
-    cols_v, data_v, forward_v, inverse_v, out_v, edge_v, held, in_sems, data_sems, out_sems,
-):
+            out[n, f] = dot(place[...], rows, ((1,), (1,))).astype(jnp.bfloat16)
+
+
+def columns(cols, data, twiddle, forward, inverse, out, held):
     chunk = 32
     steps = LANES // chunk
     dims = ((1,), (0,))
-
-    def incoming(step):
-        rows = pl.ds(pl.multiple_of(step * chunk, chunk), chunk)
-        return pltpu.make_async_copy(
-            cols.at[:, :, rows, :], cols_v.at[:, :, rows, :], in_sems.at[step]
-        )
-
-    def incoming_data(step):
-        rows = pl.ds(pl.multiple_of(step * chunk, chunk), chunk)
-        return pltpu.make_async_copy(
-            data.at[:, :, rows, :], data_v.at[:, :, rows, :], data_sems.at[step]
-        )
-
-    def outgoing(step, c):
-        rows = pl.ds(pl.multiple_of(step * chunk, chunk), chunk)
-        to_rows = pl.ds(pl.multiple_of(c * LANES + step * chunk, chunk), chunk)
-        return pltpu.make_async_copy(
-            out_v.at[:, c, rows, :], out.at[:, to_rows, :], out_sems.at[step, c]
-        )
-
-    for step in range(steps):
-        incoming(step).start()
-        incoming_data(step).start()
-    get_forward = fetched(forward, forward_v, in_sems.at[steps])
-    get_inverse = fetched(inverse, inverse_v, in_sems.at[steps + 1])
-    edge_v[...] = jnp.zeros_like(edge_v)
-    get_forward.wait()
-    get_inverse.wait()
+    out[:, 2 * LANES :, :] = jnp.zeros((RADIX, 8, LANES), jnp.float32)
     lane_at = lax.broadcasted_iota(jnp.int32, (8, LANES), 1)
 
     def body(step, carry):
-        incoming(step).wait()
-        here = pl.ds(pl.multiple_of(step * chunk, chunk), chunk)
-        mixed = sixteen([(cols_v[b, 0, here, :], cols_v[b, 1, here, :]) for b in range(RADIX)], -1)
+        at = pl.multiple_of(step * chunk, chunk)
+        here = pl.ds(at, chunk)
+        imag_here = pl.ds(pl.multiple_of(LANES + at, chunk), chunk)
+        mixed = sixteen([(cols[b, here, :], cols[b, imag_here, :]) for b in range(RADIX)], -1)
         for f in range(RADIX):
             real, imag = mixed[f]
             cos, sin = twiddle[0, f : f + 1, :], twiddle[1, f : f + 1, :]
             rows = slice(f * chunk, (f + 1) * chunk)
             store_pair(held, rows, real * cos + imag * sin, imag * cos - real * sin)
-        incoming_data(step).wait()
-        spectrum = three_pass(held[...], forward_v, dims)
+        spectrum = three_pass(held[...], forward, dims)
         for f in range(RADIX):
             rows = slice(f * chunk, (f + 1) * chunk)
-            weight = data_v[0, f, here, :].astype(jnp.float32)
-            real = weight * spectrum[rows, :LANES] - data_v[1, f, here, :].astype(jnp.float32)
-            imag = weight * spectrum[rows, LANES:] - data_v[2, f, here, :].astype(jnp.float32)
+            weight = data[0, f, here, :].astype(jnp.float32)
+            real = weight * spectrum[rows, :LANES] - data[1, f, here, :].astype(jnp.float32)
+            imag = weight * spectrum[rows, LANES:] - data[2, f, here, :].astype(jnp.float32)
             store_pair(held, rows, real, imag)
-        back = three_pass(held[...], inverse_v, dims)
+        back = three_pass(held[...], inverse, dims)
         values = []
         for f in range(RADIX):
             rows = slice(f * chunk, (f + 1) * chunk)
@@ -272,76 +244,47 @@
         mixed = sixteen(values, 1)
         for b in range(RADIX):
             for c in range(2):
-                out_v[b, c, here, :] = mixed[b][c]
+                out[b, (here, imag_here)[c], :] = mixed[b][c]
                 if b > 0:
-                    edge = edge_v[b - 1]
+                    edge = out[b - 1, 2 * LANES :, :]
                     for i in range(chunk // 8):
                         first = mixed[b][c][8 * i : 8 * i + 8, 0:1]
                         at_lane = lane_at == c * RADIX + step * (chunk // 8) + i
                         edge = jnp.where(at_lane, first, edge)
-                    edge_v[b - 1] = edge
-        outgoing(step, 0).start()
-        outgoing(step, 1).start()
+                    out[b - 1, 2 * LANES :, :] = edge
         return carry
 
     lax.fori_loop(0, steps, body, 0)
-    send_edge = fetched(edge_v, out.at[:, 2 * LANES :, :], in_sems.at[0])
-    for step in range(steps):
-        outgoing(step, 0).wait()
-        outgoing(step, 1).wait()
-    send_edge.wait()
-
-
-def rows_back(
-    lines, twiddle, table, out, lines_v, edge_v, table_v, held, out_v, side_v, in_sems, out_sems
-):
+
+
+def rows_back(lines, twiddle, table, out, held, side_v):
     dims = ((0,), (0,))
-    get_table = fetched(table, table_v, in_sems.at[5])
-    arriving = []
-    for g in range(4):
-        for c in range(2):
-            rows = pl.ds(c * LANES + 32 * g, 32)
-            arriving.append(
-                fetched(
-                    lines.at[:, rows, :], lines_v.at[:, pl.ds(c * LANES + 32 * g, 32), :],
-                    out_sems.at[2 * g + c],
-                )
-            )
-    get_edge = fetched(lines.at[:, 2 * LANES :, :], edge_v, in_sems.at[4])
-    get_table.wait()
     for f in range(RADIX):
-        if f % 4 == 0:
-            arriving[f // 2].wait()
-            arriving[f // 2 + 1].wait()
-        real = lines_v[:, 8 * f : 8 * f + 8, :].reshape(LANES, LANES)
-        imag = lines_v[:, LANES + 8 * f : LANES + 8 * f + 8, :].reshape(LANES, LANES)
+        real = lines[:, 8 * f : 8 * f + 8, :].reshape(LANES, LANES)
+        imag = lines[:, LANES + 8 * f : LANES + 8 * f + 8, :].reshape(LANES, LANES)
         high_r, low_r = split(real)
         high_i, low_i = split(imag)
         pair = jnp.concatenate([high_r, high_i, low_r, low_i], axis=0)
-        held[f] = three_pass(pair, table_v, dims)
-    get_edge.wait()
-    high, low = split(edge_v[...].reshape(LANES, LANES))
+        held[f] = three_pass(pair, table, dims)
+    high, low = split(lines[:, 2 * LANES :, :].reshape(LANES, LANES))
     edge = (
-        dot(high, table_v[0:LANES, :], dims)
-        + dot(low, table_v[0:LANES, :], dims)
-        + dot(high, table_v[512 : 512 + LANES, :], dims)
+        dot(high, table[0:LANES, :], dims)
+        + dot(low, table[0:LANES, :], dims)
+        + dot(high, table[512 : 512 + LANES, :], dims)
     )
     edge_r = edge[:RADIX, :LANES] - edge[RADIX : 2 * RADIX, LANES:]
     edge_i = edge[:RADIX, LANES:] + edge[RADIX : 2 * RADIX, :LANES]
-    cos, sin = twiddle[0], twiddle[1]
+    scale = 1.0 / GRID
+    cos, sin = twiddle[0] * scale, twiddle[1] * scale
     edge_r, edge_i = edge_r * cos - edge_i * sin, edge_i * cos + edge_r * sin
     mixed = sixteen([(edge_r[f : f + 1], edge_i[f : f + 1]) for f in range(RADIX)], 1)
     for d in range(CHANNELS):
-        out_v[d, LANES : LANES + 1, :] = jnp.concatenate(
+        out[d, LANES : LANES + 1, :] = jnp.concatenate(
             [mixed[2 * d][0], mixed[2 * d + 1][0]], axis=1
         )
     chunk = 16
     steps = LANES // chunk
     lane_at = lax.broadcasted_iota(jnp.int32, (chunk, LANES), 1)
-
-    def outgoing(step):
-        rows = pl.ds(pl.multiple_of(step * chunk, chunk), chunk)
-        return pltpu.make_async_copy(out_v.at[:, rows, :], out.at[:, rows, :], out_sems.at[step])
 
     def body(step, carry):
         at = pl.multiple_of(step * chunk, chunk)
@@ -349,29 +292,22 @@
         values = []
         for f in range(RADIX):
             real, imag = held[f, here, :LANES], held[f, here, LANES:]
-            cos, sin = twiddle[0, f : f + 1, :], twiddle[1, f : f + 1, :]
+            cos, sin = twiddle[0, f : f + 1, :] * scale, twiddle[1, f : f + 1, :] * scale
             values.append((real * cos - imag * sin, imag * cos + real * sin))
         mixed = sixteen(values, 1)
         side = jnp.zeros((chunk, LANES), jnp.float32)
         for b in range(RADIX):
             low_lane = (b % 2) * LANES
-            out_v[b // 2, here, low_lane : low_lane + LANES] = mixed[b][0]
+            out[b // 2, here, low_lane : low_lane + LANES] = mixed[b][0]
             if b > 0 and b % 2 == 0:
                 side = jnp.where(lane_at == b // 2 - 1, mixed[b][0][:, 0:1], side)
         side_v[here, :] = side
-        outgoing(step).start()
         return carry
 
     lax.fori_loop(0, steps, body, 0)
     beside = side_v[...].T
     for d in range(CHANNELS):
-        out_v[d, LANES + 1 : LANES + 2, :LANES] = beside[d : d + 1, :]
-    last = fetched(
-        out_v.at[:, pl.ds(LANES, 8), :], out.at[:, pl.ds(LANES, 8), :], in_sems.at[4]
-    )
-    for step in range(steps):
-        outgoing(step).wait()
-    last.wait()
+        out[d, LANES + 1 : LANES + 2, :LANES] = beside[d : d + 1, :]
 
 
 def dual_edges(dual, last_row, last_column):
@@ -384,11 +320,10 @@
 
 
 def swap_ready(where, *refs):
-    pieces, out, sems = refs[:4], refs[4], refs[5]
-    lanes = pl.ds(pl.multiple_of((1 - where[1]) * 256, 256), 256)
-    copies = [fetched(pieces[k].at[:, lanes], out.at[k], sems.at[k]) for k in range(4)]
-    for copy in copies:
-        copy.wait()
+    pieces, out = refs[:4], refs[4]
+    lanes = pl.ds(pl.multiple_of((1 - where[0] % 2) * 256, 256), 256)
+    for k in range(4):
+        out[k] = pieces[k][:, lanes]
 
 
 def tile_ready(where, *refs):
@@ -398,8 +333,8 @@
     lane_at = lax.broadcasted_iota(jnp.int32, (LANES, 2 * LANES), 1)
     for k in range(4):
         for other in range(2):
-            lanes = where[1] * (1 - other) + (1 - where[1]) * other
-            c = (where[0] + 4 - k) % 4 * 2 + lanes
+            half = where[0] % 2
+            c = (where[0] // 2 + 4 - k) % 4 * 2 + (1 - half if other else half)
             p = dual[c, 0].astype(jnp.float32)
             q = dual[c, 1].astype(jnp.float32)
             beside = jnp.broadcast_to(left[pl.ds(c, 1), :], (LANES, LANES)).T[:, 0:1]
@@ -409,7 +344,7 @@
             if other:
                 image = swapped[k]
             else:
-                own = pl.ds(pl.multiple_of(where[1] * 256, 256), 256)
+                own = pl.ds(pl.multiple_of(half * 256, 256), 256)
                 image = pieces[k][:, own]
             ahead = image - adjoint
             for_image[c] = image - step_primal * adjoint
@@ -423,17 +358,17 @@
     ahead_v, side_v, image_v, dual_v, image_sems, dual_sems,
 ):
     sides = []
-    for c in range(CHANNELS):
-        sides.append(gradient[c, LANES + 1 : LANES + 2, :LANES])
-    side_v[:, :CHANNELS] = (right[...] - jnp.concatenate(sides, axis=0)).T
+    leaving = []
     for c in range(CHANNELS):
         slope = gradient[c, :LANES, :]
         image_v[c] = for_image[c] - step_primal * slope
+        leaving.append(fetched(image_v.at[c], image_next.at[c], image_sems.at[c]))
         ahead_v[c, :LANES, :] = for_ahead[c] - slope
         ahead_v[c, LANES : LANES + 1, :] = (
             below[c : c + 1, :] - gradient[c, LANES : LANES + 1, :]
         )
-        pltpu.make_async_copy(image_v.at[c], image_next.at[c], image_sems.at[c]).start()
+        sides.append(gradient[c, LANES + 1 : LANES + 2, :LANES])
+    side_v[:, :CHANNELS] = (right[...] - jnp.concatenate(sides, axis=0)).T
     chunk = 16
     steps = LANES // chunk
     row_at = lax.broadcasted_iota(jnp.int32, (chunk, 2 * LANES), 0)
@@ -473,8 +408,8 @@
         return carry
 
     lax.fori_loop(0, steps, body, 0)
-    for c in range(CHANNELS):
-        pltpu.make_async_copy(image_v.at[c], image_next.at[c], image_sems.at[c]).wait()
+    for copy in leaving:
+        copy.wait()
     for step in range(steps):
         outgoing(step).wait()
 
@@ -496,7 +431,7 @@
 DMA = pltpu.SemaphoreType.DMA
 
 
-def call(kernel, out_shape, in_specs, out_specs, scratch):
+def call(kernel, out_shape, in_specs, out_specs, scratch, limit=16):
     return pl.pallas_call(
         kernel,
         out_shape=out_shape,
@@ -504,7 +439,7 @@
         out_specs=out_specs,
         scratch_shapes=scratch,
         name=kernel.__name__,
-        compiler_params=PARAMS,
+        compiler_params=pltpu.CompilerParams(vmem_limit_bytes=limit * MIB),
     )
 
 
@@ -516,7 +451,7 @@
     image = image_field[0]
     f32, bf16 = jnp.float32, jnp.bfloat16
     chan = lax.axis_index("chan")
-    where = jnp.stack([chan // 2, chan % 2]).astype(jnp.int32)
+    where = chan.astype(jnp.int32).reshape(1)
 
     last_row, last_column = call(
         dual_edges,
@@ -542,6 +477,7 @@
             DMA((10,)),
             DMA((12,)),
         ],
+        63,
     )(where, image, twiddle, jnp.asarray(halves(forward * scale).T))
     for k in range(1, 4):
         pairs = [(2 * x + z, (x + k) % 4 * 2 + z) for x in range(4) for z in range(2)]
@@ -549,44 +485,44 @@
     cols = lax.all_to_all(
         spread.reshape(RADIX, 2 * LANES, LANES), "facet", split_axis=0, concat_axis=0, tiled=True
     )
-    data = call(
+    data, forward_kept, inverse_kept, twiddle_kept = call(
         data_prepared,
-        shape((3, RADIX, LANES, LANES), bf16),
-        [VM] * 3,
-        HBM,
-        [pltpu.VMEM((GRID, LANES), f32), pltpu.VMEM((3, RADIX, LANES, LANES), bf16), DMA((3,))],
-    )(weights[0], measured[0], place)
+        (
+            shape((3, RADIX, LANES, LANES), bf16),
+            shape((768, 256), bf16),
+            shape((768, 256), bf16),
+            shape((2, RADIX, LANES)),
+        ),
+        [VM] * 6,
+        (VM,) * 4,
+        [pltpu.VMEM((GRID, LANES), f32)],
+    )(
+        weights[0],
+        measured[0],
+        place,
+        jnp.asarray(halves(forward)),
+        jnp.asarray(halves(inverse)),
+        twiddle,
+    )
     to_swap = call(
-        swap_ready, shape((4, LANES, 256)), [SM] + [HBM] * 4, HBM, [DMA((4,))]
+        swap_ready, shape((4, LANES, 256)), [SM] + [VM] * 4, VM, []
     )(where, *pieces)
-    cols, to_swap, above, left, data = lax.optimization_barrier(
-        (cols, to_swap, above, left, data)
-    )
+    cols, above, left = lax.optimization_barrier((cols, above, left))
     swapped = lax.ppermute(to_swap, "chan", [(i, i ^ 1) for i in range(8)])
     back = call(
         columns,
         shape((RADIX, 2 * LANES + 8, LANES)),
-        [HBM, HBM, VM, HBM, HBM],
-        HBM,
-        [
-            pltpu.VMEM((RADIX, 2, LANES, LANES), f32),
-            pltpu.VMEM((3, RADIX, LANES, LANES), bf16),
-            pltpu.VMEM((768, 256), bf16),
-            pltpu.VMEM((768, 256), bf16),
-            pltpu.VMEM((RADIX, 2, LANES, LANES), f32),
-            pltpu.VMEM((RADIX, 8, LANES), f32),
-            pltpu.VMEM((RADIX * 32, 512), bf16),
-            DMA((6,)),
-            DMA((4,)),
-            DMA((4, 2)),
-        ],
+        [VM] * 5,
+        VM,
+        [pltpu.VMEM((RADIX * 32, 512), bf16)],
     )(
-        cols.reshape(RADIX, 2, LANES, LANES),
+        cols,
         data,
-        twiddle,
-        jnp.asarray(halves(forward)),
-        jnp.asarray(halves(inverse)),
-    )
+        twiddle_kept,
+        forward_kept,
+        inverse_kept,
+    )
+    back, swapped = lax.optimization_barrier((back, swapped))
     lines = lax.all_to_all(back, "facet", split_axis=0, concat_axis=0, tiled=True)
     for_image, for_ahead, first_row, first_column = call(
         tile_ready,
@@ -602,31 +538,20 @@
     )(where, *pieces, swapped, dual_field, above, left)
     below = passed_along(first_row, "facet", -1)
     right = passed_along(first_column, "chan", -1)
-    lines, for_image, for_ahead, below, right = lax.optimization_barrier(
-        (lines, for_image, for_ahead, below, right)
-    )
+    lines, below, right = lax.optimization_barrier((lines, below, right))
     slopes = call(
         rows_back,
         shape((CHANNELS, LANES + 8, 2 * LANES)),
-        [ANY, VM, HBM],
-        ANY,
-        [
-            pltpu.VMEM((RADIX, 2 * LANES, LANES), f32),
-            pltpu.VMEM((RADIX, 8, LANES), f32),
-            pltpu.VMEM((768, 256), bf16),
-            pltpu.VMEM((RADIX, LANES, 256), f32),
-            pltpu.VMEM((CHANNELS, LANES + 8, 2 * LANES), f32),
-            pltpu.VMEM((LANES, LANES), f32),
-            DMA((6,)),
-            DMA((8,)),
-        ],
-    )(lines, twiddle, jnp.asarray(halves(inverse * scale)))
+        [VM] * 3,
+        VM,
+        [pltpu.VMEM((RADIX, LANES, 256), f32), pltpu.VMEM((LANES, LANES), f32)],
+    )(lines, twiddle_kept, inverse_kept)
     gradient = lax.all_to_all(slopes, "chan", split_axis=0, concat_axis=0, tiled=True)
     return call(
         finish,
         (shape((CHANNELS, LANES, 2 * LANES)), shape((CHANNELS, 2, LANES, 2 * LANES), bf16)),
         [VM] * 6,
-        (ANY, ANY),
+        (HBM, HBM),
         [
             pltpu.VMEM((CHANNELS, LANES + 8, 2 * LANES), f32),
             pltpu.VMEM((LANES, LANES), f32),

time: 146 us -> 124 us (0.85)
  waiting for transfers between devices: 49.1 us -> 34.4 us
  local copies, waits for them, and re-layouts: 20.2 us -> 11.4 us
  Pallas kernels: 24.2 us -> 20.3 us
  blocking collectives: 18.6 us -> 21.4 us
    ppermute x1, waiting for transfers between devices: 35.6 us -> 0.01 us  [shards(): swapped = lax.ppermute(to_swap, 'chan', [(i, i ^ 1) for i in range(8)])]
    ppermute x3, waiting for transfers between devices: 1.56 us -> 10.7 us  [shards(): pieces[k] = lax.ppermute(pieces[k], 'chan', pairs)]
    unnamed x56 -> x58, local copies, waits for them, and re-layouts: 20.2 us -> 11.4 us
    ppermute x4, waiting for transfers between devices: 11.6 us -> 19.4 us  [passed_along(): return lax.ppermute(x, axis, pairs)]
    all_to_all x1, waiting for transfers between devices: 0.01 us -> 4.22 us  [shards(): lax.all_to_all(back, 'facet', split_axis=0, concat_axis=0, tiled=True)]
    all_to_all x1, blocking collectives: 18.6 us -> 21.4 us  [shards(): lax.all_to_all(slopes, 'chan', split_axis=0, concat_axis=0, tiled=True)]
    pallas_call x1, Pallas kernels: 6.49 us -> 4.11 us  [shards(): call(rows_forward, (shape((RADIX, 2, RADIX, 8, LANES)),) + (shape((LANES,...]
    pallas_call x4, Pallas kernels: 13.8 us -> 11.8 us  [the longest x1 7.08 us: shards(): call(columns, shape((RADIX, 2 * LANES + 8, LANES)), [VM] * 5, VM, [pltpu....]
  transfers between devices with their start and end apart: 10 -> 10, of which waited for: 5 -> 6; matrix products, arithmetic and copies ran while one was open for 0% -> 0% of each run, Pallas kernels for 3% -> 9%
where the time goes in v3:
time: 124 us; the launch traced here: 122 us
  waiting for transfers between devices  34.4 us (28%)
  starting transfers between devices  33.6 us (27%)
  blocking collectives  21.4 us (17%)
  Pallas kernels  20.3 us (16%)
  local copies, waits for them, and re-layouts  11.4 us (9%)
    all_to_all x1, blocking collectives, shards(): lax.all_to_all(slopes, 'chan', split_axis=0, concat_axis=0, tiled=True)  21.4 us
    ppermute x4, waiting for transfers between devices, passed_along(): return lax.ppermute(x, axis, pairs)  19.4 us
    unnamed x58, local copies, waits for them, and re-layouts  11.4 us
    ppermute x4, starting transfers between devices, passed_along(): return lax.ppermute(x, axis, pairs)  10.7 us
    ppermute x3, waiting for transfers between devices, shards(): pieces[k] = lax.ppermute(pieces[k], 'chan', pairs)  10.7 us
    all_to_all x1, starting transfers between devices, shards(): lax.all_to_all(spread.reshape(RADIX, 2 * LANES, LANES), 'facet', split_ax...  8.39 us
    all_to_all x1, starting transfers between devices, shards(): lax.all_to_all(back, 'facet', split_axis=0, concat_axis=0, tiled=True)  7.75 us
    pallas_call x1, Pallas kernels, shards(): call(columns, shape((RADIX, 2 * LANES + 8, LANES)), [VM] * 5, VM, [pltpu....  7.08 us
  transfers between devices with their start and end apart: 10, of which 6 were waited for; matrix products, arithmetic and copies ran while one was open for 0% of the time, Pallas kernels for 9%

profile of v3, /device:TPU:8, one launch (start us, length us, event | category | flops | bytes accessed | tf_op | source)
XLA Modules:
  0.0 122.0 jit_solution(10034242813916592141)
XLA Ops:
  0.6 4.1 %rows_forward.1 = (f32[16,2,16,8,128]{4,3,2,1,0:T(8,128)}, f32[128,512]{1,0:T(8,128)}, f32[128,512]{1,0:T(8,128)}, f32[128,512]{1,0:T(8,128)}, f32[128,512]{1,0:T(8,128)}) custom-call(s32[1]{0:T(128)} %bitcast.where, f32[128,2048]{1,0:T(8,128)} %bitcast.8, f32[2,16,128]{2,1,0:T(8,128)} %constant.17.clone.twiddle, bf16[256,768]{1,0:T(8,128)(2,1)} %constant.18.clone.table), custom_call_target="tpu_custom_call" | custom-call | tf_op jit(solution)/shard_map/rows_forward/pallas_call | solution.py:466
  4.8 0.0 copy-start
  4.8 8.4 %all-to-all-start = ((f32[16,256,128]{2,1,0:T(8,128)}), f32[16,256,128]{2,1,0:T(8,128)S(1)}, u32[]{:S(2)}, u32[]{:S(2)}) async-start(f32[16,256,128]{2,1,0:T(8,128)} %bitcast.7), calls=%async_computation | async-start | bytes 4194304 | tf_op jit(solution)/shard_map/all_to_all | solution.py:485
  13.2 0.0 copy-start.18
  13.2 0.0 copy-start.19
  13.2 0.0 copy-start.20
  13.2 0.0 copy-start.23
  13.2 0.0 copy-start.24
  13.2 1.6 %collective-permute-start.2 = (f32[128,512]{1,0:T(8,128)}, f32[128,512]{1,0:T(8,128)S(1)}, u32[]{:S(2)}, u32[]{:S(2)}) collective-permute-start(f32[128,512]{1,0:T(8,128)} %get-tuple-element.34), channel_id=1, source_target_pairs={{0,32},{16,48},{32,64},{48,80},{64,96},{80,112},{96,0},{112,16},{1... | collective-permute-start | bytes 786440 | tf_op jit(solution)/shard_map/ppermute | solution.py:484
  14.8 2.7 %collective-permute-start.3 = (f32[128,512]{1,0:T(8,128)}, f32[128,512]{1,0:T(8,128)S(1)}, u32[]{:S(2)}, u32[]{:S(2)}) collective-permute-start(f32[128,512]{1,0:T(8,128)} %get-tuple-element.35), channel_id=1, source_target_pairs={{0,64},{16,80},{32,96},{48,112},{64,0},{80,16},{96,32},{112,48},{1... | collective-permute-start | bytes 786440 | tf_op jit(solution)/shard_map/ppermute | solution.py:484
  17.5 1.4 %collective-permute-start.4 = (f32[128,512]{1,0:T(8,128)}, f32[128,512]{1,0:T(8,128)S(1)}, u32[]{:S(2)}, u32[]{:S(2)}) collective-permute-start(f32[128,512]{1,0:T(8,128)} %get-tuple-element.36), channel_id=1, source_target_pairs={{0,96},{16,112},{32,0},{48,16},{64,32},{80,48},{96,64},{112,80},{1... | collective-permute-start | bytes 786440 | tf_op jit(solution)/shard_map/ppermute | solution.py:484
  19.0 4.1 %collective-permute-done.2.refs_1_ = f32[128,512]{1,0:T(8,128)S(1)} collective-permute-done((f32[128,512]{1,0:T(8,128)}, f32[128,512]{1,0:T(8,128)S(1)}, u32[]{:S(2)}, u32[]{:S(2)}) %collective-permute-start.2) | collective-permute-done | bytes 262176 | tf_op jit(solution)/shard_map/ppermute | solution.py:484
  23.1 6.6 %collective-permute-done.3.refs_2_ = f32[128,512]{1,0:T(8,128)S(1)} collective-permute-done((f32[128,512]{1,0:T(8,128)}, f32[128,512]{1,0:T(8,128)S(1)}, u32[]{:S(2)}, u32[]{:S(2)}) %collective-permute-start.3) | collective-permute-done | bytes 262176 | tf_op jit(solution)/shard_map/ppermute | solution.py:484
  29.7 0.0 collective-permute-done.4.refs_3_
  29.7 0.9 swap_ready.1
  30.6 1.0 collective-permute-start.5
  31.6 0.2 dual_edges.1
  31.8 1.9 %collective-permute-start = (f32[8,256]{1,0:T(8,128)S(1)}, f32[8,256]{1,0:T(8,128)S(1)}, u32[]{:S(2)}, u32[]{:S(2)}) collective-permute-start(f32[8,256]{1,0:T(8,128)S(1)} %get-tuple-element.26), channel_id=1, source_target_pairs={{0,1},{1,2},{2,3},{3,4},{4,5},{5,6},{6,7},{7,8},{8,9},{9,10},{10,1... | collective-permute-start | bytes 24584 | tf_op jit(solution)/shard_map/ppermute | solution.py:424
  33.7 2.9 %collective-permute-start.1 = (f32[8,128]{1,0:T(8,128)S(1)}, f32[8,128]{1,0:T(8,128)S(1)}, u32[]{:S(2)}, u32[]{:S(2)}) collective-permute-start(f32[8,128]{1,0:T(8,128)S(1)} %get-tuple-element.27), channel_id=1, source_target_pairs={{0,16},{16,32},{32,48},{48,64},{64,80},{80,96},{96,112},{1,17},{17... | collective-permute-start | bytes 12296 | tf_op jit(solution)/shard_map/ppermute | solution.py:424
  36.7 1.6 %data_prepared.1 = (bf16[3,16,128,128]{3,2,1,0:T(8,128)(2,1)S(1)}, bf16[768,256]{1,0:T(8,128)(2,1)S(1)}, bf16[768,256]{1,0:T(8,128)(2,1)S(1)}, f32[2,16,128]{2,1,0:T(8,128)S(1)}) custom-call(bf16[2048,128]{1,0:T(8,128)(2,1)S(1)} %bitcast.6, bf16[2,2048,128]{2,1,0:T(8,128)(2,1)S(1)} %bitcast.5, bf16[128,128]{1,0:T(8,128)(2,1)S(1)} %copy-done.24, ...), custom_call_target="tpu_custom_call" | custom-call | tf_op jit(solution)/shard_map/data_prepared/pallas_call | solution.py:488
  38.3 1.2 copy-done.3
  39.5 0.7 copy-done.21
  40.2 7.9 %collective-permute-done.1.refs_7_ = f32[8,128]{1,0:T(8,128)S(1)} collective-permute-done((f32[8,128]{1,0:T(8,128)S(1)}, f32[8,128]{1,0:T(8,128)S(1)}, u32[]{:S(2)}, u32[]{:S(2)}) %collective-permute-start.1) | collective-permute-done | bytes 4128 | tf_op jit(solution)/shard_map/ppermute | solution.py:424
  48.1 0.6 copy-done.27
  48.7 0.0 collective-permute-done.refs_6_
  48.7 0.6 copy-done.25
  49.3 0.0 all-to-all-done.cols
  49.3 1.4 %copy-done.4 = bf16[3,16,128,128]{3,2,1,0:T(8,128)(2,1)S(1)} copy-done((bf16[3,16,128,128]{3,2,1,0:T(8,128)(2,1)S(1)}, bf16[3,16,128,128]{3,2,1,0:T(8,128)(2,1)}, u32[]{:S(2)}) %copy-start.4) | copy-done | bytes 1572888
  50.7 1.0 copy-done.22
  51.7 7.1 %columns.1 = f32[16,264,128]{2,1,0:T(8,128)} custom-call(f32[16,256,128]{2,1,0:T(8,128)S(1)} %all-to-all-done.cols, bf16[3,16,128,128]{3,2,1,0:T(8,128)(2,1)S(1)} %copy-done.4, f32[2,16,128]{2,1,0:T(8,128)S(1)} %get-tuple-element.30.twiddle, bf16[768,256]{1,0:T(8,128)(2,1)S(1)} %copy-done.22, bf16[768,256]{1,0:T(8,128)(2,1)S(1)} %get-tuple-element.32.inverse.table), custom_call_target="tpu_custom_call" | custom-call | tf_op jit(solution)/shard_map/columns/pallas_call | solution.py:512
  58.8 0.0 copy-done.1
  58.8 0.0 collective-permute-done.5.refs_4_
  58.8 7.7 %all-to-all-start.1 = ((f32[16,264,128]{2,1,0:T(8,128)}), f32[16,264,128]{2,1,0:T(8,128)S(1)}, u32[]{:S(2)}, u32[]{:S(2)}) async-start(f32[16,264,128]{2,1,0:T(8,128)} %columns.1), calls=%async_computation.1 | async-start | bytes 4325376 | tf_op jit(solution)/shard_map/all_to_all | solution.py:526
  66.6 0.9 copy-done.13
  67.5 0.9 copy-done.15
  68.5 0.9 copy-done.17
  69.4 1.8 %tile_ready.1 = (f32[8,128,256]{2,1,0:T(8,128)S(1)}, f32[8,128,256]{2,1,0:T(8,128)S(1)}, f32[8,256]{1,0:T(8,128)S(1)}, f32[8,128]{1,0:T(8,128)S(1)}) custom-call(s32[1]{0:T(128)} %bitcast.where, f32[128,512]{1,0:T(8,128)S(1)} %copy-done.11, f32[128,512]{1,0:T(8,128)S(1)} %copy-done.13, f32[128,512]{1,0:T(8,128)S(1)} %copy-done.15, ...), custom_call_target="tpu_custom_call" | custom-call | tf_op jit(solution)/shard_map/tile_ready/pallas_call | solution.py:527
  71.3 1.0 copy-done.5
  72.3 1.0 copy-done.7
  73.2 4.6 %collective-permute-start.6 = (f32[8,256]{1,0:T(8,128)S(1)}, f32[8,256]{1,0:T(8,128)S(1)}, u32[]{:S(2)}, u32[]{:S(2)}) collective-permute-start(f32[8,256]{1,0:T(8,128)S(1)} %get-tuple-element.41), channel_id=1, source_target_pairs={{1,0},{2,1},{3,2},{4,3},{5,4},{6,5},{7,6},{8,7},{9,8},{10,9},{11,1... | collective-permute-start | bytes 24584 | tf_op jit(solution)/shard_map/ppermute | solution.py:424
  77.8 1.3 %collective-permute-start.7 = (f32[8,128]{1,0:T(8,128)S(1)}, f32[8,128]{1,0:T(8,128)S(1)}, u32[]{:S(2)}, u32[]{:S(2)}) collective-permute-start(f32[8,128]{1,0:T(8,128)S(1)} %get-tuple-element.42), channel_id=1, source_target_pairs={{16,0},{32,16},{48,32},{64,48},{80,64},{96,80},{112,96},{17,1},{33... | collective-permute-start | bytes 12296 | tf_op jit(solution)/shard_map/ppermute | solution.py:424
  79.1 4.9 %collective-permute-done.7.right = f32[8,128]{1,0:T(8,128)S(1)} collective-permute-done((f32[8,128]{1,0:T(8,128)S(1)}, f32[8,128]{1,0:T(8,128)S(1)}, u32[]{:S(2)}, u32[]{:S(2)}) %collective-permute-start.7) | collective-permute-done | bytes 4128 | tf_op jit(solution)/shard_map/ppermute | solution.py:424
  84.0 6.6 %collective-permute-done.6.below = f32[8,256]{1,0:T(8,128)S(1)} collective-permute-done((f32[8,256]{1,0:T(8,128)S(1)}, f32[8,256]{1,0:T(8,128)S(1)}, u32[]{:S(2)}, u32[]{:S(2)}) %collective-permute-start.6) | collective-permute-done | bytes 8224 | tf_op jit(solution)/shard_map/ppermute | solution.py:424
  90.7 4.2 %all-to-all-done.1.lines = f32[16,264,128]{2,1,0:T(8,128)S(1)} async-done(((f32[16,264,128]{2,1,0:T(8,128)}), f32[16,264,128]{2,1,0:T(8,128)S(1)}, u32[]{:S(2)}, u32[]{:S(2)}) %all-to-all-start.1) | async-done | bytes 2162720 | tf_op jit(solution)/shard_map/all_to_all | solution.py:526
  94.9 1.0 copy-done.2
  95.9 2.3 %rows_back.1 = f32[8,136,256]{2,1,0:T(8,128)S(1)} custom-call(f32[16,264,128]{2,1,0:T(8,128)S(1)} %all-to-all-done.1.lines, f32[2,16,128]{2,1,0:T(8,128)S(1)} %get-tuple-element.30.twiddle, bf16[768,256]{1,0:T(8,128)(2,1)S(1)} %copy-done.2), custom_call_target="tpu_custom_call" | custom-call | tf_op jit(solution)/shard_map/rows_back/pallas_call | solution.py:542
  98.2 21.4 %all_to_all.15.gradient = f32[8,136,256]{2,1,0:T(8,128)S(1)} all-to-all(f32[8,136,256]{2,1,0:T(8,128)S(1)} %rows_back.1), channel_id=1, replica_groups=mesh['chan'=8,'facet'=16] {'chan'}, dimensions={0} | all-to-all | bytes 2228224 | tf_op jit(solution)/shard_map/all_to_all | solution.py:549
  119.6 2.4 %finish.1 = (f32[8,128,256]{2,1,0:T(8,128)}, bf16[8,2,128,256]{3,2,1,0:T(8,128)(2,1)}) custom-call(f32[8,136,256]{2,1,0:T(8,128)S(1)} %all_to_all.15.gradient, f32[8,128,256]{2,1,0:T(8,128)S(1)} %copy-done.6, f32[8,128,256]{2,1,0:T(8,128)S(1)} %copy-done.8, bf16[8,2,128,256]{3,2,1,0:T(8,128)(2,1)S(1)} %copy-done, f32[8,256]{1,0:T(8,128)S(1)} %collective-permute-done.6.below, ...), custom_call_target="tpu_custom_call" | custom-call | tf_op jit(solution)/shard_map/finish/pallas_call | solution.py:550
  (39 shorter events, 0.1 us)
Async XLA Ops:
  4.8 24.9 %copy-start.10 = (f32[128,512]{1,0:T(8,128)S(1)}, f32[128,512]{1,0:T(8,128)}, u32[]{:S(2)}) copy-start(f32[128,512]{1,0:T(8,128)} %get-tuple-element.33.refs_0_) | copy-start | bytes 786436
  4.8 26.9 %copy-start = (bf16[8,2,128,256]{3,2,1,0:T(8,128)(2,1)S(1)}, bf16[8,2,128,256]{3,2,1,0:T(8,128)(2,1)}, u32[]{:S(2)}) copy-start(bf16[8,2,128,256]{3,2,1,0:T(8,128)(2,1)} %dual.3) | copy-start | bytes 3145732
  4.8 44.5 %all-to-all-start = ((f32[16,256,128]{2,1,0:T(8,128)}), f32[16,256,128]{2,1,0:T(8,128)S(1)}, u32[]{:S(2)}, u32[]{:S(2)}) async-start(f32[16,256,128]{2,1,0:T(8,128)} %bitcast.7), calls=%async_computation | async-start | bytes 4194304 | tf_op jit(solution)/shard_map/all_to_all | solution.py:485
  13.2 23.5 %copy-start.9 = (bf16[1,2,2048,128]{3,2,1,0:T(8,128)(2,1)S(1)}, bf16[1,2,2048,128]{3,2,1,0:T(8,128)(2,1)}, u32[]{:S(2)}) copy-start(bf16[1,2,2048,128]{3,2,1,0:T(8,128)(2,1)} %param.11) | copy-start | bytes 3145732
  13.2 23.5 %copy-start.18 = (bf16[1,2048,128]{2,1,0:T(8,128)(2,1)S(1)}, bf16[1,2048,128]{2,1,0:T(8,128)(2,1)}, u32[]{:S(2)}) copy-start(bf16[1,2048,128]{2,1,0:T(8,128)(2,1)} %param.10) | copy-start | bytes 1572868
  13.2 23.5 %copy-start.19 = (bf16[768,256]{1,0:T(8,128)(2,1)S(1)}, bf16[768,256]{1,0:T(8,128)(2,1)}, u32[]{:S(2)}) copy-start(bf16[768,256]{1,0:T(8,128)(2,1)} %constant.20.clone.inverse) | copy-start | bytes 1179652
  13.2 23.5 %copy-start.20 = (bf16[768,256]{1,0:T(8,128)(2,1)S(1)}, bf16[768,256]{1,0:T(8,128)(2,1)}, u32[]{:S(2)}) copy-start(bf16[768,256]{1,0:T(8,128)(2,1)} %constant.19.clone.forward) | copy-start | bytes 1179652
  13.2 23.5 %copy-start.23 = (f32[2,16,128]{2,1,0:T(8,128)S(1)}, f32[2,16,128]{2,1,0:T(8,128)}, u32[]{:S(2)}) copy-start(f32[2,16,128]{2,1,0:T(8,128)} %constant.17.clone.twiddle) | copy-start | bytes 49156
  13.2 23.5 %copy-start.24 = (bf16[128,128]{1,0:T(8,128)(2,1)S(1)}, bf16[128,128]{1,0:T(8,128)(2,1)}, u32[]{:S(2)}) copy-start(bf16[128,128]{1,0:T(8,128)(2,1)} %constant.16.clone.place) | copy-start | bytes 98308
  13.2 9.8 %collective-permute-start.2 = (f32[128,512]{1,0:T(8,128)}, f32[128,512]{1,0:T(8,128)S(1)}, u32[]{:S(2)}, u32[]{:S(2)}) collective-permute-start(f32[128,512]{1,0:T(8,128)} %get-tuple-element.34), channel_id=1, source_target_pairs={{0,32},{16,48},{32,64},{48,80},{64,96},{80,112},{96,0},{112,16},{1... | collective-permute-start | bytes 786440 | tf_op jit(solution)/shard_map/ppermute | solution.py:484
  14.8 14.9 %collective-permute-start.3 = (f32[128,512]{1,0:T(8,128)}, f32[128,512]{1,0:T(8,128)S(1)}, u32[]{:S(2)}, u32[]{:S(2)}) collective-permute-start(f32[128,512]{1,0:T(8,128)} %get-tuple-element.35), channel_id=1, source_target_pairs={{0,64},{16,80},{32,96},{48,112},{64,0},{80,16},{96,32},{112,48},{1... | collective-permute-start | bytes 786440 | tf_op jit(solution)/shard_map/ppermute | solution.py:484
  17.5 12.2 %collective-permute-start.4 = (f32[128,512]{1,0:T(8,128)}, f32[128,512]{1,0:T(8,128)S(1)}, u32[]{:S(2)}, u32[]{:S(2)}) collective-permute-start(f32[128,512]{1,0:T(8,128)} %get-tuple-element.36), channel_id=1, source_target_pairs={{0,96},{16,112},{32,0},{48,16},{64,32},{80,48},{96,64},{112,80},{1... | collective-permute-start | bytes 786440 | tf_op jit(solution)/shard_map/ppermute | solution.py:484
  23.1 13.6 %copy-start.12 = (f32[128,512]{1,0:T(8,128)}, f32[128,512]{1,0:T(8,128)S(1)}, u32[]{:S(2)}) copy-start(f32[128,512]{1,0:T(8,128)S(1)} %collective-permute-done.2.refs_1_) | copy-start | bytes 786436
  29.7 7.0 %copy-start.14 = (f32[128,512]{1,0:T(8,128)}, f32[128,512]{1,0:T(8,128)S(1)}, u32[]{:S(2)}) copy-start(f32[128,512]{1,0:T(8,128)S(1)} %collective-permute-done.3.refs_2_) | copy-start | bytes 786436
  29.7 7.0 %copy-start.16 = (f32[128,512]{1,0:T(8,128)}, f32[128,512]{1,0:T(8,128)S(1)}, u32[]{:S(2)}) copy-start(f32[128,512]{1,0:T(8,128)S(1)} %collective-permute-done.4.refs_3_) | copy-start | bytes 786436
  30.6 28.2 %collective-permute-start.5 = (f32[4,128,256]{2,1,0:T(8,128)}, f32[4,128,256]{2,1,0:T(8,128)}, u32[]{:S(2)}, u32[]{:S(2)}) collective-permute-start(f32[4,128,256]{2,1,0:T(8,128)} %swap_ready.1), channel_id=1, source_target_pairs={{0,16},{16,0},{32,48},{48,32},{64,80},{80,64},{96,112},{112,96},{1... | collective-permute-start | bytes 1572872 | tf_op jit(solution)/shard_map/ppermute | solution.py:511
  31.8 16.9 %collective-permute-start = (f32[8,256]{1,0:T(8,128)S(1)}, f32[8,256]{1,0:T(8,128)S(1)}, u32[]{:S(2)}, u32[]{:S(2)}) collective-permute-start(f32[8,256]{1,0:T(8,128)S(1)} %get-tuple-element.26), channel_id=1, source_target_pairs={{0,1},{1,2},{2,3},{3,4},{4,5},{5,6},{6,7},{7,8},{8,9},{9,10},{10,1... | collective-permute-start | bytes 24584 | tf_op jit(solution)/shard_map/ppermute | solution.py:424
  33.7 14.4 %collective-permute-start.1 = (f32[8,128]{1,0:T(8,128)S(1)}, f32[8,128]{1,0:T(8,128)S(1)}, u32[]{:S(2)}, u32[]{:S(2)}) collective-permute-start(f32[8,128]{1,0:T(8,128)S(1)} %get-tuple-element.27), channel_id=1, source_target_pairs={{0,16},{16,32},{32,48},{48,64},{64,80},{80,96},{96,112},{1,17},{17... | collective-permute-start | bytes 12296 | tf_op jit(solution)/shard_map/ppermute | solution.py:424
  38.3 1.2 copy-start.3
  39.5 0.7 copy-start.21
  40.2 18.6 %copy-start.1 = (bf16[768,256]{1,0:T(8,128)(2,1)}, bf16[768,256]{1,0:T(8,128)(2,1)S(1)}, u32[]{:S(2)}) copy-start(bf16[768,256]{1,0:T(8,128)(2,1)S(1)} %get-tuple-element.32.inverse.table) | copy-start | bytes 1179652
  48.1 0.6 copy-start.27
  48.7 0.6 copy-start.25
  49.3 1.4 %copy-start.4 = (bf16[3,16,128,128]{3,2,1,0:T(8,128)(2,1)S(1)}, bf16[3,16,128,128]{3,2,1,0:T(8,128)(2,1)}, u32[]{:S(2)}) copy-start(bf16[3,16,128,128]{3,2,1,0:T(8,128)(2,1)} %copy-done.3) | copy-start | bytes 4718596
  50.7 1.0 copy-start.22
  58.8 7.8 %copy-start.11 = (f32[128,512]{1,0:T(8,128)S(1)}, f32[128,512]{1,0:T(8,128)}, u32[]{:S(2)}) copy-start(f32[128,512]{1,0:T(8,128)} %get-tuple-element.33.refs_0_) | copy-start | bytes 786436
  58.8 7.8 %copy-start.26 = (f32[8,256]{1,0:T(8,128)S(1)}, f32[8,256]{1,0:T(8,128)}, u32[]{:S(2)}) copy-start(f32[8,256]{1,0:T(8,128)} %copy-done.25) | copy-start | bytes 24580
  58.8 7.8 %copy-start.28 = (f32[8,128]{1,0:T(8,128)S(1)}, f32[8,128]{1,0:T(8,128)}, u32[]{:S(2)}) copy-start(f32[8,128]{1,0:T(8,128)} %copy-done.27) | copy-start | bytes 12292
  58.8 36.1 %all-to-all-start.1 = ((f32[16,264,128]{2,1,0:T(8,128)}), f32[16,264,128]{2,1,0:T(8,128)S(1)}, u32[]{:S(2)}, u32[]{:S(2)}) async-start(f32[16,264,128]{2,1,0:T(8,128)} %columns.1), calls=%async_computation.1 | async-start | bytes 4325376 | tf_op jit(solution)/shard_map/all_to_all | solution.py:526
  66.6 1.0 copy-start.13
  67.5 0.9 copy-start.15
  68.5 0.9 copy-start.17
  71.3 1.0 copy-start.5
  72.2 1.0 copy-start.7
  73.2 17.5 %collective-permute-start.6 = (f32[8,256]{1,0:T(8,128)S(1)}, f32[8,256]{1,0:T(8,128)S(1)}, u32[]{:S(2)}, u32[]{:S(2)}) collective-permute-start(f32[8,256]{1,0:T(8,128)S(1)} %get-tuple-element.41), channel_id=1, source_target_pairs={{1,0},{2,1},{3,2},{4,3},{5,4},{6,5},{7,6},{8,7},{9,8},{10,9},{11,1... | collective-permute-start | bytes 24584 | tf_op jit(solution)/shard_map/ppermute | solution.py:424
  77.8 6.2 %collective-permute-start.7 = (f32[8,128]{1,0:T(8,128)S(1)}, f32[8,128]{1,0:T(8,128)S(1)}, u32[]{:S(2)}, u32[]{:S(2)}) collective-permute-start(f32[8,128]{1,0:T(8,128)S(1)} %get-tuple-element.42), channel_id=1, source_target_pairs={{16,0},{32,16},{48,32},{64,48},{80,64},{96,80},{112,96},{17,1},{33... | collective-permute-start | bytes 12296 | tf_op jit(solution)/shard_map/ppermute | solution.py:424
  94.9 1.0 copy-start.2
  95.9 23.7 %copy-start.6 = (f32[8,128,256]{2,1,0:T(8,128)S(1)}, f32[8,128,256]{2,1,0:T(8,128)}, u32[]{:S(2)}) copy-start(f32[8,128,256]{2,1,0:T(8,128)} %copy-done.5) | copy-start | bytes 3145732
  95.9 23.7 %copy-start.8 = (f32[8,128,256]{2,1,0:T(8,128)S(1)}, f32[8,128,256]{2,1,0:T(8,128)}, u32[]{:S(2)}) copy-start(f32[8,128,256]{2,1,0:T(8,128)} %copy-done.7) | copy-start | bytes 3145732

commit v4 on v3

--- a/solution.py
+++ b/solution.py
@@ -3,7 +3,6 @@
 
 import jax
 import jax.numpy as jnp
-import ml_dtypes
 import numpy as np
 from jax import lax
 from jax.experimental import pallas as pl
@@ -24,22 +23,12 @@
 
 def host_tables():
     index = np.arange(LANES)
-    angle = 2.0 * np.pi * (index[:, None] * index[None, :] % LANES) / LANES
-    cos, sin = np.cos(angle), np.sin(angle)
-    forward = np.block([[cos, -sin], [sin, cos]])
-    inverse = np.block([[cos, sin], [-sin, cos]])
-    turn = 2.0 * np.pi * np.arange(RADIX)[:, None] * index[None, :] / GRID
+    turn = 2.0 * np.pi * np.arange(RADIX + 8)[:, None] * index[None, :] / GRID
     twiddle = np.stack([np.cos(turn), np.sin(turn)]).astype(np.float32)
     place = np.zeros((LANES, LANES))
     for at in range(LANES):
         place[at, 16 * (at % 8) + at // 8] = 1.0
-    return forward, inverse, twiddle, place
-
-
-def halves(table):
-    high = table.astype(ml_dtypes.bfloat16)
-    low = (table - high.astype(np.float64)).astype(ml_dtypes.bfloat16)
-    return np.concatenate([high, high, low], axis=0)
+    return twiddle, place
 
 
 def c_add(a, b):
@@ -124,6 +113,28 @@
     return copy
 
 
+def fill_table(table, twiddle, sign, transposed):
+    shape = (LANES, LANES)
+    row, col = (lax.broadcasted_iota(jnp.int32, shape, n) for n in range(2))
+    at = jnp.bitwise_and(row * col, LANES - 1)
+    cos, sin = (
+        jnp.take_along_axis(
+            jnp.broadcast_to(twiddle[n, RADIX : RADIX + 1, :], shape), at, axis=1
+        )
+        for n in range(2)
+    )
+    for n, value in enumerate((cos, sign * sin, -sign * sin, cos)):
+        high, low = split(value)
+        into, out = ((n // 2, n % 2), (n % 2, n // 2))[transposed]
+        for m, half in enumerate((high, high, low)):
+            if transposed:
+                lane = 256 * m + LANES * out
+                table[LANES * into : LANES * into + LANES, lane : lane + LANES] = half
+            else:
+                at_row = 256 * m + LANES * into
+                table[at_row : at_row + LANES, LANES * out : LANES * out + LANES] = half
+
+
 def three_pass(pair, table, dims):
     high = pair[:, :256] if dims[0][0] == 1 else pair[:256, :]
     return dot(pair, table[:512, :], dims) + dot(high, table[512:, :], dims)
@@ -138,36 +149,49 @@
     held[rows, 3 * LANES : 4 * LANES] = low_i
 
 
+def cross_ready(where, image, *pieces):
+    for k in range(4):
+        to = (where[0] // 2 + k) % 4
+        pieces[k][...] = image[:, pl.ds(pl.multiple_of(to * 512, 512), 512)]
+
+
+def swap_ready(where, *refs):
+    pieces, early, late = refs[:4], refs[4], refs[5]
+    lanes = pl.ds(pl.multiple_of((1 - where[0] % 2) * 256, 256), 256)
+    for k in range(4):
+        early[k] = pieces[k][: LANES // 2, lanes]
+        late[k] = pieces[k][LANES // 2 :, lanes]
+
+
 def rows_forward(
-    where, image, twiddle, table, out, *rest
+    image_in, twiddle_in, out, image, twiddle, out_v, held, table, in_sems, sems
 ):
-    pieces, (image_v, twiddle_v, table_v, out_v, held, in_sems, out_sems) = rest[:4], rest[4:]
     chunk = 16
     steps = LANES // chunk
 
     def incoming(step):
         rows = pl.ds(pl.multiple_of(step * chunk, chunk), chunk)
-        return pltpu.make_async_copy(image.at[rows, :], image_v.at[rows, :], in_sems.at[step])
-
+        return pltpu.make_async_copy(image_in.at[rows, :], image.at[rows, :], in_sems.at[step])
+
+    get_twiddle = fetched(twiddle_in, twiddle, in_sems.at[steps])
     for step in range(steps):
         incoming(step).start()
-    get_twiddle = fetched(twiddle, twiddle_v, in_sems.at[steps])
-    get_table = fetched(table, table_v, in_sems.at[steps + 1])
-    sent = []
     get_twiddle.wait()
+    fill_table(table, twiddle, -1, True)
 
     def body(step, carry):
         incoming(step).wait()
         at = pl.multiple_of(step * chunk, chunk)
         values = [
-            (image_v[pl.ds(at, chunk), b * LANES : (b + 1) * LANES], None) for b in range(RADIX)
+            (image[pl.ds(at, chunk), b * LANES : (b + 1) * LANES], None) for b in range(RADIX)
         ]
         mixed = sixteen(values, -1)
         for f in range(RADIX):
             real, imag = mixed[f]
             if imag is None:
                 imag = jnp.zeros_like(real)
-            cos, sin = twiddle_v[0, f : f + 1, :], twiddle_v[1, f : f + 1, :]
+            cos = twiddle[0, f : f + 1, :] * (1.0 / GRID)
+            sin = twiddle[1, f : f + 1, :] * (1.0 / GRID)
             store_pair(
                 held,
                 pl.ds(f * LANES + at, chunk),
@@ -177,31 +201,24 @@
         return carry
 
     lax.fori_loop(0, steps, body, 0)
-    for k in range(4):
-        lanes = pl.ds(pl.multiple_of((where[0] // 2 + k) % 4 * 512, 512), 512)
-        sent.append(fetched(image_v.at[:, lanes], pieces[k], out_sems.at[8 + k]))
-    get_table.wait()
     dims = ((1,), (1,))
+    sent = []
     for g in range(RADIX // 2):
         pair = held[256 * g : 256 * g + 256, :]
-        result = dot(table_v[:, :512], pair, dims) + dot(table_v[:, 512:], pair[:, :256], dims)
+        result = dot(table[:, :512], pair, dims) + dot(table[:, 512:], pair[:, :256], dims)
         for h in range(2):
             for c in range(2):
                 block = result[c * LANES : (c + 1) * LANES, h * LANES : (h + 1) * LANES]
                 out_v[:, c, 2 * g + h] = block.reshape(RADIX, 8, LANES)
         both = pl.ds(2 * g, 2)
-        sent.append(fetched(out_v.at[:, :, both], out.at[:, :, both], out_sems.at[g]))
+        sent.append(fetched(out_v.at[:, :, both], out.at[:, :, both], sems.at[g]))
     for copy in sent:
         copy.wait()
 
 
-def data_prepared(
-    weights, measured, place, forward, inverse, twiddle,
-    out, forward_kept, inverse_kept, twiddle_kept, held,
-):
-    forward_kept[...] = forward[...]
-    inverse_kept[...] = inverse[...]
-    twiddle_kept[...] = twiddle[...]
+def data_prepared(weights, measured, place, twiddle, out, forward, inverse, held):
+    fill_table(forward, twiddle, -1, False)
+    fill_table(inverse, twiddle, 1, False)
     for n in range(3):
         source = weights[...] if n == 0 else measured[n - 1]
         held[...] = source.astype(jnp.float32)
@@ -210,54 +227,91 @@
             out[n, f] = dot(place[...], rows, ((1,), (1,))).astype(jnp.bfloat16)
 
 
-def columns(cols, data, twiddle, forward, inverse, out, held):
-    chunk = 32
+def columns(
+    cols, data_in, twiddle, forward_in, inverse_in, out_all,
+    data, forward, inverse, out, held, turned_v, in_sems, out_sems,
+):
+    chunk = 16
     steps = LANES // chunk
     dims = ((1,), (0,))
+    many = 4
+    get_forward = fetched(forward_in, forward, in_sems.at[4])
+    get_inverse = fetched(inverse_in, inverse, in_sems.at[5])
+    get_data = []
+    for g in range(RADIX // many):
+        part = pl.ds(g * many, many)
+        get_data.append(fetched(data_in.at[:, part], data.at[:, part], in_sems.at[g]))
     out[:, 2 * LANES :, :] = jnp.zeros((RADIX, 8, LANES), jnp.float32)
     lane_at = lax.broadcasted_iota(jnp.int32, (8, LANES), 1)
 
-    def body(step, carry):
+    def first(step, carry):
         at = pl.multiple_of(step * chunk, chunk)
-        here = pl.ds(at, chunk)
-        imag_here = pl.ds(pl.multiple_of(LANES + at, chunk), chunk)
-        mixed = sixteen([(cols[b, here, :], cols[b, imag_here, :]) for b in range(RADIX)], -1)
+        imag_at = pl.ds(pl.multiple_of(LANES + at, chunk), chunk)
+        mixed = sixteen([(cols[b, pl.ds(at, chunk), :], cols[b, imag_at, :]) for b in range(RADIX)], -1)
         for f in range(RADIX):
             real, imag = mixed[f]
             cos, sin = twiddle[0, f : f + 1, :], twiddle[1, f : f + 1, :]
-            rows = slice(f * chunk, (f + 1) * chunk)
+            rows = pl.ds(f * LANES + at, chunk)
             store_pair(held, rows, real * cos + imag * sin, imag * cos - real * sin)
-        spectrum = three_pass(held[...], forward, dims)
-        for f in range(RADIX):
-            rows = slice(f * chunk, (f + 1) * chunk)
-            weight = data[0, f, here, :].astype(jnp.float32)
-            real = weight * spectrum[rows, :LANES] - data[1, f, here, :].astype(jnp.float32)
-            imag = weight * spectrum[rows, LANES:] - data[2, f, here, :].astype(jnp.float32)
-            store_pair(held, rows, real, imag)
-        back = three_pass(held[...], inverse, dims)
+        return carry
+
+    lax.fori_loop(0, steps, first, 0)
+    get_forward.wait()
+    get_inverse.wait()
+    for g in range(RADIX // many):
+        get_data[g].wait()
+        block = slice(g * many * LANES, (g + 1) * many * LANES)
+        spectrum = three_pass(held[block, :], forward, dims)
+        for i in range(many):
+            f = g * many + i
+            rows = slice(i * LANES, (i + 1) * LANES)
+            weight = data[0, f].astype(jnp.float32)
+            real = weight * spectrum[rows, :LANES] - data[1, f].astype(jnp.float32)
+            imag = weight * spectrum[rows, LANES:] - data[2, f].astype(jnp.float32)
+            store_pair(held, slice(f * LANES, (f + 1) * LANES), real, imag)
+        turned_v[block, :] = three_pass(held[block, :], inverse, dims)
+
+    def last(step, carry):
+        at = pl.multiple_of(step * chunk, chunk)
+        places = pl.ds(at, chunk), pl.ds(pl.multiple_of(LANES + at, chunk), chunk)
         values = []
         for f in range(RADIX):
-            rows = slice(f * chunk, (f + 1) * chunk)
-            real, imag = back[rows, :LANES], back[rows, LANES:]
+            rows = pl.ds(f * LANES + at, chunk)
+            real, imag = turned_v[rows, :LANES], turned_v[rows, LANES:]
             cos, sin = twiddle[0, f : f + 1, :], twiddle[1, f : f + 1, :]
             values.append((real * cos - imag * sin, imag * cos + real * sin))
         mixed = sixteen(values, 1)
         for b in range(RADIX):
             for c in range(2):
-                out[b, (here, imag_here)[c], :] = mixed[b][c]
+                out[b, places[c], :] = mixed[b][c]
                 if b > 0:
                     edge = out[b - 1, 2 * LANES :, :]
                     for i in range(chunk // 8):
-                        first = mixed[b][c][8 * i : 8 * i + 8, 0:1]
+                        one = mixed[b][c][8 * i : 8 * i + 8, 0:1]
                         at_lane = lane_at == c * RADIX + step * (chunk // 8) + i
-                        edge = jnp.where(at_lane, first, edge)
+                        edge = jnp.where(at_lane, one, edge)
                     out[b - 1, 2 * LANES :, :] = edge
+        for c in range(2):
+            outgoing(step, c).start()
         return carry
 
-    lax.fori_loop(0, steps, body, 0)
-
-
-def rows_back(lines, twiddle, table, out, held, side_v):
+    def outgoing(step, c):
+        rows = pl.ds(pl.multiple_of(c * LANES + step * chunk, chunk), chunk)
+        return pltpu.make_async_copy(
+            out.at[:, rows, :], out_all.at[:, rows, :], out_sems.at[step, c]
+        )
+
+    lax.fori_loop(0, steps, last, 0)
+    rows = pl.ds(2 * LANES, 8)
+    edges = fetched(out.at[:, rows, :], out_all.at[:, rows, :], in_sems.at[0])
+    for step in range(steps):
+        for c in range(2):
+            outgoing(step, c).wait()
+    edges.wait()
+
+
+def rows_back(lines, twiddle, out, held, side_v, table):
+    fill_table(table, twiddle, 1, False)
     dims = ((0,), (0,))
     for f in range(RADIX):
         real = lines[:, 8 * f : 8 * f + 8, :].reshape(LANES, LANES)
@@ -275,7 +329,7 @@
     edge_r = edge[:RADIX, :LANES] - edge[RADIX : 2 * RADIX, LANES:]
     edge_i = edge[:RADIX, LANES:] + edge[RADIX : 2 * RADIX, :LANES]
     scale = 1.0 / GRID
-    cos, sin = twiddle[0] * scale, twiddle[1] * scale
+    cos, sin = twiddle[0, :RADIX] * scale, twiddle[1, :RADIX] * scale
     edge_r, edge_i = edge_r * cos - edge_i * sin, edge_i * cos + edge_r * sin
     mixed = sixteen([(edge_r[f : f + 1], edge_i[f : f + 1]) for f in range(RADIX)], 1)
     for d in range(CHANNELS):
@@ -319,16 +373,9 @@
     last_column[...] = jnp.concatenate(cols, axis=1).T
 
 
-def swap_ready(where, *refs):
-    pieces, out = refs[:4], refs[4]
-    lanes = pl.ds(pl.multiple_of((1 - where[0] % 2) * 256, 256), 256)
-    for k in range(4):
-        out[k] = pieces[k][:, lanes]
-
-
 def tile_ready(where, *refs):
-    pieces, (swapped, dual, above, left) = refs[:4], refs[4:8]
-    for_image, for_ahead, first_row, first_column = refs[8:]
+    pieces, (early, late, dual, above, left) = refs[:4], refs[4:9]
+    for_image, for_ahead, first_row, first_column = refs[9:]
     row_at = lax.broadcasted_iota(jnp.int32, (LANES, 2 * LANES), 0)
     lane_at = lax.broadcasted_iota(jnp.int32, (LANES, 2 * LANES), 1)
     for k in range(4):
@@ -342,10 +389,9 @@
             prev_q = jnp.where(lane_at == 0, beside, pltpu.roll(q, 1, 1))
             adjoint = prev_p - p + prev_q - q
             if other:
-                image = swapped[k]
+                image = jnp.concatenate([early[k], late[k]], axis=0)
             else:
-                own = pl.ds(pl.multiple_of(half * 256, 256), 256)
-                image = pieces[k][:, own]
+                image = pieces[k][:, pl.ds(pl.multiple_of(half * 256, 256), 256)]
             ahead = image - adjoint
             for_image[c] = image - step_primal * adjoint
             for_ahead[c] = ahead
@@ -444,15 +490,32 @@
 
 
 def shards(image_field, weights, measured, dual_field):
-    forward, inverse, twiddle, place = host_tables()
-    scale = 1.0 / GRID
+    twiddle, place = host_tables()
     place = jnp.asarray(place, jnp.bfloat16)
     twiddle = jnp.asarray(twiddle)
     image = image_field[0]
     f32, bf16 = jnp.float32, jnp.bfloat16
-    chan = lax.axis_index("chan")
-    where = chan.astype(jnp.int32).reshape(1)
-
+    where = lax.axis_index("chan").astype(jnp.int32).reshape(1)
+
+    spread = call(
+        rows_forward,
+        shape((RADIX, 2, RADIX, 8, LANES)),
+        [HBM, HBM],
+        HBM,
+        [
+            pltpu.VMEM((LANES, GRID), f32),
+            pltpu.VMEM((2, RADIX + 8, LANES), f32),
+            pltpu.VMEM((RADIX, 2, RADIX, 8, LANES), f32),
+            pltpu.VMEM((GRID, 512), bf16),
+            pltpu.VMEM((256, 768), bf16),
+            DMA((9,)),
+            DMA((8,)),
+        ],
+        63,
+    )(image, twiddle)
+    cols = lax.all_to_all(
+        spread.reshape(RADIX, 2 * LANES, LANES), "facet", split_axis=0, concat_axis=0, tiled=True
+    )
     last_row, last_column = call(
         dual_edges,
         (shape((CHANNELS, 2 * LANES)), shape((CHANNELS, LANES))),
@@ -462,67 +525,54 @@
     )(dual_field)
     above = passed_along(last_row, "facet", 1)
     left = passed_along(last_column, "chan", 1)
-
-    spread, *pieces = call(
-        rows_forward,
-        (shape((RADIX, 2, RADIX, 8, LANES)),) + (shape((LANES, 512)),) * 4,
-        [SM, HBM, HBM, HBM],
-        (HBM,) * 5,
-        [
-            pltpu.VMEM((LANES, GRID), f32),
-            pltpu.VMEM((2, RADIX, LANES), f32),
-            pltpu.VMEM((256, 768), bf16),
-            pltpu.VMEM((RADIX, 2, RADIX, 8, LANES), f32),
-            pltpu.VMEM((GRID, 512), bf16),
-            DMA((10,)),
-            DMA((12,)),
-        ],
-        63,
-    )(where, image, twiddle, jnp.asarray(halves(forward * scale).T))
+    pieces = list(
+        call(cross_ready, (shape((LANES, 512)),) * 4, [SM, VM], (VM,) * 4, [])(where, image)
+    )
     for k in range(1, 4):
         pairs = [(2 * x + z, (x + k) % 4 * 2 + z) for x in range(4) for z in range(2)]
         pieces[k] = lax.ppermute(pieces[k], "chan", pairs)
-    cols = lax.all_to_all(
-        spread.reshape(RADIX, 2 * LANES, LANES), "facet", split_axis=0, concat_axis=0, tiled=True
-    )
-    data, forward_kept, inverse_kept, twiddle_kept = call(
+    early, late = call(
+        swap_ready, (shape((4, LANES // 2, 256)),) * 2, [SM] + [VM] * 4, (VM, VM), []
+    )(where, *pieces)
+    other_zl = [(i, i ^ 1) for i in range(8)]
+    early = lax.ppermute(early, "chan", other_zl)
+    data, forward, inverse = call(
         data_prepared,
         (
             shape((3, RADIX, LANES, LANES), bf16),
             shape((768, 256), bf16),
             shape((768, 256), bf16),
-            shape((2, RADIX, LANES)),
         ),
-        [VM] * 6,
-        (VM,) * 4,
+        [VM] * 4,
+        (VM,) * 3,
         [pltpu.VMEM((GRID, LANES), f32)],
-    )(
-        weights[0],
-        measured[0],
-        place,
-        jnp.asarray(halves(forward)),
-        jnp.asarray(halves(inverse)),
-        twiddle,
-    )
-    to_swap = call(
-        swap_ready, shape((4, LANES, 256)), [SM] + [VM] * 4, VM, []
-    )(where, *pieces)
-    cols, above, left = lax.optimization_barrier((cols, above, left))
-    swapped = lax.ppermute(to_swap, "chan", [(i, i ^ 1) for i in range(8)])
+        63,
+    )(weights[0], measured[0], place, twiddle)
+    cols, late, data, forward, inverse = lax.optimization_barrier(
+        (cols, late, data, forward, inverse)
+    )
+    late = lax.ppermute(late, "chan", other_zl)
+    cols = pltpu.with_memory_space_constraint(cols, pltpu.VMEM)
+    data, forward, inverse = (
+        pltpu.with_memory_space_constraint(x, pltpu.HBM) for x in (data, forward, inverse)
+    )
     back = call(
         columns,
         shape((RADIX, 2 * LANES + 8, LANES)),
-        [VM] * 5,
-        VM,
-        [pltpu.VMEM((RADIX * 32, 512), bf16)],
-    )(
-        cols,
-        data,
-        twiddle_kept,
-        forward_kept,
-        inverse_kept,
-    )
-    back, swapped = lax.optimization_barrier((back, swapped))
+        [VM, HBM, VM, HBM, HBM],
+        HBM,
+        [
+            pltpu.VMEM((3, RADIX, LANES, LANES), bf16),
+            pltpu.VMEM((768, 256), bf16),
+            pltpu.VMEM((768, 256), bf16),
+            pltpu.VMEM((RADIX, 2 * LANES + 8, LANES), f32),
+            pltpu.VMEM((GRID, 512), bf16),
+            pltpu.VMEM((GRID, 256), f32),
+            DMA((6,)),
+            DMA((8, 2)),
+        ],
+    )(cols, data, twiddle, forward, inverse)
+    back, early, late = lax.optimization_barrier((back, early, late))
     lines = lax.all_to_all(back, "facet", split_axis=0, concat_axis=0, tiled=True)
     for_image, for_ahead, first_row, first_column = call(
         tile_ready,
@@ -532,20 +582,25 @@
             shape((CHANNELS, 2 * LANES)),
             shape((CHANNELS, LANES)),
         ),
-        [SM] + [VM] * 8,
+        [SM] + [VM] * 9,
         (VM,) * 4,
         [],
-    )(where, *pieces, swapped, dual_field, above, left)
+    )(where, *pieces, early, late, dual_field, above, left)
     below = passed_along(first_row, "facet", -1)
     right = passed_along(first_column, "chan", -1)
     lines, below, right = lax.optimization_barrier((lines, below, right))
+    lines = pltpu.with_memory_space_constraint(lines, pltpu.VMEM)
     slopes = call(
         rows_back,
         shape((CHANNELS, LANES + 8, 2 * LANES)),
-        [VM] * 3,
+        [VM] * 2,
         VM,
-        [pltpu.VMEM((RADIX, LANES, 256), f32), pltpu.VMEM((LANES, LANES), f32)],
-    )(lines, twiddle_kept, inverse_kept)
+        [
+            pltpu.VMEM((RADIX, LANES, 256), f32),
+            pltpu.VMEM((LANES, LANES), f32),
+            pltpu.VMEM((768, 256), bf16),
+        ],
+    )(lines, twiddle)
     gradient = lax.all_to_all(slopes, "chan", split_axis=0, concat_axis=0, tiled=True)
     return call(
         finish,

time: 124 us -> 129 us (1.040); the launches traced: 122 us -> 128 us
  waiting for transfers between devices: 34.4 us -> 43.1 us
  Pallas kernels: 20.3 us -> 26.8 us
  local copies, waits for them, and re-layouts: 11.4 us -> 7.18 us
  starting transfers between devices: 33.6 us -> 30.2 us
    ppermute x4, waiting for transfers between devices: 19.4 us -> 28.3 us  [passed_along(): return lax.ppermute(x, axis, pairs)]
    all_to_all x1, waiting for transfers between devices: 0.01 us -> 8.23 us  [shards(): lax.all_to_all(spread.reshape(RADIX, 2 * LANES, LANES), 'facet', split_ax...]
    all_to_all x1, waiting for transfers between devices: 4.22 us -> 0.01 us  [shards(): lax.all_to_all(back, 'facet', split_axis=0, concat_axis=0, tiled=True)]
    ppermute x3, waiting for transfers between devices: 10.7 us -> 6.55 us  [shards(): pieces[k] = lax.ppermute(pieces[k], 'chan', pairs)]
    unnamed x58 -> x30, local copies, waits for them, and re-layouts: 11.4 us -> 7.18 us
    pallas_call x4 -> x5, Pallas kernels: 14.4 us -> 18.3 us  [the longest x1 9.88 us: shards(): call(columns, shape((RADIX, 2 * LANES + 8, LANES)), [VM, HBM, VM, HBM, HB...]
    ppermute x4, starting transfers between devices: 10.7 us -> 6.95 us  [passed_along(): return lax.ppermute(x, axis, pairs)]
    pallas_call x1, Pallas kernels: 1.55 us -> 4.17 us  [shards(): call(data_prepared, (shape((3, RADIX, LANES, LANES), bf16), shape((768, 2...]
  transfers between devices with their start and end apart: 10 -> 11, of which waited for: 6 -> 5; matrix products, arithmetic and copies ran while one was open for 0% -> 0% of each run, Pallas kernels for 9% -> 14%
where the time goes in v4:
time: 129 us; the launch traced here: 128 us
  waiting for transfers between devices  43.1 us (33%)
  starting transfers between devices  30.2 us (23%)
  Pallas kernels  26.8 us (21%)
  blocking collectives  20.4 us (16%)
  local copies, waits for them, and re-layouts  7.18 us (6%)
    ppermute x4, waiting for transfers between devices, passed_along(): return lax.ppermute(x, axis, pairs)  28.3 us
    all_to_all x1, blocking collectives, shards(): lax.all_to_all(slopes, 'chan', split_axis=0, concat_axis=0, tiled=True)  20.4 us
    pallas_call x1, Pallas kernels, shards(): call(columns, shape((RADIX, 2 * LANES + 8, LANES)), [VM, HBM, VM, HBM, HB...  9.88 us
    all_to_all x1, starting transfers between devices, shards(): lax.all_to_all(spread.reshape(RADIX, 2 * LANES, LANES), 'facet', split_ax...  8.39 us
    all_to_all x1, waiting for transfers between devices, shards(): lax.all_to_all(spread.reshape(RADIX, 2 * LANES, LANES), 'facet', split_ax...  8.23 us
    unnamed x30, local copies, waits for them, and re-layouts  7.18 us
    all_to_all x1, starting transfers between devices, shards(): lax.all_to_all(back, 'facet', split_axis=0, concat_axis=0, tiled=True)  7.13 us
    ppermute x4, starting transfers between devices, passed_along(): return lax.ppermute(x, axis, pairs)  6.95 us
  transfers between devices with their start and end apart: 11, of which 5 were waited for; matrix products, arithmetic and copies ran while one was open for 0% of the time, Pallas kernels for 14%

profile of v4, /device:TPU:8, one launch (start us, length us, event | category | flops | bytes accessed | tf_op | source)
XLA Modules:
  0.0 128.5 jit_solution(10471604102697018925)
XLA Ops:
  0.6 3.9 %rows_forward.1 = f32[16,2,16,8,128]{4,3,2,1,0:T(8,128)} custom-call(f32[128,2048]{1,0:T(8,128)} %bitcast.5, f32[2,24,128]{2,1,0:T(8,128)} %constant.11.clone.twiddle_in.twiddle), custom_call_target="tpu_custom_call" | custom-call | tf_op jit(solution)/shard_map/rows_forward/pallas_call | solution.py:500
  4.5 0.0 copy-start.1
  4.6 8.4 %all-to-all-start = ((f32[16,256,128]{2,1,0:T(8,128)}), f32[16,256,128]{2,1,0:T(8,128)}, u32[]{:S(2)}, u32[]{:S(2)}) async-start(f32[16,256,128]{2,1,0:T(8,128)} %bitcast.7), calls=%async_computation | async-start | bytes 4194304 | tf_op jit(solution)/shard_map/all_to_all | solution.py:516
  13.0 0.0 copy-done.1
  13.0 1.0 cross_ready.1
  14.0 1.5 %collective-permute-start = (f32[128,512]{1,0:T(8,128)}, f32[128,512]{1,0:T(8,128)S(1)}, u32[]{:S(2)}, u32[]{:S(2)}) collective-permute-start(f32[128,512]{1,0:T(8,128)} %get-tuple-element.29), channel_id=1, source_target_pairs={{0,32},{16,48},{32,64},{48,80},{64,96},{80,112},{96,0},{112,16},{1... | collective-permute-start | bytes 786440 | tf_op jit(solution)/shard_map/ppermute | solution.py:533
  15.4 2.7 %collective-permute-start.1 = (f32[128,512]{1,0:T(8,128)}, f32[128,512]{1,0:T(8,128)S(1)}, u32[]{:S(2)}, u32[]{:S(2)}) collective-permute-start(f32[128,512]{1,0:T(8,128)} %get-tuple-element.30), channel_id=1, source_target_pairs={{0,64},{16,80},{32,96},{48,112},{64,0},{80,16},{96,32},{112,48},{1... | collective-permute-start | bytes 786440 | tf_op jit(solution)/shard_map/ppermute | solution.py:533
  18.2 1.4 %collective-permute-start.2 = (f32[128,512]{1,0:T(8,128)}, f32[128,512]{1,0:T(8,128)}, u32[]{:S(2)}, u32[]{:S(2)}) collective-permute-start(f32[128,512]{1,0:T(8,128)} %get-tuple-element.31), channel_id=1, source_target_pairs={{0,96},{16,112},{32,0},{48,16},{64,32},{80,48},{96,64},{112,80},{1... | collective-permute-start | bytes 786440 | tf_op jit(solution)/shard_map/ppermute | solution.py:533
  19.6 4.2 %data_prepared.1 = (bf16[3,16,128,128]{3,2,1,0:T(8,128)(2,1)}, bf16[768,256]{1,0:T(8,128)(2,1)}, bf16[768,256]{1,0:T(8,128)(2,1)}) custom-call(bf16[2048,128]{1,0:T(8,128)(2,1)} %bitcast.9, bf16[2,2048,128]{2,1,0:T(8,128)(2,1)} %bitcast.8, bf16[128,128]{1,0:T(8,128)(2,1)} %constant.10.clone.place, f32[2,24,128]{2,1,0:T(8,128)} %constant.11.clone.twiddle_in.twiddle), custom_call_target="tpu_custom_call" | custom-call | tf_op jit(solution)/shard_map/data_prepared/pallas_call | solution.py:539
  23.8 0.0 collective-permute-done.refs_1_
  23.8 6.5 %collective-permute-done.1.refs_2_ = f32[128,512]{1,0:T(8,128)S(1)} collective-permute-done((f32[128,512]{1,0:T(8,128)}, f32[128,512]{1,0:T(8,128)S(1)}, u32[]{:S(2)}, u32[]{:S(2)}) %collective-permute-start.1) | collective-permute-done | bytes 262176 | tf_op jit(solution)/shard_map/ppermute | solution.py:533
  30.3 0.0 collective-permute-done.2.refs_3_
  30.3 1.1 swap_ready.1
  31.4 1.1 collective-permute-start.3
  32.5 8.2 %all-to-all-done.cols = f32[16,256,128]{2,1,0:T(8,128)} async-done(((f32[16,256,128]{2,1,0:T(8,128)}), f32[16,256,128]{2,1,0:T(8,128)}, u32[]{:S(2)}, u32[]{:S(2)}) %all-to-all-start) | async-done | bytes 2097184 | tf_op jit(solution)/shard_map/all_to_all | solution.py:516
  40.8 1.0 collective-permute-start.4
  41.8 0.0 copy-done.10
  41.8 9.9 %columns.1 = f32[16,264,128]{2,1,0:T(8,128)} custom-call(f32[16,256,128]{2,1,0:T(8,128)} %all-to-all-done.cols, bf16[3,16,128,128]{3,2,1,0:T(8,128)(2,1)} %get-tuple-element.37.data_in, f32[2,24,128]{2,1,0:T(8,128)S(1)} %copy-done.10, bf16[768,256]{1,0:T(8,128)(2,1)} %get-tuple-element.38.forward_in, bf16[768,256]{1,0:T(8,128)(2,1)} %get-tuple-element.39.inverse_in), custom_call_target="tpu_custom_call" | custom-call | tf_op jit(solution)/shard_map/columns/pallas_call | solution.py:559
  51.7 0.0 copy-done.6
  51.7 0.0 copy-done.8
  51.7 0.0 copy-start
  51.7 0.0 collective-permute-done.3.refs_4_
  51.7 0.0 copy-start.11
  51.7 0.7 copy-done.11
  52.4 0.0 collective-permute-done.4.refs_5_
  52.4 0.7 copy-done.13
  53.1 7.1 %all-to-all-start.1 = ((f32[16,264,128]{2,1,0:T(8,128)}), f32[16,264,128]{2,1,0:T(8,128)S(1)}, u32[]{:S(2)}, u32[]{:S(2)}) async-start(f32[16,264,128]{2,1,0:T(8,128)} %columns.1), calls=%async_computation.1 | async-start | bytes 4325376 | tf_op jit(solution)/shard_map/all_to_all | solution.py:576
  60.2 0.2 dual_edges.1
  60.4 2.1 %collective-permute-start.5 = (f32[8,256]{1,0:T(8,128)S(1)}, f32[8,256]{1,0:T(8,128)S(1)}, u32[]{:S(2)}, u32[]{:S(2)}) collective-permute-start(f32[8,256]{1,0:T(8,128)S(1)} %get-tuple-element.45), channel_id=1, source_target_pairs={{0,1},{1,2},{2,3},{3,4},{4,5},{5,6},{6,7},{7,8},{8,9},{9,10},{10,1... | collective-permute-start | bytes 24584 | tf_op jit(solution)/shard_map/ppermute | solution.py:470
  62.5 1.7 %collective-permute-start.6 = (f32[8,128]{1,0:T(8,128)S(1)}, f32[8,128]{1,0:T(8,128)S(1)}, u32[]{:S(2)}, u32[]{:S(2)}) collective-permute-start(f32[8,128]{1,0:T(8,128)S(1)} %get-tuple-element.46), channel_id=1, source_target_pairs={{0,16},{16,32},{32,48},{48,64},{64,80},{80,96},{96,112},{1,17},{17... | collective-permute-start | bytes 12296 | tf_op jit(solution)/shard_map/ppermute | solution.py:470
  64.2 11.6 %collective-permute-done.6.refs_8_ = f32[8,128]{1,0:T(8,128)S(1)} collective-permute-done((f32[8,128]{1,0:T(8,128)S(1)}, f32[8,128]{1,0:T(8,128)S(1)}, u32[]{:S(2)}, u32[]{:S(2)}) %collective-permute-start.6) | collective-permute-done | bytes 4128 | tf_op jit(solution)/shard_map/ppermute | solution.py:470
  75.8 12.5 %collective-permute-done.5.refs_7_ = f32[8,256]{1,0:T(8,128)S(1)} collective-permute-done((f32[8,256]{1,0:T(8,128)S(1)}, f32[8,256]{1,0:T(8,128)S(1)}, u32[]{:S(2)}, u32[]{:S(2)}) %collective-permute-start.5) | collective-permute-done | bytes 8224 | tf_op jit(solution)/shard_map/ppermute | solution.py:470
  88.3 0.9 copy-done.7
  89.2 0.9 copy-done.9
  90.2 0.9 copy-done.12
  91.1 0.9 copy-done.14
  92.1 1.7 %tile_ready.1 = (f32[8,128,256]{2,1,0:T(8,128)S(1)}, f32[8,128,256]{2,1,0:T(8,128)S(1)}, f32[8,256]{1,0:T(8,128)S(1)}, f32[8,128]{1,0:T(8,128)S(1)}) custom-call(s32[1]{0:T(128)} %bitcast.2.where, f32[128,512]{1,0:T(8,128)S(1)} %get-tuple-element.28.refs_0_, f32[128,512]{1,0:T(8,128)S(1)} %copy-done.7, f32[128,512]{1,0:T(8,128)S(1)} %copy-done.9, ...), custom_call_target="tpu_custom_call" | custom-call | tf_op jit(solution)/shard_map/tile_ready/pallas_call | solution.py:577
  93.8 1.0 copy-done.2
  94.8 1.0 copy-done.4
  95.8 1.9 %collective-permute-start.7 = (f32[8,256]{1,0:T(8,128)S(1)}, f32[8,256]{1,0:T(8,128)S(1)}, u32[]{:S(2)}, u32[]{:S(2)}) collective-permute-start(f32[8,256]{1,0:T(8,128)S(1)} %get-tuple-element.47), channel_id=1, source_target_pairs={{1,0},{2,1},{3,2},{4,3},{5,4},{6,5},{7,6},{8,7},{9,8},{10,9},{11,1... | collective-permute-start | bytes 24584 | tf_op jit(solution)/shard_map/ppermute | solution.py:470
  97.7 1.3 %collective-permute-start.8 = (f32[8,128]{1,0:T(8,128)S(1)}, f32[8,128]{1,0:T(8,128)S(1)}, u32[]{:S(2)}, u32[]{:S(2)}) collective-permute-start(f32[8,128]{1,0:T(8,128)S(1)} %get-tuple-element.48), channel_id=1, source_target_pairs={{16,0},{32,16},{48,32},{64,48},{80,64},{96,80},{112,96},{17,1},{33... | collective-permute-start | bytes 12296 | tf_op jit(solution)/shard_map/ppermute | solution.py:470
  99.0 4.2 %collective-permute-done.8.right = f32[8,128]{1,0:T(8,128)S(1)} collective-permute-done((f32[8,128]{1,0:T(8,128)S(1)}, f32[8,128]{1,0:T(8,128)S(1)}, u32[]{:S(2)}, u32[]{:S(2)}) %collective-permute-start.8) | collective-permute-done | bytes 4128 | tf_op jit(solution)/shard_map/ppermute | solution.py:470
  103.2 0.0 collective-permute-done.7.below
  103.2 0.0 all-to-all-done.1.lines
  103.2 0.0 copy-start.5
  103.2 2.4 %rows_back.1 = f32[8,136,256]{2,1,0:T(8,128)S(1)} custom-call(f32[16,264,128]{2,1,0:T(8,128)S(1)} %all-to-all-done.1.lines, f32[2,24,128]{2,1,0:T(8,128)S(1)} %copy-done.10), custom_call_target="tpu_custom_call" | custom-call | tf_op jit(solution)/shard_map/rows_back/pallas_call | solution.py:593
  105.6 20.4 %all_to_all.15.gradient = f32[8,136,256]{2,1,0:T(8,128)S(1)} all-to-all(f32[8,136,256]{2,1,0:T(8,128)S(1)} %rows_back.1), channel_id=1, replica_groups=mesh['chan'=8,'facet'=16] {'chan'}, dimensions={0} | all-to-all | bytes 2228224 | tf_op jit(solution)/shard_map/all_to_all | solution.py:604
  126.1 2.4 %finish.1 = (f32[8,128,256]{2,1,0:T(8,128)}, bf16[8,2,128,256]{3,2,1,0:T(8,128)(2,1)}) custom-call(f32[8,136,256]{2,1,0:T(8,128)S(1)} %all_to_all.15.gradient, f32[8,128,256]{2,1,0:T(8,128)S(1)} %copy-done.3, f32[8,128,256]{2,1,0:T(8,128)S(1)} %copy-done.5, bf16[8,2,128,256]{3,2,1,0:T(8,128)(2,1)S(1)} %copy-done, f32[8,256]{1,0:T(8,128)S(1)} %collective-permute-done.7.below, ...), custom_call_target="tpu_custom_call" | custom-call | tf_op jit(solution)/shard_map/finish/pallas_call | solution.py:605
  (14 shorter events, 0.0 us)
Async XLA Ops:
  4.5 8.4 %copy-start.1 = (f32[1,128,2048]{2,1,0:T(8,128)S(1)}, f32[1,128,2048]{2,1,0:T(8,128)}, u32[]{:S(2)}) copy-start(f32[1,128,2048]{2,1,0:T(8,128)} %param.6) | copy-start | bytes 3145732
  4.6 36.2 %all-to-all-start = ((f32[16,256,128]{2,1,0:T(8,128)}), f32[16,256,128]{2,1,0:T(8,128)}, u32[]{:S(2)}, u32[]{:S(2)}) async-start(f32[16,256,128]{2,1,0:T(8,128)} %bitcast.7), calls=%async_computation | async-start | bytes 4194304 | tf_op jit(solution)/shard_map/all_to_all | solution.py:516
  12.9 28.8 %copy-start.10 = (f32[2,24,128]{2,1,0:T(8,128)S(1)}, f32[2,24,128]{2,1,0:T(8,128)}, u32[]{:S(2)}) copy-start(f32[2,24,128]{2,1,0:T(8,128)} %constant.11.clone.twiddle_in.twiddle) | copy-start | bytes 73732
  14.0 9.8 %collective-permute-start = (f32[128,512]{1,0:T(8,128)}, f32[128,512]{1,0:T(8,128)S(1)}, u32[]{:S(2)}, u32[]{:S(2)}) collective-permute-start(f32[128,512]{1,0:T(8,128)} %get-tuple-element.29), channel_id=1, source_target_pairs={{0,32},{16,48},{32,64},{48,80},{64,96},{80,112},{96,0},{112,16},{1... | collective-permute-start | bytes 786440 | tf_op jit(solution)/shard_map/ppermute | solution.py:533
  15.4 14.9 %collective-permute-start.1 = (f32[128,512]{1,0:T(8,128)}, f32[128,512]{1,0:T(8,128)S(1)}, u32[]{:S(2)}, u32[]{:S(2)}) collective-permute-start(f32[128,512]{1,0:T(8,128)} %get-tuple-element.30), channel_id=1, source_target_pairs={{0,64},{16,80},{32,96},{48,112},{64,0},{80,16},{96,32},{112,48},{1... | collective-permute-start | bytes 786440 | tf_op jit(solution)/shard_map/ppermute | solution.py:533
  18.2 12.2 %collective-permute-start.2 = (f32[128,512]{1,0:T(8,128)}, f32[128,512]{1,0:T(8,128)}, u32[]{:S(2)}, u32[]{:S(2)}) collective-permute-start(f32[128,512]{1,0:T(8,128)} %get-tuple-element.31), channel_id=1, source_target_pairs={{0,96},{16,112},{32,0},{48,16},{64,32},{80,48},{96,64},{112,80},{1... | collective-permute-start | bytes 786440 | tf_op jit(solution)/shard_map/ppermute | solution.py:533
  23.8 27.9 %copy-start.6 = (f32[128,512]{1,0:T(8,128)}, f32[128,512]{1,0:T(8,128)S(1)}, u32[]{:S(2)}) copy-start(f32[128,512]{1,0:T(8,128)S(1)} %collective-permute-done.refs_1_) | copy-start | bytes 786436
  30.3 21.3 %copy-start.8 = (f32[128,512]{1,0:T(8,128)}, f32[128,512]{1,0:T(8,128)S(1)}, u32[]{:S(2)}) copy-start(f32[128,512]{1,0:T(8,128)S(1)} %collective-permute-done.1.refs_2_) | copy-start | bytes 786436
  31.4 20.3 %collective-permute-start.3 = (f32[4,64,256]{2,1,0:T(8,128)S(1)}, f32[4,64,256]{2,1,0:T(8,128)S(1)}, u32[]{:S(2)}, u32[]{:S(2)}) collective-permute-start(f32[4,64,256]{2,1,0:T(8,128)S(1)} %get-tuple-element.40), channel_id=1, source_target_pairs={{0,16},{16,0},{32,48},{48,32},{64,80},{80,64},{96,112},{112,96},{1... | collective-permute-start | bytes 786440 | tf_op jit(solution)/shard_map/ppermute | solution.py:538
  40.8 11.7 %collective-permute-start.4 = (f32[4,64,256]{2,1,0:T(8,128)S(1)}, f32[4,64,256]{2,1,0:T(8,128)S(1)}, u32[]{:S(2)}, u32[]{:S(2)}) collective-permute-start(f32[4,64,256]{2,1,0:T(8,128)S(1)} %get-tuple-element.41), channel_id=1, source_target_pairs={{0,16},{16,0},{32,48},{48,32},{64,80},{80,64},{96,112},{112,96},{1... | collective-permute-start | bytes 786440 | tf_op jit(solution)/shard_map/ppermute | solution.py:554
  51.7 8.6 %copy-start = (bf16[8,2,128,256]{3,2,1,0:T(8,128)(2,1)S(1)}, bf16[8,2,128,256]{3,2,1,0:T(8,128)(2,1)}, u32[]{:S(2)}) copy-start(bf16[8,2,128,256]{3,2,1,0:T(8,128)(2,1)} %dual.3) | copy-start | bytes 3145732
  51.7 0.7 copy-start.11
  52.4 0.7 copy-start.13
  53.1 50.1 %all-to-all-start.1 = ((f32[16,264,128]{2,1,0:T(8,128)}), f32[16,264,128]{2,1,0:T(8,128)S(1)}, u32[]{:S(2)}, u32[]{:S(2)}) async-start(f32[16,264,128]{2,1,0:T(8,128)} %columns.1), calls=%async_computation.1 | async-start | bytes 4325376 | tf_op jit(solution)/shard_map/all_to_all | solution.py:576
  60.4 27.9 %collective-permute-start.5 = (f32[8,256]{1,0:T(8,128)S(1)}, f32[8,256]{1,0:T(8,128)S(1)}, u32[]{:S(2)}, u32[]{:S(2)}) collective-permute-start(f32[8,256]{1,0:T(8,128)S(1)} %get-tuple-element.45), channel_id=1, source_target_pairs={{0,1},{1,2},{2,3},{3,4},{4,5},{5,6},{6,7},{7,8},{8,9},{9,10},{10,1... | collective-permute-start | bytes 24584 | tf_op jit(solution)/shard_map/ppermute | solution.py:470
  62.5 13.3 %collective-permute-start.6 = (f32[8,128]{1,0:T(8,128)S(1)}, f32[8,128]{1,0:T(8,128)S(1)}, u32[]{:S(2)}, u32[]{:S(2)}) collective-permute-start(f32[8,128]{1,0:T(8,128)S(1)} %get-tuple-element.46), channel_id=1, source_target_pairs={{0,16},{16,32},{32,48},{48,64},{64,80},{80,96},{96,112},{1,17},{17... | collective-permute-start | bytes 12296 | tf_op jit(solution)/shard_map/ppermute | solution.py:470
  88.3 1.0 copy-start.7
  89.2 0.9 copy-start.9
  90.2 0.9 copy-start.12
  91.1 0.9 copy-start.14
  93.8 1.0 copy-start.2
  94.8 1.0 copy-start.4
  95.8 7.4 %collective-permute-start.7 = (f32[8,256]{1,0:T(8,128)S(1)}, f32[8,256]{1,0:T(8,128)S(1)}, u32[]{:S(2)}, u32[]{:S(2)}) collective-permute-start(f32[8,256]{1,0:T(8,128)S(1)} %get-tuple-element.47), channel_id=1, source_target_pairs={{1,0},{2,1},{3,2},{4,3},{5,4},{6,5},{7,6},{8,7},{9,8},{10,9},{11,1... | collective-permute-start | bytes 24584 | tf_op jit(solution)/shard_map/ppermute | solution.py:470
  97.7 5.5 %collective-permute-start.8 = (f32[8,128]{1,0:T(8,128)S(1)}, f32[8,128]{1,0:T(8,128)S(1)}, u32[]{:S(2)}, u32[]{:S(2)}) collective-permute-start(f32[8,128]{1,0:T(8,128)S(1)} %get-tuple-element.48), channel_id=1, source_target_pairs={{16,0},{32,16},{48,32},{64,48},{80,64},{96,80},{112,96},{17,1},{33... | collective-permute-start | bytes 12296 | tf_op jit(solution)/shard_map/ppermute | solution.py:470
  103.2 22.9 %copy-start.3 = (f32[8,128,256]{2,1,0:T(8,128)S(1)}, f32[8,128,256]{2,1,0:T(8,128)}, u32[]{:S(2)}) copy-start(f32[8,128,256]{2,1,0:T(8,128)} %copy-done.2) | copy-start | bytes 3145732
  103.2 22.9 %copy-start.5 = (f32[8,128,256]{2,1,0:T(8,128)S(1)}, f32[8,128,256]{2,1,0:T(8,128)}, u32[]{:S(2)}) copy-start(f32[8,128,256]{2,1,0:T(8,128)} %copy-done.4) | copy-start | bytes 3145732

commit v5 on v4

--- a/solution.py
+++ b/solution.py
@@ -228,80 +228,96 @@
 
 
 def columns(
-    cols, data_in, twiddle, forward_in, inverse_in, out_all,
-    data, forward, inverse, out, held, turned_v, in_sems, out_sems,
+    cols_in, data_in, twiddle_in, forward_in, inverse_in, out_all,
+    cols, data, twiddle, forward, inverse, out, held, in_sems, chunk_sems, out_sems,
 ):
-    chunk = 16
+    chunk = 32
     steps = LANES // chunk
     dims = ((1,), (0,))
-    many = 4
-    get_forward = fetched(forward_in, forward, in_sems.at[4])
-    get_inverse = fetched(inverse_in, inverse, in_sems.at[5])
-    get_data = []
-    for g in range(RADIX // many):
-        part = pl.ds(g * many, many)
-        get_data.append(fetched(data_in.at[:, part], data.at[:, part], in_sems.at[g]))
+
+    def incoming_cols(step):
+        rows = pl.ds(pl.multiple_of(step * chunk, chunk), chunk)
+        imag_rows = pl.ds(pl.multiple_of(LANES + step * chunk, chunk), chunk)
+        return [
+            pltpu.make_async_copy(cols_in.at[:, r, :], cols.at[:, r, :], chunk_sems.at[step, n])
+            for n, r in enumerate((rows, imag_rows))
+        ]
+
+    def incoming(step):
+        rows = pl.ds(pl.multiple_of(step * chunk, chunk), chunk)
+        return pltpu.make_async_copy(
+            data_in.at[:, :, rows, :], data.at[:, :, rows, :], chunk_sems.at[step, 2]
+        )
+
+    def outgoing(step, c):
+        rows = pl.ds(pl.multiple_of(c * LANES + step * chunk, chunk), chunk)
+        return pltpu.make_async_copy(
+            out.at[:, rows, :], out_all.at[:, rows, :], out_sems.at[step, c]
+        )
+
+    for copy in incoming_cols(0):
+        copy.start()
+    get_twiddle = fetched(twiddle_in, twiddle, in_sems.at[2])
+    get_forward = fetched(forward_in, forward, in_sems.at[0])
+    incoming(0).start()
+    get_inverse = fetched(inverse_in, inverse, in_sems.at[1])
+    for step in range(1, steps):
+        for copy in incoming_cols(step):
+            copy.start()
+        incoming(step).start()
     out[:, 2 * LANES :, :] = jnp.zeros((RADIX, 8, LANES), jnp.float32)
     lane_at = lax.broadcasted_iota(jnp.int32, (8, LANES), 1)
-
-    def first(step, carry):
+    get_twiddle.wait()
+
+    def body(step, carry):
         at = pl.multiple_of(step * chunk, chunk)
-        imag_at = pl.ds(pl.multiple_of(LANES + at, chunk), chunk)
-        mixed = sixteen([(cols[b, pl.ds(at, chunk), :], cols[b, imag_at, :]) for b in range(RADIX)], -1)
+        here = pl.ds(at, chunk)
+        for copy in incoming_cols(step):
+            copy.wait()
+        imag_here = pl.ds(pl.multiple_of(LANES + at, chunk), chunk)
+        mixed = sixteen([(cols[b, here, :], cols[b, imag_here, :]) for b in range(RADIX)], -1)
         for f in range(RADIX):
             real, imag = mixed[f]
             cos, sin = twiddle[0, f : f + 1, :], twiddle[1, f : f + 1, :]
-            rows = pl.ds(f * LANES + at, chunk)
+            rows = slice(f * chunk, (f + 1) * chunk)
             store_pair(held, rows, real * cos + imag * sin, imag * cos - real * sin)
-        return carry
-
-    lax.fori_loop(0, steps, first, 0)
-    get_forward.wait()
-    get_inverse.wait()
-    for g in range(RADIX // many):
-        get_data[g].wait()
-        block = slice(g * many * LANES, (g + 1) * many * LANES)
-        spectrum = three_pass(held[block, :], forward, dims)
-        for i in range(many):
-            f = g * many + i
-            rows = slice(i * LANES, (i + 1) * LANES)
-            weight = data[0, f].astype(jnp.float32)
-            real = weight * spectrum[rows, :LANES] - data[1, f].astype(jnp.float32)
-            imag = weight * spectrum[rows, LANES:] - data[2, f].astype(jnp.float32)
-            store_pair(held, slice(f * LANES, (f + 1) * LANES), real, imag)
-        turned_v[block, :] = three_pass(held[block, :], inverse, dims)
-
-    def last(step, carry):
-        at = pl.multiple_of(step * chunk, chunk)
-        places = pl.ds(at, chunk), pl.ds(pl.multiple_of(LANES + at, chunk), chunk)
+
+        @pl.when(step == 0)
+        def _():
+            get_forward.wait()
+            get_inverse.wait()
+
+        spectrum = three_pass(held[...], forward, dims)
+        incoming(step).wait()
+        for f in range(RADIX):
+            rows = slice(f * chunk, (f + 1) * chunk)
+            weight = data[0, f, here, :].astype(jnp.float32)
+            real = weight * spectrum[rows, :LANES] - data[1, f, here, :].astype(jnp.float32)
+            imag = weight * spectrum[rows, LANES:] - data[2, f, here, :].astype(jnp.float32)
+            store_pair(held, rows, real, imag)
+        back = three_pass(held[...], inverse, dims)
         values = []
         for f in range(RADIX):
-            rows = pl.ds(f * LANES + at, chunk)
-            real, imag = turned_v[rows, :LANES], turned_v[rows, LANES:]
+            rows = slice(f * chunk, (f + 1) * chunk)
+            real, imag = back[rows, :LANES], back[rows, LANES:]
             cos, sin = twiddle[0, f : f + 1, :], twiddle[1, f : f + 1, :]
             values.append((real * cos - imag * sin, imag * cos + real * sin))
         mixed = sixteen(values, 1)
         for b in range(RADIX):
             for c in range(2):
-                out[b, places[c], :] = mixed[b][c]
+                out[b, (here, imag_here)[c], :] = mixed[b][c]
                 if b > 0:
                     edge = out[b - 1, 2 * LANES :, :]
                     for i in range(chunk // 8):
-                        one = mixed[b][c][8 * i : 8 * i + 8, 0:1]
+                        first = mixed[b][c][8 * i : 8 * i + 8, 0:1]
                         at_lane = lane_at == c * RADIX + step * (chunk // 8) + i
-                        edge = jnp.where(at_lane, one, edge)
+                        edge = jnp.where(at_lane, first, edge)
                     out[b - 1, 2 * LANES :, :] = edge
         for c in range(2):
             outgoing(step, c).start()
         return carry
 
-    def outgoing(step, c):
-        rows = pl.ds(pl.multiple_of(c * LANES + step * chunk, chunk), chunk)
-        return pltpu.make_async_copy(
-            out.at[:, rows, :], out_all.at[:, rows, :], out_sems.at[step, c]
-        )
-
-    lax.fori_loop(0, steps, last, 0)
+    lax.fori_loop(0, steps, body, 0)
     rows = pl.ds(2 * LANES, 8)
     edges = fetched(out.at[:, rows, :], out_all.at[:, rows, :], in_sems.at[0])
     for step in range(steps):
@@ -310,7 +326,11 @@
     edges.wait()
 
 
-def rows_back(lines, twiddle, out, held, side_v, table):
+def tied(value, after_one, after_two, out):
+    pass
+
+
+def rows_back(lines, twiddle, after_one, after_two, out, held, side_v, table):
     fill_table(table, twiddle, 1, False)
     dims = ((0,), (0,))
     for f in range(RADIX):
@@ -548,31 +568,40 @@
         [pltpu.VMEM((GRID, LANES), f32)],
         63,
     )(weights[0], measured[0], place, twiddle)
-    cols, late, data, forward, inverse = lax.optimization_barrier(
-        (cols, late, data, forward, inverse)
+    cols, late, above, left, data, forward, inverse = lax.optimization_barrier(
+        (cols, late, above, left, data, forward, inverse)
     )
     late = lax.ppermute(late, "chan", other_zl)
-    cols = pltpu.with_memory_space_constraint(cols, pltpu.VMEM)
     data, forward, inverse = (
         pltpu.with_memory_space_constraint(x, pltpu.HBM) for x in (data, forward, inverse)
     )
     back = call(
         columns,
         shape((RADIX, 2 * LANES + 8, LANES)),
-        [VM, HBM, VM, HBM, HBM],
+        [HBM] * 5,
         HBM,
         [
+            pltpu.VMEM((RADIX, 2 * LANES, LANES), f32),
             pltpu.VMEM((3, RADIX, LANES, LANES), bf16),
+            pltpu.VMEM((2, RADIX + 8, LANES), f32),
             pltpu.VMEM((768, 256), bf16),
             pltpu.VMEM((768, 256), bf16),
             pltpu.VMEM((RADIX, 2 * LANES + 8, LANES), f32),
-            pltpu.VMEM((GRID, 512), bf16),
-            pltpu.VMEM((GRID, 256), f32),
-            DMA((6,)),
-            DMA((8, 2)),
+            pltpu.VMEM((RADIX * 32, 512), bf16),
+            DMA((3,)),
+            DMA((4, 3)),
+            DMA((4, 2)),
         ],
+        63,
     )(cols, data, twiddle, forward, inverse)
-    back, early, late = lax.optimization_barrier((back, early, late))
+    back = pl.pallas_call(
+        tied,
+        out_shape=shape((RADIX, 2 * LANES + 8, LANES)),
+        in_specs=[ANY] * 3,
+        out_specs=ANY,
+        input_output_aliases={0: 0},
+        name="tied",
+    )(back, early, late)
     lines = lax.all_to_all(back, "facet", split_axis=0, concat_axis=0, tiled=True)
     for_image, for_ahead, first_row, first_column = call(
         tile_ready,
@@ -588,19 +617,17 @@
     )(where, *pieces, early, late, dual_field, above, left)
     below = passed_along(first_row, "facet", -1)
     right = passed_along(first_column, "chan", -1)
-    lines, below, right = lax.optimization_barrier((lines, below, right))
-    lines = pltpu.with_memory_space_constraint(lines, pltpu.VMEM)
     slopes = call(
         rows_back,
         shape((CHANNELS, LANES + 8, 2 * LANES)),
-        [VM] * 2,
+        [VM] * 2 + [ANY] * 2,
         VM,
         [
             pltpu.VMEM((RADIX, LANES, 256), f32),
             pltpu.VMEM((LANES, LANES), f32),
             pltpu.VMEM((768, 256), bf16),
         ],
-    )(lines, twiddle)
+    )(lines, twiddle, below, right)
     gradient = lax.all_to_all(slopes, "chan", split_axis=0, concat_axis=0, tiled=True)
     return call(
         finish,

time: 129 us -> 116 us (0.90); the launches traced: 128 us -> 114 us
  waiting for transfers between devices: 43.1 us -> 24 us
  starting transfers between devices: 30.2 us -> 34.1 us
    ppermute x4, waiting for transfers between devices: 28.3 us -> 17.8 us  [passed_along(): return lax.ppermute(x, axis, pairs)]
    all_to_all x1, waiting for transfers between devices: 8.23 us -> 0.5 us  [shards(): lax.all_to_all(spread.reshape(RADIX, 2 * LANES, LANES), 'facet', split_ax...]
    ppermute x3, waiting for transfers between devices: 6.55 us -> 1.5 us  [shards(): pieces[k] = lax.ppermute(pieces[k], 'chan', pairs)]
    all_to_all x1, waiting for transfers between devices: 0.01 us -> 4.22 us  [shards(): lax.all_to_all(back, 'facet', split_axis=0, concat_axis=0, tiled=True)]
    ppermute x4, starting transfers between devices: 6.95 us -> 10.7 us  [passed_along(): return lax.ppermute(x, axis, pairs)]
    pallas_call x2 -> x3, Pallas kernels: 12.3 us -> 12.2 us  [the longest x1 9.8 us: shards(): call(columns, shape((RADIX, 2 * LANES + 8, LANES)), [HBM] * 5, HBM, [pltp...]
    unnamed x30 -> x36, local copies, waits for them, and re-layouts: 7.18 us -> 7.17 us
  transfers between devices with their start and end apart: 11 -> 11, of which waited for: 5 -> 6; matrix products, arithmetic and copies ran while one was open for 0% -> 0% of each run, Pallas kernels for 14% -> 16%
where the time goes in v5:
time: 116 us; the launch traced here: 114 us
  starting transfers between devices  34.1 us (29%)
  Pallas kernels  27.4 us (24%)
  waiting for transfers between devices  24 us (21%)
  blocking collectives  20.4 us (18%)
  local copies, waits for them, and re-layouts  7.17 us (6%)
    all_to_all x1, blocking collectives, shards(): lax.all_to_all(slopes, 'chan', split_axis=0, concat_axis=0, tiled=True)  20.4 us
    ppermute x4, waiting for transfers between devices, passed_along(): return lax.ppermute(x, axis, pairs)  17.8 us
    ppermute x4, starting transfers between devices, passed_along(): return lax.ppermute(x, axis, pairs)  10.7 us
    pallas_call x1, Pallas kernels, shards(): call(columns, shape((RADIX, 2 * LANES + 8, LANES)), [HBM] * 5, HBM, [pltp...  9.8 us
    all_to_all x1, starting transfers between devices, shards(): lax.all_to_all(spread.reshape(RADIX, 2 * LANES, LANES), 'facet', split_ax...  8.39 us
    all_to_all x1, starting transfers between devices, shards(): lax.all_to_all(back, 'facet', split_axis=0, concat_axis=0, tiled=True)  7.21 us
    unnamed x36, local copies, waits for them, and re-layouts  7.17 us
    ppermute x3, starting transfers between devices, shards(): pieces[k] = lax.ppermute(pieces[k], 'chan', pairs)  5.66 us
  transfers between devices with their start and end apart: 11, of which 6 were waited for; matrix products, arithmetic and copies ran while one was open for 0% of the time, Pallas kernels for 16%

profile of v5, /device:TPU:8, one launch (start us, length us, event | category | flops | bytes accessed | tf_op | source)
XLA Modules:
  0.0 113.9 jit_solution(16613455290350815984)
XLA Ops:
  0.6 3.9 %rows_forward.1 = f32[16,2,16,8,128]{4,3,2,1,0:T(8,128)} custom-call(f32[128,2048]{1,0:T(8,128)} %bitcast.5, f32[2,24,128]{2,1,0:T(8,128)} %constant.11.clone.twiddle_in.twiddle), custom_call_target="tpu_custom_call" | custom-call | tf_op jit(solution)/shard_map/rows_forward/pallas_call | solution.py:520
  4.5 0.0 copy-start.2
  4.6 0.0 copy-start
  4.6 8.4 %all-to-all-start = ((f32[16,256,128]{2,1,0:T(8,128)}), f32[16,256,128]{2,1,0:T(8,128)}, u32[]{:S(2)}, u32[]{:S(2)}) async-start(f32[16,256,128]{2,1,0:T(8,128)} %bitcast.7), calls=%async_computation | async-start | bytes 4194304 | tf_op jit(solution)/shard_map/all_to_all | solution.py:536
  13.0 0.0 copy-done.2
  13.0 0.9 cross_ready.1
  13.9 1.5 %collective-permute-start = (f32[128,512]{1,0:T(8,128)}, f32[128,512]{1,0:T(8,128)S(1)}, u32[]{:S(2)}, u32[]{:S(2)}) collective-permute-start(f32[128,512]{1,0:T(8,128)} %get-tuple-element.25), channel_id=1, source_target_pairs={{0,32},{16,48},{32,64},{48,80},{64,96},{80,112},{96,0},{112,16},{1... | collective-permute-start | bytes 786440 | tf_op jit(solution)/shard_map/ppermute | solution.py:553
  15.4 2.7 %collective-permute-start.1 = (f32[128,512]{1,0:T(8,128)}, f32[128,512]{1,0:T(8,128)S(1)}, u32[]{:S(2)}, u32[]{:S(2)}) collective-permute-start(f32[128,512]{1,0:T(8,128)} %get-tuple-element.26), channel_id=1, source_target_pairs={{0,64},{16,80},{32,96},{48,112},{64,0},{80,16},{96,32},{112,48},{1... | collective-permute-start | bytes 786440 | tf_op jit(solution)/shard_map/ppermute | solution.py:553
  18.1 1.4 %collective-permute-start.2 = (f32[128,512]{1,0:T(8,128)}, f32[128,512]{1,0:T(8,128)}, u32[]{:S(2)}, u32[]{:S(2)}) collective-permute-start(f32[128,512]{1,0:T(8,128)} %get-tuple-element.27), channel_id=1, source_target_pairs={{0,96},{16,112},{32,0},{48,16},{64,32},{80,48},{96,64},{112,80},{1... | collective-permute-start | bytes 786440 | tf_op jit(solution)/shard_map/ppermute | solution.py:553
  19.6 0.0 copy-done
  19.6 0.2 dual_edges.1
  19.7 1.9 %collective-permute-start.3 = (f32[8,256]{1,0:T(8,128)S(1)}, f32[8,256]{1,0:T(8,128)S(1)}, u32[]{:S(2)}, u32[]{:S(2)}) collective-permute-start(f32[8,256]{1,0:T(8,128)S(1)} %get-tuple-element.29), channel_id=1, source_target_pairs={{0,1},{1,2},{2,3},{3,4},{4,5},{5,6},{6,7},{7,8},{8,9},{9,10},{10,1... | collective-permute-start | bytes 24584 | tf_op jit(solution)/shard_map/ppermute | solution.py:490
  21.7 2.9 %collective-permute-start.4 = (f32[8,128]{1,0:T(8,128)S(1)}, f32[8,128]{1,0:T(8,128)S(1)}, u32[]{:S(2)}, u32[]{:S(2)}) collective-permute-start(f32[8,128]{1,0:T(8,128)S(1)} %get-tuple-element.30), channel_id=1, source_target_pairs={{0,16},{16,32},{32,48},{48,64},{64,80},{80,96},{96,112},{1,17},{17... | collective-permute-start | bytes 12296 | tf_op jit(solution)/shard_map/ppermute | solution.py:490
  24.6 4.2 %data_prepared.1 = (bf16[3,16,128,128]{3,2,1,0:T(8,128)(2,1)}, bf16[768,256]{1,0:T(8,128)(2,1)}, bf16[768,256]{1,0:T(8,128)(2,1)}) custom-call(bf16[2048,128]{1,0:T(8,128)(2,1)} %bitcast.9, bf16[2,2048,128]{2,1,0:T(8,128)(2,1)} %bitcast.8, bf16[128,128]{1,0:T(8,128)(2,1)} %constant.10.clone.place, f32[2,24,128]{2,1,0:T(8,128)} %constant.11.clone.twiddle_in.twiddle), custom_call_target="tpu_custom_call" | custom-call | tf_op jit(solution)/shard_map/data_prepared/pallas_call | solution.py:559
  28.8 0.0 collective-permute-done.refs_1_
  28.8 1.5 %collective-permute-done.1.refs_2_ = f32[128,512]{1,0:T(8,128)S(1)} collective-permute-done((f32[128,512]{1,0:T(8,128)}, f32[128,512]{1,0:T(8,128)S(1)}, u32[]{:S(2)}, u32[]{:S(2)}) %collective-permute-start.1) | collective-permute-done | bytes 262176 | tf_op jit(solution)/shard_map/ppermute | solution.py:553
  30.3 0.0 collective-permute-done.2.refs_3_
  30.3 1.9 %swap_ready.1 = (f32[4,64,256]{2,1,0:T(8,128)}, f32[4,64,256]{2,1,0:T(8,128)}) custom-call(s32[1]{0:T(128)} %bitcast.2.where, f32[128,512]{1,0:T(8,128)S(1)} %get-tuple-element.24.refs_0_, f32[128,512]{1,0:T(8,128)S(1)} %collective-permute-done.refs_1_, f32[128,512]{1,0:T(8,128)S(1)} %collective-permute-done.1.refs_2_, f32[128,512]{1,0:T(8,128)} %collective-permute-done.2.refs_3_), custom_call_target="tpu_custom_call" | custom-call | tf_op jit(solution)/shard_map/swap_ready/pallas_call | solution.py:554
  32.2 0.0 copy-done.15
  32.2 1.1 collective-permute-start.5
  33.2 0.0 collective-permute-done.4.refs_8_
  33.2 7.1 %collective-permute-done.3.refs_7_ = f32[8,256]{1,0:T(8,128)S(1)} collective-permute-done((f32[8,256]{1,0:T(8,128)S(1)}, f32[8,256]{1,0:T(8,128)S(1)}, u32[]{:S(2)}, u32[]{:S(2)}) %collective-permute-start.3) | collective-permute-done | bytes 8224 | tf_op jit(solution)/shard_map/ppermute | solution.py:490
  40.3 0.5 all-to-all-done.cols_in
  40.8 0.0 copy-done.11
  40.8 1.0 collective-permute-start.6
  41.9 9.8 %columns.1.value = f32[16,264,128]{2,1,0:T(8,128)} custom-call(f32[16,256,128]{2,1,0:T(8,128)} %all-to-all-done.cols_in, bf16[3,16,128,128]{3,2,1,0:T(8,128)(2,1)} %get-tuple-element.35.data_in, f32[2,24,128]{2,1,0:T(8,128)} %constant.11.clone.twiddle_in.twiddle, bf16[768,256]{1,0:T(8,128)(2,1)} %get-tuple-element.36.forward_in, ...), custom_call_target="tpu_custom_call" | custom-call | tf_op jit(solution)/shard_map/columns/pallas_call | solution.py:578
  51.7 0.0 collective-permute-done.5.after_one.refs_4_
  51.7 0.0 copy-start.7
  51.7 0.0 collective-permute-done.6.after_two.refs_5_
  51.7 0.7 copy-done.7
  52.4 0.7 copy-done.9
  53.1 7.2 %all-to-all-start.1 = ((f32[16,264,128]{2,1,0:T(8,128)}), f32[16,264,128]{2,1,0:T(8,128)S(1)}, u32[]{:S(2)}, u32[]{:S(2)}) async-start(f32[16,264,128]{2,1,0:T(8,128)} %tied.1), calls=%async_computation.1 | async-start | bytes 4325376 | tf_op jit(solution)/shard_map/all_to_all | solution.py:605
  60.3 0.0 copy-start.10
  60.3 0.9 copy-done.10
  61.3 0.9 copy-done.12
  62.2 0.9 copy-done.14
  63.2 0.9 copy-done.16
  64.1 1.7 %tile_ready.1 = (f32[8,128,256]{2,1,0:T(8,128)S(1)}, f32[8,128,256]{2,1,0:T(8,128)S(1)}, f32[8,256]{1,0:T(8,128)S(1)}, f32[8,128]{1,0:T(8,128)S(1)}) custom-call(s32[1]{0:T(128)} %bitcast.2.where, f32[128,512]{1,0:T(8,128)S(1)} %copy-done.12, f32[128,512]{1,0:T(8,128)S(1)} %copy-done.14, f32[128,512]{1,0:T(8,128)S(1)} %copy-done.16, ...), custom_call_target="tpu_custom_call" | custom-call | tf_op jit(solution)/shard_map/tile_ready/pallas_call | solution.py:606
  65.9 1.0 copy-done.3
  66.9 1.0 copy-done.5
  67.8 4.6 %collective-permute-start.7 = (f32[8,256]{1,0:T(8,128)S(1)}, f32[8,256]{1,0:T(8,128)S(1)}, u32[]{:S(2)}, u32[]{:S(2)}) collective-permute-start(f32[8,256]{1,0:T(8,128)S(1)} %get-tuple-element.42), channel_id=1, source_target_pairs={{1,0},{2,1},{3,2},{4,3},{5,4},{6,5},{7,6},{8,7},{9,8},{10,9},{11,1... | collective-permute-start | bytes 24584 | tf_op jit(solution)/shard_map/ppermute | solution.py:490
  72.5 1.3 %collective-permute-start.8 = (f32[8,128]{1,0:T(8,128)S(1)}, f32[8,128]{1,0:T(8,128)S(1)}, u32[]{:S(2)}, u32[]{:S(2)}) collective-permute-start(f32[8,128]{1,0:T(8,128)S(1)} %get-tuple-element.43), channel_id=1, source_target_pairs={{16,0},{32,16},{48,32},{64,48},{80,64},{96,80},{112,96},{17,1},{33... | collective-permute-start | bytes 12296 | tf_op jit(solution)/shard_map/ppermute | solution.py:490
  73.8 4.6 %collective-permute-done.8.after_two.right = f32[8,128]{1,0:T(8,128)S(1)} collective-permute-done((f32[8,128]{1,0:T(8,128)S(1)}, f32[8,128]{1,0:T(8,128)S(1)}, u32[]{:S(2)}, u32[]{:S(2)}) %collective-permute-start.8) | collective-permute-done | bytes 4128 | tf_op jit(solution)/shard_map/ppermute | solution.py:490
  78.4 6.1 %collective-permute-done.7.after_one.below = f32[8,256]{1,0:T(8,128)S(1)} collective-permute-done((f32[8,256]{1,0:T(8,128)S(1)}, f32[8,256]{1,0:T(8,128)S(1)}, u32[]{:S(2)}, u32[]{:S(2)}) %collective-permute-start.7) | collective-permute-done | bytes 8224 | tf_op jit(solution)/shard_map/ppermute | solution.py:490
  84.4 4.2 %all-to-all-done.1.lines = f32[16,264,128]{2,1,0:T(8,128)S(1)} async-done(((f32[16,264,128]{2,1,0:T(8,128)}), f32[16,264,128]{2,1,0:T(8,128)S(1)}, u32[]{:S(2)}, u32[]{:S(2)}) %all-to-all-start.1) | async-done | bytes 2162720 | tf_op jit(solution)/shard_map/all_to_all | solution.py:605
  88.7 2.4 %rows_back.1 = f32[8,136,256]{2,1,0:T(8,128)S(1)} custom-call(f32[16,264,128]{2,1,0:T(8,128)S(1)} %all-to-all-done.1.lines, f32[2,24,128]{2,1,0:T(8,128)S(1)} %copy-done.17, f32[8,256]{1,0:T(8,128)S(1)} %collective-permute-done.7.after_one.below, f32[8,128]{1,0:T(8,128)S(1)} %collective-permute-done.8.after_two.right), custom_call_target="tpu_custom_call" | custom-call | tf_op jit(solution)/shard_map/rows_back/pallas_call | solution.py:620
  91.1 20.4 %all_to_all.15.gradient = f32[8,136,256]{2,1,0:T(8,128)S(1)} all-to-all(f32[8,136,256]{2,1,0:T(8,128)S(1)} %rows_back.1), channel_id=1, replica_groups=mesh['chan'=8,'facet'=16] {'chan'}, dimensions={0} | all-to-all | bytes 2228224 | tf_op jit(solution)/shard_map/all_to_all | solution.py:631
  111.5 2.4 %finish.1 = (f32[8,128,256]{2,1,0:T(8,128)}, bf16[8,2,128,256]{3,2,1,0:T(8,128)(2,1)}) custom-call(f32[8,136,256]{2,1,0:T(8,128)S(1)} %all_to_all.15.gradient, f32[8,128,256]{2,1,0:T(8,128)S(1)} %copy-done.4, f32[8,128,256]{2,1,0:T(8,128)S(1)} %copy-done.6, bf16[8,2,128,256]{3,2,1,0:T(8,128)(2,1)S(1)} %copy-done.1, ...), custom_call_target="tpu_custom_call" | custom-call | tf_op jit(solution)/shard_map/finish/pallas_call | solution.py:632
  (21 shorter events, 0.0 us)
Async XLA Ops:
  4.5 8.4 %copy-start.2 = (f32[1,128,2048]{2,1,0:T(8,128)S(1)}, f32[1,128,2048]{2,1,0:T(8,128)}, u32[]{:S(2)}) copy-start(f32[1,128,2048]{2,1,0:T(8,128)} %param.6) | copy-start | bytes 3145732
  4.6 15.0 %copy-start = (bf16[8,2,128,256]{3,2,1,0:T(8,128)(2,1)S(1)}, bf16[8,2,128,256]{3,2,1,0:T(8,128)(2,1)}, u32[]{:S(2)}) copy-start(bf16[8,2,128,256]{3,2,1,0:T(8,128)(2,1)} %dual.3) | copy-start | bytes 3145732
  4.6 36.3 %all-to-all-start = ((f32[16,256,128]{2,1,0:T(8,128)}), f32[16,256,128]{2,1,0:T(8,128)}, u32[]{:S(2)}, u32[]{:S(2)}) async-start(f32[16,256,128]{2,1,0:T(8,128)} %bitcast.7), calls=%async_computation | async-start | bytes 4194304 | tf_op jit(solution)/shard_map/all_to_all | solution.py:536
  13.9 26.9 %copy-start.11 = (f32[128,512]{1,0:T(8,128)}, f32[128,512]{1,0:T(8,128)S(1)}, u32[]{:S(2)}) copy-start(f32[128,512]{1,0:T(8,128)S(1)} %get-tuple-element.24.refs_0_) | copy-start | bytes 786436
  13.9 14.9 %collective-permute-start = (f32[128,512]{1,0:T(8,128)}, f32[128,512]{1,0:T(8,128)S(1)}, u32[]{:S(2)}, u32[]{:S(2)}) collective-permute-start(f32[128,512]{1,0:T(8,128)} %get-tuple-element.25), channel_id=1, source_target_pairs={{0,32},{16,48},{32,64},{48,80},{64,96},{80,112},{96,0},{112,16},{1... | collective-permute-start | bytes 786440 | tf_op jit(solution)/shard_map/ppermute | solution.py:553
  15.4 14.9 %collective-permute-start.1 = (f32[128,512]{1,0:T(8,128)}, f32[128,512]{1,0:T(8,128)S(1)}, u32[]{:S(2)}, u32[]{:S(2)}) collective-permute-start(f32[128,512]{1,0:T(8,128)} %get-tuple-element.26), channel_id=1, source_target_pairs={{0,64},{16,80},{32,96},{48,112},{64,0},{80,16},{96,32},{112,48},{1... | collective-permute-start | bytes 786440 | tf_op jit(solution)/shard_map/ppermute | solution.py:553
  18.1 12.2 %collective-permute-start.2 = (f32[128,512]{1,0:T(8,128)}, f32[128,512]{1,0:T(8,128)}, u32[]{:S(2)}, u32[]{:S(2)}) collective-permute-start(f32[128,512]{1,0:T(8,128)} %get-tuple-element.27), channel_id=1, source_target_pairs={{0,96},{16,112},{32,0},{48,16},{64,32},{80,48},{96,64},{112,80},{1... | collective-permute-start | bytes 786440 | tf_op jit(solution)/shard_map/ppermute | solution.py:553
  19.7 20.6 %collective-permute-start.3 = (f32[8,256]{1,0:T(8,128)S(1)}, f32[8,256]{1,0:T(8,128)S(1)}, u32[]{:S(2)}, u32[]{:S(2)}) collective-permute-start(f32[8,256]{1,0:T(8,128)S(1)} %get-tuple-element.29), channel_id=1, source_target_pairs={{0,1},{1,2},{2,3},{3,4},{4,5},{5,6},{6,7},{7,8},{8,9},{9,10},{10,1... | collective-permute-start | bytes 24584 | tf_op jit(solution)/shard_map/ppermute | solution.py:490
  21.7 11.5 %collective-permute-start.4 = (f32[8,128]{1,0:T(8,128)S(1)}, f32[8,128]{1,0:T(8,128)S(1)}, u32[]{:S(2)}, u32[]{:S(2)}) collective-permute-start(f32[8,128]{1,0:T(8,128)S(1)} %get-tuple-element.30), channel_id=1, source_target_pairs={{0,16},{16,32},{32,48},{48,64},{64,80},{80,96},{96,112},{1,17},{17... | collective-permute-start | bytes 12296 | tf_op jit(solution)/shard_map/ppermute | solution.py:490
  28.8 22.9 %copy-start.13 = (f32[128,512]{1,0:T(8,128)}, f32[128,512]{1,0:T(8,128)S(1)}, u32[]{:S(2)}) copy-start(f32[128,512]{1,0:T(8,128)S(1)} %collective-permute-done.refs_1_) | copy-start | bytes 786436
  30.3 1.9 %copy-start.15 = (f32[128,512]{1,0:T(8,128)}, f32[128,512]{1,0:T(8,128)S(1)}, u32[]{:S(2)}) copy-start(f32[128,512]{1,0:T(8,128)S(1)} %collective-permute-done.1.refs_2_) | copy-start | bytes 786436
  32.2 19.5 %collective-permute-start.5 = (f32[4,64,256]{2,1,0:T(8,128)}, f32[4,64,256]{2,1,0:T(8,128)S(1)}, u32[]{:S(2)}, u32[]{:S(2)}) collective-permute-start(f32[4,64,256]{2,1,0:T(8,128)} %get-tuple-element.38), channel_id=1, source_target_pairs={{0,16},{16,0},{32,48},{48,32},{64,80},{80,64},{96,112},{112,96},{1... | collective-permute-start | bytes 786440 | tf_op jit(solution)/shard_map/ppermute | solution.py:558
  40.8 10.9 %collective-permute-start.6 = (f32[4,64,256]{2,1,0:T(8,128)}, f32[4,64,256]{2,1,0:T(8,128)S(1)}, u32[]{:S(2)}, u32[]{:S(2)}) collective-permute-start(f32[4,64,256]{2,1,0:T(8,128)} %get-tuple-element.39), channel_id=1, source_target_pairs={{0,16},{16,0},{32,48},{48,32},{64,80},{80,64},{96,112},{112,96},{1... | collective-permute-start | bytes 786440 | tf_op jit(solution)/shard_map/ppermute | solution.py:574
  51.7 0.7 copy-start.7
  52.4 0.7 copy-start.9
  53.1 7.2 %copy-start.1 = (bf16[8,2,128,256]{3,2,1,0:T(8,128)(2,1)S(1)}, bf16[8,2,128,256]{3,2,1,0:T(8,128)(2,1)}, u32[]{:S(2)}) copy-start(bf16[8,2,128,256]{3,2,1,0:T(8,128)(2,1)} %dual.3) | copy-start | bytes 3145732
  53.1 7.2 %copy-start.8 = (f32[4,64,256]{2,1,0:T(8,128)S(1)}, f32[4,64,256]{2,1,0:T(8,128)}, u32[]{:S(2)}) copy-start(f32[4,64,256]{2,1,0:T(8,128)} %copy-done.7) | copy-start | bytes 786436
  53.1 35.5 %all-to-all-start.1 = ((f32[16,264,128]{2,1,0:T(8,128)}), f32[16,264,128]{2,1,0:T(8,128)S(1)}, u32[]{:S(2)}, u32[]{:S(2)}) async-start(f32[16,264,128]{2,1,0:T(8,128)} %tied.1), calls=%async_computation.1 | async-start | bytes 4325376 | tf_op jit(solution)/shard_map/all_to_all | solution.py:605
  60.3 1.0 copy-start.10
  61.3 0.9 copy-start.12
  62.2 0.9 copy-start.14
  63.2 0.9 copy-start.16
  64.1 24.5 %copy-start.17 = (f32[2,24,128]{2,1,0:T(8,128)S(1)}, f32[2,24,128]{2,1,0:T(8,128)}, u32[]{:S(2)}) copy-start(f32[2,24,128]{2,1,0:T(8,128)} %constant.11.clone.twiddle_in.twiddle) | copy-start | bytes 73732
  65.9 1.0 copy-start.3
  66.9 1.0 copy-start.5
  67.8 16.6 %collective-permute-start.7 = (f32[8,256]{1,0:T(8,128)S(1)}, f32[8,256]{1,0:T(8,128)S(1)}, u32[]{:S(2)}, u32[]{:S(2)}) collective-permute-start(f32[8,256]{1,0:T(8,128)S(1)} %get-tuple-element.42), channel_id=1, source_target_pairs={{1,0},{2,1},{3,2},{4,3},{5,4},{6,5},{7,6},{8,7},{9,8},{10,9},{11,1... | collective-permute-start | bytes 24584 | tf_op jit(solution)/shard_map/ppermute | solution.py:490
  72.5 5.9 %collective-permute-start.8 = (f32[8,128]{1,0:T(8,128)S(1)}, f32[8,128]{1,0:T(8,128)S(1)}, u32[]{:S(2)}, u32[]{:S(2)}) collective-permute-start(f32[8,128]{1,0:T(8,128)S(1)} %get-tuple-element.43), channel_id=1, source_target_pairs={{16,0},{32,16},{48,32},{64,48},{80,64},{96,80},{112,96},{17,1},{33... | collective-permute-start | bytes 12296 | tf_op jit(solution)/shard_map/ppermute | solution.py:490
  88.7 22.9 %copy-start.4 = (f32[8,128,256]{2,1,0:T(8,128)S(1)}, f32[8,128,256]{2,1,0:T(8,128)}, u32[]{:S(2)}) copy-start(f32[8,128,256]{2,1,0:T(8,128)} %copy-done.3) | copy-start | bytes 3145732
  88.7 22.9 %copy-start.6 = (f32[8,128,256]{2,1,0:T(8,128)S(1)}, f32[8,128,256]{2,1,0:T(8,128)}, u32[]{:S(2)}) copy-start(f32[8,128,256]{2,1,0:T(8,128)} %copy-done.5) | copy-start | bytes 3145732

commit v6 on v5

--- a/solution.py
+++ b/solution.py
@@ -229,28 +229,28 @@
 
 def columns(
     cols_in, data_in, twiddle_in, forward_in, inverse_in, out_all,
-    cols, data, twiddle, forward, inverse, out, held, in_sems, chunk_sems, out_sems,
+    cols, data, twiddle, forward, inverse, out, held_all, in_sems, chunk_sems, out_sems,
 ):
-    chunk = 32
+    chunk = 64
     steps = LANES // chunk
     dims = ((1,), (0,))
 
     def incoming_cols(step):
-        rows = pl.ds(pl.multiple_of(step * chunk, chunk), chunk)
-        imag_rows = pl.ds(pl.multiple_of(LANES + step * chunk, chunk), chunk)
+        rows = pl.ds(step * chunk, chunk)
+        imag_rows = pl.ds(LANES + step * chunk, chunk)
         return [
             pltpu.make_async_copy(cols_in.at[:, r, :], cols.at[:, r, :], chunk_sems.at[step, n])
             for n, r in enumerate((rows, imag_rows))
         ]
 
     def incoming(step):
-        rows = pl.ds(pl.multiple_of(step * chunk, chunk), chunk)
+        rows = pl.ds(step * chunk, chunk)
         return pltpu.make_async_copy(
             data_in.at[:, :, rows, :], data.at[:, :, rows, :], chunk_sems.at[step, 2]
         )
 
     def outgoing(step, c):
-        rows = pl.ds(pl.multiple_of(c * LANES + step * chunk, chunk), chunk)
+        rows = pl.ds(c * LANES + step * chunk, chunk)
         return pltpu.make_async_copy(
             out.at[:, rows, :], out_all.at[:, rows, :], out_sems.at[step, c]
         )
@@ -269,24 +269,22 @@
     lane_at = lax.broadcasted_iota(jnp.int32, (8, LANES), 1)
     get_twiddle.wait()
 
-    def body(step, carry):
-        at = pl.multiple_of(step * chunk, chunk)
+    for step in range(steps):
+        held = held_all.at[step % 2]
+        at = step * chunk
         here = pl.ds(at, chunk)
         for copy in incoming_cols(step):
             copy.wait()
-        imag_here = pl.ds(pl.multiple_of(LANES + at, chunk), chunk)
+        imag_here = pl.ds(LANES + at, chunk)
         mixed = sixteen([(cols[b, here, :], cols[b, imag_here, :]) for b in range(RADIX)], -1)
         for f in range(RADIX):
             real, imag = mixed[f]
             cos, sin = twiddle[0, f : f + 1, :], twiddle[1, f : f + 1, :]
             rows = slice(f * chunk, (f + 1) * chunk)
             store_pair(held, rows, real * cos + imag * sin, imag * cos - real * sin)
-
-        @pl.when(step == 0)
-        def _():
+        if step == 0:
             get_forward.wait()
             get_inverse.wait()
-
         spectrum = three_pass(held[...], forward, dims)
         incoming(step).wait()
         for f in range(RADIX):
@@ -315,9 +313,6 @@
                     out[b - 1, 2 * LANES :, :] = edge
         for c in range(2):
             outgoing(step, c).start()
-        return carry
-
-    lax.fori_loop(0, steps, body, 0)
     rows = pl.ds(2 * LANES, 8)
     edges = fetched(out.at[:, rows, :], out_all.at[:, rows, :], in_sems.at[0])
     for step in range(steps):
@@ -587,10 +582,10 @@
             pltpu.VMEM((768, 256), bf16),
             pltpu.VMEM((768, 256), bf16),
             pltpu.VMEM((RADIX, 2 * LANES + 8, LANES), f32),
-            pltpu.VMEM((RADIX * 32, 512), bf16),
+            pltpu.VMEM((2, RADIX * 64, 512), bf16),
             DMA((3,)),
-            DMA((4, 3)),
-            DMA((4, 2)),
+            DMA((2, 3)),
+            DMA((2, 2)),
         ],
         63,
     )(cols, data, twiddle, forward, inverse)
@@ -601,7 +596,7 @@
         out_specs=ANY,
         input_output_aliases={0: 0},
         name="tied",
-    )(back, early, late)
+    )(back, early[0, :8, :LANES], late[0, :8, :LANES])
     lines = lax.all_to_all(back, "facet", split_axis=0, concat_axis=0, tiled=True)
     for_image, for_ahead, first_row, first_column = call(
         tile_ready,

time: 116 us -> 117 us (level)
  Pallas kernels: 27.4 us -> 22.9 us
  waiting for transfers between devices: 24 us -> 26.8 us
  local copies, waits for them, and re-layouts: 7.17 us -> 8.73 us
  starting transfers between devices: 34.1 us -> 35.6 us
    ppermute x3, waiting for transfers between devices: 1.5 us -> 10.5 us  [shards(): pieces[k] = lax.ppermute(pieces[k], 'chan', pairs)]
    ppermute x4, waiting for transfers between devices: 17.8 us -> 12.1 us  [passed_along(): return lax.ppermute(x, axis, pairs)]
    pallas_call x1, Pallas kernels: 9.8 us -> 8.09 us  [shards(): call(columns, shape((RADIX, 2 * LANES + 8, LANES)), [HBM] * 5, HBM, [pltp...]
    ppermute x1, starting transfers between devices: 1.02 us -> 2.42 us  [shards(): late = lax.ppermute(late, 'chan', other_zl)]
    squeeze x0 -> x2, local copies, waits for them, and re-layouts: none -> 1.24 us  [the longest x1 0.63 us: shards(): late[0, :8, :LANES]]
    unnamed x36 -> x38, local copies, waits for them, and re-layouts: 7.17 us -> 7.49 us
  transfers between devices with their start and end apart: 11 -> 11, of which waited for: 6 -> 6; matrix products, arithmetic and copies ran while one was open for 0% -> 1% of each run, Pallas kernels for 16% -> 12%
where the time goes in v6:
time: 117 us; the launch traced here: 115 us
  starting transfers between devices  35.6 us (30%)
  waiting for transfers between devices  26.8 us (23%)
  Pallas kernels  22.9 us (20%)
  blocking collectives  20.4 us (17%)
  local copies, waits for them, and re-layouts  8.73 us (7%)
    all_to_all x1, blocking collectives, shards(): lax.all_to_all(slopes, 'chan', split_axis=0, concat_axis=0, tiled=True)  20.4 us
    ppermute x4, waiting for transfers between devices, passed_along(): return lax.ppermute(x, axis, pairs)  12.1 us
    ppermute x4, starting transfers between devices, passed_along(): return lax.ppermute(x, axis, pairs)  10.7 us
    ppermute x3, waiting for transfers between devices, shards(): pieces[k] = lax.ppermute(pieces[k], 'chan', pairs)  10.5 us
    all_to_all x1, starting transfers between devices, shards(): lax.all_to_all(spread.reshape(RADIX, 2 * LANES, LANES), 'facet', split_ax...  8.39 us
    pallas_call x1, Pallas kernels, shards(): call(columns, shape((RADIX, 2 * LANES + 8, LANES)), [HBM] * 5, HBM, [pltp...  8.09 us
    unnamed x38, local copies, waits for them, and re-layouts  7.49 us
    all_to_all x1, starting transfers between devices, shards(): lax.all_to_all(back, 'facet', split_axis=0, concat_axis=0, tiled=True)  7.32 us
  transfers between devices with their start and end apart: 11, of which 6 were waited for; matrix products, arithmetic and copies ran while one was open for 1% of the time, Pallas kernels for 12%

profile of v6, /device:TPU:8, one launch (start us, length us, event | category | flops | bytes accessed | tf_op | source)
XLA Modules:
  0.0 115.3 jit_solution(3895522200920854285)
XLA Ops:
  0.6 3.9 %rows_forward.1 = f32[16,2,16,8,128]{4,3,2,1,0:T(8,128)} custom-call(f32[128,2048]{1,0:T(8,128)} %bitcast.9, f32[2,24,128]{2,1,0:T(8,128)} %constant.11.clone.twiddle_in.twiddle), custom_call_target="tpu_custom_call" | custom-call | tf_op jit(solution)/shard_map/rows_forward/pallas_call | solution.py:515
  4.5 0.0 copy-start.2
  4.6 8.4 %all-to-all-start = ((f32[16,256,128]{2,1,0:T(8,128)}), f32[16,256,128]{2,1,0:T(8,128)}, u32[]{:S(2)}, u32[]{:S(2)}) async-start(f32[16,256,128]{2,1,0:T(8,128)} %bitcast.11), calls=%async_computation | async-start | bytes 4194304 | tf_op jit(solution)/shard_map/all_to_all | solution.py:531
  13.0 0.1 cross_ready.1
  13.1 1.6 %collective-permute-start = (f32[128,512]{1,0:T(8,128)S(1)}, f32[128,512]{1,0:T(8,128)S(1)}, u32[]{:S(2)}, u32[]{:S(2)}) collective-permute-start(f32[128,512]{1,0:T(8,128)S(1)} %get-tuple-element.25), channel_id=1, source_target_pairs={{0,32},{16,48},{32,64},{48,80},{64,96},{80,112},{96,0},{112,16},{1... | collective-permute-start | bytes 786440 | tf_op jit(solution)/shard_map/ppermute | solution.py:548
  14.6 2.7 %collective-permute-start.1 = (f32[128,512]{1,0:T(8,128)S(1)}, f32[128,512]{1,0:T(8,128)S(1)}, u32[]{:S(2)}, u32[]{:S(2)}) collective-permute-start(f32[128,512]{1,0:T(8,128)S(1)} %get-tuple-element.26), channel_id=1, source_target_pairs={{0,64},{16,80},{32,96},{48,112},{64,0},{80,16},{96,32},{112,48},{1... | collective-permute-start | bytes 786440 | tf_op jit(solution)/shard_map/ppermute | solution.py:548
  17.4 1.4 %collective-permute-start.2 = (f32[128,512]{1,0:T(8,128)S(1)}, f32[128,512]{1,0:T(8,128)S(1)}, u32[]{:S(2)}, u32[]{:S(2)}) collective-permute-start(f32[128,512]{1,0:T(8,128)S(1)} %get-tuple-element.27), channel_id=1, source_target_pairs={{0,96},{16,112},{32,0},{48,16},{64,32},{80,48},{96,64},{112,80},{1... | collective-permute-start | bytes 786440 | tf_op jit(solution)/shard_map/ppermute | solution.py:548
  18.8 3.9 %collective-permute-done.refs_1_ = f32[128,512]{1,0:T(8,128)S(1)} collective-permute-done((f32[128,512]{1,0:T(8,128)S(1)}, f32[128,512]{1,0:T(8,128)S(1)}, u32[]{:S(2)}, u32[]{:S(2)}) %collective-permute-start) | collective-permute-done | bytes 262176 | tf_op jit(solution)/shard_map/ppermute | solution.py:548
  22.7 6.6 %collective-permute-done.1.refs_2_ = f32[128,512]{1,0:T(8,128)S(1)} collective-permute-done((f32[128,512]{1,0:T(8,128)S(1)}, f32[128,512]{1,0:T(8,128)S(1)}, u32[]{:S(2)}, u32[]{:S(2)}) %collective-permute-start.1) | collective-permute-done | bytes 262176 | tf_op jit(solution)/shard_map/ppermute | solution.py:548
  29.3 0.0 collective-permute-done.2.refs_3_
  29.3 0.8 swap_ready.1
  30.1 0.7 copy-done.18
  30.8 1.0 collective-permute-start.5
  31.8 0.0 copy-done
  31.8 0.2 dual_edges.1
  32.0 0.0 copy-done.9
  32.0 1.9 %collective-permute-start.3 = (f32[8,256]{1,0:T(8,128)S(1)}, f32[8,256]{1,0:T(8,128)S(1)}, u32[]{:S(2)}, u32[]{:S(2)}) collective-permute-start(f32[8,256]{1,0:T(8,128)S(1)} %get-tuple-element.29), channel_id=1, source_target_pairs={{0,1},{1,2},{2,3},{3,4},{4,5},{5,6},{6,7},{7,8},{8,9},{9,10},{10,1... | collective-permute-start | bytes 24584 | tf_op jit(solution)/shard_map/ppermute | solution.py:485
  34.0 0.0 copy-done.11
  34.0 2.9 %collective-permute-start.4 = (f32[8,128]{1,0:T(8,128)S(1)}, f32[8,128]{1,0:T(8,128)S(1)}, u32[]{:S(2)}, u32[]{:S(2)}) collective-permute-start(f32[8,128]{1,0:T(8,128)S(1)} %get-tuple-element.30), channel_id=1, source_target_pairs={{0,16},{16,32},{32,48},{48,64},{64,80},{80,96},{96,112},{1,17},{17... | collective-permute-start | bytes 12296 | tf_op jit(solution)/shard_map/ppermute | solution.py:485
  36.9 4.2 %data_prepared.1 = (bf16[3,16,128,128]{3,2,1,0:T(8,128)(2,1)}, bf16[768,256]{1,0:T(8,128)(2,1)}, bf16[768,256]{1,0:T(8,128)(2,1)}) custom-call(bf16[2048,128]{1,0:T(8,128)(2,1)} %bitcast.13, bf16[2,2048,128]{2,1,0:T(8,128)(2,1)} %bitcast.12, bf16[128,128]{1,0:T(8,128)(2,1)} %constant.10.clone.place, f32[2,24,128]{2,1,0:T(8,128)} %constant.11.clone.twiddle_in.twiddle), custom_call_target="tpu_custom_call" | custom-call | tf_op jit(solution)/shard_map/data_prepared/pallas_call | solution.py:554
  41.1 1.4 %collective-permute-done.4.refs_8_ = f32[8,128]{1,0:T(8,128)S(1)} collective-permute-done((f32[8,128]{1,0:T(8,128)S(1)}, f32[8,128]{1,0:T(8,128)S(1)}, u32[]{:S(2)}, u32[]{:S(2)}) %collective-permute-start.4) | collective-permute-done | bytes 4128 | tf_op jit(solution)/shard_map/ppermute | solution.py:485
  42.5 0.0 collective-permute-done.3.refs_7_
  42.5 0.0 all-to-all-done.cols_in
  42.5 2.4 %collective-permute-start.6 = (f32[4,64,256]{2,1,0:T(8,128)}, f32[4,64,256]{2,1,0:T(8,128)S(1)}, u32[]{:S(2)}, u32[]{:S(2)}) collective-permute-start(f32[4,64,256]{2,1,0:T(8,128)} %copy-done.18), channel_id=1, source_target_pairs={{0,16},{16,0},{32,48},{48,32},{64,80},{80,64},{96,112},{112,96},{1... | collective-permute-start | bytes 786440 | tf_op jit(solution)/shard_map/ppermute | solution.py:569
  44.9 0.0 collective-permute-done.5.refs_4_
  44.9 0.6 slice_bitcast_fusion.1.after_one
  45.5 8.1 %columns.1.value = f32[16,264,128]{2,1,0:T(8,128)} custom-call(f32[16,256,128]{2,1,0:T(8,128)} %all-to-all-done.cols_in, bf16[3,16,128,128]{3,2,1,0:T(8,128)(2,1)} %get-tuple-element.35.data_in, f32[2,24,128]{2,1,0:T(8,128)} %constant.11.clone.twiddle_in.twiddle, bf16[768,256]{1,0:T(8,128)(2,1)} %get-tuple-element.36.forward_in, ...), custom_call_target="tpu_custom_call" | custom-call | tf_op jit(solution)/shard_map/columns/pallas_call | solution.py:573
  53.6 0.0 collective-permute-done.6.refs_5_
  53.6 0.0 copy-start.16
  53.7 0.6 slice_bitcast_fusion.after_two
  54.3 0.1 copy-done.16
  54.4 7.3 %all-to-all-start.1 = ((f32[16,264,128]{2,1,0:T(8,128)}), f32[16,264,128]{2,1,0:T(8,128)S(1)}, u32[]{:S(2)}, u32[]{:S(2)}) async-start(f32[16,264,128]{2,1,0:T(8,128)} %tied.1), calls=%async_computation.1 | async-start | bytes 4325376 | tf_op jit(solution)/shard_map/all_to_all | solution.py:600
  61.7 0.9 copy-done.8
  62.6 0.9 copy-done.10
  63.6 0.9 copy-done.12
  64.5 0.9 copy-done.15
  65.5 0.9 copy-done.17
  66.4 0.8 tile_ready.1
  67.2 1.0 copy-done.3
  68.2 1.0 copy-done.5
  69.2 4.6 %collective-permute-start.7 = (f32[8,256]{1,0:T(8,128)S(1)}, f32[8,256]{1,0:T(8,128)S(1)}, u32[]{:S(2)}, u32[]{:S(2)}) collective-permute-start(f32[8,256]{1,0:T(8,128)S(1)} %get-tuple-element.42), channel_id=1, source_target_pairs={{1,0},{2,1},{3,2},{4,3},{5,4},{6,5},{7,6},{8,7},{9,8},{10,9},{11,1... | collective-permute-start | bytes 24584 | tf_op jit(solution)/shard_map/ppermute | solution.py:485
  73.8 1.3 %collective-permute-start.8 = (f32[8,128]{1,0:T(8,128)S(1)}, f32[8,128]{1,0:T(8,128)S(1)}, u32[]{:S(2)}, u32[]{:S(2)}) collective-permute-start(f32[8,128]{1,0:T(8,128)S(1)} %get-tuple-element.43), channel_id=1, source_target_pairs={{16,0},{32,16},{48,32},{64,48},{80,64},{96,80},{112,96},{17,1},{33... | collective-permute-start | bytes 12296 | tf_op jit(solution)/shard_map/ppermute | solution.py:485
  75.1 4.6 %collective-permute-done.8.after_two.right = f32[8,128]{1,0:T(8,128)S(1)} collective-permute-done((f32[8,128]{1,0:T(8,128)S(1)}, f32[8,128]{1,0:T(8,128)S(1)}, u32[]{:S(2)}, u32[]{:S(2)}) %collective-permute-start.8) | collective-permute-done | bytes 4128 | tf_op jit(solution)/shard_map/ppermute | solution.py:485
  79.7 6.1 %collective-permute-done.7.after_one.below = f32[8,256]{1,0:T(8,128)S(1)} collective-permute-done((f32[8,256]{1,0:T(8,128)S(1)}, f32[8,256]{1,0:T(8,128)S(1)}, u32[]{:S(2)}, u32[]{:S(2)}) %collective-permute-start.7) | collective-permute-done | bytes 8224 | tf_op jit(solution)/shard_map/ppermute | solution.py:485
  85.8 4.2 %all-to-all-done.1.lines = f32[16,264,128]{2,1,0:T(8,128)S(1)} async-done(((f32[16,264,128]{2,1,0:T(8,128)}), f32[16,264,128]{2,1,0:T(8,128)S(1)}, u32[]{:S(2)}, u32[]{:S(2)}) %all-to-all-start.1) | async-done | bytes 2162720 | tf_op jit(solution)/shard_map/all_to_all | solution.py:600
  90.0 2.4 %rows_back.1 = f32[8,136,256]{2,1,0:T(8,128)S(1)} custom-call(f32[16,264,128]{2,1,0:T(8,128)S(1)} %all-to-all-done.1.lines, f32[2,24,128]{2,1,0:T(8,128)S(1)} %copy-done.13, f32[8,256]{1,0:T(8,128)S(1)} %collective-permute-done.7.after_one.below, f32[8,128]{1,0:T(8,128)S(1)} %collective-permute-done.8.after_two.right), custom_call_target="tpu_custom_call" | custom-call | tf_op jit(solution)/shard_map/rows_back/pallas_call | solution.py:615
  92.5 20.4 %all_to_all.15.gradient = f32[8,136,256]{2,1,0:T(8,128)S(1)} all-to-all(f32[8,136,256]{2,1,0:T(8,128)S(1)} %rows_back.1), channel_id=1, replica_groups=mesh['chan'=8,'facet'=16] {'chan'}, dimensions={0} | all-to-all | bytes 2228224 | tf_op jit(solution)/shard_map/all_to_all | solution.py:626
  112.9 2.4 %finish.1 = (f32[8,128,256]{2,1,0:T(8,128)}, bf16[8,2,128,256]{3,2,1,0:T(8,128)(2,1)}) custom-call(f32[8,136,256]{2,1,0:T(8,128)S(1)} %all_to_all.15.gradient, f32[8,128,256]{2,1,0:T(8,128)S(1)} %copy-done.4, f32[8,128,256]{2,1,0:T(8,128)S(1)} %copy-done.6, bf16[8,2,128,256]{3,2,1,0:T(8,128)(2,1)S(1)} %copy-done.1, ...), custom_call_target="tpu_custom_call" | custom-call | tf_op jit(solution)/shard_map/finish/pallas_call | solution.py:627
  (25 shorter events, 0.0 us)
Async XLA Ops:
  4.5 8.4 %copy-start.2 = (f32[1,128,2048]{2,1,0:T(8,128)S(1)}, f32[1,128,2048]{2,1,0:T(8,128)}, u32[]{:S(2)}) copy-start(f32[1,128,2048]{2,1,0:T(8,128)} %param.6) | copy-start | bytes 3145732
  4.6 37.9 %all-to-all-start = ((f32[16,256,128]{2,1,0:T(8,128)}), f32[16,256,128]{2,1,0:T(8,128)}, u32[]{:S(2)}, u32[]{:S(2)}) async-start(f32[16,256,128]{2,1,0:T(8,128)} %bitcast.11), calls=%async_computation | async-start | bytes 4194304 | tf_op jit(solution)/shard_map/all_to_all | solution.py:531
  12.9 18.9 %copy-start = (bf16[8,2,128,256]{3,2,1,0:T(8,128)(2,1)S(1)}, bf16[8,2,128,256]{3,2,1,0:T(8,128)(2,1)}, u32[]{:S(2)}) copy-start(bf16[8,2,128,256]{3,2,1,0:T(8,128)(2,1)} %dual.3) | copy-start | bytes 3145732
  13.1 9.6 %collective-permute-start = (f32[128,512]{1,0:T(8,128)S(1)}, f32[128,512]{1,0:T(8,128)S(1)}, u32[]{:S(2)}, u32[]{:S(2)}) collective-permute-start(f32[128,512]{1,0:T(8,128)S(1)} %get-tuple-element.25), channel_id=1, source_target_pairs={{0,32},{16,48},{32,64},{48,80},{64,96},{80,112},{96,0},{112,16},{1... | collective-permute-start | bytes 786440 | tf_op jit(solution)/shard_map/ppermute | solution.py:548
  14.6 14.7 %collective-permute-start.1 = (f32[128,512]{1,0:T(8,128)S(1)}, f32[128,512]{1,0:T(8,128)S(1)}, u32[]{:S(2)}, u32[]{:S(2)}) collective-permute-start(f32[128,512]{1,0:T(8,128)S(1)} %get-tuple-element.26), channel_id=1, source_target_pairs={{0,64},{16,80},{32,96},{48,112},{64,0},{80,16},{96,32},{112,48},{1... | collective-permute-start | bytes 786440 | tf_op jit(solution)/shard_map/ppermute | solution.py:548
  17.4 12.0 %collective-permute-start.2 = (f32[128,512]{1,0:T(8,128)S(1)}, f32[128,512]{1,0:T(8,128)S(1)}, u32[]{:S(2)}, u32[]{:S(2)}) collective-permute-start(f32[128,512]{1,0:T(8,128)S(1)} %get-tuple-element.27), channel_id=1, source_target_pairs={{0,96},{16,112},{32,0},{48,16},{64,32},{80,48},{96,64},{112,80},{1... | collective-permute-start | bytes 786440 | tf_op jit(solution)/shard_map/ppermute | solution.py:548
  22.7 9.3 %copy-start.7 = (f32[128,512]{1,0:T(8,128)}, f32[128,512]{1,0:T(8,128)S(1)}, u32[]{:S(2)}) copy-start(f32[128,512]{1,0:T(8,128)S(1)} %collective-permute-done.refs_1_) | copy-start | bytes 786436
  29.3 2.7 %copy-start.9 = (f32[128,512]{1,0:T(8,128)}, f32[128,512]{1,0:T(8,128)S(1)}, u32[]{:S(2)}) copy-start(f32[128,512]{1,0:T(8,128)S(1)} %collective-permute-done.1.refs_2_) | copy-start | bytes 786436
  29.3 4.6 %copy-start.11 = (f32[128,512]{1,0:T(8,128)}, f32[128,512]{1,0:T(8,128)S(1)}, u32[]{:S(2)}) copy-start(f32[128,512]{1,0:T(8,128)S(1)} %collective-permute-done.2.refs_3_) | copy-start | bytes 786436
  30.1 0.7 copy-start.18
  30.8 14.1 %collective-permute-start.5 = (f32[4,64,256]{2,1,0:T(8,128)}, f32[4,64,256]{2,1,0:T(8,128)S(1)}, u32[]{:S(2)}, u32[]{:S(2)}) collective-permute-start(f32[4,64,256]{2,1,0:T(8,128)} %get-tuple-element.38), channel_id=1, source_target_pairs={{0,16},{16,0},{32,48},{48,32},{64,80},{80,64},{96,112},{112,96},{1... | collective-permute-start | bytes 786440 | tf_op jit(solution)/shard_map/ppermute | solution.py:553
  32.0 10.5 %collective-permute-start.3 = (f32[8,256]{1,0:T(8,128)S(1)}, f32[8,256]{1,0:T(8,128)S(1)}, u32[]{:S(2)}, u32[]{:S(2)}) collective-permute-start(f32[8,256]{1,0:T(8,128)S(1)} %get-tuple-element.29), channel_id=1, source_target_pairs={{0,1},{1,2},{2,3},{3,4},{4,5},{5,6},{6,7},{7,8},{8,9},{9,10},{10,1... | collective-permute-start | bytes 24584 | tf_op jit(solution)/shard_map/ppermute | solution.py:485
  34.0 8.5 %collective-permute-start.4 = (f32[8,128]{1,0:T(8,128)S(1)}, f32[8,128]{1,0:T(8,128)S(1)}, u32[]{:S(2)}, u32[]{:S(2)}) collective-permute-start(f32[8,128]{1,0:T(8,128)S(1)} %get-tuple-element.30), channel_id=1, source_target_pairs={{0,16},{16,32},{32,48},{48,64},{64,80},{80,96},{96,112},{1,17},{17... | collective-permute-start | bytes 12296 | tf_op jit(solution)/shard_map/ppermute | solution.py:485
  42.5 11.1 %collective-permute-start.6 = (f32[4,64,256]{2,1,0:T(8,128)}, f32[4,64,256]{2,1,0:T(8,128)S(1)}, u32[]{:S(2)}, u32[]{:S(2)}) collective-permute-start(f32[4,64,256]{2,1,0:T(8,128)} %copy-done.18), channel_id=1, source_target_pairs={{0,16},{16,0},{32,48},{48,32},{64,80},{80,64},{96,112},{112,96},{1... | collective-permute-start | bytes 786440 | tf_op jit(solution)/shard_map/ppermute | solution.py:569
  44.9 8.7 %copy-start.14 = (f32[4,64,256]{2,1,0:T(8,128)}, f32[4,64,256]{2,1,0:T(8,128)S(1)}, u32[]{:S(2)}) copy-start(f32[4,64,256]{2,1,0:T(8,128)S(1)} %collective-permute-done.5.refs_4_) | copy-start | bytes 786436
  53.6 0.7 copy-start.16
  54.4 7.3 %copy-start.1 = (bf16[8,2,128,256]{3,2,1,0:T(8,128)(2,1)S(1)}, bf16[8,2,128,256]{3,2,1,0:T(8,128)(2,1)}, u32[]{:S(2)}) copy-start(bf16[8,2,128,256]{3,2,1,0:T(8,128)(2,1)} %dual.3) | copy-start | bytes 3145732
  54.4 35.7 %all-to-all-start.1 = ((f32[16,264,128]{2,1,0:T(8,128)}), f32[16,264,128]{2,1,0:T(8,128)S(1)}, u32[]{:S(2)}, u32[]{:S(2)}) async-start(f32[16,264,128]{2,1,0:T(8,128)} %tied.1), calls=%async_computation.1 | async-start | bytes 4325376 | tf_op jit(solution)/shard_map/all_to_all | solution.py:600
  61.7 1.0 copy-start.8
  62.6 0.9 copy-start.10
  63.6 0.9 copy-start.12
  64.5 0.9 copy-start.15
  65.5 0.9 copy-start.17
  66.4 23.6 %copy-start.13 = (f32[2,24,128]{2,1,0:T(8,128)S(1)}, f32[2,24,128]{2,1,0:T(8,128)}, u32[]{:S(2)}) copy-start(f32[2,24,128]{2,1,0:T(8,128)} %constant.11.clone.twiddle_in.twiddle) | copy-start | bytes 73732
  67.2 1.0 copy-start.3
  68.2 1.0 copy-start.5
  69.2 16.6 %collective-permute-start.7 = (f32[8,256]{1,0:T(8,128)S(1)}, f32[8,256]{1,0:T(8,128)S(1)}, u32[]{:S(2)}, u32[]{:S(2)}) collective-permute-start(f32[8,256]{1,0:T(8,128)S(1)} %get-tuple-element.42), channel_id=1, source_target_pairs={{1,0},{2,1},{3,2},{4,3},{5,4},{6,5},{7,6},{8,7},{9,8},{10,9},{11,1... | collective-permute-start | bytes 24584 | tf_op jit(solution)/shard_map/ppermute | solution.py:485
  73.8 5.9 %collective-permute-start.8 = (f32[8,128]{1,0:T(8,128)S(1)}, f32[8,128]{1,0:T(8,128)S(1)}, u32[]{:S(2)}, u32[]{:S(2)}) collective-permute-start(f32[8,128]{1,0:T(8,128)S(1)} %get-tuple-element.43), channel_id=1, source_target_pairs={{16,0},{32,16},{48,32},{64,48},{80,64},{96,80},{112,96},{17,1},{33... | collective-permute-start | bytes 12296 | tf_op jit(solution)/shard_map/ppermute | solution.py:485
  90.0 22.9 %copy-start.4 = (f32[8,128,256]{2,1,0:T(8,128)S(1)}, f32[8,128,256]{2,1,0:T(8,128)}, u32[]{:S(2)}) copy-start(f32[8,128,256]{2,1,0:T(8,128)} %copy-done.3) | copy-start | bytes 3145732
  90.0 22.9 %copy-start.6 = (f32[8,128,256]{2,1,0:T(8,128)S(1)}, f32[8,128,256]{2,1,0:T(8,128)}, u32[]{:S(2)}) copy-start(f32[8,128,256]{2,1,0:T(8,128)} %copy-done.5) | copy-start | bytes 3145732

commit v7 on v6

--- a/solution.py
+++ b/solution.py
@@ -156,7 +156,7 @@
 
 
 def swap_ready(where, *refs):
-    pieces, early, late = refs[:4], refs[4], refs[5]
+    pieces, early, late = refs[:4], refs[-2], refs[-1]
     lanes = pl.ds(pl.multiple_of((1 - where[0] % 2) * 256, 256), 256)
     for k in range(4):
         early[k] = pieces[k][: LANES // 2, lanes]
@@ -321,7 +321,7 @@
     edges.wait()
 
 
-def tied(value, after_one, after_two, out):
+def tied(value, after, out):
     pass
 
 
@@ -546,11 +546,6 @@
     for k in range(1, 4):
         pairs = [(2 * x + z, (x + k) % 4 * 2 + z) for x in range(4) for z in range(2)]
         pieces[k] = lax.ppermute(pieces[k], "chan", pairs)
-    early, late = call(
-        swap_ready, (shape((4, LANES // 2, 256)),) * 2, [SM] + [VM] * 4, (VM, VM), []
-    )(where, *pieces)
-    other_zl = [(i, i ^ 1) for i in range(8)]
-    early = lax.ppermute(early, "chan", other_zl)
     data, forward, inverse = call(
         data_prepared,
         (
@@ -563,6 +558,15 @@
         [pltpu.VMEM((GRID, LANES), f32)],
         63,
     )(weights[0], measured[0], place, twiddle)
+    early, late = call(
+        swap_ready,
+        (shape((4, LANES // 2, 256)),) * 2,
+        [SM] + [VM] * 4 + [ANY] * 2,
+        (VM, VM),
+        [],
+    )(where, *pieces, data, last_row)
+    other_zl = [(i, i ^ 1) for i in range(8)]
+    early = lax.ppermute(early, "chan", other_zl)
     cols, late, above, left, data, forward, inverse = lax.optimization_barrier(
         (cols, late, above, left, data, forward, inverse)
     )
@@ -592,11 +596,11 @@
     back = pl.pallas_call(
         tied,
         out_shape=shape((RADIX, 2 * LANES + 8, LANES)),
-        in_specs=[ANY] * 3,
+        in_specs=[ANY] * 2,
         out_specs=ANY,
         input_output_aliases={0: 0},
         name="tied",
-    )(back, early[0, :8, :LANES], late[0, :8, :LANES])
+    )(back, early[0, :8, :LANES] + late[0, :8, :LANES])
     lines = lax.all_to_all(back, "facet", split_axis=0, concat_axis=0, tiled=True)
     for_image, for_ahead, first_row, first_column = call(
         tile_ready,

time: 117 us -> 115 us (0.983)
  local copies, waits for them, and re-layouts: 8.73 us -> 5.38 us
  Pallas kernels: 22.9 us -> 25.9 us
  waiting for transfers between devices: 26.8 us -> 24.4 us
  starting transfers between devices: 35.6 us -> 34.3 us
  other arithmetic: 0 us -> 1.28 us
    ppermute x3, waiting for transfers between devices: 10.5 us -> 1.52 us  [shards(): pieces[k] = lax.ppermute(pieces[k], 'chan', pairs)]
    ppermute x4, waiting for transfers between devices: 12.1 us -> 18.2 us  [passed_along(): return lax.ppermute(x, axis, pairs)]
    unnamed x38 -> x26, local copies, waits for them, and re-layouts: 7.49 us -> 5.38 us
    ppermute x1, starting transfers between devices: 2.42 us -> 1.02 us  [shards(): late = lax.ppermute(late, 'chan', other_zl)]
    add x0 -> x1, other arithmetic: none -> 1.28 us  [shards(): early[0, :8, :LANES] + late[0, :8, :LANES]]
    squeeze x2 -> x0, local copies, waits for them, and re-layouts: 1.24 us -> none  [the longest x1 0.63 us: shards(): late[0, :8, :LANES]]
  transfers between devices with their start and end apart: 11 -> 11, of which waited for: 6 -> 6; matrix products, arithmetic and copies ran while one was open for 1% -> 0% of each run, Pallas kernels for 12% -> 15%
where the time goes in v7:
time: 115 us; the launch traced here: 112 us
  starting transfers between devices  34.3 us (30%)
  Pallas kernels  25.9 us (23%)
  waiting for transfers between devices  24.4 us (21%)
  blocking collectives  20.5 us (18%)
  local copies, waits for them, and re-layouts  5.38 us (5%)
  other arithmetic  1.28 us (1%)
    all_to_all x1, blocking collectives, shards(): lax.all_to_all(slopes, 'chan', split_axis=0, concat_axis=0, tiled=True)  20.5 us
    ppermute x4, waiting for transfers between devices, passed_along(): return lax.ppermute(x, axis, pairs)  18.2 us
    ppermute x4, starting transfers between devices, passed_along(): return lax.ppermute(x, axis, pairs)  10.7 us
    all_to_all x1, starting transfers between devices, shards(): lax.all_to_all(spread.reshape(RADIX, 2 * LANES, LANES), 'facet', split_ax...  8.39 us
    pallas_call x1, Pallas kernels, shards(): call(columns, shape((RADIX, 2 * LANES + 8, LANES)), [HBM] * 5, HBM, [pltp...  8.08 us
    all_to_all x1, starting transfers between devices, shards(): lax.all_to_all(back, 'facet', split_axis=0, concat_axis=0, tiled=True)  7.41 us
    ppermute x3, starting transfers between devices, shards(): pieces[k] = lax.ppermute(pieces[k], 'chan', pairs)  5.66 us
    unnamed x26, local copies, waits for them, and re-layouts  5.38 us
  transfers between devices with their start and end apart: 11, of which 6 were waited for; matrix products, arithmetic and copies ran while one was open for 0% of the time, Pallas kernels for 15%

profile of v7, /device:TPU:8, one launch (start us, length us, event | category | flops | bytes accessed | tf_op | source)
XLA Modules:
  0.0 112.5 jit_solution(12635555118603584940)
XLA Ops:
  0.6 3.9 %rows_forward.1 = f32[16,2,16,8,128]{4,3,2,1,0:T(8,128)} custom-call(f32[128,2048]{1,0:T(8,128)} %bitcast.7, f32[2,24,128]{2,1,0:T(8,128)} %constant.11.clone.twiddle_in.twiddle), custom_call_target="tpu_custom_call" | custom-call | tf_op jit(solution)/shard_map/rows_forward/pallas_call | solution.py:515
  4.6 0.0 copy-start.3
  4.6 0.0 copy-start
  4.6 8.4 %all-to-all-start = ((f32[16,256,128]{2,1,0:T(8,128)}), f32[16,256,128]{2,1,0:T(8,128)}, u32[]{:S(2)}, u32[]{:S(2)}) async-start(f32[16,256,128]{2,1,0:T(8,128)} %bitcast.9), calls=%async_computation | async-start | bytes 4194304 | tf_op jit(solution)/shard_map/all_to_all | solution.py:531
  13.0 0.0 copy-done.3
  13.0 1.0 cross_ready.1
  14.0 1.5 %collective-permute-start = (f32[128,512]{1,0:T(8,128)}, f32[128,512]{1,0:T(8,128)S(1)}, u32[]{:S(2)}, u32[]{:S(2)}) collective-permute-start(f32[128,512]{1,0:T(8,128)} %get-tuple-element.25), channel_id=1, source_target_pairs={{0,32},{16,48},{32,64},{48,80},{64,96},{80,112},{96,0},{112,16},{1... | collective-permute-start | bytes 786440 | tf_op jit(solution)/shard_map/ppermute | solution.py:548
  15.5 2.7 %collective-permute-start.1 = (f32[128,512]{1,0:T(8,128)}, f32[128,512]{1,0:T(8,128)S(1)}, u32[]{:S(2)}, u32[]{:S(2)}) collective-permute-start(f32[128,512]{1,0:T(8,128)} %get-tuple-element.26), channel_id=1, source_target_pairs={{0,64},{16,80},{32,96},{48,112},{64,0},{80,16},{96,32},{112,48},{1... | collective-permute-start | bytes 786440 | tf_op jit(solution)/shard_map/ppermute | solution.py:548
  18.2 1.4 %collective-permute-start.2 = (f32[128,512]{1,0:T(8,128)}, f32[128,512]{1,0:T(8,128)}, u32[]{:S(2)}, u32[]{:S(2)}) collective-permute-start(f32[128,512]{1,0:T(8,128)} %get-tuple-element.27), channel_id=1, source_target_pairs={{0,96},{16,112},{32,0},{48,16},{64,32},{80,48},{96,64},{112,80},{1... | collective-permute-start | bytes 786440 | tf_op jit(solution)/shard_map/ppermute | solution.py:548
  19.6 0.0 copy-done
  19.6 0.2 dual_edges.1
  19.8 1.9 %collective-permute-start.3 = (f32[8,256]{1,0:T(8,128)S(1)}, f32[8,256]{1,0:T(8,128)S(1)}, u32[]{:S(2)}, u32[]{:S(2)}) collective-permute-start(f32[8,256]{1,0:T(8,128)S(1)} %get-tuple-element.29.refs_5_), channel_id=1, source_target_pairs={{0,1},{1,2},{2,3},{3,4},{4,5},{5,6},{6,7},{7,8},{8,9},{9,10},{10,1... | collective-permute-start | bytes 24584 | tf_op jit(solution)/shard_map/ppermute | solution.py:485
  21.7 2.9 %collective-permute-start.4 = (f32[8,128]{1,0:T(8,128)S(1)}, f32[8,128]{1,0:T(8,128)S(1)}, u32[]{:S(2)}, u32[]{:S(2)}) collective-permute-start(f32[8,128]{1,0:T(8,128)S(1)} %get-tuple-element.31), channel_id=1, source_target_pairs={{0,16},{16,32},{32,48},{48,64},{64,80},{80,96},{96,112},{1,17},{17... | collective-permute-start | bytes 12296 | tf_op jit(solution)/shard_map/ppermute | solution.py:485
  24.7 4.2 %data_prepared.1 = (bf16[3,16,128,128]{3,2,1,0:T(8,128)(2,1)}, bf16[768,256]{1,0:T(8,128)(2,1)}, bf16[768,256]{1,0:T(8,128)(2,1)}) custom-call(bf16[2048,128]{1,0:T(8,128)(2,1)} %bitcast.11, bf16[2,2048,128]{2,1,0:T(8,128)(2,1)} %bitcast.10, bf16[128,128]{1,0:T(8,128)(2,1)} %constant.10.clone.place, f32[2,24,128]{2,1,0:T(8,128)} %constant.11.clone.twiddle_in.twiddle), custom_call_target="tpu_custom_call" | custom-call | tf_op jit(solution)/shard_map/data_prepared/pallas_call | solution.py:549
  28.8 0.0 collective-permute-done.refs_1_
  28.8 1.5 %collective-permute-done.1.refs_2_ = f32[128,512]{1,0:T(8,128)S(1)} collective-permute-done((f32[128,512]{1,0:T(8,128)}, f32[128,512]{1,0:T(8,128)S(1)}, u32[]{:S(2)}, u32[]{:S(2)}) %collective-permute-start.1) | collective-permute-done | bytes 262176 | tf_op jit(solution)/shard_map/ppermute | solution.py:548
  30.4 0.0 collective-permute-done.2.refs_3_
  30.4 1.5 %copy-done.2 = bf16[3,16,128,128]{3,2,1,0:T(8,128)(2,1)S(1)} copy-done((bf16[3,16,128,128]{3,2,1,0:T(8,128)(2,1)S(1)}, bf16[3,16,128,128]{3,2,1,0:T(8,128)(2,1)}, u32[]{:S(2)}) %copy-start.2) | copy-done | bytes 1572888
  31.9 1.8 %swap_ready.1 = (f32[4,64,256]{2,1,0:T(8,128)}, f32[4,64,256]{2,1,0:T(8,128)}) custom-call(s32[1]{0:T(128)} %bitcast.2.where, f32[128,512]{1,0:T(8,128)S(1)} %get-tuple-element.24.refs_0_, f32[128,512]{1,0:T(8,128)S(1)} %collective-permute-done.refs_1_, f32[128,512]{1,0:T(8,128)S(1)} %collective-permute-done.1.refs_2_, ...), custom_call_target="tpu_custom_call" | custom-call | tf_op jit(solution)/shard_map/swap_ready/pallas_call | solution.py:561
  33.7 1.1 collective-permute-start.5
  34.7 0.0 collective-permute-done.4.refs_8_
  34.7 5.7 %collective-permute-done.3.refs_7_ = f32[8,256]{1,0:T(8,128)S(1)} collective-permute-done((f32[8,256]{1,0:T(8,128)S(1)}, f32[8,256]{1,0:T(8,128)S(1)}, u32[]{:S(2)}, u32[]{:S(2)}) %collective-permute-start.3) | collective-permute-done | bytes 8224 | tf_op jit(solution)/shard_map/ppermute | solution.py:485
  40.4 0.5 all-to-all-done.cols_in
  40.9 1.0 collective-permute-start.6
  41.9 8.1 %columns.1.value = f32[16,264,128]{2,1,0:T(8,128)} custom-call(f32[16,256,128]{2,1,0:T(8,128)} %all-to-all-done.cols_in, bf16[3,16,128,128]{3,2,1,0:T(8,128)(2,1)} %get-tuple-element.35.refs_4_.data_in, f32[2,24,128]{2,1,0:T(8,128)} %constant.11.clone.twiddle_in.twiddle, bf16[768,256]{1,0:T(8,128)(2,1)} %get-tuple-element.36.forward_in, ...), custom_call_target="tpu_custom_call" | custom-call | tf_op jit(solution)/shard_map/columns/pallas_call | solution.py:577
  50.0 0.0 copy-done.8
  50.0 0.0 copy-done.10
  50.0 0.0 collective-permute-done.5.refs_4_
  50.1 0.0 collective-permute-done.6.refs_5_
  50.1 1.3 %fusion.after = f32[8,128]{1,0:T(8,128)} fusion(f32[4,64,256]{2,1,0:T(8,128)} %collective-permute-done.6.refs_5_, f32[4,64,256]{2,1,0:T(8,128)} %collective-permute-done.5.refs_4_), kind=kLoop, calls=%fused_computation.1 | loop fusion | flops 1024 | bytes 12288 | tf_op jit(solution)/shard_map/add | solution.py:603
  51.4 7.4 %all-to-all-start.1 = ((f32[16,264,128]{2,1,0:T(8,128)}), f32[16,264,128]{2,1,0:T(8,128)S(1)}, u32[]{:S(2)}, u32[]{:S(2)}) async-start(f32[16,264,128]{2,1,0:T(8,128)} %tied.1), calls=%async_computation.1 | async-start | bytes 4325376 | tf_op jit(solution)/shard_map/all_to_all | solution.py:604
  58.8 0.0 copy-done.1
  58.8 0.0 copy-start.9
  58.8 0.9 copy-done.9
  59.7 0.9 copy-done.11
  60.7 1.9 %tile_ready.1 = (f32[8,128,256]{2,1,0:T(8,128)S(1)}, f32[8,128,256]{2,1,0:T(8,128)S(1)}, f32[8,256]{1,0:T(8,128)S(1)}, f32[8,128]{1,0:T(8,128)S(1)}) custom-call(s32[1]{0:T(128)} %bitcast.2.where, f32[128,512]{1,0:T(8,128)S(1)} %get-tuple-element.24.refs_0_, f32[128,512]{1,0:T(8,128)S(1)} %copy-done.9, f32[128,512]{1,0:T(8,128)S(1)} %copy-done.11, ...), custom_call_target="tpu_custom_call" | custom-call | tf_op jit(solution)/shard_map/tile_ready/pallas_call | solution.py:605
  62.6 1.0 copy-done.4
  63.6 1.0 copy-done.6
  64.5 4.6 %collective-permute-start.7 = (f32[8,256]{1,0:T(8,128)S(1)}, f32[8,256]{1,0:T(8,128)S(1)}, u32[]{:S(2)}, u32[]{:S(2)}) collective-permute-start(f32[8,256]{1,0:T(8,128)S(1)} %get-tuple-element.42), channel_id=1, source_target_pairs={{1,0},{2,1},{3,2},{4,3},{5,4},{6,5},{7,6},{8,7},{9,8},{10,9},{11,1... | collective-permute-start | bytes 24584 | tf_op jit(solution)/shard_map/ppermute | solution.py:485
  69.1 1.3 %collective-permute-start.8 = (f32[8,128]{1,0:T(8,128)S(1)}, f32[8,128]{1,0:T(8,128)S(1)}, u32[]{:S(2)}, u32[]{:S(2)}) collective-permute-start(f32[8,128]{1,0:T(8,128)S(1)} %get-tuple-element.43), channel_id=1, source_target_pairs={{16,0},{32,16},{48,32},{64,48},{80,64},{96,80},{112,96},{17,1},{33... | collective-permute-start | bytes 12296 | tf_op jit(solution)/shard_map/ppermute | solution.py:485
  70.4 4.8 %collective-permute-done.8.after_two.right = f32[8,128]{1,0:T(8,128)S(1)} collective-permute-done((f32[8,128]{1,0:T(8,128)S(1)}, f32[8,128]{1,0:T(8,128)S(1)}, u32[]{:S(2)}, u32[]{:S(2)}) %collective-permute-start.8) | collective-permute-done | bytes 4128 | tf_op jit(solution)/shard_map/ppermute | solution.py:485
  75.3 7.7 %collective-permute-done.7.after_one.below = f32[8,256]{1,0:T(8,128)S(1)} collective-permute-done((f32[8,256]{1,0:T(8,128)S(1)}, f32[8,256]{1,0:T(8,128)S(1)}, u32[]{:S(2)}, u32[]{:S(2)}) %collective-permute-start.7) | collective-permute-done | bytes 8224 | tf_op jit(solution)/shard_map/ppermute | solution.py:485
  82.9 4.2 %all-to-all-done.1.lines = f32[16,264,128]{2,1,0:T(8,128)S(1)} async-done(((f32[16,264,128]{2,1,0:T(8,128)}), f32[16,264,128]{2,1,0:T(8,128)S(1)}, u32[]{:S(2)}, u32[]{:S(2)}) %all-to-all-start.1) | async-done | bytes 2162720 | tf_op jit(solution)/shard_map/all_to_all | solution.py:604
  87.1 0.0 copy-done.12
  87.1 2.4 %rows_back.1 = f32[8,136,256]{2,1,0:T(8,128)S(1)} custom-call(f32[16,264,128]{2,1,0:T(8,128)S(1)} %all-to-all-done.1.lines, f32[2,24,128]{2,1,0:T(8,128)S(1)} %copy-done.12, f32[8,256]{1,0:T(8,128)S(1)} %collective-permute-done.7.after_one.below, f32[8,128]{1,0:T(8,128)S(1)} %collective-permute-done.8.after_two.right), custom_call_target="tpu_custom_call" | custom-call | tf_op jit(solution)/shard_map/rows_back/pallas_call | solution.py:619
  89.5 20.5 %all_to_all.15.gradient = f32[8,136,256]{2,1,0:T(8,128)S(1)} all-to-all(f32[8,136,256]{2,1,0:T(8,128)S(1)} %rows_back.1), channel_id=1, replica_groups=mesh['chan'=8,'facet'=16] {'chan'}, dimensions={0} | all-to-all | bytes 2228224 | tf_op jit(solution)/shard_map/all_to_all | solution.py:630
  110.1 0.0 copy-done.5
  110.1 2.4 %finish.1 = (f32[8,128,256]{2,1,0:T(8,128)}, bf16[8,2,128,256]{3,2,1,0:T(8,128)(2,1)}) custom-call(f32[8,136,256]{2,1,0:T(8,128)S(1)} %all_to_all.15.gradient, f32[8,128,256]{2,1,0:T(8,128)S(1)} %copy-done.5, f32[8,128,256]{2,1,0:T(8,128)S(1)} %copy-done.7, bf16[8,2,128,256]{3,2,1,0:T(8,128)(2,1)S(1)} %copy-done.1, ...), custom_call_target="tpu_custom_call" | custom-call | tf_op jit(solution)/shard_map/finish/pallas_call | solution.py:631
  (12 shorter events, 0.0 us)
Async XLA Ops:
  4.6 8.4 %copy-start.3 = (f32[1,128,2048]{2,1,0:T(8,128)S(1)}, f32[1,128,2048]{2,1,0:T(8,128)}, u32[]{:S(2)}) copy-start(f32[1,128,2048]{2,1,0:T(8,128)} %param.6) | copy-start | bytes 3145732
  4.6 15.1 %copy-start = (bf16[8,2,128,256]{3,2,1,0:T(8,128)(2,1)S(1)}, bf16[8,2,128,256]{3,2,1,0:T(8,128)(2,1)}, u32[]{:S(2)}) copy-start(bf16[8,2,128,256]{3,2,1,0:T(8,128)(2,1)} %dual.3) | copy-start | bytes 3145732
  4.6 36.3 %all-to-all-start = ((f32[16,256,128]{2,1,0:T(8,128)}), f32[16,256,128]{2,1,0:T(8,128)}, u32[]{:S(2)}, u32[]{:S(2)}) async-start(f32[16,256,128]{2,1,0:T(8,128)} %bitcast.9), calls=%async_computation | async-start | bytes 4194304 | tf_op jit(solution)/shard_map/all_to_all | solution.py:531
  14.0 14.9 %collective-permute-start = (f32[128,512]{1,0:T(8,128)}, f32[128,512]{1,0:T(8,128)S(1)}, u32[]{:S(2)}, u32[]{:S(2)}) collective-permute-start(f32[128,512]{1,0:T(8,128)} %get-tuple-element.25), channel_id=1, source_target_pairs={{0,32},{16,48},{32,64},{48,80},{64,96},{80,112},{96,0},{112,16},{1... | collective-permute-start | bytes 786440 | tf_op jit(solution)/shard_map/ppermute | solution.py:548
  15.5 14.9 %collective-permute-start.1 = (f32[128,512]{1,0:T(8,128)}, f32[128,512]{1,0:T(8,128)S(1)}, u32[]{:S(2)}, u32[]{:S(2)}) collective-permute-start(f32[128,512]{1,0:T(8,128)} %get-tuple-element.26), channel_id=1, source_target_pairs={{0,64},{16,80},{32,96},{48,112},{64,0},{80,16},{96,32},{112,48},{1... | collective-permute-start | bytes 786440 | tf_op jit(solution)/shard_map/ppermute | solution.py:548
  18.2 12.2 %collective-permute-start.2 = (f32[128,512]{1,0:T(8,128)}, f32[128,512]{1,0:T(8,128)}, u32[]{:S(2)}, u32[]{:S(2)}) collective-permute-start(f32[128,512]{1,0:T(8,128)} %get-tuple-element.27), channel_id=1, source_target_pairs={{0,96},{16,112},{32,0},{48,16},{64,32},{80,48},{96,64},{112,80},{1... | collective-permute-start | bytes 786440 | tf_op jit(solution)/shard_map/ppermute | solution.py:548
  19.8 20.6 %collective-permute-start.3 = (f32[8,256]{1,0:T(8,128)S(1)}, f32[8,256]{1,0:T(8,128)S(1)}, u32[]{:S(2)}, u32[]{:S(2)}) collective-permute-start(f32[8,256]{1,0:T(8,128)S(1)} %get-tuple-element.29.refs_5_), channel_id=1, source_target_pairs={{0,1},{1,2},{2,3},{3,4},{4,5},{5,6},{6,7},{7,8},{8,9},{9,10},{10,1... | collective-permute-start | bytes 24584 | tf_op jit(solution)/shard_map/ppermute | solution.py:485
  21.7 13.0 %collective-permute-start.4 = (f32[8,128]{1,0:T(8,128)S(1)}, f32[8,128]{1,0:T(8,128)S(1)}, u32[]{:S(2)}, u32[]{:S(2)}) collective-permute-start(f32[8,128]{1,0:T(8,128)S(1)} %get-tuple-element.31), channel_id=1, source_target_pairs={{0,16},{16,32},{32,48},{48,64},{64,80},{80,96},{96,112},{1,17},{17... | collective-permute-start | bytes 12296 | tf_op jit(solution)/shard_map/ppermute | solution.py:485
  28.8 21.2 %copy-start.8 = (f32[128,512]{1,0:T(8,128)}, f32[128,512]{1,0:T(8,128)S(1)}, u32[]{:S(2)}) copy-start(f32[128,512]{1,0:T(8,128)S(1)} %collective-permute-done.refs_1_) | copy-start | bytes 786436
  30.4 19.7 %copy-start.10 = (f32[128,512]{1,0:T(8,128)}, f32[128,512]{1,0:T(8,128)S(1)}, u32[]{:S(2)}) copy-start(f32[128,512]{1,0:T(8,128)S(1)} %collective-permute-done.1.refs_2_) | copy-start | bytes 786436
  30.4 1.5 %copy-start.2 = (bf16[3,16,128,128]{3,2,1,0:T(8,128)(2,1)S(1)}, bf16[3,16,128,128]{3,2,1,0:T(8,128)(2,1)}, u32[]{:S(2)}) copy-start(bf16[3,16,128,128]{3,2,1,0:T(8,128)(2,1)} %get-tuple-element.35.refs_4_.data_in) | copy-start | bytes 4718596
  33.7 16.4 %collective-permute-start.5 = (f32[4,64,256]{2,1,0:T(8,128)}, f32[4,64,256]{2,1,0:T(8,128)}, u32[]{:S(2)}, u32[]{:S(2)}) collective-permute-start(f32[4,64,256]{2,1,0:T(8,128)} %get-tuple-element.38), channel_id=1, source_target_pairs={{0,16},{16,0},{32,48},{48,32},{64,80},{80,64},{96,112},{112,96},{1... | collective-permute-start | bytes 786440 | tf_op jit(solution)/shard_map/ppermute | solution.py:569
  40.9 9.1 %collective-permute-start.6 = (f32[4,64,256]{2,1,0:T(8,128)}, f32[4,64,256]{2,1,0:T(8,128)}, u32[]{:S(2)}, u32[]{:S(2)}) collective-permute-start(f32[4,64,256]{2,1,0:T(8,128)} %get-tuple-element.39), channel_id=1, source_target_pairs={{0,16},{16,0},{32,48},{48,32},{64,80},{80,64},{96,112},{112,96},{1... | collective-permute-start | bytes 786440 | tf_op jit(solution)/shard_map/ppermute | solution.py:573
  51.4 7.4 %copy-start.1 = (bf16[8,2,128,256]{3,2,1,0:T(8,128)(2,1)S(1)}, bf16[8,2,128,256]{3,2,1,0:T(8,128)(2,1)}, u32[]{:S(2)}) copy-start(bf16[8,2,128,256]{3,2,1,0:T(8,128)(2,1)} %dual.3) | copy-start | bytes 3145732
  51.4 35.7 %all-to-all-start.1 = ((f32[16,264,128]{2,1,0:T(8,128)}), f32[16,264,128]{2,1,0:T(8,128)S(1)}, u32[]{:S(2)}, u32[]{:S(2)}) async-start(f32[16,264,128]{2,1,0:T(8,128)} %tied.1), calls=%async_computation.1 | async-start | bytes 4325376 | tf_op jit(solution)/shard_map/all_to_all | solution.py:604
  58.8 1.0 copy-start.9
  59.7 0.9 copy-start.11
  60.7 26.4 %copy-start.12 = (f32[2,24,128]{2,1,0:T(8,128)S(1)}, f32[2,24,128]{2,1,0:T(8,128)}, u32[]{:S(2)}) copy-start(f32[2,24,128]{2,1,0:T(8,128)} %constant.11.clone.twiddle_in.twiddle) | copy-start | bytes 73732
  62.6 1.0 copy-start.4
  63.6 1.0 copy-start.6
  64.5 18.4 %collective-permute-start.7 = (f32[8,256]{1,0:T(8,128)S(1)}, f32[8,256]{1,0:T(8,128)S(1)}, u32[]{:S(2)}, u32[]{:S(2)}) collective-permute-start(f32[8,256]{1,0:T(8,128)S(1)} %get-tuple-element.42), channel_id=1, source_target_pairs={{1,0},{2,1},{3,2},{4,3},{5,4},{6,5},{7,6},{8,7},{9,8},{10,9},{11,1... | collective-permute-start | bytes 24584 | tf_op jit(solution)/shard_map/ppermute | solution.py:485
  69.1 6.1 %collective-permute-start.8 = (f32[8,128]{1,0:T(8,128)S(1)}, f32[8,128]{1,0:T(8,128)S(1)}, u32[]{:S(2)}, u32[]{:S(2)}) collective-permute-start(f32[8,128]{1,0:T(8,128)S(1)} %get-tuple-element.43), channel_id=1, source_target_pairs={{16,0},{32,16},{48,32},{64,48},{80,64},{96,80},{112,96},{17,1},{33... | collective-permute-start | bytes 12296 | tf_op jit(solution)/shard_map/ppermute | solution.py:485
  87.1 23.0 %copy-start.5 = (f32[8,128,256]{2,1,0:T(8,128)S(1)}, f32[8,128,256]{2,1,0:T(8,128)}, u32[]{:S(2)}) copy-start(f32[8,128,256]{2,1,0:T(8,128)} %copy-done.4) | copy-start | bytes 3145732
  87.1 23.0 %copy-start.7 = (f32[8,128,256]{2,1,0:T(8,128)S(1)}, f32[8,128,256]{2,1,0:T(8,128)}, u32[]{:S(2)}) copy-start(f32[8,128,256]{2,1,0:T(8,128)} %copy-done.6) | copy-start | bytes 3145732

commit v8 on v7

--- a/solution.py
+++ b/solution.py
@@ -13,6 +13,7 @@
 RADIX = 16
 LANES = 128
 CHANNELS = 8
+EARLY = 80
 
 step_primal = 0.5
 step_dual = 0.5
@@ -159,8 +160,8 @@
     pieces, early, late = refs[:4], refs[-2], refs[-1]
     lanes = pl.ds(pl.multiple_of((1 - where[0] % 2) * 256, 256), 256)
     for k in range(4):
-        early[k] = pieces[k][: LANES // 2, lanes]
-        late[k] = pieces[k][LANES // 2 :, lanes]
+        early[k] = pieces[k][:EARLY, lanes]
+        late[k] = pieces[k][EARLY:, lanes]
 
 
 def rows_forward(
@@ -170,7 +171,7 @@
     steps = LANES // chunk
 
     def incoming(step):
-        rows = pl.ds(pl.multiple_of(step * chunk, chunk), chunk)
+        rows = pl.ds(step * chunk, chunk)
         return pltpu.make_async_copy(image_in.at[rows, :], image.at[rows, :], in_sems.at[step])
 
     get_twiddle = fetched(twiddle_in, twiddle, in_sems.at[steps])
@@ -179,9 +180,9 @@
     get_twiddle.wait()
     fill_table(table, twiddle, -1, True)
 
-    def body(step, carry):
+    def body(step):
         incoming(step).wait()
-        at = pl.multiple_of(step * chunk, chunk)
+        at = step * chunk
         values = [
             (image[pl.ds(at, chunk), b * LANES : (b + 1) * LANES], None) for b in range(RADIX)
         ]
@@ -198,9 +199,9 @@
                 real * cos + imag * sin,
                 imag * cos - real * sin,
             )
-        return carry
-
-    lax.fori_loop(0, steps, body, 0)
+
+    for step in range(steps):
+        body(step)
     dims = ((1,), (1,))
     sent = []
     for g in range(RADIX // 2):
@@ -355,8 +356,8 @@
     steps = LANES // chunk
     lane_at = lax.broadcasted_iota(jnp.int32, (chunk, LANES), 1)
 
-    def body(step, carry):
-        at = pl.multiple_of(step * chunk, chunk)
+    def body(step):
+        at = step * chunk
         here = pl.ds(at, chunk)
         values = []
         for f in range(RADIX):
@@ -371,9 +372,9 @@
             if b > 0 and b % 2 == 0:
                 side = jnp.where(lane_at == b // 2 - 1, mixed[b][0][:, 0:1], side)
         side_v[here, :] = side
-        return carry
-
-    lax.fori_loop(0, steps, body, 0)
+
+    for step in range(steps):
+        body(step)
     beside = side_v[...].T
     for d in range(CHANNELS):
         out[d, LANES + 1 : LANES + 2, :LANES] = beside[d : d + 1, :]
@@ -436,15 +437,15 @@
     lane_at = lax.broadcasted_iota(jnp.int32, (chunk, 2 * LANES), 1)
 
     def outgoing(step):
-        rows = pl.ds(pl.multiple_of(step * chunk, chunk), chunk)
+        rows = pl.ds(step * chunk, chunk)
         return pltpu.make_async_copy(
             dual_v.at[:, :, rows, :], dual_next.at[:, :, rows, :], dual_sems.at[step]
         )
 
-    def body(step, carry):
-        at = pl.multiple_of(step * chunk, chunk)
+    def body(step):
+        at = step * chunk
         here = pl.ds(at, chunk)
-        after = pl.ds(pl.multiple_of(at + chunk, chunk), 8)
+        after = pl.ds(at + chunk, 8)
         firsts, seconds, total = [], [], None
         for c in range(CHANNELS):
             ahead = ahead_v[c, here, :]
@@ -466,9 +467,9 @@
             dual_v[c, 0, here, :] = (firsts[c] * factor).astype(jnp.bfloat16)
             dual_v[c, 1, here, :] = (seconds[c] * factor).astype(jnp.bfloat16)
         outgoing(step).start()
-        return carry
-
-    lax.fori_loop(0, steps, body, 0)
+
+    for step in range(steps):
+        body(step)
     for copy in leaving:
         copy.wait()
     for step in range(steps):
@@ -560,11 +561,11 @@
     )(weights[0], measured[0], place, twiddle)
     early, late = call(
         swap_ready,
-        (shape((4, LANES // 2, 256)),) * 2,
-        [SM] + [VM] * 4 + [ANY] * 2,
+        (shape((4, EARLY, 256)), shape((4, LANES - EARLY, 256))),
+        [SM] + [VM] * 4 + [ANY],
         (VM, VM),
         [],
-    )(where, *pieces, data, last_row)
+    )(where, *pieces, last_row)
     other_zl = [(i, i ^ 1) for i in range(8)]
     early = lax.ppermute(early, "chan", other_zl)
     cols, late, above, left, data, forward, inverse = lax.optimization_barrier(

time: 115 us -> 117 us (1.017)
  Pallas kernels: 25.9 us -> 21.7 us
  waiting for transfers between devices: 24.4 us -> 28.1 us
  local copies, waits for them, and re-layouts: 5.38 us -> 7.54 us
  starting transfers between devices: 34.3 us -> 35.8 us
    ppermute x3, waiting for transfers between devices: 1.52 us -> 10.3 us  [shards(): pieces[k] = lax.ppermute(pieces[k], 'chan', pairs)]
    ppermute x4, waiting for transfers between devices: 18.2 us -> 13.5 us  [passed_along(): return lax.ppermute(x, axis, pairs)]
    unnamed x26 -> x38, local copies, waits for them, and re-layouts: 5.38 us -> 7.54 us
    ppermute x1, starting transfers between devices: 1.02 us -> 2.42 us  [shards(): late = lax.ppermute(late, 'chan', other_zl)]
  transfers between devices with their start and end apart: 11 -> 11, of which waited for: 6 -> 6; matrix products, arithmetic and copies ran while one was open for 0% -> 0% of each run, Pallas kernels for 15% -> 12%
where the time goes in v8:
time: 117 us; the launch traced here: 115 us
  starting transfers between devices  35.8 us (31%)
  waiting for transfers between devices  28.1 us (24%)
  Pallas kernels  21.7 us (19%)
  blocking collectives  20.4 us (17%)
  local copies, waits for them, and re-layouts  7.54 us (6%)
    all_to_all x1, blocking collectives, shards(): lax.all_to_all(slopes, 'chan', split_axis=0, concat_axis=0, tiled=True)  20.4 us
    ppermute x4, waiting for transfers between devices, passed_along(): return lax.ppermute(x, axis, pairs)  13.5 us
    ppermute x4, starting transfers between devices, passed_along(): return lax.ppermute(x, axis, pairs)  10.9 us
    ppermute x3, waiting for transfers between devices, shards(): pieces[k] = lax.ppermute(pieces[k], 'chan', pairs)  10.3 us
    all_to_all x1, starting transfers between devices, shards(): lax.all_to_all(spread.reshape(RADIX, 2 * LANES, LANES), 'facet', split_ax...  8.39 us
    pallas_call x1, Pallas kernels, shards(): call(columns, shape((RADIX, 2 * LANES + 8, LANES)), [HBM] * 5, HBM, [pltp...  8.09 us
    unnamed x38, local copies, waits for them, and re-layouts  7.54 us
    all_to_all x1, starting transfers between devices, shards(): lax.all_to_all(back, 'facet', split_axis=0, concat_axis=0, tiled=True)  7.31 us
  transfers between devices with their start and end apart: 11, of which 6 were waited for; matrix products, arithmetic and copies ran while one was open for 0% of the time, Pallas kernels for 12%

profile of v8, /device:TPU:8, one launch (start us, length us, event | category | flops | bytes accessed | tf_op | source)
XLA Modules:
  0.0 115.1 jit_solution(125842924594116750)
XLA Ops:
  0.6 3.7 %rows_forward.1 = f32[16,2,16,8,128]{4,3,2,1,0:T(8,128)} custom-call(f32[128,2048]{1,0:T(8,128)} %bitcast.7, f32[2,24,128]{2,1,0:T(8,128)} %constant.11.clone.twiddle_in.twiddle), custom_call_target="tpu_custom_call" | custom-call | tf_op jit(solution)/shard_map/rows_forward/pallas_call | solution.py:516
  4.3 0.0 copy-start.2
  4.3 0.0 copy-start
  4.4 8.4 %all-to-all-start = ((f32[16,256,128]{2,1,0:T(8,128)}), f32[16,256,128]{2,1,0:T(8,128)}, u32[]{:S(2)}, u32[]{:S(2)}) async-start(f32[16,256,128]{2,1,0:T(8,128)} %bitcast.9), calls=%async_computation | async-start | bytes 4194304 | tf_op jit(solution)/shard_map/all_to_all | solution.py:532
  12.7 0.1 cross_ready.1
  12.8 1.6 %collective-permute-start = (f32[128,512]{1,0:T(8,128)S(1)}, f32[128,512]{1,0:T(8,128)S(1)}, u32[]{:S(2)}, u32[]{:S(2)}) collective-permute-start(f32[128,512]{1,0:T(8,128)S(1)} %get-tuple-element.25), channel_id=1, source_target_pairs={{0,32},{16,48},{32,64},{48,80},{64,96},{80,112},{96,0},{112,16},{1... | collective-permute-start | bytes 786440 | tf_op jit(solution)/shard_map/ppermute | solution.py:549
  14.4 2.7 %collective-permute-start.1 = (f32[128,512]{1,0:T(8,128)S(1)}, f32[128,512]{1,0:T(8,128)S(1)}, u32[]{:S(2)}, u32[]{:S(2)}) collective-permute-start(f32[128,512]{1,0:T(8,128)S(1)} %get-tuple-element.26), channel_id=1, source_target_pairs={{0,64},{16,80},{32,96},{48,112},{64,0},{80,16},{96,32},{112,48},{1... | collective-permute-start | bytes 786440 | tf_op jit(solution)/shard_map/ppermute | solution.py:549
  17.1 1.4 %collective-permute-start.2 = (f32[128,512]{1,0:T(8,128)S(1)}, f32[128,512]{1,0:T(8,128)S(1)}, u32[]{:S(2)}, u32[]{:S(2)}) collective-permute-start(f32[128,512]{1,0:T(8,128)S(1)} %get-tuple-element.27), channel_id=1, source_target_pairs={{0,96},{16,112},{32,0},{48,16},{64,32},{80,48},{96,64},{112,80},{1... | collective-permute-start | bytes 786440 | tf_op jit(solution)/shard_map/ppermute | solution.py:549
  18.6 0.2 dual_edges.1
  18.7 3.7 %collective-permute-done.refs_1_ = f32[128,512]{1,0:T(8,128)S(1)} collective-permute-done((f32[128,512]{1,0:T(8,128)S(1)}, f32[128,512]{1,0:T(8,128)S(1)}, u32[]{:S(2)}, u32[]{:S(2)}) %collective-permute-start) | collective-permute-done | bytes 262176 | tf_op jit(solution)/shard_map/ppermute | solution.py:549
  22.5 6.6 %collective-permute-done.1.refs_2_ = f32[128,512]{1,0:T(8,128)S(1)} collective-permute-done((f32[128,512]{1,0:T(8,128)S(1)}, f32[128,512]{1,0:T(8,128)S(1)}, u32[]{:S(2)}, u32[]{:S(2)}) %collective-permute-start.1) | collective-permute-done | bytes 262176 | tf_op jit(solution)/shard_map/ppermute | solution.py:549
  29.1 0.0 collective-permute-done.2.refs_3_
  29.1 0.8 swap_ready.1
  29.9 0.7 copy-done.7
  30.6 0.0 copy-done.11
  30.6 1.0 collective-permute-start.5
  31.7 1.9 %collective-permute-start.3 = (f32[8,256]{1,0:T(8,128)S(1)}, f32[8,256]{1,0:T(8,128)S(1)}, u32[]{:S(2)}, u32[]{:S(2)}) collective-permute-start(f32[8,256]{1,0:T(8,128)S(1)} %get-tuple-element.28.refs_4_), channel_id=1, source_target_pairs={{0,1},{1,2},{2,3},{3,4},{4,5},{5,6},{6,7},{7,8},{8,9},{9,10},{10,1... | collective-permute-start | bytes 24584 | tf_op jit(solution)/shard_map/ppermute | solution.py:486
  33.6 2.9 %collective-permute-start.4 = (f32[8,128]{1,0:T(8,128)S(1)}, f32[8,128]{1,0:T(8,128)S(1)}, u32[]{:S(2)}, u32[]{:S(2)}) collective-permute-start(f32[8,128]{1,0:T(8,128)S(1)} %get-tuple-element.30), channel_id=1, source_target_pairs={{0,16},{16,32},{32,48},{48,64},{64,80},{80,96},{96,112},{1,17},{17... | collective-permute-start | bytes 12296 | tf_op jit(solution)/shard_map/ppermute | solution.py:486
  36.5 4.2 %data_prepared.1 = (bf16[3,16,128,128]{3,2,1,0:T(8,128)(2,1)}, bf16[768,256]{1,0:T(8,128)(2,1)}, bf16[768,256]{1,0:T(8,128)(2,1)}) custom-call(bf16[2048,128]{1,0:T(8,128)(2,1)} %bitcast.11, bf16[2,2048,128]{2,1,0:T(8,128)(2,1)} %bitcast.10, bf16[128,128]{1,0:T(8,128)(2,1)} %constant.10.clone.place, f32[2,24,128]{2,1,0:T(8,128)} %constant.11.clone.twiddle_in.twiddle), custom_call_target="tpu_custom_call" | custom-call | tf_op jit(solution)/shard_map/data_prepared/pallas_call | solution.py:550
  40.7 3.0 %collective-permute-done.4.refs_8_ = f32[8,128]{1,0:T(8,128)S(1)} collective-permute-done((f32[8,128]{1,0:T(8,128)S(1)}, f32[8,128]{1,0:T(8,128)S(1)}, u32[]{:S(2)}, u32[]{:S(2)}) %collective-permute-start.4) | collective-permute-done | bytes 4128 | tf_op jit(solution)/shard_map/ppermute | solution.py:486
  43.7 0.0 collective-permute-done.3.refs_7_
  43.7 0.0 all-to-all-done.cols_in
  43.7 2.4 %collective-permute-start.6 = (f32[4,48,256]{2,1,0:T(8,128)}, f32[4,48,256]{2,1,0:T(8,128)S(1)}, u32[]{:S(2)}, u32[]{:S(2)}) collective-permute-start(f32[4,48,256]{2,1,0:T(8,128)} %copy-done.18), channel_id=1, source_target_pairs={{0,16},{16,0},{32,48},{48,32},{64,80},{80,64},{96,112},{112,96},{1... | collective-permute-start | bytes 589832 | tf_op jit(solution)/shard_map/ppermute | solution.py:574
  46.1 8.1 %columns.1.value = f32[16,264,128]{2,1,0:T(8,128)} custom-call(f32[16,256,128]{2,1,0:T(8,128)} %all-to-all-done.cols_in, bf16[3,16,128,128]{3,2,1,0:T(8,128)(2,1)} %get-tuple-element.35.data_in, f32[2,24,128]{2,1,0:T(8,128)} %constant.11.clone.twiddle_in.twiddle, bf16[768,256]{1,0:T(8,128)(2,1)} %get-tuple-element.36.forward_in, ...), custom_call_target="tpu_custom_call" | custom-call | tf_op jit(solution)/shard_map/columns/pallas_call | solution.py:578
  54.2 0.0 collective-permute-done.5.refs_4_
  54.2 0.0 copy-start.14
  54.2 0.0 collective-permute-done.6.refs_5_
  54.3 0.0 copy-start.16
  54.3 0.7 fusion.after
  54.9 0.0 copy-done.14
  55.0 0.1 copy-done.16
  55.0 7.3 %all-to-all-start.1 = ((f32[16,264,128]{2,1,0:T(8,128)}), f32[16,264,128]{2,1,0:T(8,128)S(1)}, u32[]{:S(2)}, u32[]{:S(2)}) async-start(f32[16,264,128]{2,1,0:T(8,128)} %tied.1), calls=%async_computation.1 | async-start | bytes 4325376 | tf_op jit(solution)/shard_map/all_to_all | solution.py:605
  62.4 0.9 copy-done.8
  63.3 0.9 copy-done.10
  64.3 0.9 copy-done.12
  65.2 1.0 copy-done.15
  66.2 0.9 copy-done.17
  67.1 0.8 tile_ready.1
  67.9 1.0 copy-done.3
  68.9 1.0 copy-done.5
  69.9 4.6 %collective-permute-start.7 = (f32[8,256]{1,0:T(8,128)S(1)}, f32[8,256]{1,0:T(8,128)S(1)}, u32[]{:S(2)}, u32[]{:S(2)}) collective-permute-start(f32[8,256]{1,0:T(8,128)S(1)} %get-tuple-element.42), channel_id=1, source_target_pairs={{1,0},{2,1},{3,2},{4,3},{5,4},{6,5},{7,6},{8,7},{9,8},{10,9},{11,1... | collective-permute-start | bytes 24584 | tf_op jit(solution)/shard_map/ppermute | solution.py:486
  74.5 1.5 %collective-permute-start.8 = (f32[8,128]{1,0:T(8,128)S(1)}, f32[8,128]{1,0:T(8,128)S(1)}, u32[]{:S(2)}, u32[]{:S(2)}) collective-permute-start(f32[8,128]{1,0:T(8,128)S(1)} %get-tuple-element.43), channel_id=1, source_target_pairs={{16,0},{32,16},{48,32},{64,48},{80,64},{96,80},{112,96},{17,1},{33... | collective-permute-start | bytes 12296 | tf_op jit(solution)/shard_map/ppermute | solution.py:486
  76.0 4.4 %collective-permute-done.8.after_two.right = f32[8,128]{1,0:T(8,128)S(1)} collective-permute-done((f32[8,128]{1,0:T(8,128)S(1)}, f32[8,128]{1,0:T(8,128)S(1)}, u32[]{:S(2)}, u32[]{:S(2)}) %collective-permute-start.8) | collective-permute-done | bytes 4128 | tf_op jit(solution)/shard_map/ppermute | solution.py:486
  80.4 6.1 %collective-permute-done.7.after_one.below = f32[8,256]{1,0:T(8,128)S(1)} collective-permute-done((f32[8,256]{1,0:T(8,128)S(1)}, f32[8,256]{1,0:T(8,128)S(1)}, u32[]{:S(2)}, u32[]{:S(2)}) %collective-permute-start.7) | collective-permute-done | bytes 8224 | tf_op jit(solution)/shard_map/ppermute | solution.py:486
  86.5 4.2 %all-to-all-done.1.lines = f32[16,264,128]{2,1,0:T(8,128)S(1)} async-done(((f32[16,264,128]{2,1,0:T(8,128)}), f32[16,264,128]{2,1,0:T(8,128)S(1)}, u32[]{:S(2)}, u32[]{:S(2)}) %all-to-all-start.1) | async-done | bytes 2162720 | tf_op jit(solution)/shard_map/all_to_all | solution.py:605
  90.7 1.5 %rows_back.1 = f32[8,136,256]{2,1,0:T(8,128)S(1)} custom-call(f32[16,264,128]{2,1,0:T(8,128)S(1)} %all-to-all-done.1.lines, f32[2,24,128]{2,1,0:T(8,128)S(1)} %copy-done.13, f32[8,256]{1,0:T(8,128)S(1)} %collective-permute-done.7.after_one.below, f32[8,128]{1,0:T(8,128)S(1)} %collective-permute-done.8.after_two.right), custom_call_target="tpu_custom_call" | custom-call | tf_op jit(solution)/shard_map/rows_back/pallas_call | solution.py:620
  92.2 20.4 %all_to_all.15.gradient = f32[8,136,256]{2,1,0:T(8,128)S(1)} all-to-all(f32[8,136,256]{2,1,0:T(8,128)S(1)} %rows_back.1), channel_id=1, replica_groups=mesh['chan'=8,'facet'=16] {'chan'}, dimensions={0} | all-to-all | bytes 2228224 | tf_op jit(solution)/shard_map/all_to_all | solution.py:631
  112.6 2.3 %finish.1 = (f32[8,128,256]{2,1,0:T(8,128)}, bf16[8,2,128,256]{3,2,1,0:T(8,128)(2,1)}) custom-call(f32[8,136,256]{2,1,0:T(8,128)S(1)} %all_to_all.15.gradient, f32[8,128,256]{2,1,0:T(8,128)S(1)} %copy-done.4, f32[8,128,256]{2,1,0:T(8,128)S(1)} %copy-done.6, bf16[8,2,128,256]{3,2,1,0:T(8,128)(2,1)S(1)} %copy-done.1, ...), custom_call_target="tpu_custom_call" | custom-call | tf_op jit(solution)/shard_map/finish/pallas_call | solution.py:632
  (24 shorter events, 0.0 us)
Async XLA Ops:
  4.3 8.4 %copy-start.2 = (f32[1,128,2048]{2,1,0:T(8,128)S(1)}, f32[1,128,2048]{2,1,0:T(8,128)}, u32[]{:S(2)}) copy-start(f32[1,128,2048]{2,1,0:T(8,128)} %param.6) | copy-start | bytes 3145732
  4.3 14.2 %copy-start = (bf16[8,2,128,256]{3,2,1,0:T(8,128)(2,1)S(1)}, bf16[8,2,128,256]{3,2,1,0:T(8,128)(2,1)}, u32[]{:S(2)}) copy-start(bf16[8,2,128,256]{3,2,1,0:T(8,128)(2,1)} %dual.3) | copy-start | bytes 3145732
  4.4 39.4 %all-to-all-start = ((f32[16,256,128]{2,1,0:T(8,128)}), f32[16,256,128]{2,1,0:T(8,128)}, u32[]{:S(2)}, u32[]{:S(2)}) async-start(f32[16,256,128]{2,1,0:T(8,128)} %bitcast.9), calls=%async_computation | async-start | bytes 4194304 | tf_op jit(solution)/shard_map/all_to_all | solution.py:532
  12.8 9.6 %collective-permute-start = (f32[128,512]{1,0:T(8,128)S(1)}, f32[128,512]{1,0:T(8,128)S(1)}, u32[]{:S(2)}, u32[]{:S(2)}) collective-permute-start(f32[128,512]{1,0:T(8,128)S(1)} %get-tuple-element.25), channel_id=1, source_target_pairs={{0,32},{16,48},{32,64},{48,80},{64,96},{80,112},{96,0},{112,16},{1... | collective-permute-start | bytes 786440 | tf_op jit(solution)/shard_map/ppermute | solution.py:549
  14.4 14.7 %collective-permute-start.1 = (f32[128,512]{1,0:T(8,128)S(1)}, f32[128,512]{1,0:T(8,128)S(1)}, u32[]{:S(2)}, u32[]{:S(2)}) collective-permute-start(f32[128,512]{1,0:T(8,128)S(1)} %get-tuple-element.26), channel_id=1, source_target_pairs={{0,64},{16,80},{32,96},{48,112},{64,0},{80,16},{96,32},{112,48},{1... | collective-permute-start | bytes 786440 | tf_op jit(solution)/shard_map/ppermute | solution.py:549
  17.1 12.0 %collective-permute-start.2 = (f32[128,512]{1,0:T(8,128)S(1)}, f32[128,512]{1,0:T(8,128)S(1)}, u32[]{:S(2)}, u32[]{:S(2)}) collective-permute-start(f32[128,512]{1,0:T(8,128)S(1)} %get-tuple-element.27), channel_id=1, source_target_pairs={{0,96},{16,112},{32,0},{48,16},{64,32},{80,48},{96,64},{112,80},{1... | collective-permute-start | bytes 786440 | tf_op jit(solution)/shard_map/ppermute | solution.py:549
  29.1 0.8 copy-start.9
  29.1 1.6 %copy-start.11 = (f32[128,512]{1,0:T(8,128)}, f32[128,512]{1,0:T(8,128)S(1)}, u32[]{:S(2)}) copy-start(f32[128,512]{1,0:T(8,128)S(1)} %collective-permute-done.2.refs_3_) | copy-start | bytes 786436
  29.9 0.7 copy-start.7
  30.6 2.9 %copy-start.18 = (f32[4,48,256]{2,1,0:T(8,128)}, f32[4,48,256]{2,1,0:T(8,128)S(1)}, u32[]{:S(2)}) copy-start(f32[4,48,256]{2,1,0:T(8,128)S(1)} %get-tuple-element.39) | copy-start | bytes 589828
  30.6 23.6 %collective-permute-start.5 = (f32[4,80,256]{2,1,0:T(8,128)}, f32[4,80,256]{2,1,0:T(8,128)S(1)}, u32[]{:S(2)}, u32[]{:S(2)}) collective-permute-start(f32[4,80,256]{2,1,0:T(8,128)} %get-tuple-element.38), channel_id=1, source_target_pairs={{0,16},{16,0},{32,48},{48,32},{64,80},{80,64},{96,112},{112,96},{1... | collective-permute-start | bytes 983048 | tf_op jit(solution)/shard_map/ppermute | solution.py:570
  31.7 12.0 %collective-permute-start.3 = (f32[8,256]{1,0:T(8,128)S(1)}, f32[8,256]{1,0:T(8,128)S(1)}, u32[]{:S(2)}, u32[]{:S(2)}) collective-permute-start(f32[8,256]{1,0:T(8,128)S(1)} %get-tuple-element.28.refs_4_), channel_id=1, source_target_pairs={{0,1},{1,2},{2,3},{3,4},{4,5},{5,6},{6,7},{7,8},{8,9},{9,10},{10,1... | collective-permute-start | bytes 24584 | tf_op jit(solution)/shard_map/ppermute | solution.py:486
  33.6 10.1 %collective-permute-start.4 = (f32[8,128]{1,0:T(8,128)S(1)}, f32[8,128]{1,0:T(8,128)S(1)}, u32[]{:S(2)}, u32[]{:S(2)}) collective-permute-start(f32[8,128]{1,0:T(8,128)S(1)} %get-tuple-element.30), channel_id=1, source_target_pairs={{0,16},{16,32},{32,48},{48,64},{64,80},{80,96},{96,112},{1,17},{17... | collective-permute-start | bytes 12296 | tf_op jit(solution)/shard_map/ppermute | solution.py:486
  43.7 10.5 %collective-permute-start.6 = (f32[4,48,256]{2,1,0:T(8,128)}, f32[4,48,256]{2,1,0:T(8,128)S(1)}, u32[]{:S(2)}, u32[]{:S(2)}) collective-permute-start(f32[4,48,256]{2,1,0:T(8,128)} %copy-done.18), channel_id=1, source_target_pairs={{0,16},{16,0},{32,48},{48,32},{64,80},{80,64},{96,112},{112,96},{1... | collective-permute-start | bytes 589832 | tf_op jit(solution)/shard_map/ppermute | solution.py:574
  54.2 0.7 copy-start.14
  54.3 0.8 copy-start.16
  55.0 7.3 %copy-start.1 = (bf16[8,2,128,256]{3,2,1,0:T(8,128)(2,1)S(1)}, bf16[8,2,128,256]{3,2,1,0:T(8,128)(2,1)}, u32[]{:S(2)}) copy-start(bf16[8,2,128,256]{3,2,1,0:T(8,128)(2,1)} %dual.3) | copy-start | bytes 3145732
  55.0 35.7 %all-to-all-start.1 = ((f32[16,264,128]{2,1,0:T(8,128)}), f32[16,264,128]{2,1,0:T(8,128)S(1)}, u32[]{:S(2)}, u32[]{:S(2)}) async-start(f32[16,264,128]{2,1,0:T(8,128)} %tied.1), calls=%async_computation.1 | async-start | bytes 4325376 | tf_op jit(solution)/shard_map/all_to_all | solution.py:605
  62.4 1.0 copy-start.8
  63.3 0.9 copy-start.10
  64.3 0.9 copy-start.12
  65.2 1.0 copy-start.15
  66.2 0.9 copy-start.17
  67.1 23.6 %copy-start.13 = (f32[2,24,128]{2,1,0:T(8,128)S(1)}, f32[2,24,128]{2,1,0:T(8,128)}, u32[]{:S(2)}) copy-start(f32[2,24,128]{2,1,0:T(8,128)} %constant.11.clone.twiddle_in.twiddle) | copy-start | bytes 73732
  67.9 1.0 copy-start.3
  68.9 1.0 copy-start.5
  69.9 16.6 %collective-permute-start.7 = (f32[8,256]{1,0:T(8,128)S(1)}, f32[8,256]{1,0:T(8,128)S(1)}, u32[]{:S(2)}, u32[]{:S(2)}) collective-permute-start(f32[8,256]{1,0:T(8,128)S(1)} %get-tuple-element.42), channel_id=1, source_target_pairs={{1,0},{2,1},{3,2},{4,3},{5,4},{6,5},{7,6},{8,7},{9,8},{10,9},{11,1... | collective-permute-start | bytes 24584 | tf_op jit(solution)/shard_map/ppermute | solution.py:486
  74.5 5.9 %collective-permute-start.8 = (f32[8,128]{1,0:T(8,128)S(1)}, f32[8,128]{1,0:T(8,128)S(1)}, u32[]{:S(2)}, u32[]{:S(2)}) collective-permute-start(f32[8,128]{1,0:T(8,128)S(1)} %get-tuple-element.43), channel_id=1, source_target_pairs={{16,0},{32,16},{48,32},{64,48},{80,64},{96,80},{112,96},{17,1},{33... | collective-permute-start | bytes 12296 | tf_op jit(solution)/shard_map/ppermute | solution.py:486
  90.7 21.9 %copy-start.4 = (f32[8,128,256]{2,1,0:T(8,128)S(1)}, f32[8,128,256]{2,1,0:T(8,128)}, u32[]{:S(2)}) copy-start(f32[8,128,256]{2,1,0:T(8,128)} %copy-done.3) | copy-start | bytes 3145732
  90.7 21.9 %copy-start.6 = (f32[8,128,256]{2,1,0:T(8,128)S(1)}, f32[8,128,256]{2,1,0:T(8,128)}, u32[]{:S(2)}) copy-start(f32[8,128,256]{2,1,0:T(8,128)} %copy-done.5) | copy-start | bytes 3145732

commit v9 on v8

--- a/solution.py
+++ b/solution.py
@@ -13,7 +13,7 @@
 RADIX = 16
 LANES = 128
 CHANNELS = 8
-EARLY = 80
+EARLY = 64
 
 step_primal = 0.5
 step_dual = 0.5
@@ -562,10 +562,10 @@
     early, late = call(
         swap_ready,
         (shape((4, EARLY, 256)), shape((4, LANES - EARLY, 256))),
-        [SM] + [VM] * 4 + [ANY],
+        [SM] + [VM] * 4 + [ANY] * 2,
         (VM, VM),
         [],
-    )(where, *pieces, last_row)
+    )(where, *pieces, data, last_row)
     other_zl = [(i, i ^ 1) for i in range(8)]
     early = lax.ppermute(early, "chan", other_zl)
     cols, late, above, left, data, forward, inverse = lax.optimization_barrier(

time: 117 us -> 114 us (0.974)
  waiting for transfers between devices: 28.1 us -> 24.2 us
  Pallas kernels: 21.7 us -> 24.6 us
  local copies, waits for them, and re-layouts: 7.54 us -> 5.38 us
  starting transfers between devices: 35.8 us -> 34.5 us
    ppermute x3, waiting for transfers between devices: 10.3 us -> 1.52 us  [shards(): pieces[k] = lax.ppermute(pieces[k], 'chan', pairs)]
    ppermute x4, waiting for transfers between devices: 13.5 us -> 18 us  [passed_along(): return lax.ppermute(x, axis, pairs)]
    unnamed x38 -> x26, local copies, waits for them, and re-layouts: 7.54 us -> 5.38 us
    ppermute x1, starting transfers between devices: 2.42 us -> 1.03 us  [shards(): late = lax.ppermute(late, 'chan', other_zl)]
  transfers between devices with their start and end apart: 11 -> 11, of which waited for: 6 -> 6; matrix products, arithmetic and copies ran while one was open for 0% -> 0% of each run, Pallas kernels for 12% -> 15%
where the time goes in v9:
time: 114 us; the launch traced here: 111 us
  starting transfers between devices  34.5 us (30%)
  Pallas kernels  24.6 us (22%)
  waiting for transfers between devices  24.2 us (21%)
  blocking collectives  20.5 us (18%)
  local copies, waits for them, and re-layouts  5.38 us (5%)
  other arithmetic  1.28 us (1%)
    all_to_all x1, blocking collectives, shards(): lax.all_to_all(slopes, 'chan', split_axis=0, concat_axis=0, tiled=True)  20.5 us
    ppermute x4, waiting for transfers between devices, passed_along(): return lax.ppermute(x, axis, pairs)  18 us
    ppermute x4, starting transfers between devices, passed_along(): return lax.ppermute(x, axis, pairs)  10.9 us
    all_to_all x1, starting transfers between devices, shards(): lax.all_to_all(spread.reshape(RADIX, 2 * LANES, LANES), 'facet', split_ax...  8.39 us
    pallas_call x1, Pallas kernels, shards(): call(columns, shape((RADIX, 2 * LANES + 8, LANES)), [HBM] * 5, HBM, [pltp...  8.08 us
    all_to_all x1, starting transfers between devices, shards(): lax.all_to_all(back, 'facet', split_axis=0, concat_axis=0, tiled=True)  7.41 us
    ppermute x3, starting transfers between devices, shards(): pieces[k] = lax.ppermute(pieces[k], 'chan', pairs)  5.66 us
    unnamed x26, local copies, waits for them, and re-layouts  5.38 us
  transfers between devices with their start and end apart: 11, of which 6 were waited for; matrix products, arithmetic and copies ran while one was open for 0% of the time, Pallas kernels for 15%

profile of v9, /device:TPU:8, one launch (start us, length us, event | category | flops | bytes accessed | tf_op | source)
XLA Modules:
  0.0 111.4 jit_solution(17747977167395369244)
XLA Ops:
  0.6 3.7 %rows_forward.1 = f32[16,2,16,8,128]{4,3,2,1,0:T(8,128)} custom-call(f32[128,2048]{1,0:T(8,128)} %bitcast.7, f32[2,24,128]{2,1,0:T(8,128)} %constant.11.clone.twiddle_in.twiddle), custom_call_target="tpu_custom_call" | custom-call | tf_op jit(solution)/shard_map/rows_forward/pallas_call | solution.py:516
  4.4 0.0 copy-start.3
  4.4 0.0 copy-start
  4.4 8.4 %all-to-all-start = ((f32[16,256,128]{2,1,0:T(8,128)}), f32[16,256,128]{2,1,0:T(8,128)}, u32[]{:S(2)}, u32[]{:S(2)}) async-start(f32[16,256,128]{2,1,0:T(8,128)} %bitcast.9), calls=%async_computation | async-start | bytes 4194304 | tf_op jit(solution)/shard_map/all_to_all | solution.py:532
  12.8 0.0 copy-done.3
  12.8 1.0 cross_ready.1
  13.8 1.5 %collective-permute-start = (f32[128,512]{1,0:T(8,128)}, f32[128,512]{1,0:T(8,128)S(1)}, u32[]{:S(2)}, u32[]{:S(2)}) collective-permute-start(f32[128,512]{1,0:T(8,128)} %get-tuple-element.25), channel_id=1, source_target_pairs={{0,32},{16,48},{32,64},{48,80},{64,96},{80,112},{96,0},{112,16},{1... | collective-permute-start | bytes 786440 | tf_op jit(solution)/shard_map/ppermute | solution.py:549
  15.2 2.7 %collective-permute-start.1 = (f32[128,512]{1,0:T(8,128)}, f32[128,512]{1,0:T(8,128)S(1)}, u32[]{:S(2)}, u32[]{:S(2)}) collective-permute-start(f32[128,512]{1,0:T(8,128)} %get-tuple-element.26), channel_id=1, source_target_pairs={{0,64},{16,80},{32,96},{48,112},{64,0},{80,16},{96,32},{112,48},{1... | collective-permute-start | bytes 786440 | tf_op jit(solution)/shard_map/ppermute | solution.py:549
  18.0 1.4 %collective-permute-start.2 = (f32[128,512]{1,0:T(8,128)}, f32[128,512]{1,0:T(8,128)}, u32[]{:S(2)}, u32[]{:S(2)}) collective-permute-start(f32[128,512]{1,0:T(8,128)} %get-tuple-element.27), channel_id=1, source_target_pairs={{0,96},{16,112},{32,0},{48,16},{64,32},{80,48},{96,64},{112,80},{1... | collective-permute-start | bytes 786440 | tf_op jit(solution)/shard_map/ppermute | solution.py:549
  19.4 0.0 copy-done
  19.4 0.2 dual_edges.1
  19.6 1.9 %collective-permute-start.3 = (f32[8,256]{1,0:T(8,128)S(1)}, f32[8,256]{1,0:T(8,128)S(1)}, u32[]{:S(2)}, u32[]{:S(2)}) collective-permute-start(f32[8,256]{1,0:T(8,128)S(1)} %get-tuple-element.29.refs_5_), channel_id=1, source_target_pairs={{0,1},{1,2},{2,3},{3,4},{4,5},{5,6},{6,7},{7,8},{8,9},{9,10},{10,1... | collective-permute-start | bytes 24584 | tf_op jit(solution)/shard_map/ppermute | solution.py:486
  21.5 2.9 %collective-permute-start.4 = (f32[8,128]{1,0:T(8,128)S(1)}, f32[8,128]{1,0:T(8,128)S(1)}, u32[]{:S(2)}, u32[]{:S(2)}) collective-permute-start(f32[8,128]{1,0:T(8,128)S(1)} %get-tuple-element.31), channel_id=1, source_target_pairs={{0,16},{16,32},{32,48},{48,64},{64,80},{80,96},{96,112},{1,17},{17... | collective-permute-start | bytes 12296 | tf_op jit(solution)/shard_map/ppermute | solution.py:486
  24.4 4.2 %data_prepared.1 = (bf16[3,16,128,128]{3,2,1,0:T(8,128)(2,1)}, bf16[768,256]{1,0:T(8,128)(2,1)}, bf16[768,256]{1,0:T(8,128)(2,1)}) custom-call(bf16[2048,128]{1,0:T(8,128)(2,1)} %bitcast.11, bf16[2,2048,128]{2,1,0:T(8,128)(2,1)} %bitcast.10, bf16[128,128]{1,0:T(8,128)(2,1)} %constant.10.clone.place, f32[2,24,128]{2,1,0:T(8,128)} %constant.11.clone.twiddle_in.twiddle), custom_call_target="tpu_custom_call" | custom-call | tf_op jit(solution)/shard_map/data_prepared/pallas_call | solution.py:550
  28.6 0.0 collective-permute-done.refs_1_
  28.6 1.5 %collective-permute-done.1.refs_2_ = f32[128,512]{1,0:T(8,128)S(1)} collective-permute-done((f32[128,512]{1,0:T(8,128)}, f32[128,512]{1,0:T(8,128)S(1)}, u32[]{:S(2)}, u32[]{:S(2)}) %collective-permute-start.1) | collective-permute-done | bytes 262176 | tf_op jit(solution)/shard_map/ppermute | solution.py:549
  30.1 0.0 collective-permute-done.2.refs_3_
  30.1 1.5 %copy-done.2 = bf16[3,16,128,128]{3,2,1,0:T(8,128)(2,1)S(1)} copy-done((bf16[3,16,128,128]{3,2,1,0:T(8,128)(2,1)S(1)}, bf16[3,16,128,128]{3,2,1,0:T(8,128)(2,1)}, u32[]{:S(2)}) %copy-start.2) | copy-done | bytes 1572888
  31.7 1.8 %swap_ready.1 = (f32[4,64,256]{2,1,0:T(8,128)}, f32[4,64,256]{2,1,0:T(8,128)}) custom-call(s32[1]{0:T(128)} %bitcast.2.where, f32[128,512]{1,0:T(8,128)S(1)} %get-tuple-element.24.refs_0_, f32[128,512]{1,0:T(8,128)S(1)} %collective-permute-done.refs_1_, f32[128,512]{1,0:T(8,128)S(1)} %collective-permute-done.1.refs_2_, ...), custom_call_target="tpu_custom_call" | custom-call | tf_op jit(solution)/shard_map/swap_ready/pallas_call | solution.py:562
  33.4 1.1 collective-permute-start.5
  34.5 0.0 collective-permute-done.4.refs_8_
  34.5 5.7 %collective-permute-done.3.refs_7_ = f32[8,256]{1,0:T(8,128)S(1)} collective-permute-done((f32[8,256]{1,0:T(8,128)S(1)}, f32[8,256]{1,0:T(8,128)S(1)}, u32[]{:S(2)}, u32[]{:S(2)}) %collective-permute-start.3) | collective-permute-done | bytes 8224 | tf_op jit(solution)/shard_map/ppermute | solution.py:486
  40.2 0.5 all-to-all-done.cols_in
  40.7 1.0 collective-permute-start.6
  41.7 8.1 %columns.1.value = f32[16,264,128]{2,1,0:T(8,128)} custom-call(f32[16,256,128]{2,1,0:T(8,128)} %all-to-all-done.cols_in, bf16[3,16,128,128]{3,2,1,0:T(8,128)(2,1)} %get-tuple-element.35.refs_4_.data_in, f32[2,24,128]{2,1,0:T(8,128)} %constant.11.clone.twiddle_in.twiddle, bf16[768,256]{1,0:T(8,128)(2,1)} %get-tuple-element.36.forward_in, ...), custom_call_target="tpu_custom_call" | custom-call | tf_op jit(solution)/shard_map/columns/pallas_call | solution.py:578
  49.8 0.0 copy-done.8
  49.8 0.0 copy-done.10
  49.8 0.0 collective-permute-done.5.refs_4_
  49.8 0.0 collective-permute-done.6.refs_5_
  49.9 1.3 %fusion.after = f32[8,128]{1,0:T(8,128)} fusion(f32[4,64,256]{2,1,0:T(8,128)} %collective-permute-done.6.refs_5_, f32[4,64,256]{2,1,0:T(8,128)} %collective-permute-done.5.refs_4_), kind=kLoop, calls=%fused_computation.1 | loop fusion | flops 1024 | bytes 12288 | tf_op jit(solution)/shard_map/add | solution.py:604
  51.1 7.4 %all-to-all-start.1 = ((f32[16,264,128]{2,1,0:T(8,128)}), f32[16,264,128]{2,1,0:T(8,128)S(1)}, u32[]{:S(2)}, u32[]{:S(2)}) async-start(f32[16,264,128]{2,1,0:T(8,128)} %tied.1), calls=%async_computation.1 | async-start | bytes 4325376 | tf_op jit(solution)/shard_map/all_to_all | solution.py:605
  58.6 0.0 copy-done.1
  58.6 0.0 copy-start.9
  58.6 0.9 copy-done.9
  59.5 0.9 copy-done.11
  60.5 1.9 %tile_ready.1 = (f32[8,128,256]{2,1,0:T(8,128)S(1)}, f32[8,128,256]{2,1,0:T(8,128)S(1)}, f32[8,256]{1,0:T(8,128)S(1)}, f32[8,128]{1,0:T(8,128)S(1)}) custom-call(s32[1]{0:T(128)} %bitcast.2.where, f32[128,512]{1,0:T(8,128)S(1)} %get-tuple-element.24.refs_0_, f32[128,512]{1,0:T(8,128)S(1)} %copy-done.9, f32[128,512]{1,0:T(8,128)S(1)} %copy-done.11, ...), custom_call_target="tpu_custom_call" | custom-call | tf_op jit(solution)/shard_map/tile_ready/pallas_call | solution.py:606
  62.4 1.0 copy-done.4
  63.3 1.0 copy-done.6
  64.3 4.6 %collective-permute-start.7 = (f32[8,256]{1,0:T(8,128)S(1)}, f32[8,256]{1,0:T(8,128)S(1)}, u32[]{:S(2)}, u32[]{:S(2)}) collective-permute-start(f32[8,256]{1,0:T(8,128)S(1)} %get-tuple-element.42), channel_id=1, source_target_pairs={{1,0},{2,1},{3,2},{4,3},{5,4},{6,5},{7,6},{8,7},{9,8},{10,9},{11,1... | collective-permute-start | bytes 24584 | tf_op jit(solution)/shard_map/ppermute | solution.py:486
  68.9 1.5 %collective-permute-start.8 = (f32[8,128]{1,0:T(8,128)S(1)}, f32[8,128]{1,0:T(8,128)S(1)}, u32[]{:S(2)}, u32[]{:S(2)}) collective-permute-start(f32[8,128]{1,0:T(8,128)S(1)} %get-tuple-element.43), channel_id=1, source_target_pairs={{16,0},{32,16},{48,32},{64,48},{80,64},{96,80},{112,96},{17,1},{33... | collective-permute-start | bytes 12296 | tf_op jit(solution)/shard_map/ppermute | solution.py:486
  70.4 4.6 %collective-permute-done.8.after_two.right = f32[8,128]{1,0:T(8,128)S(1)} collective-permute-done((f32[8,128]{1,0:T(8,128)S(1)}, f32[8,128]{1,0:T(8,128)S(1)}, u32[]{:S(2)}, u32[]{:S(2)}) %collective-permute-start.8) | collective-permute-done | bytes 4128 | tf_op jit(solution)/shard_map/ppermute | solution.py:486
  75.0 7.7 %collective-permute-done.7.after_one.below = f32[8,256]{1,0:T(8,128)S(1)} collective-permute-done((f32[8,256]{1,0:T(8,128)S(1)}, f32[8,256]{1,0:T(8,128)S(1)}, u32[]{:S(2)}, u32[]{:S(2)}) %collective-permute-start.7) | collective-permute-done | bytes 8224 | tf_op jit(solution)/shard_map/ppermute | solution.py:486
  82.7 4.2 %all-to-all-done.1.lines = f32[16,264,128]{2,1,0:T(8,128)S(1)} async-done(((f32[16,264,128]{2,1,0:T(8,128)}), f32[16,264,128]{2,1,0:T(8,128)S(1)}, u32[]{:S(2)}, u32[]{:S(2)}) %all-to-all-start.1) | async-done | bytes 2162720 | tf_op jit(solution)/shard_map/all_to_all | solution.py:605
  86.9 0.0 copy-done.12
  86.9 1.5 %rows_back.1 = f32[8,136,256]{2,1,0:T(8,128)S(1)} custom-call(f32[16,264,128]{2,1,0:T(8,128)S(1)} %all-to-all-done.1.lines, f32[2,24,128]{2,1,0:T(8,128)S(1)} %copy-done.12, f32[8,256]{1,0:T(8,128)S(1)} %collective-permute-done.7.after_one.below, f32[8,128]{1,0:T(8,128)S(1)} %collective-permute-done.8.after_two.right), custom_call_target="tpu_custom_call" | custom-call | tf_op jit(solution)/shard_map/rows_back/pallas_call | solution.py:620
  88.4 20.5 %all_to_all.15.gradient = f32[8,136,256]{2,1,0:T(8,128)S(1)} all-to-all(f32[8,136,256]{2,1,0:T(8,128)S(1)} %rows_back.1), channel_id=1, replica_groups=mesh['chan'=8,'facet'=16] {'chan'}, dimensions={0} | all-to-all | bytes 2228224 | tf_op jit(solution)/shard_map/all_to_all | solution.py:631
  108.9 0.0 copy-done.7
  108.9 2.3 %finish.1 = (f32[8,128,256]{2,1,0:T(8,128)}, bf16[8,2,128,256]{3,2,1,0:T(8,128)(2,1)}) custom-call(f32[8,136,256]{2,1,0:T(8,128)S(1)} %all_to_all.15.gradient, f32[8,128,256]{2,1,0:T(8,128)S(1)} %copy-done.5, f32[8,128,256]{2,1,0:T(8,128)S(1)} %copy-done.7, bf16[8,2,128,256]{3,2,1,0:T(8,128)(2,1)S(1)} %copy-done.1, ...), custom_call_target="tpu_custom_call" | custom-call | tf_op jit(solution)/shard_map/finish/pallas_call | solution.py:632
  (12 shorter events, 0.0 us)
Async XLA Ops:
  4.4 8.4 %copy-start.3 = (f32[1,128,2048]{2,1,0:T(8,128)S(1)}, f32[1,128,2048]{2,1,0:T(8,128)}, u32[]{:S(2)}) copy-start(f32[1,128,2048]{2,1,0:T(8,128)} %param.6) | copy-start | bytes 3145732
  4.4 15.1 %copy-start = (bf16[8,2,128,256]{3,2,1,0:T(8,128)(2,1)S(1)}, bf16[8,2,128,256]{3,2,1,0:T(8,128)(2,1)}, u32[]{:S(2)}) copy-start(bf16[8,2,128,256]{3,2,1,0:T(8,128)(2,1)} %dual.3) | copy-start | bytes 3145732
  4.4 36.3 %all-to-all-start = ((f32[16,256,128]{2,1,0:T(8,128)}), f32[16,256,128]{2,1,0:T(8,128)}, u32[]{:S(2)}, u32[]{:S(2)}) async-start(f32[16,256,128]{2,1,0:T(8,128)} %bitcast.9), calls=%async_computation | async-start | bytes 4194304 | tf_op jit(solution)/shard_map/all_to_all | solution.py:532
  13.8 14.9 %collective-permute-start = (f32[128,512]{1,0:T(8,128)}, f32[128,512]{1,0:T(8,128)S(1)}, u32[]{:S(2)}, u32[]{:S(2)}) collective-permute-start(f32[128,512]{1,0:T(8,128)} %get-tuple-element.25), channel_id=1, source_target_pairs={{0,32},{16,48},{32,64},{48,80},{64,96},{80,112},{96,0},{112,16},{1... | collective-permute-start | bytes 786440 | tf_op jit(solution)/shard_map/ppermute | solution.py:549
  15.2 14.9 %collective-permute-start.1 = (f32[128,512]{1,0:T(8,128)}, f32[128,512]{1,0:T(8,128)S(1)}, u32[]{:S(2)}, u32[]{:S(2)}) collective-permute-start(f32[128,512]{1,0:T(8,128)} %get-tuple-element.26), channel_id=1, source_target_pairs={{0,64},{16,80},{32,96},{48,112},{64,0},{80,16},{96,32},{112,48},{1... | collective-permute-start | bytes 786440 | tf_op jit(solution)/shard_map/ppermute | solution.py:549
  18.0 12.2 %collective-permute-start.2 = (f32[128,512]{1,0:T(8,128)}, f32[128,512]{1,0:T(8,128)}, u32[]{:S(2)}, u32[]{:S(2)}) collective-permute-start(f32[128,512]{1,0:T(8,128)} %get-tuple-element.27), channel_id=1, source_target_pairs={{0,96},{16,112},{32,0},{48,16},{64,32},{80,48},{96,64},{112,80},{1... | collective-permute-start | bytes 786440 | tf_op jit(solution)/shard_map/ppermute | solution.py:549
  19.6 20.6 %collective-permute-start.3 = (f32[8,256]{1,0:T(8,128)S(1)}, f32[8,256]{1,0:T(8,128)S(1)}, u32[]{:S(2)}, u32[]{:S(2)}) collective-permute-start(f32[8,256]{1,0:T(8,128)S(1)} %get-tuple-element.29.refs_5_), channel_id=1, source_target_pairs={{0,1},{1,2},{2,3},{3,4},{4,5},{5,6},{6,7},{7,8},{8,9},{9,10},{10,1... | collective-permute-start | bytes 24584 | tf_op jit(solution)/shard_map/ppermute | solution.py:486
  21.5 13.0 %collective-permute-start.4 = (f32[8,128]{1,0:T(8,128)S(1)}, f32[8,128]{1,0:T(8,128)S(1)}, u32[]{:S(2)}, u32[]{:S(2)}) collective-permute-start(f32[8,128]{1,0:T(8,128)S(1)} %get-tuple-element.31), channel_id=1, source_target_pairs={{0,16},{16,32},{32,48},{48,64},{64,80},{80,96},{96,112},{1,17},{17... | collective-permute-start | bytes 12296 | tf_op jit(solution)/shard_map/ppermute | solution.py:486
  28.6 21.2 %copy-start.8 = (f32[128,512]{1,0:T(8,128)}, f32[128,512]{1,0:T(8,128)S(1)}, u32[]{:S(2)}) copy-start(f32[128,512]{1,0:T(8,128)S(1)} %collective-permute-done.refs_1_) | copy-start | bytes 786436
  30.1 19.7 %copy-start.10 = (f32[128,512]{1,0:T(8,128)}, f32[128,512]{1,0:T(8,128)S(1)}, u32[]{:S(2)}) copy-start(f32[128,512]{1,0:T(8,128)S(1)} %collective-permute-done.1.refs_2_) | copy-start | bytes 786436
  30.1 1.5 %copy-start.2 = (bf16[3,16,128,128]{3,2,1,0:T(8,128)(2,1)S(1)}, bf16[3,16,128,128]{3,2,1,0:T(8,128)(2,1)}, u32[]{:S(2)}) copy-start(bf16[3,16,128,128]{3,2,1,0:T(8,128)(2,1)} %get-tuple-element.35.refs_4_.data_in) | copy-start | bytes 4718596
  33.4 16.4 %collective-permute-start.5 = (f32[4,64,256]{2,1,0:T(8,128)}, f32[4,64,256]{2,1,0:T(8,128)}, u32[]{:S(2)}, u32[]{:S(2)}) collective-permute-start(f32[4,64,256]{2,1,0:T(8,128)} %get-tuple-element.38), channel_id=1, source_target_pairs={{0,16},{16,0},{32,48},{48,32},{64,80},{80,64},{96,112},{112,96},{1... | collective-permute-start | bytes 786440 | tf_op jit(solution)/shard_map/ppermute | solution.py:570
  40.7 9.2 %collective-permute-start.6 = (f32[4,64,256]{2,1,0:T(8,128)}, f32[4,64,256]{2,1,0:T(8,128)}, u32[]{:S(2)}, u32[]{:S(2)}) collective-permute-start(f32[4,64,256]{2,1,0:T(8,128)} %get-tuple-element.39), channel_id=1, source_target_pairs={{0,16},{16,0},{32,48},{48,32},{64,80},{80,64},{96,112},{112,96},{1... | collective-permute-start | bytes 786440 | tf_op jit(solution)/shard_map/ppermute | solution.py:574
  51.1 7.4 %copy-start.1 = (bf16[8,2,128,256]{3,2,1,0:T(8,128)(2,1)S(1)}, bf16[8,2,128,256]{3,2,1,0:T(8,128)(2,1)}, u32[]{:S(2)}) copy-start(bf16[8,2,128,256]{3,2,1,0:T(8,128)(2,1)} %dual.3) | copy-start | bytes 3145732
  51.1 35.7 %all-to-all-start.1 = ((f32[16,264,128]{2,1,0:T(8,128)}), f32[16,264,128]{2,1,0:T(8,128)S(1)}, u32[]{:S(2)}, u32[]{:S(2)}) async-start(f32[16,264,128]{2,1,0:T(8,128)} %tied.1), calls=%async_computation.1 | async-start | bytes 4325376 | tf_op jit(solution)/shard_map/all_to_all | solution.py:605
  58.6 1.0 copy-start.9
  59.5 0.9 copy-start.11
  60.5 26.4 %copy-start.12 = (f32[2,24,128]{2,1,0:T(8,128)S(1)}, f32[2,24,128]{2,1,0:T(8,128)}, u32[]{:S(2)}) copy-start(f32[2,24,128]{2,1,0:T(8,128)} %constant.11.clone.twiddle_in.twiddle) | copy-start | bytes 73732
  62.4 1.0 copy-start.4
  63.3 1.0 copy-start.6
  64.3 18.4 %collective-permute-start.7 = (f32[8,256]{1,0:T(8,128)S(1)}, f32[8,256]{1,0:T(8,128)S(1)}, u32[]{:S(2)}, u32[]{:S(2)}) collective-permute-start(f32[8,256]{1,0:T(8,128)S(1)} %get-tuple-element.42), channel_id=1, source_target_pairs={{1,0},{2,1},{3,2},{4,3},{5,4},{6,5},{7,6},{8,7},{9,8},{10,9},{11,1... | collective-permute-start | bytes 24584 | tf_op jit(solution)/shard_map/ppermute | solution.py:486
  68.9 6.1 %collective-permute-start.8 = (f32[8,128]{1,0:T(8,128)S(1)}, f32[8,128]{1,0:T(8,128)S(1)}, u32[]{:S(2)}, u32[]{:S(2)}) collective-permute-start(f32[8,128]{1,0:T(8,128)S(1)} %get-tuple-element.43), channel_id=1, source_target_pairs={{16,0},{32,16},{48,32},{64,48},{80,64},{96,80},{112,96},{17,1},{33... | collective-permute-start | bytes 12296 | tf_op jit(solution)/shard_map/ppermute | solution.py:486
  86.9 22.0 %copy-start.5 = (f32[8,128,256]{2,1,0:T(8,128)S(1)}, f32[8,128,256]{2,1,0:T(8,128)}, u32[]{:S(2)}) copy-start(f32[8,128,256]{2,1,0:T(8,128)} %copy-done.4) | copy-start | bytes 3145732
  86.9 22.0 %copy-start.7 = (f32[8,128,256]{2,1,0:T(8,128)S(1)}, f32[8,128,256]{2,1,0:T(8,128)}, u32[]{:S(2)}) copy-start(f32[8,128,256]{2,1,0:T(8,128)} %copy-done.6) | copy-start | bytes 3145732

commit v10 on v9

--- a/solution.py
+++ b/solution.py
@@ -217,7 +217,8 @@
         copy.wait()
 
 
-def data_prepared(weights, measured, place, twiddle, out, forward, inverse, held):
+def data_prepared(weights, measured, place, twiddle, out, forward, inverse, mark, held):
+    mark[...] = jnp.zeros_like(mark)
     fill_table(forward, twiddle, -1, False)
     fill_table(inverse, twiddle, 1, False)
     for n in range(3):
@@ -547,15 +548,16 @@
     for k in range(1, 4):
         pairs = [(2 * x + z, (x + k) % 4 * 2 + z) for x in range(4) for z in range(2)]
         pieces[k] = lax.ppermute(pieces[k], "chan", pairs)
-    data, forward, inverse = call(
+    data, forward, inverse, mark = call(
         data_prepared,
         (
             shape((3, RADIX, LANES, LANES), bf16),
             shape((768, 256), bf16),
             shape((768, 256), bf16),
+            shape((8, LANES)),
         ),
         [VM] * 4,
-        (VM,) * 3,
+        (VM,) * 4,
         [pltpu.VMEM((GRID, LANES), f32)],
         63,
     )(weights[0], measured[0], place, twiddle)
@@ -565,7 +567,7 @@
         [SM] + [VM] * 4 + [ANY] * 2,
         (VM, VM),
         [],
-    )(where, *pieces, data, last_row)
+    )(where, *pieces, mark, last_row)
     other_zl = [(i, i ^ 1) for i in range(8)]
     early = lax.ppermute(early, "chan", other_zl)
     cols, late, above, left, data, forward, inverse = lax.optimization_barrier(

time: 114 us -> 113 us (level)
  no operation moved by 1% of the time
where the time goes in v10:
time: 113 us; the launch traced here: 111 us
  starting transfers between devices  34.5 us (31%)
  waiting for transfers between devices  25 us (22%)
  Pallas kernels  24.6 us (22%)
  blocking collectives  20.3 us (18%)
  local copies, waits for them, and re-layouts  4.56 us (4%)
  other arithmetic  1.28 us (1%)
    all_to_all x1, blocking collectives, shards(): lax.all_to_all(slopes, 'chan', split_axis=0, concat_axis=0, tiled=True)  20.3 us
    ppermute x4, waiting for transfers between devices, passed_along(): return lax.ppermute(x, axis, pairs)  18.8 us
    ppermute x4, starting transfers between devices, passed_along(): return lax.ppermute(x, axis, pairs)  10.9 us
    all_to_all x1, starting transfers between devices, shards(): lax.all_to_all(spread.reshape(RADIX, 2 * LANES, LANES), 'facet', split_ax...  8.39 us
    pallas_call x1, Pallas kernels, shards(): call(columns, shape((RADIX, 2 * LANES + 8, LANES)), [HBM] * 5, HBM, [pltp...  8.08 us
    all_to_all x1, starting transfers between devices, shards(): lax.all_to_all(back, 'facet', split_axis=0, concat_axis=0, tiled=True)  7.43 us
    ppermute x3, starting transfers between devices, shards(): pieces[k] = lax.ppermute(pieces[k], 'chan', pairs)  5.66 us
    unnamed x26, local copies, waits for them, and re-layouts  4.56 us
  transfers between devices with their start and end apart: 11, of which 6 were waited for; matrix products, arithmetic and copies ran while one was open for 0% of the time, Pallas kernels for 15%

profile of v10, /device:TPU:8, one launch (start us, length us, event | category | flops | bytes accessed | tf_op | source)
XLA Modules:
  0.0 111.2 jit_solution(18147367973449530291)
XLA Ops:
  0.6 3.7 %rows_forward.1 = f32[16,2,16,8,128]{4,3,2,1,0:T(8,128)} custom-call(f32[128,2048]{1,0:T(8,128)} %bitcast.7, f32[2,24,128]{2,1,0:T(8,128)} %constant.11.clone.twiddle_in.twiddle), custom_call_target="tpu_custom_call" | custom-call | tf_op jit(solution)/shard_map/rows_forward/pallas_call | solution.py:517
  4.4 0.0 copy-start.2
  4.4 0.0 copy-start
  4.4 8.4 %all-to-all-start = ((f32[16,256,128]{2,1,0:T(8,128)}), f32[16,256,128]{2,1,0:T(8,128)}, u32[]{:S(2)}, u32[]{:S(2)}) async-start(f32[16,256,128]{2,1,0:T(8,128)} %bitcast.9), calls=%async_computation | async-start | bytes 4194304 | tf_op jit(solution)/shard_map/all_to_all | solution.py:533
  12.8 0.0 copy-done.2
  12.8 1.0 cross_ready.1
  13.8 1.5 %collective-permute-start = (f32[128,512]{1,0:T(8,128)}, f32[128,512]{1,0:T(8,128)S(1)}, u32[]{:S(2)}, u32[]{:S(2)}) collective-permute-start(f32[128,512]{1,0:T(8,128)} %get-tuple-element.26), channel_id=1, source_target_pairs={{0,32},{16,48},{32,64},{48,80},{64,96},{80,112},{96,0},{112,16},{1... | collective-permute-start | bytes 786440 | tf_op jit(solution)/shard_map/ppermute | solution.py:550
  15.2 2.7 %collective-permute-start.1 = (f32[128,512]{1,0:T(8,128)}, f32[128,512]{1,0:T(8,128)S(1)}, u32[]{:S(2)}, u32[]{:S(2)}) collective-permute-start(f32[128,512]{1,0:T(8,128)} %get-tuple-element.27), channel_id=1, source_target_pairs={{0,64},{16,80},{32,96},{48,112},{64,0},{80,16},{96,32},{112,48},{1... | collective-permute-start | bytes 786440 | tf_op jit(solution)/shard_map/ppermute | solution.py:550
  18.0 1.4 %collective-permute-start.2 = (f32[128,512]{1,0:T(8,128)}, f32[128,512]{1,0:T(8,128)}, u32[]{:S(2)}, u32[]{:S(2)}) collective-permute-start(f32[128,512]{1,0:T(8,128)} %get-tuple-element.28), channel_id=1, source_target_pairs={{0,96},{16,112},{32,0},{48,16},{64,32},{80,48},{96,64},{112,80},{1... | collective-permute-start | bytes 786440 | tf_op jit(solution)/shard_map/ppermute | solution.py:550
  19.4 0.0 copy-done
  19.4 0.2 dual_edges.1
  19.6 1.9 %collective-permute-start.3 = (f32[8,256]{1,0:T(8,128)S(1)}, f32[8,256]{1,0:T(8,128)S(1)}, u32[]{:S(2)}, u32[]{:S(2)}) collective-permute-start(f32[8,256]{1,0:T(8,128)S(1)} %get-tuple-element.30.refs_5_), channel_id=1, source_target_pairs={{0,1},{1,2},{2,3},{3,4},{4,5},{5,6},{6,7},{7,8},{8,9},{9,10},{10,1... | collective-permute-start | bytes 24584 | tf_op jit(solution)/shard_map/ppermute | solution.py:487
  21.5 2.9 %collective-permute-start.4 = (f32[8,128]{1,0:T(8,128)S(1)}, f32[8,128]{1,0:T(8,128)S(1)}, u32[]{:S(2)}, u32[]{:S(2)}) collective-permute-start(f32[8,128]{1,0:T(8,128)S(1)} %get-tuple-element.32), channel_id=1, source_target_pairs={{0,16},{16,32},{32,48},{48,64},{64,80},{80,96},{96,112},{1,17},{17... | collective-permute-start | bytes 12296 | tf_op jit(solution)/shard_map/ppermute | solution.py:487
  24.4 4.2 %data_prepared.1 = (bf16[3,16,128,128]{3,2,1,0:T(8,128)(2,1)}, bf16[768,256]{1,0:T(8,128)(2,1)}, bf16[768,256]{1,0:T(8,128)(2,1)}, f32[8,128]{1,0:T(8,128)}) custom-call(bf16[2048,128]{1,0:T(8,128)(2,1)} %bitcast.11, bf16[2,2048,128]{2,1,0:T(8,128)(2,1)} %bitcast.10, bf16[128,128]{1,0:T(8,128)(2,1)} %constant.10.clone.place, ...), custom_call_target="tpu_custom_call" | custom-call | tf_op jit(solution)/shard_map/data_prepared/pallas_call | solution.py:551
  28.6 0.0 collective-permute-done.refs_1_
  28.6 1.5 %collective-permute-done.1.refs_2_ = f32[128,512]{1,0:T(8,128)S(1)} collective-permute-done((f32[128,512]{1,0:T(8,128)}, f32[128,512]{1,0:T(8,128)S(1)}, u32[]{:S(2)}, u32[]{:S(2)}) %collective-permute-start.1) | collective-permute-done | bytes 262176 | tf_op jit(solution)/shard_map/ppermute | solution.py:550
  30.1 0.0 collective-permute-done.2.refs_3_
  30.1 0.7 copy-done.12
  30.8 1.8 %swap_ready.1 = (f32[4,64,256]{2,1,0:T(8,128)}, f32[4,64,256]{2,1,0:T(8,128)}) custom-call(s32[1]{0:T(128)} %bitcast.2.where, f32[128,512]{1,0:T(8,128)S(1)} %get-tuple-element.25.refs_0_, f32[128,512]{1,0:T(8,128)S(1)} %collective-permute-done.refs_1_, f32[128,512]{1,0:T(8,128)S(1)} %collective-permute-done.1.refs_2_, ...), custom_call_target="tpu_custom_call" | custom-call | tf_op jit(solution)/shard_map/swap_ready/pallas_call | solution.py:564
  32.6 1.1 collective-permute-start.5
  33.7 0.0 collective-permute-done.4.refs_8_
  33.7 6.5 %collective-permute-done.3.refs_7_ = f32[8,256]{1,0:T(8,128)S(1)} collective-permute-done((f32[8,256]{1,0:T(8,128)S(1)}, f32[8,256]{1,0:T(8,128)S(1)}, u32[]{:S(2)}, u32[]{:S(2)}) %collective-permute-start.3) | collective-permute-done | bytes 8224 | tf_op jit(solution)/shard_map/ppermute | solution.py:487
  40.2 0.5 all-to-all-done.cols_in
  40.7 1.0 collective-permute-start.6
  41.7 8.1 %columns.1.value = f32[16,264,128]{2,1,0:T(8,128)} custom-call(f32[16,256,128]{2,1,0:T(8,128)} %all-to-all-done.cols_in, bf16[3,16,128,128]{3,2,1,0:T(8,128)(2,1)} %get-tuple-element.37.data_in, f32[2,24,128]{2,1,0:T(8,128)} %constant.11.clone.twiddle_in.twiddle, bf16[768,256]{1,0:T(8,128)(2,1)} %get-tuple-element.38.forward_in, ...), custom_call_target="tpu_custom_call" | custom-call | tf_op jit(solution)/shard_map/columns/pallas_call | solution.py:580
  49.8 0.0 copy-done.7
  49.8 0.0 copy-done.9
  49.8 0.0 collective-permute-done.5.refs_4_
  49.8 0.0 collective-permute-done.6.refs_5_
  49.8 1.3 %fusion.after = f32[8,128]{1,0:T(8,128)} fusion(f32[4,64,256]{2,1,0:T(8,128)} %collective-permute-done.6.refs_5_, f32[4,64,256]{2,1,0:T(8,128)} %collective-permute-done.5.refs_4_), kind=kLoop, calls=%fused_computation.1 | loop fusion | flops 1024 | bytes 12288 | tf_op jit(solution)/shard_map/add | solution.py:606
  51.1 7.4 %all-to-all-start.1 = ((f32[16,264,128]{2,1,0:T(8,128)}), f32[16,264,128]{2,1,0:T(8,128)S(1)}, u32[]{:S(2)}, u32[]{:S(2)}) async-start(f32[16,264,128]{2,1,0:T(8,128)} %tied.1), calls=%async_computation.1 | async-start | bytes 4325376 | tf_op jit(solution)/shard_map/all_to_all | solution.py:607
  58.6 0.0 copy-done.1
  58.6 0.0 copy-start.8
  58.6 0.9 copy-done.8
  59.5 0.9 copy-done.10
  60.5 1.9 %tile_ready.1 = (f32[8,128,256]{2,1,0:T(8,128)S(1)}, f32[8,128,256]{2,1,0:T(8,128)S(1)}, f32[8,256]{1,0:T(8,128)S(1)}, f32[8,128]{1,0:T(8,128)S(1)}) custom-call(s32[1]{0:T(128)} %bitcast.2.where, f32[128,512]{1,0:T(8,128)S(1)} %get-tuple-element.25.refs_0_, f32[128,512]{1,0:T(8,128)S(1)} %copy-done.8, f32[128,512]{1,0:T(8,128)S(1)} %copy-done.10, ...), custom_call_target="tpu_custom_call" | custom-call | tf_op jit(solution)/shard_map/tile_ready/pallas_call | solution.py:608
  62.4 1.0 copy-done.3
  63.3 1.0 copy-done.5
  64.3 4.6 %collective-permute-start.7 = (f32[8,256]{1,0:T(8,128)S(1)}, f32[8,256]{1,0:T(8,128)S(1)}, u32[]{:S(2)}, u32[]{:S(2)}) collective-permute-start(f32[8,256]{1,0:T(8,128)S(1)} %get-tuple-element.44), channel_id=1, source_target_pairs={{1,0},{2,1},{3,2},{4,3},{5,4},{6,5},{7,6},{8,7},{9,8},{10,9},{11,1... | collective-permute-start | bytes 24584 | tf_op jit(solution)/shard_map/ppermute | solution.py:487
  68.9 1.5 %collective-permute-start.8 = (f32[8,128]{1,0:T(8,128)S(1)}, f32[8,128]{1,0:T(8,128)S(1)}, u32[]{:S(2)}, u32[]{:S(2)}) collective-permute-start(f32[8,128]{1,0:T(8,128)S(1)} %get-tuple-element.45), channel_id=1, source_target_pairs={{16,0},{32,16},{48,32},{64,48},{80,64},{96,80},{112,96},{17,1},{33... | collective-permute-start | bytes 12296 | tf_op jit(solution)/shard_map/ppermute | solution.py:487
  70.4 4.6 %collective-permute-done.8.after_two.right = f32[8,128]{1,0:T(8,128)S(1)} collective-permute-done((f32[8,128]{1,0:T(8,128)S(1)}, f32[8,128]{1,0:T(8,128)S(1)}, u32[]{:S(2)}, u32[]{:S(2)}) %collective-permute-start.8) | collective-permute-done | bytes 4128 | tf_op jit(solution)/shard_map/ppermute | solution.py:487
  75.0 7.7 %collective-permute-done.7.after_one.below = f32[8,256]{1,0:T(8,128)S(1)} collective-permute-done((f32[8,256]{1,0:T(8,128)S(1)}, f32[8,256]{1,0:T(8,128)S(1)}, u32[]{:S(2)}, u32[]{:S(2)}) %collective-permute-start.7) | collective-permute-done | bytes 8224 | tf_op jit(solution)/shard_map/ppermute | solution.py:487
  82.7 4.2 %all-to-all-done.1.lines = f32[16,264,128]{2,1,0:T(8,128)S(1)} async-done(((f32[16,264,128]{2,1,0:T(8,128)}), f32[16,264,128]{2,1,0:T(8,128)S(1)}, u32[]{:S(2)}, u32[]{:S(2)}) %all-to-all-start.1) | async-done | bytes 2162720 | tf_op jit(solution)/shard_map/all_to_all | solution.py:607
  86.9 0.0 copy-done.11
  86.9 1.5 %rows_back.1 = f32[8,136,256]{2,1,0:T(8,128)S(1)} custom-call(f32[16,264,128]{2,1,0:T(8,128)S(1)} %all-to-all-done.1.lines, f32[2,24,128]{2,1,0:T(8,128)S(1)} %copy-done.11, f32[8,256]{1,0:T(8,128)S(1)} %collective-permute-done.7.after_one.below, f32[8,128]{1,0:T(8,128)S(1)} %collective-permute-done.8.after_two.right), custom_call_target="tpu_custom_call" | custom-call | tf_op jit(solution)/shard_map/rows_back/pallas_call | solution.py:622
  88.4 20.3 %all_to_all.15.gradient = f32[8,136,256]{2,1,0:T(8,128)S(1)} all-to-all(f32[8,136,256]{2,1,0:T(8,128)S(1)} %rows_back.1), channel_id=1, replica_groups=mesh['chan'=8,'facet'=16] {'chan'}, dimensions={0} | all-to-all | bytes 2228224 | tf_op jit(solution)/shard_map/all_to_all | solution.py:633
  108.7 0.0 copy-done.4
  108.8 2.3 %finish.1 = (f32[8,128,256]{2,1,0:T(8,128)}, bf16[8,2,128,256]{3,2,1,0:T(8,128)(2,1)}) custom-call(f32[8,136,256]{2,1,0:T(8,128)S(1)} %all_to_all.15.gradient, f32[8,128,256]{2,1,0:T(8,128)S(1)} %copy-done.4, f32[8,128,256]{2,1,0:T(8,128)S(1)} %copy-done.6, bf16[8,2,128,256]{3,2,1,0:T(8,128)(2,1)S(1)} %copy-done.1, ...), custom_call_target="tpu_custom_call" | custom-call | tf_op jit(solution)/shard_map/finish/pallas_call | solution.py:634
  (12 shorter events, 0.0 us)
Async XLA Ops:
  4.4 8.4 %copy-start.2 = (f32[1,128,2048]{2,1,0:T(8,128)S(1)}, f32[1,128,2048]{2,1,0:T(8,128)}, u32[]{:S(2)}) copy-start(f32[1,128,2048]{2,1,0:T(8,128)} %param.6) | copy-start | bytes 3145732
  4.4 15.1 %copy-start = (bf16[8,2,128,256]{3,2,1,0:T(8,128)(2,1)S(1)}, bf16[8,2,128,256]{3,2,1,0:T(8,128)(2,1)}, u32[]{:S(2)}) copy-start(bf16[8,2,128,256]{3,2,1,0:T(8,128)(2,1)} %dual.3) | copy-start | bytes 3145732
  4.4 36.3 %all-to-all-start = ((f32[16,256,128]{2,1,0:T(8,128)}), f32[16,256,128]{2,1,0:T(8,128)}, u32[]{:S(2)}, u32[]{:S(2)}) async-start(f32[16,256,128]{2,1,0:T(8,128)} %bitcast.9), calls=%async_computation | async-start | bytes 4194304 | tf_op jit(solution)/shard_map/all_to_all | solution.py:533
  13.8 14.9 %collective-permute-start = (f32[128,512]{1,0:T(8,128)}, f32[128,512]{1,0:T(8,128)S(1)}, u32[]{:S(2)}, u32[]{:S(2)}) collective-permute-start(f32[128,512]{1,0:T(8,128)} %get-tuple-element.26), channel_id=1, source_target_pairs={{0,32},{16,48},{32,64},{48,80},{64,96},{80,112},{96,0},{112,16},{1... | collective-permute-start | bytes 786440 | tf_op jit(solution)/shard_map/ppermute | solution.py:550
  15.2 14.9 %collective-permute-start.1 = (f32[128,512]{1,0:T(8,128)}, f32[128,512]{1,0:T(8,128)S(1)}, u32[]{:S(2)}, u32[]{:S(2)}) collective-permute-start(f32[128,512]{1,0:T(8,128)} %get-tuple-element.27), channel_id=1, source_target_pairs={{0,64},{16,80},{32,96},{48,112},{64,0},{80,16},{96,32},{112,48},{1... | collective-permute-start | bytes 786440 | tf_op jit(solution)/shard_map/ppermute | solution.py:550
  18.0 12.2 %collective-permute-start.2 = (f32[128,512]{1,0:T(8,128)}, f32[128,512]{1,0:T(8,128)}, u32[]{:S(2)}, u32[]{:S(2)}) collective-permute-start(f32[128,512]{1,0:T(8,128)} %get-tuple-element.28), channel_id=1, source_target_pairs={{0,96},{16,112},{32,0},{48,16},{64,32},{80,48},{96,64},{112,80},{1... | collective-permute-start | bytes 786440 | tf_op jit(solution)/shard_map/ppermute | solution.py:550
  19.6 20.6 %collective-permute-start.3 = (f32[8,256]{1,0:T(8,128)S(1)}, f32[8,256]{1,0:T(8,128)S(1)}, u32[]{:S(2)}, u32[]{:S(2)}) collective-permute-start(f32[8,256]{1,0:T(8,128)S(1)} %get-tuple-element.30.refs_5_), channel_id=1, source_target_pairs={{0,1},{1,2},{2,3},{3,4},{4,5},{5,6},{6,7},{7,8},{8,9},{9,10},{10,1... | collective-permute-start | bytes 24584 | tf_op jit(solution)/shard_map/ppermute | solution.py:487
  21.5 12.2 %collective-permute-start.4 = (f32[8,128]{1,0:T(8,128)S(1)}, f32[8,128]{1,0:T(8,128)S(1)}, u32[]{:S(2)}, u32[]{:S(2)}) collective-permute-start(f32[8,128]{1,0:T(8,128)S(1)} %get-tuple-element.32), channel_id=1, source_target_pairs={{0,16},{16,32},{32,48},{48,64},{64,80},{80,96},{96,112},{1,17},{17... | collective-permute-start | bytes 12296 | tf_op jit(solution)/shard_map/ppermute | solution.py:487
  28.6 21.2 %copy-start.7 = (f32[128,512]{1,0:T(8,128)}, f32[128,512]{1,0:T(8,128)S(1)}, u32[]{:S(2)}) copy-start(f32[128,512]{1,0:T(8,128)S(1)} %collective-permute-done.refs_1_) | copy-start | bytes 786436
  30.1 19.7 %copy-start.9 = (f32[128,512]{1,0:T(8,128)}, f32[128,512]{1,0:T(8,128)S(1)}, u32[]{:S(2)}) copy-start(f32[128,512]{1,0:T(8,128)S(1)} %collective-permute-done.1.refs_2_) | copy-start | bytes 786436
  30.1 0.7 copy-start.12
  32.6 17.2 %collective-permute-start.5 = (f32[4,64,256]{2,1,0:T(8,128)}, f32[4,64,256]{2,1,0:T(8,128)}, u32[]{:S(2)}, u32[]{:S(2)}) collective-permute-start(f32[4,64,256]{2,1,0:T(8,128)} %get-tuple-element.40), channel_id=1, source_target_pairs={{0,16},{16,0},{32,48},{48,32},{64,80},{80,64},{96,112},{112,96},{1... | collective-permute-start | bytes 786440 | tf_op jit(solution)/shard_map/ppermute | solution.py:572
  40.7 9.2 %collective-permute-start.6 = (f32[4,64,256]{2,1,0:T(8,128)}, f32[4,64,256]{2,1,0:T(8,128)}, u32[]{:S(2)}, u32[]{:S(2)}) collective-permute-start(f32[4,64,256]{2,1,0:T(8,128)} %get-tuple-element.41), channel_id=1, source_target_pairs={{0,16},{16,0},{32,48},{48,32},{64,80},{80,64},{96,112},{112,96},{1... | collective-permute-start | bytes 786440 | tf_op jit(solution)/shard_map/ppermute | solution.py:576
  51.1 7.4 %copy-start.1 = (bf16[8,2,128,256]{3,2,1,0:T(8,128)(2,1)S(1)}, bf16[8,2,128,256]{3,2,1,0:T(8,128)(2,1)}, u32[]{:S(2)}) copy-start(bf16[8,2,128,256]{3,2,1,0:T(8,128)(2,1)} %dual.3) | copy-start | bytes 3145732
  51.1 35.8 %all-to-all-start.1 = ((f32[16,264,128]{2,1,0:T(8,128)}), f32[16,264,128]{2,1,0:T(8,128)S(1)}, u32[]{:S(2)}, u32[]{:S(2)}) async-start(f32[16,264,128]{2,1,0:T(8,128)} %tied.1), calls=%async_computation.1 | async-start | bytes 4325376 | tf_op jit(solution)/shard_map/all_to_all | solution.py:607
  58.6 1.0 copy-start.8
  59.5 0.9 copy-start.10
  60.5 26.4 %copy-start.11 = (f32[2,24,128]{2,1,0:T(8,128)S(1)}, f32[2,24,128]{2,1,0:T(8,128)}, u32[]{:S(2)}) copy-start(f32[2,24,128]{2,1,0:T(8,128)} %constant.11.clone.twiddle_in.twiddle) | copy-start | bytes 73732
  62.4 1.0 copy-start.3
  63.3 1.0 copy-start.5
  64.3 18.4 %collective-permute-start.7 = (f32[8,256]{1,0:T(8,128)S(1)}, f32[8,256]{1,0:T(8,128)S(1)}, u32[]{:S(2)}, u32[]{:S(2)}) collective-permute-start(f32[8,256]{1,0:T(8,128)S(1)} %get-tuple-element.44), channel_id=1, source_target_pairs={{1,0},{2,1},{3,2},{4,3},{5,4},{6,5},{7,6},{8,7},{9,8},{10,9},{11,1... | collective-permute-start | bytes 24584 | tf_op jit(solution)/shard_map/ppermute | solution.py:487
  68.9 6.1 %collective-permute-start.8 = (f32[8,128]{1,0:T(8,128)S(1)}, f32[8,128]{1,0:T(8,128)S(1)}, u32[]{:S(2)}, u32[]{:S(2)}) collective-permute-start(f32[8,128]{1,0:T(8,128)S(1)} %get-tuple-element.45), channel_id=1, source_target_pairs={{16,0},{32,16},{48,32},{64,48},{80,64},{96,80},{112,96},{17,1},{33... | collective-permute-start | bytes 12296 | tf_op jit(solution)/shard_map/ppermute | solution.py:487
  86.9 21.9 %copy-start.4 = (f32[8,128,256]{2,1,0:T(8,128)S(1)}, f32[8,128,256]{2,1,0:T(8,128)}, u32[]{:S(2)}) copy-start(f32[8,128,256]{2,1,0:T(8,128)} %copy-done.3) | copy-start | bytes 3145732
  86.9 21.9 %copy-start.6 = (f32[8,128,256]{2,1,0:T(8,128)S(1)}, f32[8,128,256]{2,1,0:T(8,128)}, u32[]{:S(2)}) copy-start(f32[8,128,256]{2,1,0:T(8,128)} %copy-done.5) | copy-start | bytes 3145732

commit v11 on v10

--- a/solution.py
+++ b/solution.py
@@ -323,6 +323,10 @@
     edges.wait()
 
 
+def arrived(early, late, out):
+    out[...] = early[0, :8, :LANES] + late[0, :8, :LANES]
+
+
 def tied(value, after, out):
     pass
 
@@ -596,6 +600,7 @@
         ],
         63,
     )(cols, data, twiddle, forward, inverse)
+    mark = call(arrived, shape((8, LANES)), [VM, VM], VM, [])(early, late)
     back = pl.pallas_call(
         tied,
         out_shape=shape((RADIX, 2 * LANES + 8, LANES)),
@@ -603,7 +608,7 @@
         out_specs=ANY,
         input_output_aliases={0: 0},
         name="tied",
-    )(back, early[0, :8, :LANES] + late[0, :8, :LANES])
+    )(back, mark)
     lines = lax.all_to_all(back, "facet", split_axis=0, concat_axis=0, tiled=True)
     for_image, for_ahead, first_row, first_column = call(
         tile_ready,

time: 113 us -> 113 us (level)
  local copies, waits for them, and re-layouts: 4.56 us -> 7.14 us
  waiting for transfers between devices: 25 us -> 23.3 us
  other arithmetic: 1.28 us -> 0 us
    unnamed x26 -> x36, local copies, waits for them, and re-layouts: 4.56 us -> 7.14 us
    ppermute x4, waiting for transfers between devices: 18.8 us -> 17.1 us  [passed_along(): return lax.ppermute(x, axis, pairs)]
    add x1 -> x0, other arithmetic: 1.28 us -> none  [shards(): early[0, :8, :LANES] + late[0, :8, :LANES]]
where the time goes in v11:
time: 113 us; the launch traced here: 110 us
  starting transfers between devices  34.4 us (30%)
  Pallas kernels  24.4 us (22%)
  waiting for transfers between devices  23.3 us (21%)
  blocking collectives  20.3 us (18%)
  local copies, waits for them, and re-layouts  7.14 us (6%)
    all_to_all x1, blocking collectives, shards(): lax.all_to_all(slopes, 'chan', split_axis=0, concat_axis=0, tiled=True)  20.3 us
    ppermute x4, waiting for transfers between devices, passed_along(): return lax.ppermute(x, axis, pairs)  17.1 us
    ppermute x4, starting transfers between devices, passed_along(): return lax.ppermute(x, axis, pairs)  10.9 us
    all_to_all x1, starting transfers between devices, shards(): lax.all_to_all(spread.reshape(RADIX, 2 * LANES, LANES), 'facet', split_ax...  8.39 us
    pallas_call x1, Pallas kernels, shards(): call(columns, shape((RADIX, 2 * LANES + 8, LANES)), [HBM] * 5, HBM, [pltp...  8.1 us
    all_to_all x1, starting transfers between devices, shards(): lax.all_to_all(back, 'facet', split_axis=0, concat_axis=0, tiled=True)  7.32 us
    unnamed x36, local copies, waits for them, and re-layouts  7.14 us
    ppermute x3, starting transfers between devices, shards(): pieces[k] = lax.ppermute(pieces[k], 'chan', pairs)  5.66 us
  transfers between devices with their start and end apart: 11, of which 6 were waited for; matrix products, arithmetic and copies ran while one was open for 0% of the time, Pallas kernels for 15%

profile of v11, /device:TPU:8, one launch (start us, length us, event | category | flops | bytes accessed | tf_op | source)
XLA Modules:
  0.0 110.5 jit_solution(12230920209332452300)
XLA Ops:
  0.6 3.7 %rows_forward.1 = f32[16,2,16,8,128]{4,3,2,1,0:T(8,128)} custom-call(f32[128,2048]{1,0:T(8,128)} %bitcast.5, f32[2,24,128]{2,1,0:T(8,128)} %constant.11.clone.twiddle_in.twiddle), custom_call_target="tpu_custom_call" | custom-call | tf_op jit(solution)/shard_map/rows_forward/pallas_call | solution.py:521
  4.3 0.0 copy-start.2
  4.3 0.0 copy-start
  4.3 8.4 %all-to-all-start = ((f32[16,256,128]{2,1,0:T(8,128)}), f32[16,256,128]{2,1,0:T(8,128)}, u32[]{:S(2)}, u32[]{:S(2)}) async-start(f32[16,256,128]{2,1,0:T(8,128)} %bitcast.7), calls=%async_computation | async-start | bytes 4194304 | tf_op jit(solution)/shard_map/all_to_all | solution.py:537
  12.7 0.0 copy-done.2
  12.7 0.9 cross_ready.1
  13.7 1.5 %collective-permute-start = (f32[128,512]{1,0:T(8,128)}, f32[128,512]{1,0:T(8,128)S(1)}, u32[]{:S(2)}, u32[]{:S(2)}) collective-permute-start(f32[128,512]{1,0:T(8,128)} %get-tuple-element.26), channel_id=1, source_target_pairs={{0,32},{16,48},{32,64},{48,80},{64,96},{80,112},{96,0},{112,16},{1... | collective-permute-start | bytes 786440 | tf_op jit(solution)/shard_map/ppermute | solution.py:554
  15.2 2.7 %collective-permute-start.1 = (f32[128,512]{1,0:T(8,128)}, f32[128,512]{1,0:T(8,128)S(1)}, u32[]{:S(2)}, u32[]{:S(2)}) collective-permute-start(f32[128,512]{1,0:T(8,128)} %get-tuple-element.27), channel_id=1, source_target_pairs={{0,64},{16,80},{32,96},{48,112},{64,0},{80,16},{96,32},{112,48},{1... | collective-permute-start | bytes 786440 | tf_op jit(solution)/shard_map/ppermute | solution.py:554
  17.9 1.4 %collective-permute-start.2 = (f32[128,512]{1,0:T(8,128)}, f32[128,512]{1,0:T(8,128)}, u32[]{:S(2)}, u32[]{:S(2)}) collective-permute-start(f32[128,512]{1,0:T(8,128)} %get-tuple-element.28), channel_id=1, source_target_pairs={{0,96},{16,112},{32,0},{48,16},{64,32},{80,48},{96,64},{112,80},{1... | collective-permute-start | bytes 786440 | tf_op jit(solution)/shard_map/ppermute | solution.py:554
  19.4 0.0 copy-done
  19.4 0.2 dual_edges.1
  19.5 1.9 %collective-permute-start.3 = (f32[8,256]{1,0:T(8,128)S(1)}, f32[8,256]{1,0:T(8,128)S(1)}, u32[]{:S(2)}, u32[]{:S(2)}) collective-permute-start(f32[8,256]{1,0:T(8,128)S(1)} %get-tuple-element.30.refs_5_), channel_id=1, source_target_pairs={{0,1},{1,2},{2,3},{3,4},{4,5},{5,6},{6,7},{7,8},{8,9},{9,10},{10,1... | collective-permute-start | bytes 24584 | tf_op jit(solution)/shard_map/ppermute | solution.py:491
  21.5 2.9 %collective-permute-start.4 = (f32[8,128]{1,0:T(8,128)S(1)}, f32[8,128]{1,0:T(8,128)S(1)}, u32[]{:S(2)}, u32[]{:S(2)}) collective-permute-start(f32[8,128]{1,0:T(8,128)S(1)} %get-tuple-element.32), channel_id=1, source_target_pairs={{0,16},{16,32},{32,48},{48,64},{64,80},{80,96},{96,112},{1,17},{17... | collective-permute-start | bytes 12296 | tf_op jit(solution)/shard_map/ppermute | solution.py:491
  24.4 4.2 %data_prepared.1 = (bf16[3,16,128,128]{3,2,1,0:T(8,128)(2,1)}, bf16[768,256]{1,0:T(8,128)(2,1)}, bf16[768,256]{1,0:T(8,128)(2,1)}, f32[8,128]{1,0:T(8,128)}) custom-call(bf16[2048,128]{1,0:T(8,128)(2,1)} %bitcast.9, bf16[2,2048,128]{2,1,0:T(8,128)(2,1)} %bitcast.8, bf16[128,128]{1,0:T(8,128)(2,1)} %constant.10.clone.place, ...), custom_call_target="tpu_custom_call" | custom-call | tf_op jit(solution)/shard_map/data_prepared/pallas_call | solution.py:555
  28.6 0.0 collective-permute-done.refs_1_
  28.6 1.5 %collective-permute-done.1.refs_2_ = f32[128,512]{1,0:T(8,128)S(1)} collective-permute-done((f32[128,512]{1,0:T(8,128)}, f32[128,512]{1,0:T(8,128)S(1)}, u32[]{:S(2)}, u32[]{:S(2)}) %collective-permute-start.1) | collective-permute-done | bytes 262176 | tf_op jit(solution)/shard_map/ppermute | solution.py:554
  30.1 0.0 collective-permute-done.2.refs_3_
  30.1 0.7 copy-done.17
  30.8 1.8 %swap_ready.1 = (f32[4,64,256]{2,1,0:T(8,128)}, f32[4,64,256]{2,1,0:T(8,128)}) custom-call(s32[1]{0:T(128)} %bitcast.2.where, f32[128,512]{1,0:T(8,128)S(1)} %get-tuple-element.25.refs_0_, f32[128,512]{1,0:T(8,128)S(1)} %collective-permute-done.refs_1_, f32[128,512]{1,0:T(8,128)S(1)} %collective-permute-done.1.refs_2_, ...), custom_call_target="tpu_custom_call" | custom-call | tf_op jit(solution)/shard_map/swap_ready/pallas_call | solution.py:568
  32.5 1.1 collective-permute-start.5
  33.6 0.0 collective-permute-done.4.refs_8_
  33.6 6.6 %collective-permute-done.3.refs_7_ = f32[8,256]{1,0:T(8,128)S(1)} collective-permute-done((f32[8,256]{1,0:T(8,128)S(1)}, f32[8,256]{1,0:T(8,128)S(1)}, u32[]{:S(2)}, u32[]{:S(2)}) %collective-permute-start.3) | collective-permute-done | bytes 8224 | tf_op jit(solution)/shard_map/ppermute | solution.py:491
  40.1 0.5 all-to-all-done.cols_in
  40.6 1.0 collective-permute-start.6
  41.7 8.1 %columns.1.value = f32[16,264,128]{2,1,0:T(8,128)} custom-call(f32[16,256,128]{2,1,0:T(8,128)} %all-to-all-done.cols_in, bf16[3,16,128,128]{3,2,1,0:T(8,128)(2,1)} %get-tuple-element.37.data_in, f32[2,24,128]{2,1,0:T(8,128)} %constant.11.clone.twiddle_in.twiddle, bf16[768,256]{1,0:T(8,128)(2,1)} %get-tuple-element.38.forward_in, ...), custom_call_target="tpu_custom_call" | custom-call | tf_op jit(solution)/shard_map/columns/pallas_call | solution.py:584
  49.8 0.0 collective-permute-done.5.early.refs_4_
  49.8 0.0 collective-permute-done.6.late.refs_5_
  49.8 0.0 copy-start.7
  49.8 0.0 copy-start.16
  49.9 0.6 copy-done.16
  50.5 0.0 copy-done.7
  50.5 7.3 %all-to-all-start.1 = ((f32[16,264,128]{2,1,0:T(8,128)}), f32[16,264,128]{2,1,0:T(8,128)S(1)}, u32[]{:S(2)}, u32[]{:S(2)}) async-start(f32[16,264,128]{2,1,0:T(8,128)} %tied.1), calls=%async_computation.1 | async-start | bytes 4325376 | tf_op jit(solution)/shard_map/all_to_all | solution.py:612
  57.8 0.0 copy-start.8
  57.9 0.9 copy-done.8
  58.8 0.9 copy-done.10
  59.8 0.9 copy-done.12
  60.7 0.9 copy-done.14
  61.7 1.7 %tile_ready.1 = (f32[8,128,256]{2,1,0:T(8,128)S(1)}, f32[8,128,256]{2,1,0:T(8,128)S(1)}, f32[8,256]{1,0:T(8,128)S(1)}, f32[8,128]{1,0:T(8,128)S(1)}) custom-call(s32[1]{0:T(128)} %bitcast.2.where, f32[128,512]{1,0:T(8,128)S(1)} %copy-done.10, f32[128,512]{1,0:T(8,128)S(1)} %copy-done.12, f32[128,512]{1,0:T(8,128)S(1)} %copy-done.14, ...), custom_call_target="tpu_custom_call" | custom-call | tf_op jit(solution)/shard_map/tile_ready/pallas_call | solution.py:613
  63.4 1.0 copy-done.3
  64.4 1.0 copy-done.5
  65.4 4.6 %collective-permute-start.7 = (f32[8,256]{1,0:T(8,128)S(1)}, f32[8,256]{1,0:T(8,128)S(1)}, u32[]{:S(2)}, u32[]{:S(2)}) collective-permute-start(f32[8,256]{1,0:T(8,128)S(1)} %get-tuple-element.44), channel_id=1, source_target_pairs={{1,0},{2,1},{3,2},{4,3},{5,4},{6,5},{7,6},{8,7},{9,8},{10,9},{11,1... | collective-permute-start | bytes 24584 | tf_op jit(solution)/shard_map/ppermute | solution.py:491
  70.0 1.5 %collective-permute-start.8 = (f32[8,128]{1,0:T(8,128)S(1)}, f32[8,128]{1,0:T(8,128)S(1)}, u32[]{:S(2)}, u32[]{:S(2)}) collective-permute-start(f32[8,128]{1,0:T(8,128)S(1)} %get-tuple-element.45), channel_id=1, source_target_pairs={{16,0},{32,16},{48,32},{64,48},{80,64},{96,80},{112,96},{17,1},{33... | collective-permute-start | bytes 12296 | tf_op jit(solution)/shard_map/ppermute | solution.py:491
  71.5 4.4 %collective-permute-done.8.after_two.right = f32[8,128]{1,0:T(8,128)S(1)} collective-permute-done((f32[8,128]{1,0:T(8,128)S(1)}, f32[8,128]{1,0:T(8,128)S(1)}, u32[]{:S(2)}, u32[]{:S(2)}) %collective-permute-start.8) | collective-permute-done | bytes 4128 | tf_op jit(solution)/shard_map/ppermute | solution.py:491
  75.9 6.1 %collective-permute-done.7.after_one.below = f32[8,256]{1,0:T(8,128)S(1)} collective-permute-done((f32[8,256]{1,0:T(8,128)S(1)}, f32[8,256]{1,0:T(8,128)S(1)}, u32[]{:S(2)}, u32[]{:S(2)}) %collective-permute-start.7) | collective-permute-done | bytes 8224 | tf_op jit(solution)/shard_map/ppermute | solution.py:491
  82.0 4.2 %all-to-all-done.1.lines = f32[16,264,128]{2,1,0:T(8,128)S(1)} async-done(((f32[16,264,128]{2,1,0:T(8,128)}), f32[16,264,128]{2,1,0:T(8,128)S(1)}, u32[]{:S(2)}, u32[]{:S(2)}) %all-to-all-start.1) | async-done | bytes 2162720 | tf_op jit(solution)/shard_map/all_to_all | solution.py:612
  86.2 1.5 %rows_back.1 = f32[8,136,256]{2,1,0:T(8,128)S(1)} custom-call(f32[16,264,128]{2,1,0:T(8,128)S(1)} %all-to-all-done.1.lines, f32[2,24,128]{2,1,0:T(8,128)S(1)} %copy-done.15, f32[8,256]{1,0:T(8,128)S(1)} %collective-permute-done.7.after_one.below, f32[8,128]{1,0:T(8,128)S(1)} %collective-permute-done.8.after_two.right), custom_call_target="tpu_custom_call" | custom-call | tf_op jit(solution)/shard_map/rows_back/pallas_call | solution.py:627
  87.7 20.3 %all_to_all.15.gradient = f32[8,136,256]{2,1,0:T(8,128)S(1)} all-to-all(f32[8,136,256]{2,1,0:T(8,128)S(1)} %rows_back.1), channel_id=1, replica_groups=mesh['chan'=8,'facet'=16] {'chan'}, dimensions={0} | all-to-all | bytes 2228224 | tf_op jit(solution)/shard_map/all_to_all | solution.py:638
  108.0 2.3 %finish.1 = (f32[8,128,256]{2,1,0:T(8,128)}, bf16[8,2,128,256]{3,2,1,0:T(8,128)(2,1)}) custom-call(f32[8,136,256]{2,1,0:T(8,128)S(1)} %all_to_all.15.gradient, f32[8,128,256]{2,1,0:T(8,128)S(1)} %copy-done.4, f32[8,128,256]{2,1,0:T(8,128)S(1)} %copy-done.6, bf16[8,2,128,256]{3,2,1,0:T(8,128)(2,1)S(1)} %copy-done.1, ...), custom_call_target="tpu_custom_call" | custom-call | tf_op jit(solution)/shard_map/finish/pallas_call | solution.py:639
  (22 shorter events, 0.0 us)
Async XLA Ops:
  4.3 8.4 %copy-start.2 = (f32[1,128,2048]{2,1,0:T(8,128)S(1)}, f32[1,128,2048]{2,1,0:T(8,128)}, u32[]{:S(2)}) copy-start(f32[1,128,2048]{2,1,0:T(8,128)} %param.6) | copy-start | bytes 3145732
  4.3 15.0 %copy-start = (bf16[8,2,128,256]{3,2,1,0:T(8,128)(2,1)S(1)}, bf16[8,2,128,256]{3,2,1,0:T(8,128)(2,1)}, u32[]{:S(2)}) copy-start(bf16[8,2,128,256]{3,2,1,0:T(8,128)(2,1)} %dual.3) | copy-start | bytes 3145732
  4.3 36.3 %all-to-all-start = ((f32[16,256,128]{2,1,0:T(8,128)}), f32[16,256,128]{2,1,0:T(8,128)}, u32[]{:S(2)}, u32[]{:S(2)}) async-start(f32[16,256,128]{2,1,0:T(8,128)} %bitcast.7), calls=%async_computation | async-start | bytes 4194304 | tf_op jit(solution)/shard_map/all_to_all | solution.py:537
  13.7 27.0 %copy-start.9 = (f32[128,512]{1,0:T(8,128)}, f32[128,512]{1,0:T(8,128)S(1)}, u32[]{:S(2)}) copy-start(f32[128,512]{1,0:T(8,128)S(1)} %get-tuple-element.25.refs_0_) | copy-start | bytes 786436
  13.7 14.9 %collective-permute-start = (f32[128,512]{1,0:T(8,128)}, f32[128,512]{1,0:T(8,128)S(1)}, u32[]{:S(2)}, u32[]{:S(2)}) collective-permute-start(f32[128,512]{1,0:T(8,128)} %get-tuple-element.26), channel_id=1, source_target_pairs={{0,32},{16,48},{32,64},{48,80},{64,96},{80,112},{96,0},{112,16},{1... | collective-permute-start | bytes 786440 | tf_op jit(solution)/shard_map/ppermute | solution.py:554
  15.2 14.9 %collective-permute-start.1 = (f32[128,512]{1,0:T(8,128)}, f32[128,512]{1,0:T(8,128)S(1)}, u32[]{:S(2)}, u32[]{:S(2)}) collective-permute-start(f32[128,512]{1,0:T(8,128)} %get-tuple-element.27), channel_id=1, source_target_pairs={{0,64},{16,80},{32,96},{48,112},{64,0},{80,16},{96,32},{112,48},{1... | collective-permute-start | bytes 786440 | tf_op jit(solution)/shard_map/ppermute | solution.py:554
  17.9 12.2 %collective-permute-start.2 = (f32[128,512]{1,0:T(8,128)}, f32[128,512]{1,0:T(8,128)}, u32[]{:S(2)}, u32[]{:S(2)}) collective-permute-start(f32[128,512]{1,0:T(8,128)} %get-tuple-element.28), channel_id=1, source_target_pairs={{0,96},{16,112},{32,0},{48,16},{64,32},{80,48},{96,64},{112,80},{1... | collective-permute-start | bytes 786440 | tf_op jit(solution)/shard_map/ppermute | solution.py:554
  19.5 20.6 %collective-permute-start.3 = (f32[8,256]{1,0:T(8,128)S(1)}, f32[8,256]{1,0:T(8,128)S(1)}, u32[]{:S(2)}, u32[]{:S(2)}) collective-permute-start(f32[8,256]{1,0:T(8,128)S(1)} %get-tuple-element.30.refs_5_), channel_id=1, source_target_pairs={{0,1},{1,2},{2,3},{3,4},{4,5},{5,6},{6,7},{7,8},{8,9},{9,10},{10,1... | collective-permute-start | bytes 24584 | tf_op jit(solution)/shard_map/ppermute | solution.py:491
  21.5 12.1 %collective-permute-start.4 = (f32[8,128]{1,0:T(8,128)S(1)}, f32[8,128]{1,0:T(8,128)S(1)}, u32[]{:S(2)}, u32[]{:S(2)}) collective-permute-start(f32[8,128]{1,0:T(8,128)S(1)} %get-tuple-element.32), channel_id=1, source_target_pairs={{0,16},{16,32},{32,48},{48,64},{64,80},{80,96},{96,112},{1,17},{17... | collective-permute-start | bytes 12296 | tf_op jit(solution)/shard_map/ppermute | solution.py:491
  28.6 21.2 %copy-start.11 = (f32[128,512]{1,0:T(8,128)}, f32[128,512]{1,0:T(8,128)S(1)}, u32[]{:S(2)}) copy-start(f32[128,512]{1,0:T(8,128)S(1)} %collective-permute-done.refs_1_) | copy-start | bytes 786436
  30.1 2.4 %copy-start.13 = (f32[128,512]{1,0:T(8,128)}, f32[128,512]{1,0:T(8,128)S(1)}, u32[]{:S(2)}) copy-start(f32[128,512]{1,0:T(8,128)S(1)} %collective-permute-done.1.refs_2_) | copy-start | bytes 786436
  30.1 0.7 copy-start.17
  32.5 17.3 %collective-permute-start.5 = (f32[4,64,256]{2,1,0:T(8,128)}, f32[4,64,256]{2,1,0:T(8,128)S(1)}, u32[]{:S(2)}, u32[]{:S(2)}) collective-permute-start(f32[4,64,256]{2,1,0:T(8,128)} %get-tuple-element.40), channel_id=1, source_target_pairs={{0,16},{16,0},{32,48},{48,32},{64,80},{80,64},{96,112},{112,96},{1... | collective-permute-start | bytes 786440 | tf_op jit(solution)/shard_map/ppermute | solution.py:576
  40.6 9.2 %collective-permute-start.6 = (f32[4,64,256]{2,1,0:T(8,128)}, f32[4,64,256]{2,1,0:T(8,128)S(1)}, u32[]{:S(2)}, u32[]{:S(2)}) collective-permute-start(f32[4,64,256]{2,1,0:T(8,128)} %get-tuple-element.41), channel_id=1, source_target_pairs={{0,16},{16,0},{32,48},{48,32},{64,80},{80,64},{96,112},{112,96},{1... | collective-permute-start | bytes 786440 | tf_op jit(solution)/shard_map/ppermute | solution.py:580
  49.8 0.7 copy-start.7
  49.8 0.6 copy-start.16
  50.5 7.3 %copy-start.1 = (bf16[8,2,128,256]{3,2,1,0:T(8,128)(2,1)S(1)}, bf16[8,2,128,256]{3,2,1,0:T(8,128)(2,1)}, u32[]{:S(2)}) copy-start(bf16[8,2,128,256]{3,2,1,0:T(8,128)(2,1)} %dual.3) | copy-start | bytes 3145732
  50.5 35.7 %all-to-all-start.1 = ((f32[16,264,128]{2,1,0:T(8,128)}), f32[16,264,128]{2,1,0:T(8,128)S(1)}, u32[]{:S(2)}, u32[]{:S(2)}) async-start(f32[16,264,128]{2,1,0:T(8,128)} %tied.1), calls=%async_computation.1 | async-start | bytes 4325376 | tf_op jit(solution)/shard_map/all_to_all | solution.py:612
  57.8 1.0 copy-start.8
  58.8 0.9 copy-start.10
  59.8 0.9 copy-start.12
  60.7 0.9 copy-start.14
  61.7 24.5 %copy-start.15 = (f32[2,24,128]{2,1,0:T(8,128)S(1)}, f32[2,24,128]{2,1,0:T(8,128)}, u32[]{:S(2)}) copy-start(f32[2,24,128]{2,1,0:T(8,128)} %constant.11.clone.twiddle_in.twiddle) | copy-start | bytes 73732
  63.4 1.0 copy-start.3
  64.4 1.0 copy-start.5
  65.4 16.6 %collective-permute-start.7 = (f32[8,256]{1,0:T(8,128)S(1)}, f32[8,256]{1,0:T(8,128)S(1)}, u32[]{:S(2)}, u32[]{:S(2)}) collective-permute-start(f32[8,256]{1,0:T(8,128)S(1)} %get-tuple-element.44), channel_id=1, source_target_pairs={{1,0},{2,1},{3,2},{4,3},{5,4},{6,5},{7,6},{8,7},{9,8},{10,9},{11,1... | collective-permute-start | bytes 24584 | tf_op jit(solution)/shard_map/ppermute | solution.py:491
  70.0 5.9 %collective-permute-start.8 = (f32[8,128]{1,0:T(8,128)S(1)}, f32[8,128]{1,0:T(8,128)S(1)}, u32[]{:S(2)}, u32[]{:S(2)}) collective-permute-start(f32[8,128]{1,0:T(8,128)S(1)} %get-tuple-element.45), channel_id=1, source_target_pairs={{16,0},{32,16},{48,32},{64,48},{80,64},{96,80},{112,96},{17,1},{33... | collective-permute-start | bytes 12296 | tf_op jit(solution)/shard_map/ppermute | solution.py:491
  86.2 21.9 %copy-start.4 = (f32[8,128,256]{2,1,0:T(8,128)S(1)}, f32[8,128,256]{2,1,0:T(8,128)}, u32[]{:S(2)}) copy-start(f32[8,128,256]{2,1,0:T(8,128)} %copy-done.3) | copy-start | bytes 3145732
  86.2 21.9 %copy-start.6 = (f32[8,128,256]{2,1,0:T(8,128)S(1)}, f32[8,128,256]{2,1,0:T(8,128)}, u32[]{:S(2)}) copy-start(f32[8,128,256]{2,1,0:T(8,128)} %copy-done.5) | copy-start | bytes 3145732

commit v12 on v11

--- a/solution.py
+++ b/solution.py
@@ -568,10 +568,10 @@
     early, late = call(
         swap_ready,
         (shape((4, EARLY, 256)), shape((4, LANES - EARLY, 256))),
-        [SM] + [VM] * 4 + [ANY] * 2,
+        [SM] + [VM] * 4 + [HBM, ANY],
         (VM, VM),
         [],
-    )(where, *pieces, mark, last_row)
+    )(where, *pieces, pltpu.with_memory_space_constraint(mark, pltpu.HBM), last_row)
     other_zl = [(i, i ^ 1) for i in range(8)]
     early = lax.ppermute(early, "chan", other_zl)
     cols, late, above, left, data, forward, inverse = lax.optimization_barrier(

time: 113 us -> 112 us (level)
    unnamed x36 -> x34, local copies, waits for them, and re-layouts: 7.14 us -> 6.46 us
where the time goes in v12:
time: 112 us; the launch traced here: 110 us
  starting transfers between devices  34.4 us (31%)
  Pallas kernels  24.5 us (22%)
  waiting for transfers between devices  23.9 us (21%)
  blocking collectives  20.3 us (18%)
  local copies, waits for them, and re-layouts  6.46 us (6%)
    all_to_all x1, blocking collectives, shards(): lax.all_to_all(slopes, 'chan', split_axis=0, concat_axis=0, tiled=True)  20.3 us
    ppermute x4, waiting for transfers between devices, passed_along(): return lax.ppermute(x, axis, pairs)  17.6 us
    ppermute x4, starting transfers between devices, passed_along(): return lax.ppermute(x, axis, pairs)  10.9 us
    all_to_all x1, starting transfers between devices, shards(): lax.all_to_all(spread.reshape(RADIX, 2 * LANES, LANES), 'facet', split_ax...  8.39 us
    pallas_call x1, Pallas kernels, shards(): call(columns, shape((RADIX, 2 * LANES + 8, LANES)), [HBM] * 5, HBM, [pltp...  8.09 us
    all_to_all x1, starting transfers between devices, shards(): lax.all_to_all(back, 'facet', split_axis=0, concat_axis=0, tiled=True)  7.35 us
    unnamed x34, local copies, waits for them, and re-layouts  6.46 us
    ppermute x3, starting transfers between devices, shards(): pieces[k] = lax.ppermute(pieces[k], 'chan', pairs)  5.66 us
  transfers between devices with their start and end apart: 11, of which 6 were waited for; matrix products, arithmetic and copies ran while one was open for 0% of the time, Pallas kernels for 15%

profile of v12, /device:TPU:8, one launch (start us, length us, event | category | flops | bytes accessed | tf_op | source)
XLA Modules:
  0.0 110.5 jit_solution(16238943431687920948)
XLA Ops:
  0.6 3.7 %rows_forward.1 = f32[16,2,16,8,128]{4,3,2,1,0:T(8,128)} custom-call(f32[128,2048]{1,0:T(8,128)} %bitcast.5, f32[2,24,128]{2,1,0:T(8,128)} %constant.11.clone.twiddle_in.twiddle), custom_call_target="tpu_custom_call" | custom-call | tf_op jit(solution)/shard_map/rows_forward/pallas_call | solution.py:521
  4.3 0.0 copy-start.2
  4.3 0.0 copy-start
  4.3 8.4 %all-to-all-start = ((f32[16,256,128]{2,1,0:T(8,128)}), f32[16,256,128]{2,1,0:T(8,128)}, u32[]{:S(2)}, u32[]{:S(2)}) async-start(f32[16,256,128]{2,1,0:T(8,128)} %bitcast.7), calls=%async_computation | async-start | bytes 4194304 | tf_op jit(solution)/shard_map/all_to_all | solution.py:537
  12.7 0.0 copy-done.2
  12.7 0.9 cross_ready.1
  13.7 1.5 %collective-permute-start = (f32[128,512]{1,0:T(8,128)}, f32[128,512]{1,0:T(8,128)S(1)}, u32[]{:S(2)}, u32[]{:S(2)}) collective-permute-start(f32[128,512]{1,0:T(8,128)} %get-tuple-element.26), channel_id=1, source_target_pairs={{0,32},{16,48},{32,64},{48,80},{64,96},{80,112},{96,0},{112,16},{1... | collective-permute-start | bytes 786440 | tf_op jit(solution)/shard_map/ppermute | solution.py:554
  15.2 2.7 %collective-permute-start.1 = (f32[128,512]{1,0:T(8,128)}, f32[128,512]{1,0:T(8,128)S(1)}, u32[]{:S(2)}, u32[]{:S(2)}) collective-permute-start(f32[128,512]{1,0:T(8,128)} %get-tuple-element.27), channel_id=1, source_target_pairs={{0,64},{16,80},{32,96},{48,112},{64,0},{80,16},{96,32},{112,48},{1... | collective-permute-start | bytes 786440 | tf_op jit(solution)/shard_map/ppermute | solution.py:554
  17.9 1.4 %collective-permute-start.2 = (f32[128,512]{1,0:T(8,128)}, f32[128,512]{1,0:T(8,128)}, u32[]{:S(2)}, u32[]{:S(2)}) collective-permute-start(f32[128,512]{1,0:T(8,128)} %get-tuple-element.28), channel_id=1, source_target_pairs={{0,96},{16,112},{32,0},{48,16},{64,32},{80,48},{96,64},{112,80},{1... | collective-permute-start | bytes 786440 | tf_op jit(solution)/shard_map/ppermute | solution.py:554
  19.4 0.0 copy-done
  19.4 0.2 dual_edges.1
  19.5 1.9 %collective-permute-start.3 = (f32[8,256]{1,0:T(8,128)S(1)}, f32[8,256]{1,0:T(8,128)S(1)}, u32[]{:S(2)}, u32[]{:S(2)}) collective-permute-start(f32[8,256]{1,0:T(8,128)S(1)} %get-tuple-element.30.refs_5_), channel_id=1, source_target_pairs={{0,1},{1,2},{2,3},{3,4},{4,5},{5,6},{6,7},{7,8},{8,9},{9,10},{10,1... | collective-permute-start | bytes 24584 | tf_op jit(solution)/shard_map/ppermute | solution.py:491
  21.5 2.9 %collective-permute-start.4 = (f32[8,128]{1,0:T(8,128)S(1)}, f32[8,128]{1,0:T(8,128)S(1)}, u32[]{:S(2)}, u32[]{:S(2)}) collective-permute-start(f32[8,128]{1,0:T(8,128)S(1)} %get-tuple-element.32), channel_id=1, source_target_pairs={{0,16},{16,32},{32,48},{48,64},{64,80},{80,96},{96,112},{1,17},{17... | collective-permute-start | bytes 12296 | tf_op jit(solution)/shard_map/ppermute | solution.py:491
  24.4 4.2 %data_prepared.1 = (bf16[3,16,128,128]{3,2,1,0:T(8,128)(2,1)}, bf16[768,256]{1,0:T(8,128)(2,1)}, bf16[768,256]{1,0:T(8,128)(2,1)}, f32[8,128]{1,0:T(8,128)}) custom-call(bf16[2048,128]{1,0:T(8,128)(2,1)} %bitcast.9, bf16[2,2048,128]{2,1,0:T(8,128)(2,1)} %bitcast.8, bf16[128,128]{1,0:T(8,128)(2,1)} %constant.10.clone.place, ...), custom_call_target="tpu_custom_call" | custom-call | tf_op jit(solution)/shard_map/data_prepared/pallas_call | solution.py:555
  28.6 0.0 collective-permute-done.refs_1_
  28.6 1.5 %collective-permute-done.1.refs_2_ = f32[128,512]{1,0:T(8,128)S(1)} collective-permute-done((f32[128,512]{1,0:T(8,128)}, f32[128,512]{1,0:T(8,128)S(1)}, u32[]{:S(2)}, u32[]{:S(2)}) %collective-permute-start.1) | collective-permute-done | bytes 262176 | tf_op jit(solution)/shard_map/ppermute | solution.py:554
  30.1 0.0 collective-permute-done.2.refs_3_
  30.1 1.9 %swap_ready.1 = (f32[4,64,256]{2,1,0:T(8,128)}, f32[4,64,256]{2,1,0:T(8,128)}) custom-call(s32[1]{0:T(128)} %bitcast.2.where, f32[128,512]{1,0:T(8,128)S(1)} %get-tuple-element.25.refs_0_, f32[128,512]{1,0:T(8,128)S(1)} %collective-permute-done.refs_1_, f32[128,512]{1,0:T(8,128)S(1)} %collective-permute-done.1.refs_2_, ...), custom_call_target="tpu_custom_call" | custom-call | tf_op jit(solution)/shard_map/swap_ready/pallas_call | solution.py:568
  31.9 1.1 collective-permute-start.5
  33.0 0.0 collective-permute-done.4.refs_8_
  33.0 7.1 %collective-permute-done.3.refs_7_ = f32[8,256]{1,0:T(8,128)S(1)} collective-permute-done((f32[8,256]{1,0:T(8,128)S(1)}, f32[8,256]{1,0:T(8,128)S(1)}, u32[]{:S(2)}, u32[]{:S(2)}) %collective-permute-start.3) | collective-permute-done | bytes 8224 | tf_op jit(solution)/shard_map/ppermute | solution.py:491
  40.1 0.5 all-to-all-done.cols_in
  40.6 1.0 collective-permute-start.6
  41.7 8.1 %columns.1.value = f32[16,264,128]{2,1,0:T(8,128)} custom-call(f32[16,256,128]{2,1,0:T(8,128)} %all-to-all-done.cols_in, bf16[3,16,128,128]{3,2,1,0:T(8,128)(2,1)} %get-tuple-element.37.data_in, f32[2,24,128]{2,1,0:T(8,128)} %constant.11.clone.twiddle_in.twiddle, bf16[768,256]{1,0:T(8,128)(2,1)} %get-tuple-element.38.forward_in, ...), custom_call_target="tpu_custom_call" | custom-call | tf_op jit(solution)/shard_map/columns/pallas_call | solution.py:584
  49.8 0.0 copy-done.11
  49.8 0.0 collective-permute-done.5.early.refs_4_
  49.8 0.0 collective-permute-done.6.late.refs_5_
  49.8 0.0 copy-start.7
  49.8 0.0 copy-start.16
  49.8 0.6 copy-done.16
  50.5 0.0 copy-done.7
  50.5 7.3 %all-to-all-start.1 = ((f32[16,264,128]{2,1,0:T(8,128)}), f32[16,264,128]{2,1,0:T(8,128)S(1)}, u32[]{:S(2)}, u32[]{:S(2)}) async-start(f32[16,264,128]{2,1,0:T(8,128)} %tied.1), calls=%async_computation.1 | async-start | bytes 4325376 | tf_op jit(solution)/shard_map/all_to_all | solution.py:612
  57.8 0.0 copy-start.8
  57.9 0.9 copy-done.8
  58.8 0.9 copy-done.10
  59.8 0.9 copy-done.12
  60.7 0.9 copy-done.14
  61.7 1.7 %tile_ready.1 = (f32[8,128,256]{2,1,0:T(8,128)S(1)}, f32[8,128,256]{2,1,0:T(8,128)S(1)}, f32[8,256]{1,0:T(8,128)S(1)}, f32[8,128]{1,0:T(8,128)S(1)}) custom-call(s32[1]{0:T(128)} %bitcast.2.where, f32[128,512]{1,0:T(8,128)S(1)} %copy-done.10, f32[128,512]{1,0:T(8,128)S(1)} %copy-done.12, f32[128,512]{1,0:T(8,128)S(1)} %copy-done.14, ...), custom_call_target="tpu_custom_call" | custom-call | tf_op jit(solution)/shard_map/tile_ready/pallas_call | solution.py:613
  63.4 1.0 copy-done.3
  64.4 1.0 copy-done.5
  65.4 4.6 %collective-permute-start.7 = (f32[8,256]{1,0:T(8,128)S(1)}, f32[8,256]{1,0:T(8,128)S(1)}, u32[]{:S(2)}, u32[]{:S(2)}) collective-permute-start(f32[8,256]{1,0:T(8,128)S(1)} %get-tuple-element.44), channel_id=1, source_target_pairs={{1,0},{2,1},{3,2},{4,3},{5,4},{6,5},{7,6},{8,7},{9,8},{10,9},{11,1... | collective-permute-start | bytes 24584 | tf_op jit(solution)/shard_map/ppermute | solution.py:491
  70.0 1.5 %collective-permute-start.8 = (f32[8,128]{1,0:T(8,128)S(1)}, f32[8,128]{1,0:T(8,128)S(1)}, u32[]{:S(2)}, u32[]{:S(2)}) collective-permute-start(f32[8,128]{1,0:T(8,128)S(1)} %get-tuple-element.45), channel_id=1, source_target_pairs={{16,0},{32,16},{48,32},{64,48},{80,64},{96,80},{112,96},{17,1},{33... | collective-permute-start | bytes 12296 | tf_op jit(solution)/shard_map/ppermute | solution.py:491
  71.5 4.4 %collective-permute-done.8.after_two.right = f32[8,128]{1,0:T(8,128)S(1)} collective-permute-done((f32[8,128]{1,0:T(8,128)S(1)}, f32[8,128]{1,0:T(8,128)S(1)}, u32[]{:S(2)}, u32[]{:S(2)}) %collective-permute-start.8) | collective-permute-done | bytes 4128 | tf_op jit(solution)/shard_map/ppermute | solution.py:491
  75.9 6.1 %collective-permute-done.7.after_one.below = f32[8,256]{1,0:T(8,128)S(1)} collective-permute-done((f32[8,256]{1,0:T(8,128)S(1)}, f32[8,256]{1,0:T(8,128)S(1)}, u32[]{:S(2)}, u32[]{:S(2)}) %collective-permute-start.7) | collective-permute-done | bytes 8224 | tf_op jit(solution)/shard_map/ppermute | solution.py:491
  82.0 4.2 %all-to-all-done.1.lines = f32[16,264,128]{2,1,0:T(8,128)S(1)} async-done(((f32[16,264,128]{2,1,0:T(8,128)}), f32[16,264,128]{2,1,0:T(8,128)S(1)}, u32[]{:S(2)}, u32[]{:S(2)}) %all-to-all-start.1) | async-done | bytes 2162720 | tf_op jit(solution)/shard_map/all_to_all | solution.py:612
  86.2 1.5 %rows_back.1 = f32[8,136,256]{2,1,0:T(8,128)S(1)} custom-call(f32[16,264,128]{2,1,0:T(8,128)S(1)} %all-to-all-done.1.lines, f32[2,24,128]{2,1,0:T(8,128)S(1)} %copy-done.15, f32[8,256]{1,0:T(8,128)S(1)} %collective-permute-done.7.after_one.below, f32[8,128]{1,0:T(8,128)S(1)} %collective-permute-done.8.after_two.right), custom_call_target="tpu_custom_call" | custom-call | tf_op jit(solution)/shard_map/rows_back/pallas_call | solution.py:627
  87.7 20.3 %all_to_all.15.gradient = f32[8,136,256]{2,1,0:T(8,128)S(1)} all-to-all(f32[8,136,256]{2,1,0:T(8,128)S(1)} %rows_back.1), channel_id=1, replica_groups=mesh['chan'=8,'facet'=16] {'chan'}, dimensions={0} | all-to-all | bytes 2228224 | tf_op jit(solution)/shard_map/all_to_all | solution.py:638
  108.0 2.3 %finish.1 = (f32[8,128,256]{2,1,0:T(8,128)}, bf16[8,2,128,256]{3,2,1,0:T(8,128)(2,1)}) custom-call(f32[8,136,256]{2,1,0:T(8,128)S(1)} %all_to_all.15.gradient, f32[8,128,256]{2,1,0:T(8,128)S(1)} %copy-done.4, f32[8,128,256]{2,1,0:T(8,128)S(1)} %copy-done.6, bf16[8,2,128,256]{3,2,1,0:T(8,128)(2,1)S(1)} %copy-done.1, ...), custom_call_target="tpu_custom_call" | custom-call | tf_op jit(solution)/shard_map/finish/pallas_call | solution.py:639
  (20 shorter events, 0.0 us)
Async XLA Ops:
  4.3 8.4 %copy-start.2 = (f32[1,128,2048]{2,1,0:T(8,128)S(1)}, f32[1,128,2048]{2,1,0:T(8,128)}, u32[]{:S(2)}) copy-start(f32[1,128,2048]{2,1,0:T(8,128)} %param.6) | copy-start | bytes 3145732
  4.3 15.0 %copy-start = (bf16[8,2,128,256]{3,2,1,0:T(8,128)(2,1)S(1)}, bf16[8,2,128,256]{3,2,1,0:T(8,128)(2,1)}, u32[]{:S(2)}) copy-start(bf16[8,2,128,256]{3,2,1,0:T(8,128)(2,1)} %dual.3) | copy-start | bytes 3145732
  4.3 36.3 %all-to-all-start = ((f32[16,256,128]{2,1,0:T(8,128)}), f32[16,256,128]{2,1,0:T(8,128)}, u32[]{:S(2)}, u32[]{:S(2)}) async-start(f32[16,256,128]{2,1,0:T(8,128)} %bitcast.7), calls=%async_computation | async-start | bytes 4194304 | tf_op jit(solution)/shard_map/all_to_all | solution.py:537
  13.7 26.9 %copy-start.9 = (f32[128,512]{1,0:T(8,128)}, f32[128,512]{1,0:T(8,128)S(1)}, u32[]{:S(2)}) copy-start(f32[128,512]{1,0:T(8,128)S(1)} %get-tuple-element.25.refs_0_) | copy-start | bytes 786436
  13.7 14.9 %collective-permute-start = (f32[128,512]{1,0:T(8,128)}, f32[128,512]{1,0:T(8,128)S(1)}, u32[]{:S(2)}, u32[]{:S(2)}) collective-permute-start(f32[128,512]{1,0:T(8,128)} %get-tuple-element.26), channel_id=1, source_target_pairs={{0,32},{16,48},{32,64},{48,80},{64,96},{80,112},{96,0},{112,16},{1... | collective-permute-start | bytes 786440 | tf_op jit(solution)/shard_map/ppermute | solution.py:554
  15.2 14.9 %collective-permute-start.1 = (f32[128,512]{1,0:T(8,128)}, f32[128,512]{1,0:T(8,128)S(1)}, u32[]{:S(2)}, u32[]{:S(2)}) collective-permute-start(f32[128,512]{1,0:T(8,128)} %get-tuple-element.27), channel_id=1, source_target_pairs={{0,64},{16,80},{32,96},{48,112},{64,0},{80,16},{96,32},{112,48},{1... | collective-permute-start | bytes 786440 | tf_op jit(solution)/shard_map/ppermute | solution.py:554
  17.9 12.2 %collective-permute-start.2 = (f32[128,512]{1,0:T(8,128)}, f32[128,512]{1,0:T(8,128)}, u32[]{:S(2)}, u32[]{:S(2)}) collective-permute-start(f32[128,512]{1,0:T(8,128)} %get-tuple-element.28), channel_id=1, source_target_pairs={{0,96},{16,112},{32,0},{48,16},{64,32},{80,48},{96,64},{112,80},{1... | collective-permute-start | bytes 786440 | tf_op jit(solution)/shard_map/ppermute | solution.py:554
  19.5 20.6 %collective-permute-start.3 = (f32[8,256]{1,0:T(8,128)S(1)}, f32[8,256]{1,0:T(8,128)S(1)}, u32[]{:S(2)}, u32[]{:S(2)}) collective-permute-start(f32[8,256]{1,0:T(8,128)S(1)} %get-tuple-element.30.refs_5_), channel_id=1, source_target_pairs={{0,1},{1,2},{2,3},{3,4},{4,5},{5,6},{6,7},{7,8},{8,9},{9,10},{10,1... | collective-permute-start | bytes 24584 | tf_op jit(solution)/shard_map/ppermute | solution.py:491
  21.5 11.5 %collective-permute-start.4 = (f32[8,128]{1,0:T(8,128)S(1)}, f32[8,128]{1,0:T(8,128)S(1)}, u32[]{:S(2)}, u32[]{:S(2)}) collective-permute-start(f32[8,128]{1,0:T(8,128)S(1)} %get-tuple-element.32), channel_id=1, source_target_pairs={{0,16},{16,32},{32,48},{48,64},{64,80},{80,96},{96,112},{1,17},{17... | collective-permute-start | bytes 12296 | tf_op jit(solution)/shard_map/ppermute | solution.py:491
  28.6 21.2 %copy-start.11 = (f32[128,512]{1,0:T(8,128)}, f32[128,512]{1,0:T(8,128)S(1)}, u32[]{:S(2)}) copy-start(f32[128,512]{1,0:T(8,128)S(1)} %collective-permute-done.refs_1_) | copy-start | bytes 786436
  30.1 1.9 %copy-start.13 = (f32[128,512]{1,0:T(8,128)}, f32[128,512]{1,0:T(8,128)S(1)}, u32[]{:S(2)}) copy-start(f32[128,512]{1,0:T(8,128)S(1)} %collective-permute-done.1.refs_2_) | copy-start | bytes 786436
  31.9 17.8 %collective-permute-start.5 = (f32[4,64,256]{2,1,0:T(8,128)}, f32[4,64,256]{2,1,0:T(8,128)S(1)}, u32[]{:S(2)}, u32[]{:S(2)}) collective-permute-start(f32[4,64,256]{2,1,0:T(8,128)} %get-tuple-element.40), channel_id=1, source_target_pairs={{0,16},{16,0},{32,48},{48,32},{64,80},{80,64},{96,112},{112,96},{1... | collective-permute-start | bytes 786440 | tf_op jit(solution)/shard_map/ppermute | solution.py:576
  40.6 9.1 %collective-permute-start.6 = (f32[4,64,256]{2,1,0:T(8,128)}, f32[4,64,256]{2,1,0:T(8,128)S(1)}, u32[]{:S(2)}, u32[]{:S(2)}) collective-permute-start(f32[4,64,256]{2,1,0:T(8,128)} %get-tuple-element.41), channel_id=1, source_target_pairs={{0,16},{16,0},{32,48},{48,32},{64,80},{80,64},{96,112},{112,96},{1... | collective-permute-start | bytes 786440 | tf_op jit(solution)/shard_map/ppermute | solution.py:580
  49.8 0.7 copy-start.7
  49.8 0.6 copy-start.16
  50.5 7.4 %copy-start.1 = (bf16[8,2,128,256]{3,2,1,0:T(8,128)(2,1)S(1)}, bf16[8,2,128,256]{3,2,1,0:T(8,128)(2,1)}, u32[]{:S(2)}) copy-start(bf16[8,2,128,256]{3,2,1,0:T(8,128)(2,1)} %dual.3) | copy-start | bytes 3145732
  50.5 35.7 %all-to-all-start.1 = ((f32[16,264,128]{2,1,0:T(8,128)}), f32[16,264,128]{2,1,0:T(8,128)S(1)}, u32[]{:S(2)}, u32[]{:S(2)}) async-start(f32[16,264,128]{2,1,0:T(8,128)} %tied.1), calls=%async_computation.1 | async-start | bytes 4325376 | tf_op jit(solution)/shard_map/all_to_all | solution.py:612
  57.8 1.0 copy-start.8
  58.8 0.9 copy-start.10
  59.8 0.9 copy-start.12
  60.7 0.9 copy-start.14
  61.7 24.5 %copy-start.15 = (f32[2,24,128]{2,1,0:T(8,128)S(1)}, f32[2,24,128]{2,1,0:T(8,128)}, u32[]{:S(2)}) copy-start(f32[2,24,128]{2,1,0:T(8,128)} %constant.11.clone.twiddle_in.twiddle) | copy-start | bytes 73732
  63.4 1.0 copy-start.3
  64.4 1.0 copy-start.5
  65.4 16.6 %collective-permute-start.7 = (f32[8,256]{1,0:T(8,128)S(1)}, f32[8,256]{1,0:T(8,128)S(1)}, u32[]{:S(2)}, u32[]{:S(2)}) collective-permute-start(f32[8,256]{1,0:T(8,128)S(1)} %get-tuple-element.44), channel_id=1, source_target_pairs={{1,0},{2,1},{3,2},{4,3},{5,4},{6,5},{7,6},{8,7},{9,8},{10,9},{11,1... | collective-permute-start | bytes 24584 | tf_op jit(solution)/shard_map/ppermute | solution.py:491
  70.0 5.9 %collective-permute-start.8 = (f32[8,128]{1,0:T(8,128)S(1)}, f32[8,128]{1,0:T(8,128)S(1)}, u32[]{:S(2)}, u32[]{:S(2)}) collective-permute-start(f32[8,128]{1,0:T(8,128)S(1)} %get-tuple-element.45), channel_id=1, source_target_pairs={{16,0},{32,16},{48,32},{64,48},{80,64},{96,80},{112,96},{17,1},{33... | collective-permute-start | bytes 12296 | tf_op jit(solution)/shard_map/ppermute | solution.py:491
  86.2 21.9 %copy-start.4 = (f32[8,128,256]{2,1,0:T(8,128)S(1)}, f32[8,128,256]{2,1,0:T(8,128)}, u32[]{:S(2)}) copy-start(f32[8,128,256]{2,1,0:T(8,128)} %copy-done.3) | copy-start | bytes 3145732
  86.2 21.9 %copy-start.6 = (f32[8,128,256]{2,1,0:T(8,128)S(1)}, f32[8,128,256]{2,1,0:T(8,128)}, u32[]{:S(2)}) copy-start(f32[8,128,256]{2,1,0:T(8,128)} %copy-done.5) | copy-start | bytes 3145732
